TPU v7x, 32 devices: a whole 2x2x4 slice. The times are simulated.
32 devices in a mesh: groups: 2 (over y), tm: 16 (over z, x, core).
Axes of the slice: x: 2, y: 2, z: 4, core: 2. Of those that a mesh axis runs over, the one named last changes fastest.
Arguments:
- frames: bfloat16 [128, 2, 4, 64, 128], P(('groups', 'tm')), parts along dimension 0, may hold values from -6 to 6
- row_halo: bfloat16 [128, 2, 2, 64, 128], P(('groups', 'tm')), parts along dimension 0, may hold values from -6 to 6
- clip_start: int32 [128], P(('groups', 'tm')), parts along dimension 0, may hold values from 0 to 1
- slab_counts: int32 [32], P(('groups', 'tm')), parts along dimension 0, may hold values from 0 to 4, as said below
- conv_weight: bfloat16 [3, 3, 3, 128, 128], replicated, may hold values from -0.109375 to 0.109375
- conv_bias: float32 [128], replicated, may hold values from -3 to 3
- stride_weight: bfloat16 [2, 128, 128], replicated, may hold values from -0.375 to 0.375
- stride_bias: float32 [128], replicated, may hold values from -3 to 3
- cotangent: bfloat16 [128, 1, 4, 64, 128], P(('groups', 'tm')), parts along dimension 0, may hold values from -6 to 6
Outputs:
- latents: bfloat16 [128, 1, 4, 64, 128], P(('groups', 'tm')), parts along dimension 0
- frames_grad: bfloat16 [128, 2, 4, 64, 128], P(('groups', 'tm')), parts along dimension 0
- conv_weight_grad: float32 [6, 3, 3, 128, 128], P('groups'), parts along dimension 0
- conv_bias_grad: float32 [256], P('groups'), parts along dimension 0
- stride_weight_grad: float32 [4, 128, 128], P('groups'), parts along dimension 0
- stride_bias_grad: float32 [256], P('groups'), parts along dimension 0
There are 2 independent parts, one for each index of `groups`. A program takes and returns all parts, laid end to end along the dimension named above; an argument that names none is the same for every part. Nothing has to cross between parts.
Inputs may be any that keep to these rules, and one draw needn't show every extreme that they name: `slab_counts`: the filled slots of a device are its first ones. In every draw some device has all 4 slots filled and some device has none.
All inputs are finite; a program needn't handle non-finite values.
Results may differ from a plain program's by a relative error of at most 0.0055.
Values may be sent and summed in bfloat16 or wider, within the bound.
No kernel may reach another device: no remote copies, remote signals or barrier semaphores. Data moves between devices by JAX's collectives and lax.ppermute only.
A program may use at most 192 MiB of HBM per device.

v0:
```python
import jax
import jax.numpy as jnp
from jax import lax
from jax.sharding import PartitionSpec as P


def carried_in(value, axis, join, neutral):
    count, mine = (lax.axis_size(axis), lax.axis_index(axis))
    pieces = jax.tree.map(lambda part: lax.all_gather(part, axis), value)
    total = jax.tree.map(
        lambda part, zero: jnp.full_like(part, 0) + jnp.asarray(zero, part.dtype), value, neutral
    )

    def step(position, total):
        longer = join(total, jax.tree.map(lambda part: part[position], pieces))
        return jax.tree.map(lambda new, old: jnp.where(position < mine, new, old), longer, total)

    return lax.fori_loop(0, count - 1, step, total)


def carried_in_2(x, axis, combine, identity):
    size, place = (lax.axis_size(axis), lax.axis_index(axis))
    everything = jax.tree.map(
        lambda part, kind: lax.all_gather(part.astype(kind), axis), x, (jnp.bfloat16, jnp.bfloat16)
    )
    start = jax.tree.map(
        lambda part, zero: jnp.broadcast_to(jnp.asarray(zero, part.dtype), part.shape), x, identity
    )

    def step(k, before):
        at = size - 1 - k
        reached = at > place
        new = combine(
            before, jax.tree.map(lambda part, own: part[at].astype(own.dtype), everything, x)
        )
        return jax.tree.map(lambda a, b: jnp.where(reached, a, b), new, before)

    return lax.fori_loop(0, size, step, start)


def forward_conv(extended, weight):
    return lax.conv_general_dilated(
        extended,
        weight,
        (1, 1, 1),
        ((0, 0), (0, 0), (1, 1)),
        dimension_numbers=("NDHWC", "DHWIO", "NDHWC"),
        preferred_element_type=jnp.float32,
    )


def input_grad(grad_pre, weight):
    flipped = jnp.transpose(weight[::-1, ::-1, ::-1], (0, 1, 2, 4, 3))
    return lax.conv_general_dilated(
        grad_pre,
        flipped,
        (1, 1, 1),
        ((2, 2), (2, 2), (1, 1)),
        dimension_numbers=("NDHWC", "DHWIO", "NDHWC"),
        preferred_element_type=jnp.float32,
    )


def weight_grad(extended, grad_pre):
    return lax.conv_general_dilated(
        extended,
        grad_pre,
        (1, 1, 1),
        ((0, 0), (0, 0), (1, 1)),
        dimension_numbers=("CDHWN", "IDHWO", "DHWNC"),
        preferred_element_type=jnp.float32,
    )


def newest(earlier, later):
    taken = later[1][0] > 0
    picked = lax.cond(taken, lambda: later[0], lambda: earlier[0])
    return (picked, jnp.maximum(earlier[1], later[1]))


def body(
    frames,
    row_halo,
    clip_start,
    slab_counts,
    conv_weight,
    conv_bias,
    stride_weight,
    stride_bias,
    cotangent,
):
    slot_count, frame_count, row_count, column_count, channel_count = frames.shape
    count = slab_counts[0]
    place = jnp.arange(slot_count, dtype=jnp.int32)
    filled_mask = (place < count)[:, None, None, None, None]
    latest_mask = (place == count - 1)[:, None, None, None, None]
    carried_mask = (clip_start == 0)[:, None, None, None, None]
    live = count > 0
    bordered = jnp.concatenate([row_halo[:, :, :1], frames, row_halo[:, :, 1:]], axis=2)
    own_tail = jnp.sum(jnp.where(latest_mask, bordered, jnp.zeros_like(bordered)), axis=0)
    live_flag = jnp.where(live, 1.0, 0.0).astype(jnp.bfloat16).reshape(1)
    arrived, _ = carried_in(
        (own_tail, live_flag), "tm", newest, (jnp.zeros_like(own_tail), jnp.zeros_like(live_flag))
    )
    previous = jnp.concatenate([arrived[None], bordered[:-1]], axis=0)
    previous = jnp.where(carried_mask, previous, jnp.zeros_like(previous))
    extended = jnp.concatenate([previous, bordered], axis=1)
    pre_act = forward_conv(extended, conv_weight) + conv_bias
    squash = jax.nn.sigmoid(pre_act)
    hidden = (pre_act * squash).astype(jnp.bfloat16)
    paired = hidden.reshape(slot_count, frame_count // 2, 2, row_count, column_count, channel_count)
    outputs = (
        jnp.einsum("stkhwc,kcd->sthwd", paired, stride_weight, preferred_element_type=jnp.float32)
        + stride_bias
    )
    latents = jnp.where(filled_mask, outputs, jnp.zeros_like(outputs)).astype(jnp.bfloat16)
    grad_out = jnp.where(filled_mask, cotangent, jnp.zeros_like(cotangent))
    grad_hidden = jnp.einsum(
        "sthwd,kcd->stkhwc", grad_out, stride_weight, preferred_element_type=jnp.float32
    )
    grad_hidden = grad_hidden.reshape(
        slot_count, frame_count, row_count, column_count, channel_count
    )
    stride_weight_grad = jnp.einsum(
        "stkhwc,sthwd->kcd", paired, grad_out, preferred_element_type=jnp.float32
    )
    stride_bias_grad = jnp.sum(grad_out, axis=(0, 1, 2, 3), dtype=jnp.float32)
    grad_pre = (grad_hidden * squash * (1.0 + pre_act * (1.0 - squash))).astype(jnp.bfloat16)
    conv_bias_grad = jnp.sum(grad_pre, axis=(0, 1, 2, 3), dtype=jnp.float32)
    conv_weight_grad = weight_grad(extended, grad_pre)
    extended_grad = input_grad(grad_pre, conv_weight)[:, :, 1 : row_count + 1]
    cache_grad = jnp.where(carried_mask, extended_grad[:, :2], jnp.zeros_like(extended_grad[:, :2]))
    within = jnp.concatenate([cache_grad[1:], jnp.zeros_like(cache_grad[:1])], axis=0)
    image_flag = jnp.where(live, 1.0, 0.0).astype(jnp.float32).reshape(1)
    returned, _ = carried_in_2(
        (cache_grad[0], image_flag),
        "tm",
        newest,
        (jnp.zeros_like(cache_grad[0]), jnp.zeros_like(image_flag)),
    )
    tail_grad = within + jnp.where(latest_mask, returned[None], jnp.zeros_like(within))
    head_zeros = jnp.zeros(
        (slot_count, frame_count - 2, row_count, column_count, channel_count), jnp.float32
    )
    frame_grad = extended_grad[:, 2:] + jnp.concatenate([head_zeros, tail_grad], axis=1)
    frames_grad = jnp.where(filled_mask, frame_grad, jnp.zeros_like(frame_grad)).astype(
        jnp.bfloat16
    )
    conv_weight_grad, conv_bias_grad, stride_weight_grad, stride_bias_grad = lax.psum(
        (conv_weight_grad, conv_bias_grad, stride_weight_grad, stride_bias_grad), "tm"
    )
    return (
        latents,
        frames_grad,
        conv_weight_grad,
        conv_bias_grad,
        stride_weight_grad,
        stride_bias_grad,
    )


def solution(mesh):
    return jax.shard_map(
        body,
        mesh=mesh,
        in_specs=(
            P(("groups", "tm"), None, None, None, None),
            P(("groups", "tm"), None, None, None, None),
            P(("groups", "tm")),
            P(("groups", "tm")),
            P(),
            P(),
            P(),
            P(),
            P(("groups", "tm"), None, None, None, None),
        ),
        out_specs=(
            P(("groups", "tm"), None, None, None, None),
            P(("groups", "tm"), None, None, None, None),
            P("groups", None, None, None, None),
            P("groups"),
            P("groups", None, None),
            P("groups"),
        ),
        check_vma=False,
    )
```

profile of v0, /device:TPU:0, one launch (start us, length us, event | category | flops | bytes accessed | tf_op | source)
XLA Modules:
  0.0 270.0 jit_solution(11149357752147009259)
XLA Ops:
  8.0 1.0 fusion.46
  9.1 1.5 copy_dynamic-update-slice_fusion
  10.8 1.8 select_reduce_fusion
  14.0 35.3 %all-reduce.1 = bf16[16]{0:T(256)(128)(2,1)S(1)} all-reduce(bf16[16]{0:T(256)(128)(2,1)S(1)} %dynamic-update-slice), channel_id=1, replica_groups=mesh['groups'=2,'tm'=16] {'tm'}, use_global_device_ids=true, to_apply=%add.1 | all-reduce | flops 16 | bytes 64
  49.6 11.3 %all-gather.6.cloned.1.call-done = bf16[32,6,64,128]{3,2,1,0:T(8,128)(2,1)} async-done(((bf16[2,6,64,128]{3,2,1,0:T(8,128)(2,1)}), bf16[32,6,64,128]{3,2,1,0:T(8,128)(2,1)}) %all-gather.6.cloned.1.call-update) | async-done | bytes 3145744 | tf_op jit(solution)/shard_map/all_gather | solution.py:9
  60.9 30.9 %while.36 = (s32[]{:T(128)}, bf16[2,6,64,128]{3,2,1,0:T(8,128)(2,1)S(1)}, s32[]{:T(128)}, bf16[16,1]{0,1:T(2,128)(2,1)S(1)}, bf16[16,2,6,64,128]{4,3,2,1,0:T(8,128)(2,1)}, /*index=5*/s32[]{:T(128)}, s32[]{:T(128)}) while((s32[]{:T(128)}, bf16[2,6,64,128]{3,2,1,0:T(8,128)(2,1)S(1)}, s32[]{:T(128)}, bf16[16,1]{0,1:T(2,128)(2,1)S(1)}, ...), condition=%wide.region_4.5_spmd.clone, body=%wide.region_1.4_spmd.clone.sunk | while | flops 294920 | bytes 1376394 | solution.py:18
  62.2 1.0 conditional.6
  62.2 0.9 dynamic-slice_bitcast_fusion
  69.9 1.0 conditional.6
  69.9 0.9 dynamic-slice_bitcast_fusion
  72.2 1.0 conditional.6
  72.2 0.9 dynamic-slice_bitcast_fusion
  74.5 1.0 conditional.6
  74.5 0.9 dynamic-slice_bitcast_fusion
  76.8 1.0 conditional.6
  76.8 0.9 dynamic-slice_bitcast_fusion
  79.1 1.0 conditional.6
  79.1 0.9 dynamic-slice_bitcast_fusion
  81.4 1.0 conditional.6
  81.4 0.9 dynamic-slice_bitcast_fusion
  83.7 1.0 conditional.6
  83.7 0.9 dynamic-slice_bitcast_fusion
  86.0 1.0 conditional.6
  86.0 0.9 dynamic-slice_bitcast_fusion
  88.3 1.0 conditional.6
  88.3 0.9 dynamic-slice_bitcast_fusion
  90.6 1.0 conditional.6
  90.6 0.9 dynamic-slice_bitcast_fusion
  94.0 1.0 fusion.33
  96.4 5.5 %add_divide_fusion = (f32[2,4,32,9,128]{4,2,3,1,0:T(8,128)S(1)}, f32[2,4,32,9,128]{4,2,3,1,0:T(8,128)S(1)}, bf16[2,4,32,9,128]{4,2,3,1,0:T(8,128)(2,1)}) fusion(f32[128]{0:T(128)S(1)} %copy-done.12, bf16[3,3,3,128,128]{4,3,2,1,0:T(8,128)(2,1)S(1)} %copy-done, bf16[4,6,4,7,2,128]{5,3,2,4,1,0:T(8,128)(2,1)S(1)} %slice.44, ...), kind=kOutput, calls=%fused_computation.33 | convolution fusion | flops 2047868928 | bytes 5948192 | tf_op jit(solution)/shard_map/conv_general_dilated | solution.py:42
  106.1 9.3 %convolution_select_fusion = f32[4,4,32,9,128]{4,2,3,1,0:T(8,128)S(1)} fusion(bf16[3,3,3,128,128]{4,3,2,1,0:T(8,128)(2,1)S(1)} %copy-done, pred[32,9]{0,1:T(8,128)(4,1)S(1)} %copy-done.10, bf16[2,4,4,8,11,128]{5,2,4,3,1,0:T(4,128)(2,1)S(1)} %fusion.26), kind=kOutput, calls=%fused_computation.16 | convolution fusion | flops 1699282944 | bytes 3965216 | tf_op jit(solution)/shard_map/slice | solution.py:131
  115.6 1.4 fusion.43
  118.5 9.1 %fusion.31 = f32[3,3,3,128,128]{4,3,2,1,0:T(8,128)} fusion(bf16[4,2,4,64,128]{4,3,1,2,0:T(8,128)(2,1)} %copy-done.4, bf16[4,2,6,64,128]{4,0,3,2,1:T(4,128)(2,1)S(1)} %copy_dynamic-update-slice_fusion.1, bf16[4,2,6,64,128]{4,0,3,2,1:T(4,128)(2,1)} %copy-done.3), kind=kOutput, calls=%fused_computation.54 | convolution fusion | flops 1796210688 | bytes 3866624 | tf_op jit(solution)/shard_map/conv_general_dilated | solution.py:65
  127.9 1.0 slice.45
  129.8 0.9 slice.53
  130.7 1.8 copy.64
  132.5 32.1 %all-reduce.2 = (f32[128]{0:T(128)}, f32[128]{0:T(128)}) all-reduce(f32[128]{0:T(128)S(1)} %get-tuple-element.378, f32[128]{0:T(128)S(1)} %convert_reduce_fusion.1), channel_id=1, replica_groups=mesh['groups'=2,'tm'=16] {'tm'}, use_global_device_ids=true, to_apply=%region_11.12 | all-reduce | flops 256 | bytes 2048 | tf_op jit(solution)/shard_map/psum | solution.py:149
  164.6 1.0 fusion.21
  165.7 1.0 convolution_bitcast_fusion.2
  166.8 3.5 %copy.68 = bf16[16,2,4,64,128]{4,3,2,1,0:T(8,128)(2,1)} copy(bf16[16,2,4,64,128]{4,2,3,0,1:T(4,128)(2,1)} %all-gather.4.cloned.1.call-done) | data formatting | bytes 4194304
  170.3 33.8 %while.37 = (s32[]{:T(128)}, f32[2,4,64,128]{3,2,1,0:T(8,128)S(1)}, s32[]{:T(128)}, bf16[16,1]{0,1:T(2,128)(2,1)S(1)}, bf16[16,2,4,64,128]{4,3,2,1,0:T(8,128)(2,...) while((s32[]{:T(128)}, f32[2,4,64,128]{3,2,1,0:T(8,128)S(1)}, s32[]{:T(128)}, ...), condition=%wide.region_8.9_spmd.clone, body=%wide.region_5.8_spmd.clone.sunk | while | flops 262155 | bytes 1704136 | solution.py:38
  171.5 0.9 conditional.7
  173.9 1.0 conditional.7
  173.9 0.9 bitcast_convert_fusion
  176.2 1.0 conditional.7
  176.2 0.9 bitcast_convert_fusion
  178.6 0.9 conditional.7
  180.9 1.0 conditional.7
  180.9 0.9 bitcast_convert_fusion
  183.2 1.0 conditional.7
  183.3 0.9 bitcast_convert_fusion
  185.6 1.0 conditional.7
  185.6 0.9 bitcast_convert_fusion
  187.9 0.9 conditional.7
  190.3 1.0 conditional.7
  190.3 0.9 bitcast_convert_fusion
  192.6 1.0 conditional.7
  192.7 0.9 bitcast_convert_fusion
  195.0 0.9 conditional.7
  203.0 0.9 conditional.7
  203.0 0.9 bitcast_convert_fusion
  204.2 1.6 fusion.25
  206.7 53.2 %all-reduce.6.cloned.1.call-done = (f32[3,3,3,128,128]{4,3,2,1,0:T(8,128)}, f32[2,128,128]{2,1,0:T(8,128)}) async-done(((f32[3,3,3,128,128]{4,3,2,1,0:T(8,128)}, f32[2,128,128]{2,1,0:T(8,128)}), (f32[3,3,3,128,128]{4,3,2,1,0:T(8,128)}, f32[2,128,128]{2,1,0:T(8,128)})) %all-reduce.6.cloned.1.call-update) | async-done | bytes 1900560 | tf_op jit(solution)/shard_map/psum | solution.py:149
  259.9 2.9 %copy.136 = f32[3,3,3,128,128]{4,3,2,1,0:T(8,128)} copy(f32[3,3,3,128,128]{4,3,2,1,0:T(8,128)} %get-tuple-element.494) | data formatting | bytes 3538944
  (176 shorter events, 38.8 us)
Async XLA Ops:
  7.2 89.1 %copy-start = (bf16[3,3,3,128,128]{4,3,2,1,0:T(8,128)(2,1)S(1)}, bf16[3,3,3,128,128]{4,3,2,1,0:T(8,128)(2,1)}, u32[]{:S(2)}) copy-start(bf16[3,3,3,128,128]{4,3,2,1,0:T(8,128)(2,1)} %param.21) | copy-start | bytes 2654212
  7.2 53.7 %all-gather.6.cloned.1.call-start = ((), (), s32[]{:S(2)}) async-start(), calls=%async_computation.1 | async-start | bytes 3342336 | tf_op jit(solution)/shard_map/all_gather | solution.py:9
  7.9 4.7 %copy-start.14 = (u32[32]{0:T(128)S(1)}, u32[32]{0:T(128)}, u32[]{:S(2)}) copy-start(u32[32]{0:T(128)} %constant.131) | copy-start | bytes 388
  8.0 41.4 %copy-start.5 = (bf16[4,1,4,64,128]{4,3,2,1,0:T(8,128)(2,1)S(1)}, bf16[4,1,4,64,128]{4,3,2,1,0:T(8,128)(2,1)}, u32[]{:S(2)}) copy-start(bf16[4,1,4,64,128]{4,3,2,1,0:T(8,128)(2,1)} %param.25) | copy-start | bytes 786436
  9.0 40.6 %copy-start.11 = (s32[4]{0:T(128)S(1)}, s32[4]{0:T(128)}, u32[]{:S(2)}) copy-start(s32[4]{0:T(128)} %param.19) | copy-start | bytes 52
  12.6 154.1 %all-gather.4.cloned.1.call-start = ((), (), s32[]{:S(2)}) async-start(), calls=%async_computation | async-start | bytes 2228224 | tf_op jit(solution)/shard_map/all_gather | solution.py:24
  93.1 0.9 copy-start.3
  95.7 0.7 copy-start.10
  95.7 0.7 copy-start.12
  103.5 0.8 copy-start.9
  104.9 0.8 copy-start.4
  118.2 141.7 %all-reduce.6.cloned.1.call-start = ((), (), s32[]{:S(2)}) async-start(), calls=%async_computation.2 | async-start | bytes 3801088 | tf_op jit(solution)/shard_map/psum | solution.py:149
  118.5 9.1 %copy-start.6 = (bf16[2,4,32,9,128]{4,2,3,1,0:T(8,128)(2,1)S(1)}, bf16[2,4,32,9,128]{4,2,3,1,0:T(8,128)(2,1)}, u32[]{:S(2)}) copy-start(bf16[2,4,32,9,128]{4,2,3,1,0:T(8,128)(2,1)} %get-tuple-element.375) | copy-start | bytes 1769476
  127.6 1.3 copy-start.1
  130.7 33.9 %copy-start.7 = (bf16[2,4,4,64,128]{4,1,3,2,0:T(4,128)(2,1)S(1)}, bf16[2,4,4,64,128]{4,1,3,2,0:T(4,128)(2,1)}, u32[]{:S(2)}) copy-start(bf16[2,4,4,64,128]{4,1,3,2,0:T(4,128)(2,1)} %slice.45) | copy-start | bytes 1572868
  130.7 33.9 %copy-start.13 = (f32[128]{0:T(128)S(1)}, f32[128]{0:T(128)}, u32[]{:S(2)}) copy-start(f32[128]{0:T(128)} %param.24) | copy-start | bytes 1540
  170.3 33.9 %copy-start.2 = (f32[2,4,32,9,128]{4,1,3,2,0:T(4,128)S(1)}, f32[2,4,32,9,128]{4,1,3,2,0:T(4,128)}, u32[]{:S(2)}) copy-start(f32[2,4,32,9,128]{4,1,3,2,0:T(4,128)} %copy.64) | copy-start | bytes 3538948
  259.9 2.9 %copy-start.8 = (f32[2,128,128]{2,1,0:T(8,128)S(1)}, f32[2,128,128]{2,1,0:T(8,128)}, u32[]{:S(2)}) copy-start(f32[2,128,128]{2,1,0:T(8,128)} %get-tuple-element.496) | copy-start | bytes 393220
Sparse Core Ops, SparseCore 0:
  12.7 48.1 all-gather.5
  118.3 39.3 all-gather.3
  166.9 93.0 all-reduce.5
where the time goes:
time: 270 us
  blocking collectives  67.5 us (25%)
  waiting for transfers between devices  64.5 us (24%)
  other arithmetic  39.3 us (15%)
  local copies, waits for them, and re-layouts  34.8 us (13%)
  matrix products  26.5 us (10%)
  loops' own time  22.3 us (8%)
  between operations  14.8 us (5%)
    psum x1, waiting for transfers between devices, body(): lax.psum((conv_weight_grad, conv_bias_grad, stride_weight_grad, stride_bi...  53.2 us
    unnamed x1, blocking collectives  35.3 us
    psum x1, blocking collectives, body(): lax.psum((conv_weight_grad, conv_bias_grad, stride_weight_grad, stride_bi...  32.1 us
    gt x31, other arithmetic, newest(): taken = later[1][0] > 0  18.3 us
    unnamed x40, local copies, waits for them, and re-layouts  13.3 us
    all_gather x1, waiting for transfers between devices, carried_in(): pieces = jax.tree.map(lambda part: lax.all_gather(part, axis), value)  11.3 us
    another operation x1, loops' own time, carried_in_2(): return lax.fori_loop(0, size, step, start)  11.3 us
    convert_element_type x12, other arithmetic, step(): part[at].astype(own.dtype)  11.2 us
  transfers between devices with their start and end apart: 3, of which 2 were waited for; matrix products, arithmetic and copies ran while one was open for 17% of the time, Pallas kernels for 0%

commit v1 on v0

v1 whole, which is shorter than its diff:
```python
import functools

import jax
import jax.numpy as jnp
from jax import lax
from jax.experimental import pallas as pl
from jax.experimental.pallas import tpu as pltpu
from jax.sharding import PartitionSpec as P

BF = jnp.bfloat16
F32 = jnp.float32
EMPTY_FRAME = 100.0
EMPTY_GRAD = 1e30

_VMEM = pl.BlockSpec(memory_space=pltpu.VMEM)
_SMEM = pl.BlockSpec(memory_space=pltpu.SMEM)


def _call(kernel, out_shape, in_specs, scratch=(), flops=0, moved=0):
    return pl.pallas_call(
        kernel,
        out_shape=out_shape,
        in_specs=in_specs,
        out_specs=jax.tree.map(lambda _: _VMEM, out_shape),
        scratch_shapes=list(scratch),
        compiler_params=pltpu.CompilerParams(vmem_limit_bytes=56 << 20),
        cost_estimate=pl.CostEstimate(flops=flops, bytes_accessed=moved, transcendentals=0),
    )


def _put(xk, at, rows, value):
    n, w, c = value.shape
    flat = value.astype(F32).reshape(n * w, c)
    col = lax.broadcasted_iota(jnp.int32, (n * w, c), 0) % w
    right = jnp.where(col == 0, 0.0, pltpu.roll(flat, 1, 0))
    left = jnp.where(col == w - 1, 0.0, pltpu.roll(flat, n * w - 1, 0))
    for kw, shifted in enumerate((right, flat, left)):
        xk[(kw, *at, rows)] = shifted.astype(BF).reshape(n, w, c)


def _window(xk, kw, j, kh, h):
    v = xk[kw, :, j, kh : kh + h]
    return v.reshape(v.shape[0] * v.shape[1] * v.shape[2], v.shape[3])


def _wide(xk, j, h):
    return jnp.concatenate(
        [_window(xk, kw, j, kh, h) for kh in range(3) for kw in range(3)], axis=1
    )


def _conv(xk, w_ref, h):
    c = w_ref.shape[-1]
    zero = jnp.zeros((c, c), BF)
    lhs = jnp.concatenate([_wide(xk, j, h) for j in range(4)], axis=1)
    rhs = []
    for j in range(4):
        for tap in range(9):
            rhs.append(
                jnp.concatenate(
                    [w_ref[(j - t) * 9 + tap] if 0 <= j - t <= 2 else zero for t in range(2)],
                    axis=1,
                )
            )
    return jnp.dot(lhs, jnp.concatenate(rhs, axis=0), preferred_element_type=F32)


def _conv_back(xk, w_ref, h):
    c = w_ref.shape[-1]
    zero = jnp.zeros((c, c), BF)
    lhs = jnp.concatenate([_wide(xk, j, h) for j in range(4)], axis=1)
    rhs = []
    for f in range(2):
        row = []
        for j in range(4):
            for tap in range(9):
                kt = 2 - (j - f)
                row.append(w_ref[kt * 9 + 8 - tap] if 0 <= kt <= 2 else zero)
        rhs.append(jnp.concatenate(row, axis=1))
    return lax.dot_general(
        lhs, jnp.concatenate(rhs, axis=0), (((1,), (1,)), ((), ())), preferred_element_type=F32
    )


def _head(xk, gout, w_ref, cb_ref, sw_ref, sb_ref, h):
    pre = _conv(xk, w_ref, h) + jnp.concatenate([cb_ref[...], cb_ref[...]], axis=1)
    s = 1.0 / (1.0 + jnp.exp(-pre))
    hidden = (pre * s).astype(BF)
    sw = jnp.concatenate([sw_ref[0], sw_ref[1]], axis=0)
    lat = jnp.dot(hidden, sw, preferred_element_type=F32) + sb_ref[...]
    gh = lax.dot_general(gout, sw, (((1,), (1,)), ((), ())), preferred_element_type=F32)
    g = (gh * s * (1.0 + pre * (1.0 - s))).astype(BF)
    return lat, g, hidden


def _weight_grads(xk, g, hidden, gout, h, add):
    c = gout.shape[-1]
    parts = []
    for j in range(4):
        lhs = _wide(xk, j, h)
        parts.append(
            lax.dot_general(lhs, g, (((0,), (0,)), ((), ())), preferred_element_type=F32)
        )
    for kt in range(3):
        add(kt, parts[kt][:, :c] + parts[kt + 1][:, c:])
    sg = lax.dot_general(hidden, gout, (((0,), (0,)), ((), ())), preferred_element_type=F32)
    g32 = jnp.sum(g.astype(F32), axis=0, keepdims=True)
    add(3, sg)
    add(4, g32[:, :c] + g32[:, c:])
    add(5, jnp.sum(gout.astype(F32), axis=0, keepdims=True))


def _store_g(g_ref, g, slots, h, w):
    c = g_ref.shape[-1]
    for t in range(2):
        g_ref[:, t] = g[:, t * c : (t + 1) * c].reshape(slots, h, w, c)


def _early_kernel(sc, fr, ha, co, w_ref, cb, sw, sb, lat_ref, g_ref, acc, xk):
    slots, _, h, w, c = fr.shape
    for s in range(slots):
        for f in range(2):
            mine = fr[s, f], ha[s, f]
            spots = [(s - 1, f + 2, None)] if s > 0 else []
            if s + 1 < slots:
                spots.append((s, f, sc[1 + s + 1] == 0))
            for slot, j, keep in spots:
                a, b = mine
                if keep is not None:
                    a = jnp.where(keep, a, jnp.zeros_like(a))
                    b = jnp.where(keep, b, jnp.zeros_like(b))
                _put(xk, (slot, j), slice(1, 1 + h), a)
                _put(xk, (slot, j), slice(0, 1), b[:1])
                _put(xk, (slot, j), slice(h + 1, h + 2), b[1:])
    gout = jnp.concatenate(
        [
            jnp.where(s < sc[0], co[s, 0], jnp.zeros_like(co[s, 0])).reshape(h * w, c)
            for s in range(1, slots)
        ],
        axis=0,
    )
    lat, g, hidden = _head(xk, gout, w_ref, cb, sw, sb, h)
    for s in range(1, slots):
        part = lat[(s - 1) * h * w : s * h * w]
        lat_ref[s - 1] = (
            jnp.where(s < sc[0], part, jnp.zeros_like(part)).astype(BF).reshape(h, w, c)
        )
    _store_g(g_ref, g, slots - 1, h, w)
    n9 = 9 * c

    def add(kind, value):
        if kind < 3:
            acc[kind * n9 : (kind + 1) * n9] = value
        elif kind == 3:
            acc[3 * n9 : 3 * n9 + 2 * c] = value
        else:
            at = 3 * n9 + 2 * c + (kind - 4)
            acc[at : at + 1] = value

    acc[3 * n9 + 2 * c :] = jnp.zeros((acc.shape[0] - 3 * n9 - 2 * c, c), F32)
    _weight_grads(xk, g, hidden, gout, h, add)


def _late_kernel(
    sc, fr, ha, tail, co, w_ref, cb, sw, sb, early, lat_ref, g_ref, send, keep, xk, acc
):
    _, h, w, c = fr.shape
    on = sc[1] == 0
    for f in range(2):
        _put(xk, (0, f + 2), slice(1, 1 + h), fr[f])
        _put(xk, (0, f + 2), slice(0, 1), ha[f, :1])
        _put(xk, (0, f + 2), slice(h + 1, h + 2), ha[f, 1:])
        a = tail[f * h : (f + 1) * h]
        b = tail[2 * h + 2 * f : 2 * h + 2 * f + 2]
        a = jnp.where(on, a, jnp.zeros_like(a))
        b = jnp.where(on, b, jnp.zeros_like(b))
        _put(xk, (0, f), slice(1, 1 + h), a)
        _put(xk, (0, f), slice(0, 1), b[:1])
        _put(xk, (0, f), slice(h + 1, h + 2), b[1:])
    filled = sc[0] > 0
    gout = jnp.where(filled, co[0], jnp.zeros_like(co[0])).reshape(h * w, c)
    lat, g, hidden = _head(xk, gout, w_ref, cb, sw, sb, h)
    lat_ref[...] = jnp.where(filled, lat, jnp.zeros_like(lat)).astype(BF).reshape(h, w, c)
    for t in range(2):
        g_ref[t] = g[:, t * c : (t + 1) * c].reshape(h, w, c)
    n9 = 9 * c

    def add(kind, value):
        if kind < 3:
            rows = slice(kind * n9, (kind + 1) * n9)
        elif kind == 3:
            rows = slice(3 * n9, 3 * n9 + 2 * c)
        else:
            at = 3 * n9 + 2 * c + (kind - 4)
            rows = slice(at, at + 1)
        acc[rows] = early[rows] + value

    tail_rows = slice(3 * n9 + 2 * c, acc.shape[0])
    acc[tail_rows] = early[tail_rows]
    _weight_grads(xk, g, hidden, gout, h, add)
    half = send.shape[0]
    core = sc[sc.shape[0] - 1]
    send[...] = acc[pl.ds(pl.multiple_of((1 - core) * half, 16), half)].astype(BF)
    keep[...] = acc[pl.ds(pl.multiple_of(core * half, 16), half)]


def _back_kernel(sc, g0, g1, w_ref, out_ref, cache_ref, xk):
    _, h, w, c = g0.shape
    slots = g1.shape[0] + 1
    zero = jnp.zeros((1, w, c), BF)
    for kw in range(3):
        for j in range(4):
            for s in range(slots + 1):
                xk[kw, s, j, 0:1] = zero
                xk[kw, s, j, h + 1 : h + 2] = zero
    blank = jnp.zeros((h, w, c), BF)
    for f in range(2):
        for kw in range(3):
            xk[kw, 0, f, 1 : 1 + h] = blank
            xk[kw, slots, f + 2, 1 : 1 + h] = blank
        for s in range(slots):
            v = g0[f] if s == 0 else g1[s - 1, f]
            _put(xk, (s + 1, f), slice(1, 1 + h), v)
            _put(
                xk, (s, f + 2), slice(1, 1 + h), jnp.where(sc[1 + s] == 0, v, jnp.zeros_like(v))
            )
    out = _conv_back(xk, w_ref, h)
    hw = h * w
    live = sc[0] > 0
    for f in range(2):
        lanes = slice(f * c, (f + 1) * c)
        cache = out[:hw, lanes]
        cache = jnp.where(live, cache, jnp.full_like(cache, EMPTY_GRAD))
        cache_ref[f * h : (f + 1) * h] = cache.astype(BF).reshape(h, w, c)
        out_ref[:, f] = out[hw:, lanes].reshape(slots, h, w, c)


def _cut_kernel(sc, keep, got, own, *sends):
    rows = own.shape[0]
    chip = sc[sc.shape[0] - 2]

    def piece(p):
        at = pl.ds(pl.multiple_of(p * rows, 16), rows)
        return keep[at] + got[at].astype(F32)

    own[...] = piece(chip)
    for k, ref in enumerate(sends):
        ref[...] = piece(lax.bitwise_xor(chip, k + 1)).astype(BF)


def _join_kernel(sc, own, *refs):
    half = refs[-1]
    rows = own.shape[0]
    chip = sc[sc.shape[0] - 2]
    for k, ref in enumerate((own,) + refs[:-1]):
        half[pl.ds(pl.multiple_of(lax.bitwise_xor(chip, k) * rows, 16), rows)] = ref[...]


def _xor(x, k, n, axis):
    return lax.ppermute(x, axis, [(i, i ^ k) for i in range(n)])


def _latest_before(x, empty, axis, n, reverse=False):
    index = lax.axis_index(axis)
    index = n - 1 - index if reverse else index
    core, pair = index & 1, (index >> 1) & 1

    def shift(v, k):
        pairs = [(i, i + k) for i in range(n - k)]
        return lax.ppermute(v, axis, [(b, a) for a, b in pairs] if reverse else pairs)

    def newest(early, late):
        return jnp.where(late > empty / 2, early, late)

    def part(v, at):
        half = v.shape[0] // 2
        return jnp.where(at == 0, v[:half], v[half:])

    def join(mine, other, at):
        return jnp.concatenate(
            [jnp.where(at == 0, mine, other), jnp.where(at == 0, other, mine)], axis=0
        )

    other = _xor(x, 1, n, axis)
    chip = part(jnp.where(core == 0, newest(x, other), newest(other, x)), core)
    beside = _xor(chip, 2, n, axis)
    quad = part(jnp.where(pair == 0, newest(chip, beside), newest(beside, chip)), pair)
    blocks = n // 4
    before = None
    for k in range(min(3, blocks - 1), 0, -1):
        came = shift(quad, 4 * k)
        before = came if before is None else newest(before, came)
    reach = min(3, blocks - 1)
    while reach < blocks - 1:
        before = newest(shift(before, 4 * reach), before)
        reach *= 2
    before = join(before, _xor(before, 2, n, axis), pair)
    before = jnp.where(pair == 0, before, newest(before, beside))
    before = join(before, _xor(before, 1, n, axis), core)
    before = jnp.where(core == 0, before, newest(before, other))
    return jnp.where(before > empty / 2, jnp.zeros_like(before), before)


def _sum_over(send, keep, sc, axis, n):
    rows, c = keep.shape
    chips = min(8, n // 2)
    piece = rows // chips
    got = _xor(send, 1, n, axis)
    outs = _call(
        _cut_kernel,
        [jax.ShapeDtypeStruct((piece, c), F32)]
        + [jax.ShapeDtypeStruct((piece, c), BF)] * (chips - 1),
        [_SMEM, _VMEM, _VMEM],
    )(sc, keep, got)
    total = outs[0]
    for k in range(1, chips):
        total = total + _xor(outs[k], 2 * k, n, axis).astype(F32)
    mine = total.astype(BF)
    k = 2 * chips
    while k < n:
        total = mine.astype(F32) + _xor(mine, k, n, axis).astype(F32)
        mine = total.astype(BF)
        k *= 2
    others = [_xor(mine, 2 * k, n, axis) for k in range(1, chips)]
    half = _call(
        _join_kernel, jax.ShapeDtypeStruct((rows, c), BF), [_SMEM] + [_VMEM] * chips
    )(sc, mine, *others)
    other = _xor(half, 1, n, axis)
    core = sc[-1]
    low = jnp.where(core == 0, half, other)
    high = jnp.where(core == 0, other, half)
    return jnp.concatenate([low, high], axis=0).astype(F32)


def body(
    n,
    frames,
    row_halo,
    clip_start,
    slab_counts,
    conv_weight,
    conv_bias,
    stride_weight,
    stride_bias,
    cotangent,
):
    axis = "tm"
    slots, _, h, w, c = frames.shape
    count = slab_counts[0]
    index = lax.axis_index(axis)
    chips = min(8, n // 2)
    sc = jnp.concatenate(
        [
            slab_counts,
            clip_start,
            ((index >> 1) & (chips - 1)).reshape(1).astype(jnp.int32),
            (index & 1).reshape(1).astype(jnp.int32),
        ]
    )
    wt = conv_weight.reshape(27, c, c)
    cb, sb = conv_bias.reshape(1, c), stride_bias.reshape(1, c)

    last = jnp.maximum(count - 1, 0)
    tail = jnp.concatenate(
        [
            lax.dynamic_index_in_dim(frames, last, 0, False).reshape(2 * h, w, c),
            lax.dynamic_index_in_dim(row_halo, last, 0, False).reshape(4, w, c),
        ],
        axis=0,
    )
    tail = jnp.where(count > 0, tail, jnp.asarray(EMPTY_FRAME, BF))
    arrived = _latest_before(tail, EMPTY_FRAME, axis, n)

    unit = 16 * 2 * chips
    rows = -(-(29 * c + 2) // unit) * unit
    m = h * w
    lat1, g1, early = _call(
        _early_kernel,
        [
            jax.ShapeDtypeStruct((slots - 1, h, w, c), BF),
            jax.ShapeDtypeStruct((slots - 1, 2, h, w, c), BF),
            jax.ShapeDtypeStruct((rows, c), F32),
        ],
        [_SMEM] + [_VMEM] * 7,
        [pltpu.VMEM((3, slots - 1, 4, h + 2, w, c), BF)],
        flops=2 * 2 * (slots - 1) * m * 36 * c * 2 * c,
        moved=6 << 20,
    )(sc, frames, row_halo, cotangent, wt, cb, stride_weight, sb)

    lat0, g0, send, keep = _call(
        _late_kernel,
        [
            jax.ShapeDtypeStruct((h, w, c), BF),
            jax.ShapeDtypeStruct((2, h, w, c), BF),
            jax.ShapeDtypeStruct((rows // 2, c), BF),
            jax.ShapeDtypeStruct((rows // 2, c), F32),
        ],
        [_SMEM] + [_VMEM] * 9,
        [pltpu.VMEM((3, 1, 4, h + 2, w, c), BF), pltpu.VMEM((rows, c), F32)],
        flops=2 * 2 * m * 36 * c * 2 * c,
        moved=6 << 20,
    )(sc, frames[0], row_halo[0], arrived, cotangent[0], wt, cb, stride_weight, sb, early)

    total = _sum_over(send, keep, sc, axis, n)

    grad, cache = _call(
        _back_kernel,
        [
            jax.ShapeDtypeStruct((slots, 2, h, w, c), F32),
            jax.ShapeDtypeStruct((2 * h, w, c), BF),
        ],
        [_SMEM] + [_VMEM] * 3,
        [pltpu.VMEM((3, slots + 1, 4, h + 2, w, c), BF)],
        flops=2 * (slots + 1) * m * 36 * c * 2 * c,
        moved=6 << 20,
    )(sc, g0, g1, wt)
    returned = _latest_before(cache, EMPTY_GRAD, axis, n, reverse=True)
    newest = (jnp.arange(slots, dtype=jnp.int32) == count - 1)[:, None, None, None, None]
    back = returned.reshape(1, 2, h, w, c).astype(F32)
    frames_grad = (grad + jnp.where(newest, back, jnp.zeros_like(back))).astype(BF)
    latents = jnp.concatenate([lat0[None], lat1], axis=0)[:, None]
    return (
        latents,
        frames_grad,
        total[: 27 * c].reshape(3, 3, 3, c, c),
        total[29 * c],
        total[27 * c : 29 * c].reshape(2, c, c),
        total[29 * c + 1],
    )


def solution(mesh):
    split = P(("groups", "tm"))
    return jax.shard_map(
        functools.partial(body, mesh.shape["tm"]),
        mesh=mesh,
        in_specs=(split, split, split, split, P(), P(), P(), P(), split),
        out_specs=(split, split, P("groups"), P("groups"), P("groups"), P("groups")),
        check_vma=False,
    )
```

time: 270 us -> 112 us (0.41)
  blocking collectives: 67.5 us -> 0 us
  starting transfers between devices: 0.38 us -> 43.1 us
  waiting for transfers between devices: 64.5 us -> 25.6 us
  other arithmetic: 39.3 us -> 6.71 us
  local copies, waits for them, and re-layouts: 34.8 us -> 7.39 us
  Pallas kernels: 0 us -> 26.6 us
  matrix products: 26.5 us -> 0 us
  loops' own time: 22.3 us -> 0 us
  between operations: 14.8 us -> 1.63 us
    psum x1 -> x0, waiting for transfers between devices: 53.2 us -> none  [body(): lax.psum((conv_weight_grad, conv_bias_grad, stride_weight_grad, stride_bi...]
    ppermute x0 -> x30, starting transfers between devices: none -> 43.1 us  [the longest x24 29.5 us: _xor(): return lax.ppermute(x, axis, [(i, i ^ k) for i in range(n)])]
    unnamed x1 -> x0, blocking collectives: 35.3 us -> none
    psum x1 -> x0, blocking collectives: 32.1 us -> none  [body(): lax.psum((conv_weight_grad, conv_bias_grad, stride_weight_grad, stride_bi...]
    pallas_call x0 -> x5, Pallas kernels: none -> 26.6 us  [the longest x1 10.7 us: body(): _call(_early_kernel, [jax.ShapeDtypeStruct((slots - 1, h, w, c), BF), jax...]
    ppermute x0 -> x30, waiting for transfers between devices: none -> 25.6 us  [the longest x24 19.4 us: _xor(): return lax.ppermute(x, axis, [(i, i ^ k) for i in range(n)])]
    another operation x33 -> x0, loops' own time: 22.3 us -> none  [the longest x1 11.3 us: carried_in_2(): return lax.fori_loop(0, size, step, start)]
    gt x31 -> x0, other arithmetic: 18.3 us -> none  [newest(): taken = later[1][0] > 0]
  transfers between devices with their start and end apart: 3 -> 30, of which waited for: 2 -> 14; matrix products, arithmetic and copies ran while one was open for 17% -> 4% of each run, Pallas kernels for 0% -> 12%
where the time goes in v1:
time: 112 us; the launch traced here: 111 us
  starting transfers between devices  43.1 us (38%)
  Pallas kernels  26.6 us (24%)
  waiting for transfers between devices  25.6 us (23%)
  local copies, waits for them, and re-layouts  7.39 us (7%)
  other arithmetic  6.71 us (6%)
  between operations  1.63 us (1%)
    ppermute x24, starting transfers between devices, _xor(): return lax.ppermute(x, axis, [(i, i ^ k) for i in range(n)])  29.5 us
    ppermute x24, waiting for transfers between devices, _xor(): return lax.ppermute(x, axis, [(i, i ^ k) for i in range(n)])  19.4 us
    ppermute x6, starting transfers between devices, shift(): lax.ppermute(v, axis, [(b, a) for a, b in pairs] if reverse else pairs)  13.6 us
    pallas_call x1, Pallas kernels, body(): _call(_early_kernel, [jax.ShapeDtypeStruct((slots - 1, h, w, c), BF), jax...  10.7 us
    ppermute x6, waiting for transfers between devices, shift(): lax.ppermute(v, axis, [(b, a) for a, b in pairs] if reverse else pairs)  6.27 us
    pallas_call x1, Pallas kernels, body(): _call(_back_kernel, [jax.ShapeDtypeStruct((slots, 2, h, w, c), F32), jax....  5.96 us
    pallas_call x1, Pallas kernels, body(): _call(_late_kernel, [jax.ShapeDtypeStruct((h, w, c), BF), jax.ShapeDtypeS...  5.82 us
  transfers between devices with their start and end apart: 30, of which 14 were waited for; matrix products, arithmetic and copies ran while one was open for 4% of the time, Pallas kernels for 12%

profile of v1, /device:TPU:0, one launch (start us, length us, event | category | flops | bytes accessed | tf_op | source)
XLA Modules:
  0.0 111.0 jit_solution(12866198255664110945)
XLA Ops:
  1.3 1.6 %constant_dynamic-slice_fusion.1 = (bf16[1,2,4,64,128]{4,3,2,1,0:T(8,128)(2,1)S(1)}, bf16[2,4,64,128]{3,2,1,0:T(8,128)(2,1)}) fusion(bf16[4,2,4,64,128]{4,3,2,1,0:T(8,128)(2,1)} %fr.1, s32[]{:T(128)S(6)} %max.3), kind=kLoop, calls=%fused_computation.54 | loop fusion | bytes 524292 | tf_op jit(solution)/shard_map/jit(dynamic_index_in_dim)/dynamic_slice | solution.py:366
  3.0 1.5 %constant_dynamic-slice_fusion = (bf16[1,2,2,64,128]{4,3,2,1,0:T(8,128)(2,1)S(1)}, bf16[2,2,64,128]{3,2,1,0:T(8,128)(2,1)}) fusion(bf16[4,2,2,64,128]{4,3,2,1,0:T(8,128)(2,1)} %ha.1, s32[]{:T(128)S(6)} %max.3), kind=kLoop, calls=%fused_computation.53 | loop fusion | bytes 262148 | tf_op jit(solution)/shard_map/jit(dynamic_index_in_dim)/dynamic_slice | solution.py:367
  4.5 0.5 collective-permute-start
  5.0 1.1 collective-permute-done
  6.1 3.0 %collective-permute-start.1 = (bf16[6,64,128]{2,1,0:T(8,128)(2,1)S(1)}, bf16[6,64,128]{2,1,0:T(8,128)(2,1)S(1)}, u32[]{:S(2)}, u32[]{:S(2)}) collective-permute-start(bf16[6,64,128]{2,1,0:T(8,128)(2,1)S(1)} %slice_select_fusion), channel_id=1, source_target_pairs={{0,2},{1,3},{2,0},{3,1},{4,6},{5,7},{6,4},{7,5},{8,10},{9,11},{10,... | collective-permute-start | bytes 294920 | tf_op jit(solution)/shard_map/ppermute | solution.py:260
  9.1 3.1 %collective-permute-done.1 = bf16[6,64,128]{2,1,0:T(8,128)(2,1)S(1)} collective-permute-done((bf16[6,64,128]{2,1,0:T(8,128)(2,1)S(1)}, bf16[6,64,128]{2,1,0:T(8,128)(2,1)S(1)}, u32[]{:S(2)}, u32[]{:S(2)}) %collective-permute-start.1) | collective-permute-done | bytes 98336 | tf_op jit(solution)/shard_map/ppermute | solution.py:260
  12.3 3.7 %collective-permute-start.2 = (bf16[3,64,128]{2,1,0:T(8,128)(2,1)S(1)}, bf16[3,64,128]{2,1,0:T(8,128)(2,1)S(1)}, u32[]{:S(2)}, u32[]{:S(2)}) collective-permute-start(bf16[3,64,128]{2,1,0:T(8,128)(2,1)S(1)} %slice_select_fusion.2), channel_id=1, source_target_pairs={{0,4},{1,5},{2,6},{3,7},{4,8},{5,9},{6,10},{7,11},{8,12},{9,13},{1... | collective-permute-start | bytes 147464 | tf_op jit(solution)/shard_map/ppermute | solution.py:270
  15.9 4.6 %collective-permute-start.3 = (bf16[3,64,128]{2,1,0:T(8,128)(2,1)S(1)}, bf16[3,64,128]{2,1,0:T(8,128)(2,1)S(1)}, u32[]{:S(2)}, u32[]{:S(2)}) collective-permute-start(bf16[3,64,128]{2,1,0:T(8,128)(2,1)S(1)} %slice_select_fusion.2), channel_id=1, source_target_pairs={{0,8},{1,9},{2,10},{3,11},{4,12},{5,13},{6,14},{7,15},{16,24},{17,... | collective-permute-start | bytes 147464 | tf_op jit(solution)/shard_map/ppermute | solution.py:270
  20.5 1.3 %collective-permute-start.4 = (bf16[3,64,128]{2,1,0:T(8,128)(2,1)S(1)}, bf16[3,64,128]{2,1,0:T(8,128)(2,1)S(1)}, u32[]{:S(2)}, u32[]{:S(2)}) collective-permute-start(bf16[3,64,128]{2,1,0:T(8,128)(2,1)S(1)} %slice_select_fusion.2), channel_id=1, source_target_pairs={{0,12},{1,13},{2,14},{3,15},{16,28},{17,29},{18,30},{19,31}} | collective-permute-start | bytes 147464 | tf_op jit(solution)/shard_map/ppermute | solution.py:270
  21.8 0.7 pad_add_fusion.sc
  22.5 1.1 collective-permute-done.4
  23.5 1.5 %collective-permute-start.5 = (bf16[3,64,128]{2,1,0:T(8,128)(2,1)S(1)}, bf16[3,64,128]{2,1,0:T(8,128)(2,1)S(1)}, u32[]{:S(2)}, u32[]{:S(2)}) collective-permute-start(bf16[3,64,128]{2,1,0:T(8,128)(2,1)S(1)} %compare_select_fusion.15), channel_id=1, source_target_pairs={{0,2},{1,3},{2,0},{3,1},{4,6},{5,7},{6,4},{7,5},{8,10},{9,11},{10,... | collective-permute-start | bytes 147464 | tf_op jit(solution)/shard_map/ppermute | solution.py:260
  25.0 10.7 %shard_map.136 = (bf16[3,4,64,128]{3,2,1,0:T(8,128)(2,1)}, bf16[3,2,4,64,128]{4,3,2,1,0:T(8,128)(2,1)}, f32[3840,128]{1,0:T(8,128)}) custom-call(s32[7]{0:T(128)} %pad_add_fusion.sc, bf16[4,2,4,64,128]{4,3,2,1,0:T(8,128)(2,1)} %fr.1, bf16[4,2,2,64,128]{4,3,2,1,0:T(8,128)(2,1)} %ha.1, bf16[4,1,4,64,128]{4,3,2,1,0:T(8,128)(2,1)} %co.1, ...), custom_call_target="tpu_custom_call" | custom-call | flops 3623878656 | bytes 6291456 | tf_op jit(solution)/shard_map/pallas_call | solution.py:377
  35.8 0.1 collective-permute-start.6
  35.9 1.5 %slice_bitcast_fusion.1.co = bf16[1,4,64,128]{3,2,1,0:T(8,128)(2,1)} fusion(bf16[4,1,4,64,128]{4,3,2,1,0:T(8,128)(2,1)} %co.1), kind=kLoop, calls=%fused_computation.39 | loop fusion | bytes 131072 | tf_op jit(solution)/shard_map/squeeze | solution.py:402
  37.4 0.7 compare_select_fusion.2.tail
  38.1 5.8 %shard_map.137 = (bf16[4,64,128]{2,1,0:T(8,128)(2,1)}, bf16[2,4,64,128]{3,2,1,0:T(8,128)(2,1)}, bf16[1920,128]{1,0:T(8,128)(2,1)}, f32[1920,128]{1,0:T(8,128)}) custom-call(s32[7]{0:T(128)} %pad_add_fusion.sc, bf16[2,4,64,128]{3,2,1,0:T(8,128)(2,1)} %get-tuple-element.51.fr, bf16[2,2,64,128]{3,2,1,0:T(8,128)(2,1)} %get-tuple-element.53.ha, ...), custom_call_target="tpu_custom_call" | custom-call | flops 1207959552 | bytes 6291456 | tf_op jit(solution)/shard_map/pallas_call | solution.py:390
  43.9 6.0 %shard_map.138 = (f32[4,2,4,64,128]{4,3,2,1,0:T(8,128)}, bf16[8,64,128]{2,1,0:T(8,128)(2,1)}) custom-call(s32[7]{0:T(128)} %pad_add_fusion.sc, bf16[2,4,64,128]{3,2,1,0:T(8,128)(2,1)} %get-tuple-element.26.g0, bf16[3,2,4,64,128]{4,3,2,1,0:T(8,128)(2,1)} %get-tuple-element.27.g1, bf16[27,128,128]{2,1,0:T(8,128)(2,1)} %bitcast.36), custom_call_target="tpu_custom_call" | custom-call | flops 3019898880 | bytes 6291456 | tf_op jit(solution)/shard_map/pallas_call | solution.py:406
  49.9 0.5 collective-permute-start.7
  50.4 1.2 %collective-permute-done.7 = bf16[8,64,128]{2,1,0:T(8,128)(2,1)S(1)} collective-permute-done((bf16[8,64,128]{2,1,0:T(8,128)(2,1)}, bf16[8,64,128]{2,1,0:T(8,128)(2,1)S(1)}, u32[]{:S(2)}, u32[]{:S(2)}) %collective-permute-start.7) | collective-permute-done | bytes 131104 | tf_op jit(solution)/shard_map/ppermute | solution.py:260
  51.6 0.9 fusion.4
  52.5 0.7 collective-permute-start.8
  53.2 0.1 collective-permute-start.14
  53.3 3.7 %collective-permute-done.8 = bf16[4,64,128]{2,1,0:T(8,128)(2,1)S(1)} collective-permute-done((bf16[4,64,128]{2,1,0:T(8,128)(2,1)S(1)}, bf16[4,64,128]{2,1,0:T(8,128)(2,1)S(1)}, u32[]{:S(2)}, u32[]{:S(2)}) %collective-permute-start.8) | collective-permute-done | bytes 65568 | tf_op jit(solution)/shard_map/ppermute | solution.py:260
  57.0 1.3 %collective-permute-start.10 = (bf16[2,64,128]{2,1,0:T(8,128)(2,1)S(1)}, bf16[2,64,128]{2,1,0:T(8,128)(2,1)S(1)}, u32[]{:S(2)}, u32[]{:S(2)}) collective-permute-start(bf16[2,64,128]{2,1,0:T(8,128)(2,1)S(1)} %slice_select_fusion.3), channel_id=1, source_target_pairs={{8,0},{9,1},{10,2},{11,3},{12,4},{13,5},{14,6},{15,7},{24,16},{25,... | collective-permute-start | bytes 98312 | tf_op jit(solution)/shard_map/ppermute | solution.py:270
  58.3 1.5 %collective-permute-start.11 = (bf16[2,64,128]{2,1,0:T(8,128)(2,1)S(1)}, bf16[2,64,128]{2,1,0:T(8,128)(2,1)S(1)}, u32[]{:S(2)}, u32[]{:S(2)}) collective-permute-start(bf16[2,64,128]{2,1,0:T(8,128)(2,1)S(1)} %slice_select_fusion.3), channel_id=1, source_target_pairs={{12,0},{13,1},{14,2},{15,3},{28,16},{29,17},{30,18},{31,19}} | collective-permute-start | bytes 98312 | tf_op jit(solution)/shard_map/ppermute | solution.py:270
  59.7 1.3 %collective-permute-start.9 = (bf16[2,64,128]{2,1,0:T(8,128)(2,1)S(1)}, bf16[2,64,128]{2,1,0:T(8,128)(2,1)S(1)}, u32[]{:S(2)}, u32[]{:S(2)}) collective-permute-start(bf16[2,64,128]{2,1,0:T(8,128)(2,1)S(1)} %slice_select_fusion.3), channel_id=1, source_target_pairs={{4,0},{5,1},{6,2},{7,3},{8,4},{9,5},{10,6},{11,7},{12,8},{13,9},{1... | collective-permute-start | bytes 98312 | tf_op jit(solution)/shard_map/ppermute | solution.py:270
  61.0 2.6 %collective-permute-done.10 = bf16[2,64,128]{2,1,0:T(8,128)(2,1)S(1)} collective-permute-done((bf16[2,64,128]{2,1,0:T(8,128)(2,1)S(1)}, bf16[2,64,128]{2,1,0:T(8,128)(2,1)S(1)}, u32[]{:S(2)}, u32[]{:S(2)}) %collective-permute-start.10) | collective-permute-done | bytes 32800 | tf_op jit(solution)/shard_map/ppermute | solution.py:270
  63.7 2.6 %collective-permute-done.11 = bf16[2,64,128]{2,1,0:T(8,128)(2,1)S(1)} collective-permute-done((bf16[2,64,128]{2,1,0:T(8,128)(2,1)S(1)}, bf16[2,64,128]{2,1,0:T(8,128)(2,1)S(1)}, u32[]{:S(2)}, u32[]{:S(2)}) %collective-permute-start.11) | collective-permute-done | bytes 32800 | tf_op jit(solution)/shard_map/ppermute | solution.py:270
  66.3 0.7 collective-permute-start.12
  67.0 0.8 copy-done.2
  67.7 2.2 %shard_map.139 = (f32[240,128]{1,0:T(8,128)}, bf16[240,128]{1,0:T(8,128)(2,1)}, bf16[240,128]{1,0:T(8,128)(2,1)}, bf16[240,128]{1,0:T(8,128)(2,1)}, bf16[240,128...) custom-call(s32[7]{0:T(128)} %pad_add_fusion.sc, ...), custom_call_target="tpu_custom_call" | custom-call | tf_op jit(solution)/shard_map/pallas_call | solution.py:309
  69.9 1.5 %collective-permute-start.15 = (bf16[240,128]{1,0:T(8,128)(2,1)}, bf16[240,128]{1,0:T(8,128)(2,1)S(1)}, u32[]{:S(2)}, u32[]{:S(2)}) collective-permute-start(bf16[240,128]{1,0:T(8,128)(2,1)} %get-tuple-element.33), channel_id=1, source_target_pairs={{0,2},{1,3},{2,0},{3,1},{4,6},{5,7},{6,4},{7,5},{8,10},{9,11},{10,... | collective-permute-start | bytes 184328 | tf_op jit(solution)/shard_map/ppermute | solution.py:260
  71.4 0.8 collective-permute-start.16
  72.3 1.3 %collective-permute-start.17 = (bf16[240,128]{1,0:T(8,128)(2,1)}, bf16[240,128]{1,0:T(8,128)(2,1)S(1)}, u32[]{:S(2)}, u32[]{:S(2)}) collective-permute-start(bf16[240,128]{1,0:T(8,128)(2,1)} %get-tuple-element.35), channel_id=1, source_target_pairs={{0,6},{1,7},{2,4},{3,5},{4,2},{5,3},{6,0},{7,1},{8,14},{9,15},{10,... | collective-permute-start | bytes 184328 | tf_op jit(solution)/shard_map/ppermute | solution.py:260
  73.5 2.2 %collective-permute-start.18 = (bf16[240,128]{1,0:T(8,128)(2,1)}, bf16[240,128]{1,0:T(8,128)(2,1)S(1)}, u32[]{:S(2)}, u32[]{:S(2)}) collective-permute-start(bf16[240,128]{1,0:T(8,128)(2,1)} %get-tuple-element.36), channel_id=1, source_target_pairs={{0,8},{1,9},{2,10},{3,11},{4,12},{5,13},{6,14},{7,15},{8,0},{9,1},... | collective-permute-start | bytes 184328 | tf_op jit(solution)/shard_map/ppermute | solution.py:260
  75.8 1.6 %collective-permute-start.19 = (bf16[240,128]{1,0:T(8,128)(2,1)}, bf16[240,128]{1,0:T(8,128)(2,1)S(1)}, u32[]{:S(2)}, u32[]{:S(2)}) collective-permute-start(bf16[240,128]{1,0:T(8,128)(2,1)} %get-tuple-element.37), channel_id=1, source_target_pairs={{0,10},{1,11},{2,8},{3,9},{4,14},{5,15},{6,12},{7,13},{8,2},{9,3},... | collective-permute-start | bytes 184328 | tf_op jit(solution)/shard_map/ppermute | solution.py:260
  77.3 1.6 %collective-permute-start.20 = (bf16[240,128]{1,0:T(8,128)(2,1)}, bf16[240,128]{1,0:T(8,128)(2,1)S(1)}, u32[]{:S(2)}, u32[]{:S(2)}) collective-permute-start(bf16[240,128]{1,0:T(8,128)(2,1)} %get-tuple-element.38), channel_id=1, source_target_pairs={{0,12},{1,13},{2,14},{3,15},{4,8},{5,9},{6,10},{7,11},{8,4},{9,5},... | collective-permute-start | bytes 184328 | tf_op jit(solution)/shard_map/ppermute | solution.py:260
  79.0 2.2 %collective-permute-start.21 = (bf16[240,128]{1,0:T(8,128)(2,1)}, bf16[240,128]{1,0:T(8,128)(2,1)S(1)}, u32[]{:S(2)}, u32[]{:S(2)}) collective-permute-start(bf16[240,128]{1,0:T(8,128)(2,1)} %get-tuple-element.39), channel_id=1, source_target_pairs={{0,14},{1,15},{2,12},{3,13},{4,10},{5,11},{6,8},{7,9},{8,6},{9,7},... | collective-permute-start | bytes 184328 | tf_op jit(solution)/shard_map/ppermute | solution.py:260
  81.2 0.1 collective-permute-start.13
  81.3 0.9 collective-permute-done.18
  82.2 2.2 %collective-permute-done.19 = bf16[240,128]{1,0:T(8,128)(2,1)S(1)} collective-permute-done((bf16[240,128]{1,0:T(8,128)(2,1)}, bf16[240,128]{1,0:T(8,128)(2,1)S(1)}, u32[]{:S(2)}, u32[]{:S(2)}) %collective-permute-start.19) | collective-permute-done | bytes 61472 | tf_op jit(solution)/shard_map/ppermute | solution.py:260
  84.4 1.9 %collective-permute-done.21 = bf16[240,128]{1,0:T(8,128)(2,1)S(1)} collective-permute-done((bf16[240,128]{1,0:T(8,128)(2,1)}, bf16[240,128]{1,0:T(8,128)(2,1)S(1)}, u32[]{:S(2)}, u32[]{:S(2)}) %collective-permute-start.21) | collective-permute-done | bytes 61472 | tf_op jit(solution)/shard_map/ppermute | solution.py:260
  86.3 1.0 add_convert_fusion.1.own
  87.3 0.7 collective-permute-start.22
  87.9 1.5 %collective-permute-start.23 = (bf16[240,128]{1,0:T(8,128)(2,1)S(1)}, bf16[240,128]{1,0:T(8,128)(2,1)S(1)}, u32[]{:S(2)}, u32[]{:S(2)}) collective-permute-start(bf16[240,128]{1,0:T(8,128)(2,1)S(1)} %add_convert_fusion.1.own), channel_id=1, source_target_pairs={{0,4},{1,5},{2,6},{3,7},{4,0},{5,1},{6,2},{7,3},{8,12},{9,13},{10,... | collective-permute-start | bytes 184328 | tf_op jit(solution)/shard_map/ppermute | solution.py:260
  89.4 0.7 maximum_bitcast_fusion
  90.1 1.4 %collective-permute-start.24 = (bf16[240,128]{1,0:T(8,128)(2,1)S(1)}, bf16[240,128]{1,0:T(8,128)(2,1)S(1)}, u32[]{:S(2)}, u32[]{:S(2)}) collective-permute-start(bf16[240,128]{1,0:T(8,128)(2,1)S(1)} %add_convert_fusion.1.own), channel_id=1, source_target_pairs={{0,6},{1,7},{2,4},{3,5},{4,2},{5,3},{6,0},{7,1},{8,14},{9,15},{10,... | collective-permute-start | bytes 184328 | tf_op jit(solution)/shard_map/ppermute | solution.py:260
  91.6 0.6 collective-permute-start.25
  92.2 2.3 %collective-permute-start.26 = (bf16[240,128]{1,0:T(8,128)(2,1)S(1)}, bf16[240,128]{1,0:T(8,128)(2,1)S(1)}, u32[]{:S(2)}, u32[]{:S(2)}) collective-permute-start(bf16[240,128]{1,0:T(8,128)(2,1)S(1)} %add_convert_fusion.1.own), channel_id=1, source_target_pairs={{0,10},{1,11},{2,8},{3,9},{4,14},{5,15},{6,12},{7,13},{8,2},{9,3},... | collective-permute-start | bytes 184328 | tf_op jit(solution)/shard_map/ppermute | solution.py:260
  94.5 2.2 %collective-permute-start.27 = (bf16[240,128]{1,0:T(8,128)(2,1)S(1)}, bf16[240,128]{1,0:T(8,128)(2,1)S(1)}, u32[]{:S(2)}, u32[]{:S(2)}) collective-permute-start(bf16[240,128]{1,0:T(8,128)(2,1)S(1)} %add_convert_fusion.1.own), channel_id=1, source_target_pairs={{0,12},{1,13},{2,14},{3,15},{4,8},{5,9},{6,10},{7,11},{8,4},{9,5},... | collective-permute-start | bytes 184328 | tf_op jit(solution)/shard_map/ppermute | solution.py:260
  96.7 2.5 %collective-permute-start.28 = (bf16[240,128]{1,0:T(8,128)(2,1)S(1)}, bf16[240,128]{1,0:T(8,128)(2,1)S(1)}, u32[]{:S(2)}, u32[]{:S(2)}) collective-permute-start(bf16[240,128]{1,0:T(8,128)(2,1)S(1)} %add_convert_fusion.1.own), channel_id=1, source_target_pairs={{0,14},{1,15},{2,12},{3,13},{4,10},{5,11},{6,8},{7,9},{8,6},{9,7},... | collective-permute-start | bytes 184328 | tf_op jit(solution)/shard_map/ppermute | solution.py:260
  99.3 1.1 collective-permute-done.26.refs_4_
  100.4 0.3 collective-permute-done.27.refs_5_
  100.6 3.0 %collective-permute-done.28.refs_6_ = bf16[240,128]{1,0:T(8,128)(2,1)S(1)} collective-permute-done((bf16[240,128]{1,0:T(8,128)(2,1)S(1)}, bf16[240,128]{1,0:T(8,128)(2,1)S(1)}, u32[]{:S(2)}, u32[]{:S(2)}) %collective-permute-start.28) | collective-permute-done | bytes 61472 | tf_op jit(solution)/shard_map/ppermute | solution.py:260
  103.7 0.6 copy-done.12
  104.3 1.9 %shard_map.140 = bf16[1920,128]{1,0:T(8,128)(2,1)} custom-call(s32[7]{0:T(128)} %pad_add_fusion.sc, bf16[240,128]{1,0:T(8,128)(2,1)} %copy-done.3, bf16[240,128]{1,0:T(8,128)(2,1)} %copy-done.6, bf16[240,128]{1,0:T(8,128)(2,1)} %copy-done.7, bf16[240,128]{1,0:T(8,128)(2,1)} %copy-done.8, bf16[240,128]{1,0:T(8,128)(2,1)} %copy-done.9, ...), custom_call_target="tpu_custom_call" | custom-call | tf_op jit(solution)/shard_map/pallas_call | solution.py:325
  106.3 1.0 add_convert_fusion
  107.3 1.0 collective-permute-done.29
  108.3 0.1 broadcast_select_fusion.1
  108.3 0.7 maximum_convert_fusion.1
  109.0 0.5 convert_bitcast_fusion
  109.5 0.1 maximum_convert_fusion
  109.6 1.3 %slice.68 = f32[3456,128]{1,0:T(8,128)} slice(f32[3840,128]{1,0:T(8,128)S(1)} %maximum_convert_fusion), slice={[0:3456], [0:128]} | slice | bytes 3538944 | tf_op jit(solution)/shard_map/slice | solution.py:425
  (64 shorter events, 0.4 us)
Async XLA Ops:
  0.6 21.2 %copy-start.13 = (s32[4]{0:T(128)S(1)}, s32[4]{0:T(128)}, u32[]{:S(2)}) copy-start(s32[4]{0:T(128)} %param.11) | copy-start | bytes 52
  4.5 1.6 %collective-permute-start = (bf16[12,64,128]{2,1,0:T(8,128)(2,1)S(1)}, bf16[12,64,128]{2,1,0:T(8,128)(2,1)S(1)}, u32[]{:S(2)}, u32[]{:S(2)}) collective-permute-start(bf16[12,64,128]{2,1,0:T(8,128)(2,1)S(1)} %maximum_select_fusion), channel_id=1, source_target_pairs={{0,1},{1,0},{2,3},{3,2},{4,5},{5,4},{6,7},{7,6},{8,9},{9,8},{10,11... | collective-permute-start | bytes 589832 | tf_op jit(solution)/shard_map/ppermute | solution.py:260
  6.1 6.1 %collective-permute-start.1 = (bf16[6,64,128]{2,1,0:T(8,128)(2,1)S(1)}, bf16[6,64,128]{2,1,0:T(8,128)(2,1)S(1)}, u32[]{:S(2)}, u32[]{:S(2)}) collective-permute-start(bf16[6,64,128]{2,1,0:T(8,128)(2,1)S(1)} %slice_select_fusion), channel_id=1, source_target_pairs={{0,2},{1,3},{2,0},{3,1},{4,6},{5,7},{6,4},{7,5},{8,10},{9,11},{10,... | collective-permute-start | bytes 294920 | tf_op jit(solution)/shard_map/ppermute | solution.py:260
  12.3 10.2 %collective-permute-start.2 = (bf16[3,64,128]{2,1,0:T(8,128)(2,1)S(1)}, bf16[3,64,128]{2,1,0:T(8,128)(2,1)S(1)}, u32[]{:S(2)}, u32[]{:S(2)}) collective-permute-start(bf16[3,64,128]{2,1,0:T(8,128)(2,1)S(1)} %slice_select_fusion.2), channel_id=1, source_target_pairs={{0,4},{1,5},{2,6},{3,7},{4,8},{5,9},{6,10},{7,11},{8,12},{9,13},{1... | collective-permute-start | bytes 147464 | tf_op jit(solution)/shard_map/ppermute | solution.py:270
  15.9 6.5 %collective-permute-start.3 = (bf16[3,64,128]{2,1,0:T(8,128)(2,1)S(1)}, bf16[3,64,128]{2,1,0:T(8,128)(2,1)S(1)}, u32[]{:S(2)}, u32[]{:S(2)}) collective-permute-start(bf16[3,64,128]{2,1,0:T(8,128)(2,1)S(1)} %slice_select_fusion.2), channel_id=1, source_target_pairs={{0,8},{1,9},{2,10},{3,11},{4,12},{5,13},{6,14},{7,15},{16,24},{17,... | collective-permute-start | bytes 147464 | tf_op jit(solution)/shard_map/ppermute | solution.py:270
  20.5 3.0 %collective-permute-start.4 = (bf16[3,64,128]{2,1,0:T(8,128)(2,1)S(1)}, bf16[3,64,128]{2,1,0:T(8,128)(2,1)S(1)}, u32[]{:S(2)}, u32[]{:S(2)}) collective-permute-start(bf16[3,64,128]{2,1,0:T(8,128)(2,1)S(1)} %slice_select_fusion.2), channel_id=1, source_target_pairs={{0,12},{1,13},{2,14},{3,15},{16,28},{17,29},{18,30},{19,31}} | collective-permute-start | bytes 147464 | tf_op jit(solution)/shard_map/ppermute | solution.py:270
  23.5 12.2 %collective-permute-start.5 = (bf16[3,64,128]{2,1,0:T(8,128)(2,1)S(1)}, bf16[3,64,128]{2,1,0:T(8,128)(2,1)S(1)}, u32[]{:S(2)}, u32[]{:S(2)}) collective-permute-start(bf16[3,64,128]{2,1,0:T(8,128)(2,1)S(1)} %compare_select_fusion.15), channel_id=1, source_target_pairs={{0,2},{1,3},{2,0},{3,1},{4,6},{5,7},{6,4},{7,5},{8,10},{9,11},{10,... | collective-permute-start | bytes 147464 | tf_op jit(solution)/shard_map/ppermute | solution.py:260
  35.8 1.6 %collective-permute-start.6 = (bf16[6,64,128]{2,1,0:T(8,128)(2,1)S(1)}, bf16[6,64,128]{2,1,0:T(8,128)(2,1)S(1)}, u32[]{:S(2)}, u32[]{:S(2)}) collective-permute-start(bf16[6,64,128]{2,1,0:T(8,128)(2,1)S(1)} %fusion.3), channel_id=1, source_target_pairs={{0,1},{1,0},{2,3},{3,2},{4,5},{5,4},{6,7},{7,6},{8,9},{9,8},{10,11... | collective-permute-start | bytes 294920 | tf_op jit(solution)/shard_map/ppermute | solution.py:260
  43.9 9.3 %copy-start.14 = (bf16[1920,128]{1,0:T(8,128)(2,1)S(1)}, bf16[1920,128]{1,0:T(8,128)(2,1)}, u32[]{:S(2)}) copy-start(bf16[1920,128]{1,0:T(8,128)(2,1)} %get-tuple-element.31) | copy-start | bytes 1474564
  49.9 39.5 %copy-start.4 = (bf16[3,4,64,128]{3,2,1,0:T(8,128)(2,1)S(1)}, bf16[3,4,64,128]{3,2,1,0:T(8,128)(2,1)}, u32[]{:S(2)}) copy-start(bf16[3,4,64,128]{3,2,1,0:T(8,128)(2,1)} %get-tuple-element.25) | copy-start | bytes 589828
  49.9 39.5 %copy-start.5 = (bf16[4,64,128]{2,1,0:T(8,128)(2,1)S(1)}, bf16[4,64,128]{2,1,0:T(8,128)(2,1)}, u32[]{:S(2)}) copy-start(bf16[4,64,128]{2,1,0:T(8,128)(2,1)} %get-tuple-element.24) | copy-start | bytes 196612
  49.9 1.7 %collective-permute-start.7 = (bf16[8,64,128]{2,1,0:T(8,128)(2,1)}, bf16[8,64,128]{2,1,0:T(8,128)(2,1)S(1)}, u32[]{:S(2)}, u32[]{:S(2)}) collective-permute-start(bf16[8,64,128]{2,1,0:T(8,128)(2,1)} %get-tuple-element.29), channel_id=1, source_target_pairs={{0,1},{1,0},{2,3},{3,2},{4,5},{5,4},{6,7},{7,6},{8,9},{9,8},{10,11... | collective-permute-start | bytes 393224 | tf_op jit(solution)/shard_map/ppermute | solution.py:260
  52.5 4.4 %collective-permute-start.8 = (bf16[4,64,128]{2,1,0:T(8,128)(2,1)S(1)}, bf16[4,64,128]{2,1,0:T(8,128)(2,1)S(1)}, u32[]{:S(2)}, u32[]{:S(2)}) collective-permute-start(bf16[4,64,128]{2,1,0:T(8,128)(2,1)S(1)} %slice_select_fusion.1), channel_id=1, source_target_pairs={{0,2},{1,3},{2,0},{3,1},{4,6},{5,7},{6,4},{7,5},{8,10},{9,11},{10,... | collective-permute-start | bytes 196616 | tf_op jit(solution)/shard_map/ppermute | solution.py:260
  53.2 13.8 %collective-permute-start.14 = (bf16[1920,128]{1,0:T(8,128)(2,1)S(1)}, bf16[1920,128]{1,0:T(8,128)(2,1)S(1)}, u32[]{:S(2)}, u32[]{:S(2)}) collective-permute-start(bf16[1920,128]{1,0:T(8,128)(2,1)S(1)} %copy-done.14), channel_id=1, source_target_pairs={{0,1},{1,0},{2,3},{3,2},{4,5},{5,4},{6,7},{7,6},{8,9},{9,8},{10,11... | collective-permute-start | bytes 1474568 | tf_op jit(solution)/shard_map/ppermute | solution.py:260
  57.0 6.7 %collective-permute-start.10 = (bf16[2,64,128]{2,1,0:T(8,128)(2,1)S(1)}, bf16[2,64,128]{2,1,0:T(8,128)(2,1)S(1)}, u32[]{:S(2)}, u32[]{:S(2)}) collective-permute-start(bf16[2,64,128]{2,1,0:T(8,128)(2,1)S(1)} %slice_select_fusion.3), channel_id=1, source_target_pairs={{8,0},{9,1},{10,2},{11,3},{12,4},{13,5},{14,6},{15,7},{24,16},{25,... | collective-permute-start | bytes 98312 | tf_op jit(solution)/shard_map/ppermute | solution.py:270
  58.3 8.0 %collective-permute-start.11 = (bf16[2,64,128]{2,1,0:T(8,128)(2,1)S(1)}, bf16[2,64,128]{2,1,0:T(8,128)(2,1)S(1)}, u32[]{:S(2)}, u32[]{:S(2)}) collective-permute-start(bf16[2,64,128]{2,1,0:T(8,128)(2,1)S(1)} %slice_select_fusion.3), channel_id=1, source_target_pairs={{12,0},{13,1},{14,2},{15,3},{28,16},{29,17},{30,18},{31,19}} | collective-permute-start | bytes 98312 | tf_op jit(solution)/shard_map/ppermute | solution.py:270
  59.7 6.5 %collective-permute-start.9 = (bf16[2,64,128]{2,1,0:T(8,128)(2,1)S(1)}, bf16[2,64,128]{2,1,0:T(8,128)(2,1)S(1)}, u32[]{:S(2)}, u32[]{:S(2)}) collective-permute-start(bf16[2,64,128]{2,1,0:T(8,128)(2,1)S(1)} %slice_select_fusion.3), channel_id=1, source_target_pairs={{4,0},{5,1},{6,2},{7,3},{8,4},{9,5},{10,6},{11,7},{12,8},{13,9},{1... | collective-permute-start | bytes 98312 | tf_op jit(solution)/shard_map/ppermute | solution.py:270
  66.3 6.0 %collective-permute-start.12 = (bf16[2,64,128]{2,1,0:T(8,128)(2,1)S(1)}, bf16[2,64,128]{2,1,0:T(8,128)(2,1)S(1)}, u32[]{:S(2)}, u32[]{:S(2)}) collective-permute-start(bf16[2,64,128]{2,1,0:T(8,128)(2,1)S(1)} %compare_select_fusion.17), channel_id=1, source_target_pairs={{0,2},{1,3},{2,0},{3,1},{4,6},{5,7},{6,4},{7,5},{8,10},{9,11},{10,... | collective-permute-start | bytes 98312 | tf_op jit(solution)/shard_map/ppermute | solution.py:260
  66.9 0.8 copy-start.2
  69.9 36.3 %copy-start.1 = (f32[4,2,4,64,128]{4,3,2,1,0:T(8,128)S(1)}, f32[4,2,4,64,128]{4,3,2,1,0:T(8,128)}, u32[]{:S(2)}) copy-start(f32[4,2,4,64,128]{4,3,2,1,0:T(8,128)} %get-tuple-element.28) | copy-start | bytes 3145732
  69.9 7.4 %collective-permute-start.15 = (bf16[240,128]{1,0:T(8,128)(2,1)}, bf16[240,128]{1,0:T(8,128)(2,1)S(1)}, u32[]{:S(2)}, u32[]{:S(2)}) collective-permute-start(bf16[240,128]{1,0:T(8,128)(2,1)} %get-tuple-element.33), channel_id=1, source_target_pairs={{0,2},{1,3},{2,0},{3,1},{4,6},{5,7},{6,4},{7,5},{8,10},{9,11},{10,... | collective-permute-start | bytes 184328 | tf_op jit(solution)/shard_map/ppermute | solution.py:260
  71.4 7.6 %collective-permute-start.16 = (bf16[240,128]{1,0:T(8,128)(2,1)}, bf16[240,128]{1,0:T(8,128)(2,1)S(1)}, u32[]{:S(2)}, u32[]{:S(2)}) collective-permute-start(bf16[240,128]{1,0:T(8,128)(2,1)} %get-tuple-element.34), channel_id=1, source_target_pairs={{0,4},{1,5},{2,6},{3,7},{4,0},{5,1},{6,2},{7,3},{8,12},{9,13},{10,... | collective-permute-start | bytes 184328 | tf_op jit(solution)/shard_map/ppermute | solution.py:260
  72.3 9.0 %collective-permute-start.17 = (bf16[240,128]{1,0:T(8,128)(2,1)}, bf16[240,128]{1,0:T(8,128)(2,1)S(1)}, u32[]{:S(2)}, u32[]{:S(2)}) collective-permute-start(bf16[240,128]{1,0:T(8,128)(2,1)} %get-tuple-element.35), channel_id=1, source_target_pairs={{0,6},{1,7},{2,4},{3,5},{4,2},{5,3},{6,0},{7,1},{8,14},{9,15},{10,... | collective-permute-start | bytes 184328 | tf_op jit(solution)/shard_map/ppermute | solution.py:260
  73.5 8.6 %collective-permute-start.18 = (bf16[240,128]{1,0:T(8,128)(2,1)}, bf16[240,128]{1,0:T(8,128)(2,1)S(1)}, u32[]{:S(2)}, u32[]{:S(2)}) collective-permute-start(bf16[240,128]{1,0:T(8,128)(2,1)} %get-tuple-element.36), channel_id=1, source_target_pairs={{0,8},{1,9},{2,10},{3,11},{4,12},{5,13},{6,14},{7,15},{8,0},{9,1},... | collective-permute-start | bytes 184328 | tf_op jit(solution)/shard_map/ppermute | solution.py:260
  75.8 8.6 %collective-permute-start.19 = (bf16[240,128]{1,0:T(8,128)(2,1)}, bf16[240,128]{1,0:T(8,128)(2,1)S(1)}, u32[]{:S(2)}, u32[]{:S(2)}) collective-permute-start(bf16[240,128]{1,0:T(8,128)(2,1)} %get-tuple-element.37), channel_id=1, source_target_pairs={{0,10},{1,11},{2,8},{3,9},{4,14},{5,15},{6,12},{7,13},{8,2},{9,3},... | collective-permute-start | bytes 184328 | tf_op jit(solution)/shard_map/ppermute | solution.py:260
  77.3 7.1 %collective-permute-start.20 = (bf16[240,128]{1,0:T(8,128)(2,1)}, bf16[240,128]{1,0:T(8,128)(2,1)S(1)}, u32[]{:S(2)}, u32[]{:S(2)}) collective-permute-start(bf16[240,128]{1,0:T(8,128)(2,1)} %get-tuple-element.38), channel_id=1, source_target_pairs={{0,12},{1,13},{2,14},{3,15},{4,8},{5,9},{6,10},{7,11},{8,4},{9,5},... | collective-permute-start | bytes 184328 | tf_op jit(solution)/shard_map/ppermute | solution.py:260
  79.0 7.3 %collective-permute-start.21 = (bf16[240,128]{1,0:T(8,128)(2,1)}, bf16[240,128]{1,0:T(8,128)(2,1)S(1)}, u32[]{:S(2)}, u32[]{:S(2)}) collective-permute-start(bf16[240,128]{1,0:T(8,128)(2,1)} %get-tuple-element.39), channel_id=1, source_target_pairs={{0,14},{1,15},{2,12},{3,13},{4,10},{5,11},{6,8},{7,9},{8,6},{9,7},... | collective-permute-start | bytes 184328 | tf_op jit(solution)/shard_map/ppermute | solution.py:260
  81.2 11.0 %collective-permute-start.13 = (bf16[4,64,128]{2,1,0:T(8,128)(2,1)S(1)}, bf16[4,64,128]{2,1,0:T(8,128)(2,1)S(1)}, u32[]{:S(2)}, u32[]{:S(2)}) collective-permute-start(bf16[4,64,128]{2,1,0:T(8,128)(2,1)S(1)} %fusion.5), channel_id=1, source_target_pairs={{0,1},{1,0},{2,3},{3,2},{4,5},{5,4},{6,7},{7,6},{8,9},{9,8},{10,11... | collective-permute-start | bytes 196616 | tf_op jit(solution)/shard_map/ppermute | solution.py:260
  87.3 16.4 %copy-start.3 = (bf16[240,128]{1,0:T(8,128)(2,1)}, bf16[240,128]{1,0:T(8,128)(2,1)S(1)}, u32[]{:S(2)}) copy-start(bf16[240,128]{1,0:T(8,128)(2,1)S(1)} %add_convert_fusion.1.own) | copy-start | bytes 184324
  87.3 7.2 %collective-permute-start.22 = (bf16[240,128]{1,0:T(8,128)(2,1)S(1)}, bf16[240,128]{1,0:T(8,128)(2,1)S(1)}, u32[]{:S(2)}, u32[]{:S(2)}) collective-permute-start(bf16[240,128]{1,0:T(8,128)(2,1)S(1)} %add_convert_fusion.1.own), channel_id=1, source_target_pairs={{0,2},{1,3},{2,0},{3,1},{4,6},{5,7},{6,4},{7,5},{8,10},{9,11},{10,... | collective-permute-start | bytes 184328 | tf_op jit(solution)/shard_map/ppermute | solution.py:260
  87.9 8.8 %collective-permute-start.23 = (bf16[240,128]{1,0:T(8,128)(2,1)S(1)}, bf16[240,128]{1,0:T(8,128)(2,1)S(1)}, u32[]{:S(2)}, u32[]{:S(2)}) collective-permute-start(bf16[240,128]{1,0:T(8,128)(2,1)S(1)} %add_convert_fusion.1.own), channel_id=1, source_target_pairs={{0,4},{1,5},{2,6},{3,7},{4,0},{5,1},{6,2},{7,3},{8,12},{9,13},{10,... | collective-permute-start | bytes 184328 | tf_op jit(solution)/shard_map/ppermute | solution.py:260
  90.1 9.1 %collective-permute-start.24 = (bf16[240,128]{1,0:T(8,128)(2,1)S(1)}, bf16[240,128]{1,0:T(8,128)(2,1)S(1)}, u32[]{:S(2)}, u32[]{:S(2)}) collective-permute-start(bf16[240,128]{1,0:T(8,128)(2,1)S(1)} %add_convert_fusion.1.own), channel_id=1, source_target_pairs={{0,6},{1,7},{2,4},{3,5},{4,2},{5,3},{6,0},{7,1},{8,14},{9,15},{10,... | collective-permute-start | bytes 184328 | tf_op jit(solution)/shard_map/ppermute | solution.py:260
  91.6 7.7 %collective-permute-start.25 = (bf16[240,128]{1,0:T(8,128)(2,1)S(1)}, bf16[240,128]{1,0:T(8,128)(2,1)S(1)}, u32[]{:S(2)}, u32[]{:S(2)}) collective-permute-start(bf16[240,128]{1,0:T(8,128)(2,1)S(1)} %add_convert_fusion.1.own), channel_id=1, source_target_pairs={{0,8},{1,9},{2,10},{3,11},{4,12},{5,13},{6,14},{7,15},{8,0},{9,1},... | collective-permute-start | bytes 184328 | tf_op jit(solution)/shard_map/ppermute | solution.py:260
  92.2 8.2 %collective-permute-start.26 = (bf16[240,128]{1,0:T(8,128)(2,1)S(1)}, bf16[240,128]{1,0:T(8,128)(2,1)S(1)}, u32[]{:S(2)}, u32[]{:S(2)}) collective-permute-start(bf16[240,128]{1,0:T(8,128)(2,1)S(1)} %add_convert_fusion.1.own), channel_id=1, source_target_pairs={{0,10},{1,11},{2,8},{3,9},{4,14},{5,15},{6,12},{7,13},{8,2},{9,3},... | collective-permute-start | bytes 184328 | tf_op jit(solution)/shard_map/ppermute | solution.py:260
  94.5 9.1 %copy-start.6 = (bf16[240,128]{1,0:T(8,128)(2,1)}, bf16[240,128]{1,0:T(8,128)(2,1)S(1)}, u32[]{:S(2)}) copy-start(bf16[240,128]{1,0:T(8,128)(2,1)S(1)} %collective-permute-done.22.refs_0_) | copy-start | bytes 184324
  94.5 6.1 %collective-permute-start.27 = (bf16[240,128]{1,0:T(8,128)(2,1)S(1)}, bf16[240,128]{1,0:T(8,128)(2,1)S(1)}, u32[]{:S(2)}, u32[]{:S(2)}) collective-permute-start(bf16[240,128]{1,0:T(8,128)(2,1)S(1)} %add_convert_fusion.1.own), channel_id=1, source_target_pairs={{0,12},{1,13},{2,14},{3,15},{4,8},{5,9},{6,10},{7,11},{8,4},{9,5},... | collective-permute-start | bytes 184328 | tf_op jit(solution)/shard_map/ppermute | solution.py:260
  96.7 6.9 %copy-start.7 = (bf16[240,128]{1,0:T(8,128)(2,1)}, bf16[240,128]{1,0:T(8,128)(2,1)S(1)}, u32[]{:S(2)}) copy-start(bf16[240,128]{1,0:T(8,128)(2,1)S(1)} %collective-permute-done.23.refs_1_) | copy-start | bytes 184324
  96.7 6.9 %collective-permute-start.28 = (bf16[240,128]{1,0:T(8,128)(2,1)S(1)}, bf16[240,128]{1,0:T(8,128)(2,1)S(1)}, u32[]{:S(2)}, u32[]{:S(2)}) collective-permute-start(bf16[240,128]{1,0:T(8,128)(2,1)S(1)} %add_convert_fusion.1.own), channel_id=1, source_target_pairs={{0,14},{1,15},{2,12},{3,13},{4,10},{5,11},{6,8},{7,9},{8,6},{9,7},... | collective-permute-start | bytes 184328 | tf_op jit(solution)/shard_map/ppermute | solution.py:260
  99.2 4.4 %copy-start.8 = (bf16[240,128]{1,0:T(8,128)(2,1)}, bf16[240,128]{1,0:T(8,128)(2,1)S(1)}, u32[]{:S(2)}) copy-start(bf16[240,128]{1,0:T(8,128)(2,1)S(1)} %collective-permute-done.24.refs_2_) | copy-start | bytes 184324
  99.3 4.4 %copy-start.9 = (bf16[240,128]{1,0:T(8,128)(2,1)}, bf16[240,128]{1,0:T(8,128)(2,1)S(1)}, u32[]{:S(2)}) copy-start(bf16[240,128]{1,0:T(8,128)(2,1)S(1)} %collective-permute-done.25.refs_3_) | copy-start | bytes 184324
  100.4 3.3 %copy-start.10 = (bf16[240,128]{1,0:T(8,128)(2,1)}, bf16[240,128]{1,0:T(8,128)(2,1)S(1)}, u32[]{:S(2)}) copy-start(bf16[240,128]{1,0:T(8,128)(2,1)S(1)} %collective-permute-done.26.refs_4_) | copy-start | bytes 184324
  100.6 3.0 %copy-start.11 = (bf16[240,128]{1,0:T(8,128)(2,1)}, bf16[240,128]{1,0:T(8,128)(2,1)S(1)}, u32[]{:S(2)}) copy-start(bf16[240,128]{1,0:T(8,128)(2,1)S(1)} %collective-permute-done.27.refs_5_) | copy-start | bytes 184324
  103.7 0.6 copy-start.12
  106.2 2.1 %copy-start = (bf16[1920,128]{1,0:T(8,128)(2,1)S(1)}, bf16[1920,128]{1,0:T(8,128)(2,1)}, u32[]{:S(2)}) copy-start(bf16[1920,128]{1,0:T(8,128)(2,1)} %shard_map.140) | copy-start | bytes 1474564
  106.2 2.1 %collective-permute-start.29 = (bf16[1920,128]{1,0:T(8,128)(2,1)}, bf16[1920,128]{1,0:T(8,128)(2,1)S(1)}, u32[]{:S(2)}, u32[]{:S(2)}) collective-permute-start(bf16[1920,128]{1,0:T(8,128)(2,1)} %shard_map.140), channel_id=1, source_target_pairs={{0,1},{1,0},{2,3},{3,2},{4,5},{5,4},{6,7},{7,6},{8,9},{9,8},{10,11... | collective-permute-start | bytes 1474568 | tf_op jit(solution)/shard_map/ppermute | solution.py:260

commit v2 on v1

--- a/solution.py
+++ b/solution.py
@@ -16,14 +16,15 @@
 _SMEM = pl.BlockSpec(memory_space=pltpu.SMEM)
 
 
-def _call(kernel, out_shape, in_specs, scratch=(), flops=0, moved=0):
+def _call(kernel, out_shape, in_specs, scratch=(), flops=0, moved=0, room=16, grid=()):
     return pl.pallas_call(
         kernel,
         out_shape=out_shape,
+        grid=grid,
         in_specs=in_specs,
         out_specs=jax.tree.map(lambda _: _VMEM, out_shape),
         scratch_shapes=list(scratch),
-        compiler_params=pltpu.CompilerParams(vmem_limit_bytes=56 << 20),
+        compiler_params=pltpu.CompilerParams(vmem_limit_bytes=room << 20),
         cost_estimate=pl.CostEstimate(flops=flops, bytes_accessed=moved, transcendentals=0),
     )
 
@@ -110,42 +111,50 @@
     add(5, jnp.sum(gout.astype(F32), axis=0, keepdims=True))
 
 
-def _store_g(g_ref, g, slots, h, w):
-    c = g_ref.shape[-1]
-    for t in range(2):
-        g_ref[:, t] = g[:, t * c : (t + 1) * c].reshape(slots, h, w, c)
-
-
-def _early_kernel(sc, fr, ha, co, w_ref, cb, sw, sb, lat_ref, g_ref, acc, xk):
+def _fill_early(sc, fr, ha, xk):
     slots, _, h, w, c = fr.shape
     for s in range(slots):
         for f in range(2):
-            mine = fr[s, f], ha[s, f]
             spots = [(s - 1, f + 2, None)] if s > 0 else []
             if s + 1 < slots:
                 spots.append((s, f, sc[1 + s + 1] == 0))
             for slot, j, keep in spots:
-                a, b = mine
+                a, b = fr[s, f], ha[s, f]
                 if keep is not None:
                     a = jnp.where(keep, a, jnp.zeros_like(a))
                     b = jnp.where(keep, b, jnp.zeros_like(b))
                 _put(xk, (slot, j), slice(1, 1 + h), a)
                 _put(xk, (slot, j), slice(0, 1), b[:1])
                 _put(xk, (slot, j), slice(h + 1, h + 2), b[1:])
-    gout = jnp.concatenate(
+
+
+def _early_gout(sc, co):
+    slots, _, h, w, c = co.shape
+    return jnp.concatenate(
         [
             jnp.where(s < sc[0], co[s, 0], jnp.zeros_like(co[s, 0])).reshape(h * w, c)
             for s in range(1, slots)
         ],
         axis=0,
     )
-    lat, g, hidden = _head(xk, gout, w_ref, cb, sw, sb, h)
+
+
+def _early_kernel(sc, fr, ha, co, w_ref, cb, sw, sb, lat_ref, g_ref, hid_ref, xk):
+    slots, _, h, w, c = fr.shape
+    _fill_early(sc, fr, ha, xk)
+    lat, g, hidden = _head(xk, _early_gout(sc, co), w_ref, cb, sw, sb, h)
     for s in range(1, slots):
         part = lat[(s - 1) * h * w : s * h * w]
         lat_ref[s - 1] = (
             jnp.where(s < sc[0], part, jnp.zeros_like(part)).astype(BF).reshape(h, w, c)
         )
-    _store_g(g_ref, g, slots - 1, h, w)
+    g_ref[...] = g
+    hid_ref[...] = hidden
+
+
+def _early_sums_kernel(sc, fr, ha, co, g_ref, hid_ref, acc, xk):
+    _, _, h, w, c = fr.shape
+    _fill_early(sc, fr, ha, xk)
     n9 = 9 * c
 
     def add(kind, value):
@@ -158,12 +167,13 @@
             acc[at : at + 1] = value
 
     acc[3 * n9 + 2 * c :] = jnp.zeros((acc.shape[0] - 3 * n9 - 2 * c, c), F32)
-    _weight_grads(xk, g, hidden, gout, h, add)
+    _weight_grads(xk, g_ref[...], hid_ref[...], _early_gout(sc, co), h, add)
 
 
 def _late_kernel(
-    sc, fr, ha, tail, co, w_ref, cb, sw, sb, early, lat_ref, g_ref, send, keep, xk, acc
+    sc, frs, has, tail, cos, w_ref, cb, sw, sb, early, lat_ref, g_ref, send, keep, xk, acc
 ):
+    fr, ha, co = frs.at[0], has.at[0], cos.at[0]
     _, h, w, c = fr.shape
     on = sc[1] == 0
     for f in range(2):
@@ -181,8 +191,7 @@
     gout = jnp.where(filled, co[0], jnp.zeros_like(co[0])).reshape(h * w, c)
     lat, g, hidden = _head(xk, gout, w_ref, cb, sw, sb, h)
     lat_ref[...] = jnp.where(filled, lat, jnp.zeros_like(lat)).astype(BF).reshape(h, w, c)
-    for t in range(2):
-        g_ref[t] = g[:, t * c : (t + 1) * c].reshape(h, w, c)
+    g_ref[...] = g
     n9 = 9 * c
 
     def add(kind, value):
@@ -197,7 +206,11 @@
 
     tail_rows = slice(3 * n9 + 2 * c, acc.shape[0])
     acc[tail_rows] = early[tail_rows]
-    _weight_grads(xk, g, hidden, gout, h, add)
+
+    @pl.when(sc[0] >= 0)
+    def _():
+        _weight_grads(xk, g, hidden, gout, h, add)
+
     half = send.shape[0]
     core = sc[sc.shape[0] - 1]
     send[...] = acc[pl.ds(pl.multiple_of((1 - core) * half, 16), half)].astype(BF)
@@ -205,8 +218,8 @@
 
 
 def _back_kernel(sc, g0, g1, w_ref, out_ref, cache_ref, xk):
-    _, h, w, c = g0.shape
-    slots = g1.shape[0] + 1
+    slots, _, h, w, c = out_ref.shape
+    m = h * w
     zero = jnp.zeros((1, w, c), BF)
     for kw in range(3):
         for j in range(4):
@@ -218,8 +231,10 @@
         for kw in range(3):
             xk[kw, 0, f, 1 : 1 + h] = blank
             xk[kw, slots, f + 2, 1 : 1 + h] = blank
+        lanes = slice(f * c, (f + 1) * c)
         for s in range(slots):
-            v = g0[f] if s == 0 else g1[s - 1, f]
+            v = g0[:, lanes] if s == 0 else g1[(s - 1) * m : s * m, lanes]
+            v = v.reshape(h, w, c)
             _put(xk, (s + 1, f), slice(1, 1 + h), v)
             _put(
                 xk, (s, f + 2), slice(1, 1 + h), jnp.where(sc[1 + s] == 0, v, jnp.zeros_like(v))
@@ -248,19 +263,38 @@
         ref[...] = piece(lax.bitwise_xor(chip, k + 1)).astype(BF)
 
 
-def _join_kernel(sc, own, *refs):
-    half = refs[-1]
-    rows = own.shape[0]
+def _tail_kernel(sc, fr, ha, out):
+    h2 = fr.shape[1] * fr.shape[2]
+    live = sc[0] > 0
+    for ref, rows in ((fr, slice(0, h2)), (ha, slice(h2, out.shape[0]))):
+        v = ref[...].reshape(rows.stop - rows.start, *out.shape[1:])
+        out[rows] = jnp.where(live, v, jnp.full_like(v, EMPTY_FRAME))
+
+
+def _final_kernel(sc, *refs):
+    pieces, (other, cw, sw, cb, sb, acc) = refs[:-6], refs[-6:]
+    rows, c = pieces[0].shape
+    half = rows * len(pieces)
     chip = sc[sc.shape[0] - 2]
-    for k, ref in enumerate((own,) + refs[:-1]):
-        half[pl.ds(pl.multiple_of(lax.bitwise_xor(chip, k) * rows, 16), rows)] = ref[...]
+    core = sc[sc.shape[0] - 1]
+    for k, ref in enumerate(pieces):
+        at = lax.bitwise_xor(chip, k) * rows
+        acc[pl.ds(pl.multiple_of(core * half + at, 16), rows)] = ref[...].astype(F32)
+        acc[pl.ds(pl.multiple_of((1 - core) * half + at, 16), rows)] = other[
+            k * rows : (k + 1) * rows
+        ].astype(F32)
+    n27, n29 = 27 * c, 29 * c
+    cw[...] = acc[:n27]
+    sw[...] = acc[n27:n29]
+    cb[...] = acc[n29 : n29 + 1]
+    sb[...] = acc[n29 + 1 : n29 + 2]
 
 
 def _xor(x, k, n, axis):
     return lax.ppermute(x, axis, [(i, i ^ k) for i in range(n)])
 
 
-def _latest_before(x, empty, axis, n, reverse=False):
+def _latest_before(x, empty, axis, n, reverse=False, beside_first=None, beside_second=None):
     index = lax.axis_index(axis)
     index = n - 1 - index if reverse else index
     core, pair = index & 1, (index >> 1) & 1
@@ -285,6 +319,8 @@
     chip = part(jnp.where(core == 0, newest(x, other), newest(other, x)), core)
     beside = _xor(chip, 2, n, axis)
     quad = part(jnp.where(pair == 0, newest(chip, beside), newest(beside, chip)), pair)
+    if beside_first is not None:
+        quad = beside_first(chip, quad)
     blocks = n // 4
     before = None
     for k in range(min(3, blocks - 1), 0, -1):
@@ -294,42 +330,18 @@
     while reach < blocks - 1:
         before = newest(shift(before, 4 * reach), before)
         reach *= 2
+    first = before
     before = join(before, _xor(before, 2, n, axis), pair)
     before = jnp.where(pair == 0, before, newest(before, beside))
+    if beside_second is not None:
+        before = beside_second(first, before)
     before = join(before, _xor(before, 1, n, axis), core)
     before = jnp.where(core == 0, before, newest(before, other))
     return jnp.where(before > empty / 2, jnp.zeros_like(before), before)
 
 
-def _sum_over(send, keep, sc, axis, n):
-    rows, c = keep.shape
-    chips = min(8, n // 2)
-    piece = rows // chips
-    got = _xor(send, 1, n, axis)
-    outs = _call(
-        _cut_kernel,
-        [jax.ShapeDtypeStruct((piece, c), F32)]
-        + [jax.ShapeDtypeStruct((piece, c), BF)] * (chips - 1),
-        [_SMEM, _VMEM, _VMEM],
-    )(sc, keep, got)
-    total = outs[0]
-    for k in range(1, chips):
-        total = total + _xor(outs[k], 2 * k, n, axis).astype(F32)
-    mine = total.astype(BF)
-    k = 2 * chips
-    while k < n:
-        total = mine.astype(F32) + _xor(mine, k, n, axis).astype(F32)
-        mine = total.astype(BF)
-        k *= 2
-    others = [_xor(mine, 2 * k, n, axis) for k in range(1, chips)]
-    half = _call(
-        _join_kernel, jax.ShapeDtypeStruct((rows, c), BF), [_SMEM] + [_VMEM] * chips
-    )(sc, mine, *others)
-    other = _xor(half, 1, n, axis)
-    core = sc[-1]
-    low = jnp.where(core == 0, half, other)
-    high = jnp.where(core == 0, other, half)
-    return jnp.concatenate([low, high], axis=0).astype(F32)
+def _after(value, *earlier):
+    return lax.optimization_barrier((value, *earlier))[0]
 
 
 def body(
@@ -359,49 +371,90 @@
     )
     wt = conv_weight.reshape(27, c, c)
     cb, sb = conv_bias.reshape(1, c), stride_bias.reshape(1, c)
-
-    last = jnp.maximum(count - 1, 0)
-    tail = jnp.concatenate(
-        [
-            lax.dynamic_index_in_dim(frames, last, 0, False).reshape(2 * h, w, c),
-            lax.dynamic_index_in_dim(row_halo, last, 0, False).reshape(4, w, c),
-        ],
-        axis=0,
-    )
-    tail = jnp.where(count > 0, tail, jnp.asarray(EMPTY_FRAME, BF))
-    arrived = _latest_before(tail, EMPTY_FRAME, axis, n)
-
     unit = 16 * 2 * chips
     rows = -(-(29 * c + 2) // unit) * unit
     m = h * w
-    lat1, g1, early = _call(
-        _early_kernel,
-        [
-            jax.ShapeDtypeStruct((slots - 1, h, w, c), BF),
-            jax.ShapeDtypeStruct((slots - 1, 2, h, w, c), BF),
+    conv_flops = 2 * m * 36 * c * 2 * c
+
+    def newest_slot(i, sc):
+        return (jnp.maximum(sc[0] - 1, 0), 0, 0, 0, 0)
+
+    tail = pl.pallas_call(
+        _tail_kernel,
+        out_shape=jax.ShapeDtypeStruct((2 * h + 4, w, c), BF),
+        grid_spec=pltpu.PrefetchScalarGridSpec(
+            num_scalar_prefetch=1,
+            grid=(1,),
+            in_specs=[
+                pl.BlockSpec((1, 2, h, w, c), newest_slot),
+                pl.BlockSpec((1, 2, 2, w, c), newest_slot),
+            ],
+            out_specs=pl.BlockSpec((2 * h + 4, w, c), lambda i, sc: (0, 0, 0)),
+        ),
+        compiler_params=pltpu.CompilerParams(vmem_limit_bytes=60 << 20),
+    )(slab_counts, frames, row_halo)
+
+    held = {}
+
+    def early_forward(start, follow):
+        held["early"] = _call(
+            _early_kernel,
+            [
+                jax.ShapeDtypeStruct((slots - 1, h, w, c), BF),
+                jax.ShapeDtypeStruct(((slots - 1) * m, 2 * c), BF),
+                jax.ShapeDtypeStruct(((slots - 1) * m, 2 * c), BF),
+            ],
+            [_SMEM] + [_VMEM] * 7,
+            [pltpu.VMEM((3, slots - 1, 4, h + 2, w, c), BF)],
+            flops=(slots - 1) * conv_flops,
+            moved=4 << 20,
+        )(_after(sc, start), frames, row_halo, cotangent, wt, cb, stride_weight, sb)
+        return _after(follow, held["early"][1])
+
+    def early_sums(start, follow):
+        _, g1, hid1 = held["early"]
+        held["sums"] = _call(
+            _early_sums_kernel,
             jax.ShapeDtypeStruct((rows, c), F32),
-        ],
-        [_SMEM] + [_VMEM] * 7,
-        [pltpu.VMEM((3, slots - 1, 4, h + 2, w, c), BF)],
-        flops=2 * 2 * (slots - 1) * m * 36 * c * 2 * c,
-        moved=6 << 20,
-    )(sc, frames, row_halo, cotangent, wt, cb, stride_weight, sb)
+            [_SMEM] + [_VMEM] * 5,
+            [pltpu.VMEM((3, slots - 1, 4, h + 2, w, c), BF)],
+            flops=(slots - 1) * conv_flops,
+            moved=4 << 20,
+        )(_after(sc, start), frames, row_halo, cotangent, g1, hid1)
+        return _after(follow, held["sums"])
+
+    arrived = _latest_before(
+        tail, EMPTY_FRAME, axis, n, beside_first=early_forward, beside_second=early_sums
+    )
+    lat1, g1, _ = held["early"]
+
+    def first(*shape):
+        return pl.BlockSpec((1, *shape), lambda i: (0,) * (len(shape) + 1))
 
     lat0, g0, send, keep = _call(
         _late_kernel,
         [
             jax.ShapeDtypeStruct((h, w, c), BF),
-            jax.ShapeDtypeStruct((2, h, w, c), BF),
+            jax.ShapeDtypeStruct((m, 2 * c), BF),
             jax.ShapeDtypeStruct((rows // 2, c), BF),
             jax.ShapeDtypeStruct((rows // 2, c), F32),
         ],
-        [_SMEM] + [_VMEM] * 9,
+        [_SMEM, first(2, h, w, c), first(2, 2, w, c), _VMEM, first(1, h, w, c)] + [_VMEM] * 5,
         [pltpu.VMEM((3, 1, 4, h + 2, w, c), BF), pltpu.VMEM((rows, c), F32)],
-        flops=2 * 2 * m * 36 * c * 2 * c,
+        flops=2 * conv_flops,
         moved=6 << 20,
-    )(sc, frames[0], row_halo[0], arrived, cotangent[0], wt, cb, stride_weight, sb, early)
-
-    total = _sum_over(send, keep, sc, axis, n)
+        grid=(1,),
+    )(sc, frames, row_halo, arrived, cotangent, wt, cb, stride_weight, sb, held["sums"])
+
+    got = _xor(send, 1, n, axis)
+    piece = rows // 2 // chips
+    own, *outs = _call(
+        _cut_kernel,
+        [jax.ShapeDtypeStruct((piece, c), F32)]
+        + [jax.ShapeDtypeStruct((piece, c), BF)] * (chips - 1),
+        [_SMEM, _VMEM, _VMEM],
+        room=12,
+    )(sc, keep, got)
 
     grad, cache = _call(
         _back_kernel,
@@ -411,9 +464,34 @@
         ],
         [_SMEM] + [_VMEM] * 3,
         [pltpu.VMEM((3, slots + 1, 4, h + 2, w, c), BF)],
-        flops=2 * (slots + 1) * m * 36 * c * 2 * c,
+        flops=(slots + 1) * conv_flops,
         moved=6 << 20,
-    )(sc, g0, g1, wt)
+        room=24,
+    )(_after(sc, own), g0, g1, wt)
+
+    total = _after(own, cache)
+    for k in range(1, chips):
+        total = total + _xor(outs[k - 1], 2 * k, n, axis).astype(F32)
+    mine = total.astype(BF)
+    k = 2 * chips
+    while k < n:
+        mine = (mine.astype(F32) + _xor(mine, k, n, axis).astype(F32)).astype(BF)
+        k *= 2
+    pieces = [mine] + [_xor(mine, 2 * k, n, axis) for k in range(1, chips)]
+    other = _xor(jnp.concatenate(pieces, axis=0), 1, n, axis)
+    cwg, swg, cbg, sbg = _call(
+        _final_kernel,
+        [
+            jax.ShapeDtypeStruct((27 * c, c), F32),
+            jax.ShapeDtypeStruct((2 * c, c), F32),
+            jax.ShapeDtypeStruct((1, c), F32),
+            jax.ShapeDtypeStruct((1, c), F32),
+        ],
+        [_SMEM] + [_VMEM] * (chips + 1),
+        [pltpu.VMEM((rows, c), F32)],
+        room=12,
+    )(sc, *pieces, other)
+
     returned = _latest_before(cache, EMPTY_GRAD, axis, n, reverse=True)
     newest = (jnp.arange(slots, dtype=jnp.int32) == count - 1)[:, None, None, None, None]
     back = returned.reshape(1, 2, h, w, c).astype(F32)
@@ -422,10 +500,10 @@
     return (
         latents,
         frames_grad,
-        total[: 27 * c].reshape(3, 3, 3, c, c),
-        total[29 * c],
-        total[27 * c : 29 * c].reshape(2, c, c),
-        total[29 * c + 1],
+        cwg.reshape(3, 3, 3, c, c),
+        cbg[0],
+        swg.reshape(2, c, c),
+        sbg[0],
     )
 
 

time: 112 us -> 94.2 us (0.84)
  Pallas kernels: 26.6 us -> 17.3 us
  waiting for transfers between devices: 25.6 us -> 20.2 us
  other arithmetic: 6.71 us -> 3.84 us
    ppermute x24, waiting for transfers between devices: 19.4 us -> 12.8 us  [_xor(): return lax.ppermute(x, axis, [(i, i ^ k) for i in range(n)])]
    unnamed x30, local copies, waits for them, and re-layouts: 1.44 us -> 7.35 us
    pallas_call x3 -> x5, Pallas kernels: 14.8 us -> 10.3 us  [the longest x1 3.2 us: early_forward(): _call(_early_kernel, [jax.ShapeDtypeStruct((slots - 1, h, w, c), BF), jax...]
    dynamic_slice x2 -> x0, local copies, waits for them, and re-layouts: 3.15 us -> none  [the longest x1 1.65 us: body(): lax.dynamic_index_in_dim(frames, last, 0, False).reshape(2 * h, w, c)]
    pallas_call x1, Pallas kernels: 5.82 us -> 2.83 us  [body(): _call(_late_kernel, [jax.ShapeDtypeStruct((h, w, c), BF), jax.ShapeDtypeS...]
    pallas_call x1, Pallas kernels: 5.96 us -> 4.15 us  [body(): _call(_back_kernel, [jax.ShapeDtypeStruct((slots, 2, h, w, c), F32), jax....]
    squeeze x1 -> x0, local copies, waits for them, and re-layouts: 1.47 us -> none  [body(): cotangent[0]]
    ppermute x24, starting transfers between devices: 29.5 us -> 30.8 us  [_xor(): return lax.ppermute(x, axis, [(i, i ^ k) for i in range(n)])]
  transfers between devices with their start and end apart: 30 -> 30, of which waited for: 14 -> 11; matrix products, arithmetic and copies ran while one was open for 4% -> 3% of each run, Pallas kernels for 12% -> 11%
where the time goes in v2:
time: 94.2 us; the launch traced here: 93.7 us
  starting transfers between devices  43.3 us (46%)
  waiting for transfers between devices  20.2 us (21%)
  Pallas kernels  17.3 us (18%)
  local copies, waits for them, and re-layouts  7.36 us (8%)
  other arithmetic  3.84 us (4%)
  between operations  1.67 us (2%)
    ppermute x24, starting transfers between devices, _xor(): return lax.ppermute(x, axis, [(i, i ^ k) for i in range(n)])  30.8 us
    ppermute x24, waiting for transfers between devices, _xor(): return lax.ppermute(x, axis, [(i, i ^ k) for i in range(n)])  12.8 us
    ppermute x6, starting transfers between devices, shift(): lax.ppermute(v, axis, [(b, a) for a, b in pairs] if reverse else pairs)  12.5 us
    ppermute x6, waiting for transfers between devices, shift(): lax.ppermute(v, axis, [(b, a) for a, b in pairs] if reverse else pairs)  7.39 us
    unnamed x30, local copies, waits for them, and re-layouts  7.35 us
    pallas_call x1, Pallas kernels, body(): _call(_back_kernel, [jax.ShapeDtypeStruct((slots, 2, h, w, c), F32), jax....  4.15 us
    pallas_call x1, Pallas kernels, early_forward(): _call(_early_kernel, [jax.ShapeDtypeStruct((slots - 1, h, w, c), BF), jax...  3.2 us
    pallas_call x1, Pallas kernels, body(): _call(_late_kernel, [jax.ShapeDtypeStruct((h, w, c), BF), jax.ShapeDtypeS...  2.83 us
  transfers between devices with their start and end apart: 30, of which 11 were waited for; matrix products, arithmetic and copies ran while one was open for 3% of the time, Pallas kernels for 11%

profile of v2, /device:TPU:0, one launch (start us, length us, event | category | flops | bytes accessed | tf_op | source)
XLA Modules:
  0.0 93.7 jit_solution(17230251625535918612)
XLA Ops:
  1.3 1.6 %shard_map.136 = bf16[12,64,128]{2,1,0:T(8,128)(2,1)} custom-call(s32[1]{0:T(128)S(6)} %copy.23.sc, bf16[4,2,4,64,128]{4,3,2,1,0:T(8,128)(2,1)} %frs.1, bf16[4,2,2,64,128]{4,3,2,1,0:T(8,128)(2,1)} %has.1), custom_call_target="tpu_custom_call" | custom-call | tf_op jit(solution)/shard_map/pallas_call | solution.py:382
  2.9 0.5 collective-permute-start
  3.4 0.7 pad_add_fusion.sc
  4.1 0.5 collective-permute-done
  4.7 1.0 %fusion.2 = bf16[12,64,128]{2,1,0:T(8,128)(2,1)S(1)} fusion(bf16[12,64,128]{2,1,0:T(8,128)(2,1)S(1)} %collective-permute-done, bf16[12,64,128]{2,1,0:T(8,128)(2,1)} %shard_map.136, pred[]{:T(512)S(6)} %eq.16), kind=kLoop, calls=%fused_computation.18 | loop fusion | flops 491520 | bytes 589825 | tf_op jit(solution)/shard_map/jit(_where)/select_n | solution.py:319
  5.6 2.9 %collective-permute-start.1 = (bf16[6,64,128]{2,1,0:T(8,128)(2,1)S(1)}, bf16[6,64,128]{2,1,0:T(8,128)(2,1)S(1)}, u32[]{:S(2)}, u32[]{:S(2)}) collective-permute-start(bf16[6,64,128]{2,1,0:T(8,128)(2,1)S(1)} %slice_select_fusion), channel_id=1, source_target_pairs={{0,2},{1,3},{2,0},{3,1},{4,6},{5,7},{6,4},{7,5},{8,10},{9,11},{10,... | collective-permute-start | bytes 294920 | tf_op jit(solution)/shard_map/ppermute | solution.py:294
  8.6 1.0 %copy-done = bf16[4,2,4,64,128]{4,3,2,1,0:T(8,128)(2,1)S(1)} copy-done((bf16[4,2,4,64,128]{4,3,2,1,0:T(8,128)(2,1)S(1)}, bf16[4,2,4,64,128]{4,3,2,1,0:T(8,128)(2,1)}, u32[]{:S(2)}) %copy-start) | copy-done | bytes 524312
  9.6 0.9 %copy-done.1 = bf16[4,2,2,64,128]{4,3,2,1,0:T(8,128)(2,1)S(1)} copy-done((bf16[4,2,2,64,128]{4,3,2,1,0:T(8,128)(2,1)S(1)}, bf16[4,2,2,64,128]{4,3,2,1,0:T(8,128)(2,1)}, u32[]{:S(2)}) %copy-start.1) | copy-done | bytes 262168
  10.6 1.2 %copy-done.2 = bf16[3,3,3,128,128]{4,3,2,1,0:T(8,128)(2,1)S(1)} copy-done((bf16[3,3,3,128,128]{4,3,2,1,0:T(8,128)(2,1)S(1)}, bf16[3,3,3,128,128]{4,3,2,1,0:T(8,128)(2,1)}, u32[]{:S(2)}) %copy-start.2) | copy-done | bytes 884760
  11.7 0.9 %copy-done.4 = bf16[4,1,4,64,128]{4,3,2,1,0:T(8,128)(2,1)S(1)} copy-done((bf16[4,1,4,64,128]{4,3,2,1,0:T(8,128)(2,1)S(1)}, bf16[4,1,4,64,128]{4,3,2,1,0:T(8,128)(2,1)}, u32[]{:S(2)}) %copy-start.4) | copy-done | bytes 262168
  12.7 0.8 copy-done.5
  13.5 0.7 copy-done.7
  14.2 0.7 copy-done.8
  14.8 3.2 %shard_map.137 = (bf16[3,4,64,128]{3,2,1,0:T(8,128)(2,1)S(1)}, bf16[768,256]{1,0:T(8,128)(2,1)S(1)}, bf16[768,256]{1,0:T(8,128)(2,1)S(1)}) custom-call(s32[7]{0:T(128)S(1)} %pad_add_fusion.sc, bf16[4,2,4,64,128]{4,3,2,1,0:T(8,128)(2,1)S(1)} %copy-done, bf16[4,2,2,64,128]{4,3,2,1,0:T(8,128)(2,1)S(1)} %copy-done.1, bf16[4,1,4,64,128]{4,3,2,1,0:T(8,128)(2,1)S(1)} %copy-done.4, ...), custom_call_target="tpu_custom_call" | custom-call | flops 1811939328 | bytes 4194304 | tf_op jit(solution)/shard_map/pallas_call | solution.py:400
  18.0 0.0 copy-start.10
  18.1 3.5 %collective-permute-start.2 = (bf16[3,64,128]{2,1,0:T(8,128)(2,1)S(1)}, bf16[3,64,128]{2,1,0:T(8,128)(2,1)S(1)}, u32[]{:S(2)}, u32[]{:S(2)}) collective-permute-start(bf16[3,64,128]{2,1,0:T(8,128)(2,1)S(1)} %slice_select_fusion.2), channel_id=1, source_target_pairs={{0,4},{1,5},{2,6},{3,7},{4,8},{5,9},{6,10},{7,11},{8,12},{9,13},{1... | collective-permute-start | bytes 147464 | tf_op jit(solution)/shard_map/ppermute | solution.py:304
  21.6 3.3 %collective-permute-start.4 = (bf16[3,64,128]{2,1,0:T(8,128)(2,1)S(1)}, bf16[3,64,128]{2,1,0:T(8,128)(2,1)S(1)}, u32[]{:S(2)}, u32[]{:S(2)}) collective-permute-start(bf16[3,64,128]{2,1,0:T(8,128)(2,1)S(1)} %slice_select_fusion.2), channel_id=1, source_target_pairs={{0,12},{1,13},{2,14},{3,15},{16,28},{17,29},{18,30},{19,31}} | collective-permute-start | bytes 147464 | tf_op jit(solution)/shard_map/ppermute | solution.py:304
  24.9 1.8 %collective-permute-start.3 = (bf16[3,64,128]{2,1,0:T(8,128)(2,1)S(1)}, bf16[3,64,128]{2,1,0:T(8,128)(2,1)S(1)}, u32[]{:S(2)}, u32[]{:S(2)}) collective-permute-start(bf16[3,64,128]{2,1,0:T(8,128)(2,1)S(1)} %slice_select_fusion.2), channel_id=1, source_target_pairs={{0,8},{1,9},{2,10},{3,11},{4,12},{5,13},{6,14},{7,15},{16,24},{17,... | collective-permute-start | bytes 147464 | tf_op jit(solution)/shard_map/ppermute | solution.py:304
  26.8 0.0 collective-permute-done.2
  26.8 1.7 %collective-permute-done.3 = bf16[3,64,128]{2,1,0:T(8,128)(2,1)S(1)} collective-permute-done((bf16[3,64,128]{2,1,0:T(8,128)(2,1)S(1)}, bf16[3,64,128]{2,1,0:T(8,128)(2,1)S(1)}, u32[]{:S(2)}, u32[]{:S(2)}) %collective-permute-start.3) | collective-permute-done | bytes 49184 | tf_op jit(solution)/shard_map/ppermute | solution.py:304
  28.5 0.6 collective-permute-start.5
  29.1 2.8 %shard_map.138.early = f32[3840,128]{1,0:T(8,128)S(1)} custom-call(s32[7]{0:T(128)S(1)} %pad_add_fusion.sc, bf16[4,2,4,64,128]{4,3,2,1,0:T(8,128)(2,1)S(1)} %copy-done, bf16[4,2,2,64,128]{4,3,2,1,0:T(8,128)(2,1)S(1)} %copy-done.1, bf16[4,1,4,64,128]{4,3,2,1,0:T(8,128)(2,1)S(1)} %copy-done.4, bf16[768,256]{1,0:T(8,128)(2,1)S(1)} %get-tuple-element.34.g_ref.g1, ...), custom_call_target="tpu_custom_call" | custom-call | flops 1811939328 | bytes 4194304 | tf_op jit(solution)/shard_map/pallas_call | solution.py:416
  32.0 0.7 collective-permute-done.5
  32.7 0.1 collective-permute-start.6
  32.8 1.3 %collective-permute-done.6 = bf16[6,64,128]{2,1,0:T(8,128)(2,1)S(1)} collective-permute-done((bf16[6,64,128]{2,1,0:T(8,128)(2,1)S(1)}, bf16[6,64,128]{2,1,0:T(8,128)(2,1)S(1)}, u32[]{:S(2)}, u32[]{:S(2)}) %collective-permute-start.6) | collective-permute-done | bytes 98336 | tf_op jit(solution)/shard_map/ppermute | solution.py:294
  34.2 2.8 %shard_map.139 = (bf16[4,64,128]{2,1,0:T(8,128)(2,1)S(1)}, bf16[256,256]{1,0:T(8,128)(2,1)S(1)}, bf16[1920,128]{1,0:T(8,128)(2,1)S(1)}, f32[1920,128]{1,0:T(8,128)S(1)}) custom-call(s32[7]{0:T(128)S(1)} %pad_add_fusion.sc, bf16[4,2,4,64,128]{4,3,2,1,0:T(8,128)(2,1)S(1)} %copy-done, bf16[4,2,2,64,128]{4,3,2,1,0:T(8,128)(2,1)S(1)} %copy-done.1, ...), custom_call_target="tpu_custom_call" | custom-call | flops 1207959552 | bytes 6291456 | tf_op jit(solution)/shard_map/pallas_call | solution.py:434
  37.0 0.2 collective-permute-start.7
  37.3 1.7 %collective-permute-done.7.got = bf16[1920,128]{1,0:T(8,128)(2,1)S(1)} collective-permute-done((bf16[1920,128]{1,0:T(8,128)(2,1)S(1)}, bf16[1920,128]{1,0:T(8,128)(2,1)S(1)}, u32[]{:S(2)}, u32[]{:S(2)}) %collective-permute-start.7) | collective-permute-done | bytes 491552 | tf_op jit(solution)/shard_map/ppermute | solution.py:294
  39.0 0.7 shard_map.140
  39.6 3.6 %collective-permute-start.21 = (bf16[240,128]{1,0:T(8,128)(2,1)S(1)}, bf16[240,128]{1,0:T(8,128)(2,1)S(1)}, u32[]{:S(2)}, u32[]{:S(2)}) collective-permute-start(bf16[240,128]{1,0:T(8,128)(2,1)S(1)} %get-tuple-element.55), channel_id=1, source_target_pairs={{0,14},{1,15},{2,12},{3,13},{4,10},{5,11},{6,8},{7,9},{8,6},{9,7},... | collective-permute-start | bytes 184328 | tf_op jit(solution)/shard_map/ppermute | solution.py:294
  43.2 0.5 collective-permute-start.20
  43.7 2.1 %collective-permute-start.19 = (bf16[240,128]{1,0:T(8,128)(2,1)S(1)}, bf16[240,128]{1,0:T(8,128)(2,1)S(1)}, u32[]{:S(2)}, u32[]{:S(2)}) collective-permute-start(bf16[240,128]{1,0:T(8,128)(2,1)S(1)} %get-tuple-element.53), channel_id=1, source_target_pairs={{0,10},{1,11},{2,8},{3,9},{4,14},{5,15},{6,12},{7,13},{8,2},{9,3},... | collective-permute-start | bytes 184328 | tf_op jit(solution)/shard_map/ppermute | solution.py:294
  45.8 1.5 %collective-permute-start.18 = (bf16[240,128]{1,0:T(8,128)(2,1)S(1)}, bf16[240,128]{1,0:T(8,128)(2,1)S(1)}, u32[]{:S(2)}, u32[]{:S(2)}) collective-permute-start(bf16[240,128]{1,0:T(8,128)(2,1)S(1)} %get-tuple-element.52), channel_id=1, source_target_pairs={{0,8},{1,9},{2,10},{3,11},{4,12},{5,13},{6,14},{7,15},{8,0},{9,1},... | collective-permute-start | bytes 184328 | tf_op jit(solution)/shard_map/ppermute | solution.py:294
  47.3 1.2 %collective-permute-start.17 = (bf16[240,128]{1,0:T(8,128)(2,1)S(1)}, bf16[240,128]{1,0:T(8,128)(2,1)S(1)}, u32[]{:S(2)}, u32[]{:S(2)}) collective-permute-start(bf16[240,128]{1,0:T(8,128)(2,1)S(1)} %get-tuple-element.51), channel_id=1, source_target_pairs={{0,6},{1,7},{2,4},{3,5},{4,2},{5,3},{6,0},{7,1},{8,14},{9,15},{10,... | collective-permute-start | bytes 184328 | tf_op jit(solution)/shard_map/ppermute | solution.py:294
  48.5 0.0 collective-permute-done.21
  48.5 2.5 %collective-permute-start.16 = (bf16[240,128]{1,0:T(8,128)(2,1)S(1)}, bf16[240,128]{1,0:T(8,128)(2,1)S(1)}, u32[]{:S(2)}, u32[]{:S(2)}) collective-permute-start(bf16[240,128]{1,0:T(8,128)(2,1)S(1)} %get-tuple-element.50), channel_id=1, source_target_pairs={{0,4},{1,5},{2,6},{3,7},{4,0},{5,1},{6,2},{7,3},{8,12},{9,13},{10,... | collective-permute-start | bytes 184328 | tf_op jit(solution)/shard_map/ppermute | solution.py:294
  51.0 1.4 %collective-permute-start.15 = (bf16[240,128]{1,0:T(8,128)(2,1)S(1)}, bf16[240,128]{1,0:T(8,128)(2,1)S(1)}, u32[]{:S(2)}, u32[]{:S(2)}) collective-permute-start(bf16[240,128]{1,0:T(8,128)(2,1)S(1)} %get-tuple-element.49), channel_id=1, source_target_pairs={{0,2},{1,3},{2,0},{3,1},{4,6},{5,7},{6,4},{7,5},{8,10},{9,11},{10,... | collective-permute-start | bytes 184328 | tf_op jit(solution)/shard_map/ppermute | solution.py:294
  52.5 1.0 %copy-done.11 = bf16[768,256]{1,0:T(8,128)(2,1)S(1)} copy-done((bf16[768,256]{1,0:T(8,128)(2,1)S(1)}, bf16[768,256]{1,0:T(8,128)(2,1)}, u32[]{:S(2)}) %copy-start.11) | copy-done | bytes 393240
  53.5 4.2 %shard_map.141 = (f32[4,2,4,64,128]{4,3,2,1,0:T(8,128)S(1)}, bf16[8,64,128]{2,1,0:T(8,128)(2,1)S(1)}) custom-call(s32[7]{0:T(128)S(1)} %pad_add_fusion.sc, bf16[256,256]{1,0:T(8,128)(2,1)S(1)} %get-tuple-element.45.g0, bf16[768,256]{1,0:T(8,128)(2,1)S(1)} %copy-done.11, bf16[27,128,128]{2,1,0:T(8,128)(2,1)S(1)} %bitcast.20), custom_call_target="tpu_custom_call" | custom-call | flops 3019898880 | bytes 6291456 | tf_op jit(solution)/shard_map/pallas_call | solution.py:459
  57.6 0.0 collective-permute-done.19
  57.7 0.1 constant_dynamic-update-slice_fusion.7
  57.7 0.7 collective-permute-start.22
  58.4 0.7 maximum_bitcast_fusion
  59.1 1.6 %collective-permute-start.23 = (bf16[240,128]{1,0:T(8,128)(2,1)S(1)}, bf16[240,128]{1,0:T(8,128)(2,1)S(1)}, u32[]{:S(2)}, u32[]{:S(2)}) collective-permute-start(bf16[240,128]{1,0:T(8,128)(2,1)S(1)} %get-tuple-element.67.refs_0_), channel_id=1, source_target_pairs={{0,4},{1,5},{2,6},{3,7},{4,0},{5,1},{6,2},{7,3},{8,12},{9,13},{10,... | collective-permute-start | bytes 184328 | tf_op jit(solution)/shard_map/ppermute | solution.py:294
  60.8 1.3 %collective-permute-start.24 = (bf16[240,128]{1,0:T(8,128)(2,1)S(1)}, bf16[240,128]{1,0:T(8,128)(2,1)S(1)}, u32[]{:S(2)}, u32[]{:S(2)}) collective-permute-start(bf16[240,128]{1,0:T(8,128)(2,1)S(1)} %get-tuple-element.67.refs_0_), channel_id=1, source_target_pairs={{0,6},{1,7},{2,4},{3,5},{4,2},{5,3},{6,0},{7,1},{8,14},{9,15},{10,... | collective-permute-start | bytes 184328 | tf_op jit(solution)/shard_map/ppermute | solution.py:294
  62.0 3.4 %collective-permute-start.25 = (bf16[240,128]{1,0:T(8,128)(2,1)S(1)}, bf16[240,128]{1,0:T(8,128)(2,1)S(1)}, u32[]{:S(2)}, u32[]{:S(2)}) collective-permute-start(bf16[240,128]{1,0:T(8,128)(2,1)S(1)} %get-tuple-element.67.refs_0_), channel_id=1, source_target_pairs={{0,8},{1,9},{2,10},{3,11},{4,12},{5,13},{6,14},{7,15},{8,0},{9,1},... | collective-permute-start | bytes 184328 | tf_op jit(solution)/shard_map/ppermute | solution.py:294
  65.4 0.2 collective-permute-start.26
  65.6 3.8 %collective-permute-start.27 = (bf16[240,128]{1,0:T(8,128)(2,1)S(1)}, bf16[240,128]{1,0:T(8,128)(2,1)S(1)}, u32[]{:S(2)}, u32[]{:S(2)}) collective-permute-start(bf16[240,128]{1,0:T(8,128)(2,1)S(1)} %get-tuple-element.67.refs_0_), channel_id=1, source_target_pairs={{0,12},{1,13},{2,14},{3,15},{4,8},{5,9},{6,10},{7,11},{8,4},{9,5},... | collective-permute-start | bytes 184328 | tf_op jit(solution)/shard_map/ppermute | solution.py:294
  69.5 0.8 collective-permute-start.28
  70.4 0.9 collective-permute-start.9
  71.2 4.3 %collective-permute-done.9 = bf16[4,64,128]{2,1,0:T(8,128)(2,1)S(1)} collective-permute-done((bf16[4,64,128]{2,1,0:T(8,128)(2,1)S(1)}, bf16[4,64,128]{2,1,0:T(8,128)(2,1)S(1)}, u32[]{:S(2)}, u32[]{:S(2)}) %collective-permute-start.9) | collective-permute-done | bytes 65568 | tf_op jit(solution)/shard_map/ppermute | solution.py:294
  75.6 1.3 %collective-permute-start.10 = (bf16[2,64,128]{2,1,0:T(8,128)(2,1)S(1)}, bf16[2,64,128]{2,1,0:T(8,128)(2,1)S(1)}, u32[]{:S(2)}, u32[]{:S(2)}) collective-permute-start(bf16[2,64,128]{2,1,0:T(8,128)(2,1)S(1)} %slice_select_fusion.3), channel_id=1, source_target_pairs={{4,0},{5,1},{6,2},{7,3},{8,4},{9,5},{10,6},{11,7},{12,8},{13,9},{1... | collective-permute-start | bytes 98312 | tf_op jit(solution)/shard_map/ppermute | solution.py:304
  76.9 1.3 %collective-permute-start.12 = (bf16[2,64,128]{2,1,0:T(8,128)(2,1)S(1)}, bf16[2,64,128]{2,1,0:T(8,128)(2,1)S(1)}, u32[]{:S(2)}, u32[]{:S(2)}) collective-permute-start(bf16[2,64,128]{2,1,0:T(8,128)(2,1)S(1)} %slice_select_fusion.3), channel_id=1, source_target_pairs={{12,0},{13,1},{14,2},{15,3},{28,16},{29,17},{30,18},{31,19}} | collective-permute-start | bytes 98312 | tf_op jit(solution)/shard_map/ppermute | solution.py:304
  78.2 1.3 %collective-permute-start.11 = (bf16[2,64,128]{2,1,0:T(8,128)(2,1)S(1)}, bf16[2,64,128]{2,1,0:T(8,128)(2,1)S(1)}, u32[]{:S(2)}, u32[]{:S(2)}) collective-permute-start(bf16[2,64,128]{2,1,0:T(8,128)(2,1)S(1)} %slice_select_fusion.3), channel_id=1, source_target_pairs={{8,0},{9,1},{10,2},{11,3},{12,4},{13,5},{14,6},{15,7},{24,16},{25,... | collective-permute-start | bytes 98312 | tf_op jit(solution)/shard_map/ppermute | solution.py:304
  79.5 1.9 %collective-permute-done.10 = bf16[2,64,128]{2,1,0:T(8,128)(2,1)S(1)} collective-permute-done((bf16[2,64,128]{2,1,0:T(8,128)(2,1)S(1)}, bf16[2,64,128]{2,1,0:T(8,128)(2,1)S(1)}, u32[]{:S(2)}, u32[]{:S(2)}) %collective-permute-start.10) | collective-permute-done | bytes 32800 | tf_op jit(solution)/shard_map/ppermute | solution.py:304
  81.4 3.3 %collective-permute-done.12 = bf16[2,64,128]{2,1,0:T(8,128)(2,1)S(1)} collective-permute-done((bf16[2,64,128]{2,1,0:T(8,128)(2,1)S(1)}, bf16[2,64,128]{2,1,0:T(8,128)(2,1)S(1)}, u32[]{:S(2)}, u32[]{:S(2)}) %collective-permute-start.12) | collective-permute-done | bytes 32800 | tf_op jit(solution)/shard_map/ppermute | solution.py:304
  84.7 0.5 collective-permute-done.11
  85.2 0.5 collective-permute-start.13
  85.7 3.5 %collective-permute-done.13 = bf16[2,64,128]{2,1,0:T(8,128)(2,1)S(1)} collective-permute-done((bf16[2,64,128]{2,1,0:T(8,128)(2,1)S(1)}, bf16[2,64,128]{2,1,0:T(8,128)(2,1)S(1)}, u32[]{:S(2)}, u32[]{:S(2)}) %collective-permute-start.13) | collective-permute-done | bytes 32800 | tf_op jit(solution)/shard_map/ppermute | solution.py:294
  89.2 0.1 collective-permute-start.14
  89.4 0.5 collective-permute-start.29
  89.9 0.7 collective-permute-done.14
  90.7 1.0 %add_convert_fusion = bf16[4,2,4,64,128]{4,3,2,1,0:T(8,128)(2,1)} fusion(f32[4,2,4,64,128]{4,3,2,1,0:T(8,128)S(1)} %get-tuple-element.46, f32[2,4,64,128]{3,2,1,0:T(8,128)S(1)} %convert.1, pred[4]{0:T(512)(128)(4,1)S(1)} %iota_compare_fusion), kind=kLoop, calls=%fused_computation | loop fusion | flops 786432 | bytes 1835012 | tf_op jit(solution)/shard_map/convert_element_type | solution.py:498
  91.7 2.0 %shard_map.142 = (f32[3456,128]{1,0:T(8,128)}, f32[256,128]{1,0:T(8,128)}, f32[1,128]{1,0:T(1,128)}, f32[1,128]{1,0:T(1,128)}) custom-call(s32[7]{0:T(128)S(1)} %pad_add_fusion.sc, bf16[240,128]{1,0:T(8,128)(2,1)S(1)} %get-tuple-element.67.refs_0_, bf16[240,128]{1,0:T(8,128)(2,1)S(1)} %collective-permute-done.22.refs_1_, ...), custom_call_target="tpu_custom_call" | custom-call | tf_op jit(solution)/shard_map/pallas_call | solution.py:482
  (58 shorter events, 0.5 us)
Async XLA Ops:
  2.9 1.7 %collective-permute-start = (bf16[12,64,128]{2,1,0:T(8,128)(2,1)}, bf16[12,64,128]{2,1,0:T(8,128)(2,1)S(1)}, u32[]{:S(2)}, u32[]{:S(2)}) collective-permute-start(bf16[12,64,128]{2,1,0:T(8,128)(2,1)} %shard_map.136), channel_id=1, source_target_pairs={{0,1},{1,0},{2,3},{3,2},{4,5},{5,4},{6,7},{7,6},{8,9},{9,8},{10,11... | collective-permute-start | bytes 589832 | tf_op jit(solution)/shard_map/ppermute | solution.py:294
  5.6 12.4 %collective-permute-start.1 = (bf16[6,64,128]{2,1,0:T(8,128)(2,1)S(1)}, bf16[6,64,128]{2,1,0:T(8,128)(2,1)S(1)}, u32[]{:S(2)}, u32[]{:S(2)}) collective-permute-start(bf16[6,64,128]{2,1,0:T(8,128)(2,1)S(1)} %slice_select_fusion), channel_id=1, source_target_pairs={{0,2},{1,3},{2,0},{3,1},{4,6},{5,7},{6,4},{7,5},{8,10},{9,11},{10,... | collective-permute-start | bytes 294920 | tf_op jit(solution)/shard_map/ppermute | solution.py:294
  8.6 1.0 %copy-start = (bf16[4,2,4,64,128]{4,3,2,1,0:T(8,128)(2,1)S(1)}, bf16[4,2,4,64,128]{4,3,2,1,0:T(8,128)(2,1)}, u32[]{:S(2)}) copy-start(bf16[4,2,4,64,128]{4,3,2,1,0:T(8,128)(2,1)} %frs.1) | copy-start | bytes 1572868
  9.6 0.9 %copy-start.1 = (bf16[4,2,2,64,128]{4,3,2,1,0:T(8,128)(2,1)S(1)}, bf16[4,2,2,64,128]{4,3,2,1,0:T(8,128)(2,1)}, u32[]{:S(2)}) copy-start(bf16[4,2,2,64,128]{4,3,2,1,0:T(8,128)(2,1)} %has.1) | copy-start | bytes 786436
  10.6 1.2 %copy-start.2 = (bf16[3,3,3,128,128]{4,3,2,1,0:T(8,128)(2,1)S(1)}, bf16[3,3,3,128,128]{4,3,2,1,0:T(8,128)(2,1)}, u32[]{:S(2)}) copy-start(bf16[3,3,3,128,128]{4,3,2,1,0:T(8,128)(2,1)} %param.13) | copy-start | bytes 2654212
  11.7 0.9 %copy-start.4 = (bf16[4,1,4,64,128]{4,3,2,1,0:T(8,128)(2,1)S(1)}, bf16[4,1,4,64,128]{4,3,2,1,0:T(8,128)(2,1)}, u32[]{:S(2)}) copy-start(bf16[4,1,4,64,128]{4,3,2,1,0:T(8,128)(2,1)} %cos.1) | copy-start | bytes 786436
  12.7 0.8 copy-start.5
  13.5 0.7 copy-start.7
  14.2 0.7 copy-start.8
  18.0 13.9 %copy-start.10 = (bf16[768,256]{1,0:T(8,128)(2,1)}, bf16[768,256]{1,0:T(8,128)(2,1)S(1)}, u32[]{:S(2)}) copy-start(bf16[768,256]{1,0:T(8,128)(2,1)S(1)} %get-tuple-element.34.g_ref.g1) | copy-start | bytes 1179652
  18.1 8.7 %collective-permute-start.2 = (bf16[3,64,128]{2,1,0:T(8,128)(2,1)S(1)}, bf16[3,64,128]{2,1,0:T(8,128)(2,1)S(1)}, u32[]{:S(2)}, u32[]{:S(2)}) collective-permute-start(bf16[3,64,128]{2,1,0:T(8,128)(2,1)S(1)} %slice_select_fusion.2), channel_id=1, source_target_pairs={{0,4},{1,5},{2,6},{3,7},{4,8},{5,9},{6,10},{7,11},{8,12},{9,13},{1... | collective-permute-start | bytes 147464 | tf_op jit(solution)/shard_map/ppermute | solution.py:304
  21.6 5.2 %collective-permute-start.4 = (bf16[3,64,128]{2,1,0:T(8,128)(2,1)S(1)}, bf16[3,64,128]{2,1,0:T(8,128)(2,1)S(1)}, u32[]{:S(2)}, u32[]{:S(2)}) collective-permute-start(bf16[3,64,128]{2,1,0:T(8,128)(2,1)S(1)} %slice_select_fusion.2), channel_id=1, source_target_pairs={{0,12},{1,13},{2,14},{3,15},{16,28},{17,29},{18,30},{19,31}} | collective-permute-start | bytes 147464 | tf_op jit(solution)/shard_map/ppermute | solution.py:304
  24.9 3.6 %collective-permute-start.3 = (bf16[3,64,128]{2,1,0:T(8,128)(2,1)S(1)}, bf16[3,64,128]{2,1,0:T(8,128)(2,1)S(1)}, u32[]{:S(2)}, u32[]{:S(2)}) collective-permute-start(bf16[3,64,128]{2,1,0:T(8,128)(2,1)S(1)} %slice_select_fusion.2), channel_id=1, source_target_pairs={{0,8},{1,9},{2,10},{3,11},{4,12},{5,13},{6,14},{7,15},{16,24},{17,... | collective-permute-start | bytes 147464 | tf_op jit(solution)/shard_map/ppermute | solution.py:304
  28.5 4.2 %collective-permute-start.5 = (bf16[3,64,128]{2,1,0:T(8,128)(2,1)S(1)}, bf16[3,64,128]{2,1,0:T(8,128)(2,1)S(1)}, u32[]{:S(2)}, u32[]{:S(2)}) collective-permute-start(bf16[3,64,128]{2,1,0:T(8,128)(2,1)S(1)} %compare_select_fusion.15), channel_id=1, source_target_pairs={{0,2},{1,3},{2,0},{3,1},{4,6},{5,7},{6,4},{7,5},{8,10},{9,11},{10,... | collective-permute-start | bytes 147464 | tf_op jit(solution)/shard_map/ppermute | solution.py:294
  29.1 5.0 %copy-start.3 = (bf16[3,3,3,128,128]{4,3,2,1,0:T(8,128)(2,1)S(1)}, bf16[3,3,3,128,128]{4,3,2,1,0:T(8,128)(2,1)}, u32[]{:S(2)}) copy-start(bf16[3,3,3,128,128]{4,3,2,1,0:T(8,128)(2,1)} %param.13) | copy-start | bytes 2654212
  29.1 5.1 %copy-start.6 = (bf16[2,128,128]{2,1,0:T(8,128)(2,1)S(1)}, bf16[2,128,128]{2,1,0:T(8,128)(2,1)}, u32[]{:S(2)}) copy-start(bf16[2,128,128]{2,1,0:T(8,128)(2,1)} %sw.3) | copy-start | bytes 196612
  29.1 5.1 %copy-start.9 = (f32[128]{0:T(128)S(1)}, f32[128]{0:T(128)}, u32[]{:S(2)}) copy-start(f32[128]{0:T(128)} %param.16) | copy-start | bytes 1540
  32.7 1.4 %collective-permute-start.6 = (bf16[6,64,128]{2,1,0:T(8,128)(2,1)S(1)}, bf16[6,64,128]{2,1,0:T(8,128)(2,1)S(1)}, u32[]{:S(2)}, u32[]{:S(2)}) collective-permute-start(bf16[6,64,128]{2,1,0:T(8,128)(2,1)S(1)} %fusion.3), channel_id=1, source_target_pairs={{0,1},{1,0},{2,3},{3,2},{4,5},{5,4},{6,7},{7,6},{8,9},{9,8},{10,11... | collective-permute-start | bytes 294920 | tf_op jit(solution)/shard_map/ppermute | solution.py:294
  37.0 1.9 %collective-permute-start.7 = (bf16[1920,128]{1,0:T(8,128)(2,1)S(1)}, bf16[1920,128]{1,0:T(8,128)(2,1)S(1)}, u32[]{:S(2)}, u32[]{:S(2)}) collective-permute-start(bf16[1920,128]{1,0:T(8,128)(2,1)S(1)} %get-tuple-element.42), channel_id=1, source_target_pairs={{0,1},{1,0},{2,3},{3,2},{4,5},{5,4},{6,7},{7,6},{8,9},{9,8},{10,11... | collective-permute-start | bytes 1474568 | tf_op jit(solution)/shard_map/ppermute | solution.py:294
  39.6 8.9 %collective-permute-start.21 = (bf16[240,128]{1,0:T(8,128)(2,1)S(1)}, bf16[240,128]{1,0:T(8,128)(2,1)S(1)}, u32[]{:S(2)}, u32[]{:S(2)}) collective-permute-start(bf16[240,128]{1,0:T(8,128)(2,1)S(1)} %get-tuple-element.55), channel_id=1, source_target_pairs={{0,14},{1,15},{2,12},{3,13},{4,10},{5,11},{6,8},{7,9},{8,6},{9,7},... | collective-permute-start | bytes 184328 | tf_op jit(solution)/shard_map/ppermute | solution.py:294
  43.2 7.8 %collective-permute-start.20 = (bf16[240,128]{1,0:T(8,128)(2,1)S(1)}, bf16[240,128]{1,0:T(8,128)(2,1)S(1)}, u32[]{:S(2)}, u32[]{:S(2)}) collective-permute-start(bf16[240,128]{1,0:T(8,128)(2,1)S(1)} %get-tuple-element.54), channel_id=1, source_target_pairs={{0,12},{1,13},{2,14},{3,15},{4,8},{5,9},{6,10},{7,11},{8,4},{9,5},... | collective-permute-start | bytes 184328 | tf_op jit(solution)/shard_map/ppermute | solution.py:294
  43.7 13.9 %collective-permute-start.19 = (bf16[240,128]{1,0:T(8,128)(2,1)S(1)}, bf16[240,128]{1,0:T(8,128)(2,1)S(1)}, u32[]{:S(2)}, u32[]{:S(2)}) collective-permute-start(bf16[240,128]{1,0:T(8,128)(2,1)S(1)} %get-tuple-element.53), channel_id=1, source_target_pairs={{0,10},{1,11},{2,8},{3,9},{4,14},{5,15},{6,12},{7,13},{8,2},{9,3},... | collective-permute-start | bytes 184328 | tf_op jit(solution)/shard_map/ppermute | solution.py:294
  45.8 11.8 %collective-permute-start.18 = (bf16[240,128]{1,0:T(8,128)(2,1)S(1)}, bf16[240,128]{1,0:T(8,128)(2,1)S(1)}, u32[]{:S(2)}, u32[]{:S(2)}) collective-permute-start(bf16[240,128]{1,0:T(8,128)(2,1)S(1)} %get-tuple-element.52), channel_id=1, source_target_pairs={{0,8},{1,9},{2,10},{3,11},{4,12},{5,13},{6,14},{7,15},{8,0},{9,1},... | collective-permute-start | bytes 184328 | tf_op jit(solution)/shard_map/ppermute | solution.py:294
  47.3 10.3 %collective-permute-start.17 = (bf16[240,128]{1,0:T(8,128)(2,1)S(1)}, bf16[240,128]{1,0:T(8,128)(2,1)S(1)}, u32[]{:S(2)}, u32[]{:S(2)}) collective-permute-start(bf16[240,128]{1,0:T(8,128)(2,1)S(1)} %get-tuple-element.51), channel_id=1, source_target_pairs={{0,6},{1,7},{2,4},{3,5},{4,2},{5,3},{6,0},{7,1},{8,14},{9,15},{10,... | collective-permute-start | bytes 184328 | tf_op jit(solution)/shard_map/ppermute | solution.py:294
  48.5 9.1 %collective-permute-start.16 = (bf16[240,128]{1,0:T(8,128)(2,1)S(1)}, bf16[240,128]{1,0:T(8,128)(2,1)S(1)}, u32[]{:S(2)}, u32[]{:S(2)}) collective-permute-start(bf16[240,128]{1,0:T(8,128)(2,1)S(1)} %get-tuple-element.50), channel_id=1, source_target_pairs={{0,4},{1,5},{2,6},{3,7},{4,0},{5,1},{6,2},{7,3},{8,12},{9,13},{10,... | collective-permute-start | bytes 184328 | tf_op jit(solution)/shard_map/ppermute | solution.py:294
  51.0 6.6 %collective-permute-start.15 = (bf16[240,128]{1,0:T(8,128)(2,1)S(1)}, bf16[240,128]{1,0:T(8,128)(2,1)S(1)}, u32[]{:S(2)}, u32[]{:S(2)}) collective-permute-start(bf16[240,128]{1,0:T(8,128)(2,1)S(1)} %get-tuple-element.49), channel_id=1, source_target_pairs={{0,2},{1,3},{2,0},{3,1},{4,6},{5,7},{6,4},{7,5},{8,10},{9,11},{10,... | collective-permute-start | bytes 184328 | tf_op jit(solution)/shard_map/ppermute | solution.py:294
  52.5 1.0 %copy-start.11 = (bf16[768,256]{1,0:T(8,128)(2,1)S(1)}, bf16[768,256]{1,0:T(8,128)(2,1)}, u32[]{:S(2)}) copy-start(bf16[768,256]{1,0:T(8,128)(2,1)} %copy-done.10) | copy-start | bytes 1179652
  57.7 7.6 %collective-permute-start.22 = (bf16[240,128]{1,0:T(8,128)(2,1)S(1)}, bf16[240,128]{1,0:T(8,128)(2,1)S(1)}, u32[]{:S(2)}, u32[]{:S(2)}) collective-permute-start(bf16[240,128]{1,0:T(8,128)(2,1)S(1)} %get-tuple-element.67.refs_0_), channel_id=1, source_target_pairs={{0,2},{1,3},{2,0},{3,1},{4,6},{5,7},{6,4},{7,5},{8,10},{9,11},{10,... | collective-permute-start | bytes 184328 | tf_op jit(solution)/shard_map/ppermute | solution.py:294
  59.1 11.2 %collective-permute-start.8 = (bf16[8,64,128]{2,1,0:T(8,128)(2,1)S(1)}, bf16[8,64,128]{2,1,0:T(8,128)(2,1)S(1)}, u32[]{:S(2)}, u32[]{:S(2)}) collective-permute-start(bf16[8,64,128]{2,1,0:T(8,128)(2,1)S(1)} %get-tuple-element.47), channel_id=1, source_target_pairs={{0,1},{1,0},{2,3},{3,2},{4,5},{5,4},{6,7},{7,6},{8,9},{9,8},{10,11... | collective-permute-start | bytes 393224 | tf_op jit(solution)/shard_map/ppermute | solution.py:294
  59.1 6.5 %collective-permute-start.23 = (bf16[240,128]{1,0:T(8,128)(2,1)S(1)}, bf16[240,128]{1,0:T(8,128)(2,1)S(1)}, u32[]{:S(2)}, u32[]{:S(2)}) collective-permute-start(bf16[240,128]{1,0:T(8,128)(2,1)S(1)} %get-tuple-element.67.refs_0_), channel_id=1, source_target_pairs={{0,4},{1,5},{2,6},{3,7},{4,0},{5,1},{6,2},{7,3},{8,12},{9,13},{10,... | collective-permute-start | bytes 184328 | tf_op jit(solution)/shard_map/ppermute | solution.py:294
  60.8 8.7 %collective-permute-start.24 = (bf16[240,128]{1,0:T(8,128)(2,1)S(1)}, bf16[240,128]{1,0:T(8,128)(2,1)S(1)}, u32[]{:S(2)}, u32[]{:S(2)}) collective-permute-start(bf16[240,128]{1,0:T(8,128)(2,1)S(1)} %get-tuple-element.67.refs_0_), channel_id=1, source_target_pairs={{0,6},{1,7},{2,4},{3,5},{4,2},{5,3},{6,0},{7,1},{8,14},{9,15},{10,... | collective-permute-start | bytes 184328 | tf_op jit(solution)/shard_map/ppermute | solution.py:294
  62.0 9.2 %collective-permute-start.25 = (bf16[240,128]{1,0:T(8,128)(2,1)S(1)}, bf16[240,128]{1,0:T(8,128)(2,1)S(1)}, u32[]{:S(2)}, u32[]{:S(2)}) collective-permute-start(bf16[240,128]{1,0:T(8,128)(2,1)S(1)} %get-tuple-element.67.refs_0_), channel_id=1, source_target_pairs={{0,8},{1,9},{2,10},{3,11},{4,12},{5,13},{6,14},{7,15},{8,0},{9,1},... | collective-permute-start | bytes 184328 | tf_op jit(solution)/shard_map/ppermute | solution.py:294
  65.4 12.8 %collective-permute-start.26 = (bf16[240,128]{1,0:T(8,128)(2,1)S(1)}, bf16[240,128]{1,0:T(8,128)(2,1)S(1)}, u32[]{:S(2)}, u32[]{:S(2)}) collective-permute-start(bf16[240,128]{1,0:T(8,128)(2,1)S(1)} %get-tuple-element.67.refs_0_), channel_id=1, source_target_pairs={{0,10},{1,11},{2,8},{3,9},{4,14},{5,15},{6,12},{7,13},{8,2},{9,3},... | collective-permute-start | bytes 184328 | tf_op jit(solution)/shard_map/ppermute | solution.py:294
  65.6 20.1 %collective-permute-start.27 = (bf16[240,128]{1,0:T(8,128)(2,1)S(1)}, bf16[240,128]{1,0:T(8,128)(2,1)S(1)}, u32[]{:S(2)}, u32[]{:S(2)}) collective-permute-start(bf16[240,128]{1,0:T(8,128)(2,1)S(1)} %get-tuple-element.67.refs_0_), channel_id=1, source_target_pairs={{0,12},{1,13},{2,14},{3,15},{4,8},{5,9},{6,10},{7,11},{8,4},{9,5},... | collective-permute-start | bytes 184328 | tf_op jit(solution)/shard_map/ppermute | solution.py:294
  69.5 19.9 %collective-permute-start.28 = (bf16[240,128]{1,0:T(8,128)(2,1)S(1)}, bf16[240,128]{1,0:T(8,128)(2,1)S(1)}, u32[]{:S(2)}, u32[]{:S(2)}) collective-permute-start(bf16[240,128]{1,0:T(8,128)(2,1)S(1)} %get-tuple-element.67.refs_0_), channel_id=1, source_target_pairs={{0,14},{1,15},{2,12},{3,13},{4,10},{5,11},{6,8},{7,9},{8,6},{9,7},... | collective-permute-start | bytes 184328 | tf_op jit(solution)/shard_map/ppermute | solution.py:294
  70.4 5.2 %collective-permute-start.9 = (bf16[4,64,128]{2,1,0:T(8,128)(2,1)S(1)}, bf16[4,64,128]{2,1,0:T(8,128)(2,1)S(1)}, u32[]{:S(2)}, u32[]{:S(2)}) collective-permute-start(bf16[4,64,128]{2,1,0:T(8,128)(2,1)S(1)} %slice_select_fusion.1), channel_id=1, source_target_pairs={{0,2},{1,3},{2,0},{3,1},{4,6},{5,7},{6,4},{7,5},{8,10},{9,11},{10,... | collective-permute-start | bytes 196616 | tf_op jit(solution)/shard_map/ppermute | solution.py:294
  75.6 5.8 %collective-permute-start.10 = (bf16[2,64,128]{2,1,0:T(8,128)(2,1)S(1)}, bf16[2,64,128]{2,1,0:T(8,128)(2,1)S(1)}, u32[]{:S(2)}, u32[]{:S(2)}) collective-permute-start(bf16[2,64,128]{2,1,0:T(8,128)(2,1)S(1)} %slice_select_fusion.3), channel_id=1, source_target_pairs={{4,0},{5,1},{6,2},{7,3},{8,4},{9,5},{10,6},{11,7},{12,8},{13,9},{1... | collective-permute-start | bytes 98312 | tf_op jit(solution)/shard_map/ppermute | solution.py:304
  76.9 7.8 %collective-permute-start.12 = (bf16[2,64,128]{2,1,0:T(8,128)(2,1)S(1)}, bf16[2,64,128]{2,1,0:T(8,128)(2,1)S(1)}, u32[]{:S(2)}, u32[]{:S(2)}) collective-permute-start(bf16[2,64,128]{2,1,0:T(8,128)(2,1)S(1)} %slice_select_fusion.3), channel_id=1, source_target_pairs={{12,0},{13,1},{14,2},{15,3},{28,16},{29,17},{30,18},{31,19}} | collective-permute-start | bytes 98312 | tf_op jit(solution)/shard_map/ppermute | solution.py:304
  78.2 7.0 %collective-permute-start.11 = (bf16[2,64,128]{2,1,0:T(8,128)(2,1)S(1)}, bf16[2,64,128]{2,1,0:T(8,128)(2,1)S(1)}, u32[]{:S(2)}, u32[]{:S(2)}) collective-permute-start(bf16[2,64,128]{2,1,0:T(8,128)(2,1)S(1)} %slice_select_fusion.3), channel_id=1, source_target_pairs={{8,0},{9,1},{10,2},{11,3},{12,4},{13,5},{14,6},{15,7},{24,16},{25,... | collective-permute-start | bytes 98312 | tf_op jit(solution)/shard_map/ppermute | solution.py:304
  85.2 4.0 %collective-permute-start.13 = (bf16[2,64,128]{2,1,0:T(8,128)(2,1)S(1)}, bf16[2,64,128]{2,1,0:T(8,128)(2,1)S(1)}, u32[]{:S(2)}, u32[]{:S(2)}) collective-permute-start(bf16[2,64,128]{2,1,0:T(8,128)(2,1)S(1)} %compare_select_fusion.17), channel_id=1, source_target_pairs={{0,2},{1,3},{2,0},{3,1},{4,6},{5,7},{6,4},{7,5},{8,10},{9,11},{10,... | collective-permute-start | bytes 98312 | tf_op jit(solution)/shard_map/ppermute | solution.py:294
  89.2 1.3 %collective-permute-start.14 = (bf16[4,64,128]{2,1,0:T(8,128)(2,1)S(1)}, bf16[4,64,128]{2,1,0:T(8,128)(2,1)S(1)}, u32[]{:S(2)}, u32[]{:S(2)}) collective-permute-start(bf16[4,64,128]{2,1,0:T(8,128)(2,1)S(1)} %fusion.5), channel_id=1, source_target_pairs={{0,1},{1,0},{2,3},{3,2},{4,5},{5,4},{6,7},{7,6},{8,9},{9,8},{10,11... | collective-permute-start | bytes 196616 | tf_op jit(solution)/shard_map/ppermute | solution.py:294
  89.4 2.3 %collective-permute-start.29 = (bf16[1920,128]{1,0:T(8,128)(2,1)S(1)}, bf16[1920,128]{1,0:T(8,128)(2,1)S(1)}, u32[]{:S(2)}, u32[]{:S(2)}) collective-permute-start(bf16[1920,128]{1,0:T(8,128)(2,1)S(1)} %constant_dynamic-update-slice_fusion), channel_id=1, source_target_pairs={{0,1},{1,0},{2,3},{3,2},{4,5},{5,4},{6,7},{7,6},{8,9},{9,8},{10,11... | collective-permute-start | bytes 1474568 | tf_op jit(solution)/shard_map/ppermute | solution.py:294

commit v3 on v2

--- a/solution.py
+++ b/solution.py
@@ -14,6 +14,7 @@
 
 _VMEM = pl.BlockSpec(memory_space=pltpu.VMEM)
 _SMEM = pl.BlockSpec(memory_space=pltpu.SMEM)
+_HBM = pl.BlockSpec(memory_space=pltpu.HBM)
 
 
 def _call(kernel, out_shape, in_specs, scratch=(), flops=0, moved=0, room=16, grid=()):
@@ -66,14 +67,14 @@
     return jnp.dot(lhs, jnp.concatenate(rhs, axis=0), preferred_element_type=F32)
 
 
-def _conv_back(xk, w_ref, h):
+def _conv_back(xk, w_ref, h, frames=range(4)):
     c = w_ref.shape[-1]
     zero = jnp.zeros((c, c), BF)
-    lhs = jnp.concatenate([_wide(xk, j, h) for j in range(4)], axis=1)
+    lhs = jnp.concatenate([_wide(xk, j, h) for j in frames], axis=1)
     rhs = []
     for f in range(2):
         row = []
-        for j in range(4):
+        for j in frames:
             for tap in range(9):
                 kt = 2 - (j - f)
                 row.append(w_ref[kt * 9 + 8 - tap] if 0 <= kt <= 2 else zero)
@@ -139,10 +140,22 @@
     )
 
 
-def _early_kernel(sc, fr, ha, co, w_ref, cb, sw, sb, lat_ref, g_ref, hid_ref, xk):
+def _early_kernel(
+    sc, frh, hah, coh, wh, cb, sw, sb, lat_ref, g_ref, hid_ref, gout_ref, xk, fr, ha, co, w_ref, sems
+):
     slots, _, h, w, c = fr.shape
+    pairs = ((frh, fr), (hah, ha), (coh, co), (wh, w_ref))
+    copies = [pltpu.make_async_copy(a, b, sems.at[i]) for i, (a, b) in enumerate(pairs)]
+    for copy in copies:
+        copy.start()
+    copies[0].wait()
+    copies[1].wait()
     _fill_early(sc, fr, ha, xk)
-    lat, g, hidden = _head(xk, _early_gout(sc, co), w_ref, cb, sw, sb, h)
+    copies[2].wait()
+    gout = _early_gout(sc, co)
+    gout_ref[...] = gout
+    copies[3].wait()
+    lat, g, hidden = _head(xk, gout, w_ref, cb, sw, sb, h)
     for s in range(1, slots):
         part = lat[(s - 1) * h * w : s * h * w]
         lat_ref[s - 1] = (
@@ -152,9 +165,9 @@
     hid_ref[...] = hidden
 
 
-def _early_sums_kernel(sc, fr, ha, co, g_ref, hid_ref, acc, xk):
-    _, _, h, w, c = fr.shape
-    _fill_early(sc, fr, ha, xk)
+def _early_sums_kernel(sc, g_ref, hid_ref, gout_ref, xk, acc):
+    c = gout_ref.shape[-1]
+    h = xk.shape[3] - 2
     n9 = 9 * c
 
     def add(kind, value):
@@ -167,11 +180,11 @@
             acc[at : at + 1] = value
 
     acc[3 * n9 + 2 * c :] = jnp.zeros((acc.shape[0] - 3 * n9 - 2 * c, c), F32)
-    _weight_grads(xk, g_ref[...], hid_ref[...], _early_gout(sc, co), h, add)
+    _weight_grads(xk, g_ref[...], hid_ref[...], gout_ref[...], h, add)
 
 
 def _late_kernel(
-    sc, frs, has, tail, cos, w_ref, cb, sw, sb, early, lat_ref, g_ref, send, keep, xk, acc
+    sc, frs, has, tail, cos, w_ref, cb, sw, sb, early, lat_ref, g_ref, send, keep, cache_ref, xk, acc
 ):
     fr, ha, co = frs.at[0], has.at[0], cos.at[0]
     _, h, w, c = fr.shape
@@ -211,56 +224,114 @@
     def _():
         _weight_grads(xk, g, hidden, gout, h, add)
 
-    half = send.shape[0]
-    core = sc[sc.shape[0] - 1]
-    send[...] = acc[pl.ds(pl.multiple_of((1 - core) * half, 16), half)].astype(BF)
-    keep[...] = acc[pl.ds(pl.multiple_of(core * half, 16), half)]
-
-
-def _back_kernel(sc, g0, g1, w_ref, out_ref, cache_ref, xk):
+        for t in range(2):
+            for kw in range(3):
+                xk[kw, 0, 2 + t, 0:1] = jnp.zeros((1, w, c), BF)
+                xk[kw, 0, 2 + t, h + 1 : h + 2] = jnp.zeros((1, w, c), BF)
+            v = g[:, t * c : (t + 1) * c].reshape(h, w, c)
+            _put(xk, (0, 2 + t), slice(1, 1 + h), jnp.where(on, v, jnp.zeros_like(v)))
+        back = _conv_back(xk, w_ref, h, (2, 3))
+        back = jnp.where(filled, back, jnp.full_like(back, EMPTY_GRAD)).astype(BF)
+        half = keep.shape[0]
+        for t in range(2):
+            lanes = slice(t * c, (t + 1) * c)
+            cache_ref[t * h * w : (t + 1) * h * w] = back[:, lanes]
+            send[half + t * h * w : half + (t + 1) * h * w] = back[:, lanes]
+        core = sc[sc.shape[0] - 1]
+        send[:half] = acc[pl.ds(pl.multiple_of((1 - core) * half, 16), half)].astype(BF)
+        keep[...] = acc[pl.ds(pl.multiple_of(core * half, 16), half)]
+
+
+def _back_kernel(sc, g0, g1, w_ref, out_ref, xk):
     slots, _, h, w, c = out_ref.shape
     m = h * w
     zero = jnp.zeros((1, w, c), BF)
     for kw in range(3):
         for j in range(4):
-            for s in range(slots + 1):
+            for s in range(slots):
                 xk[kw, s, j, 0:1] = zero
                 xk[kw, s, j, h + 1 : h + 2] = zero
-    blank = jnp.zeros((h, w, c), BF)
     for f in range(2):
         for kw in range(3):
-            xk[kw, 0, f, 1 : 1 + h] = blank
-            xk[kw, slots, f + 2, 1 : 1 + h] = blank
+            xk[kw, slots - 1, f + 2, 1 : 1 + h] = jnp.zeros((h, w, c), BF)
         lanes = slice(f * c, (f + 1) * c)
         for s in range(slots):
             v = g0[:, lanes] if s == 0 else g1[(s - 1) * m : s * m, lanes]
             v = v.reshape(h, w, c)
-            _put(xk, (s + 1, f), slice(1, 1 + h), v)
-            _put(
-                xk, (s, f + 2), slice(1, 1 + h), jnp.where(sc[1 + s] == 0, v, jnp.zeros_like(v))
-            )
+            _put(xk, (s, f), slice(1, 1 + h), v)
+            if s > 0:
+                on = sc[1 + s] == 0
+                _put(xk, (s - 1, f + 2), slice(1, 1 + h), jnp.where(on, v, jnp.zeros_like(v)))
     out = _conv_back(xk, w_ref, h)
-    hw = h * w
-    live = sc[0] > 0
     for f in range(2):
-        lanes = slice(f * c, (f + 1) * c)
-        cache = out[:hw, lanes]
-        cache = jnp.where(live, cache, jnp.full_like(cache, EMPTY_GRAD))
-        cache_ref[f * h : (f + 1) * h] = cache.astype(BF).reshape(h, w, c)
-        out_ref[:, f] = out[hw:, lanes].reshape(slots, h, w, c)
-
-
-def _cut_kernel(sc, keep, got, own, *sends):
-    rows = own.shape[0]
-    chip = sc[sc.shape[0] - 2]
+        out_ref[:, f] = out[:, f * c : (f + 1) * c].reshape(slots, h, w, c)
+
+
+def _first_live(a, b):
+    return jnp.where(a.astype(F32) < EMPTY_GRAD / 2, a, b)
+
+
+def _place(sc):
+    chip, core = sc[sc.shape[0] - 2], sc[sc.shape[0] - 1]
+    return lax.shift_right_logical(chip, 1), lax.bitwise_and(chip, 1), core
+
+
+def _across_x_kernel(sc, keep, got, cache, send, kept):
+    z, x, core = _place(sc)
+    del z
+    half = keep.shape[0]
+    blocks = 4
+    rows = half // (2 * blocks)
 
     def piece(p):
         at = pl.ds(pl.multiple_of(p * rows, 16), rows)
         return keep[at] + got[at].astype(F32)
 
-    own[...] = piece(chip)
-    for k, ref in enumerate(sends):
-        ref[...] = piece(lax.bitwise_xor(chip, k + 1)).astype(BF)
+    for b in range(blocks):
+        kept[b * rows : (b + 1) * rows] = piece(2 * b + x)
+        send[b * rows : (b + 1) * rows] = piece(2 * b + 1 - x).astype(BF)
+    part = cache.shape[0] // 2
+    at = pl.multiple_of(core * part, 16)
+    mine, theirs = cache[pl.ds(at, part)], got[pl.ds(half + at, part)]
+    first = jnp.where(core == 0, _first_live(mine, theirs), _first_live(theirs, mine))
+    send[blocks * rows :] = first
+
+
+def _across_z_kernel(sc, kept, got, sent, own, *sends):
+    z, x, core = _place(sc)
+    del core
+    rows = own.shape[0]
+    below = kept.shape[0]
+    part = (sent.shape[0] - below) // 2
+
+    def piece(b):
+        at = pl.ds(pl.multiple_of(b * rows, 16), rows)
+        return kept[at] + got[at].astype(F32)
+
+    at = pl.ds(pl.multiple_of(below + x * part, 16), part)
+    first = jnp.where(x == 0, _first_live(sent[at], got[at]), _first_live(got[at], sent[at]))
+    own[...] = piece(z)
+    for j, ref in enumerate(sends):
+        ref[:rows] = piece(lax.bitwise_xor(z, j + 1)).astype(BF)
+        ref[rows:] = first
+
+
+def _sum_kernel(sc, own, *refs):
+    gots, (mine, after) = refs[:-2], refs[-2:]
+    z, _, _ = _place(sc)
+    rows = own.shape[0]
+    total = own[...]
+    for ref in gots:
+        total = total + ref[:rows].astype(F32)
+    mine[...] = total.astype(BF)
+    best = jnp.full(after.shape, EMPTY_GRAD, F32)
+    for target in range(len(gots), 0, -1):
+        for j, ref in enumerate(gots):
+            here = jnp.logical_and(lax.bitwise_xor(z, j + 1) == target, target > z)
+            value = ref[rows:].astype(F32)
+            use = jnp.where(here, value, jnp.full_like(value, EMPTY_GRAD))
+            best = _first_live(use, best)
+    after[...] = best.astype(BF)
 
 
 def _tail_kernel(sc, fr, ha, out):
@@ -271,71 +342,74 @@
         out[rows] = jnp.where(live, v, jnp.full_like(v, EMPTY_FRAME))
 
 
-def _final_kernel(sc, *refs):
-    pieces, (other, cw, sw, cb, sb, acc) = refs[:-6], refs[-6:]
-    rows, c = pieces[0].shape
-    half = rows * len(pieces)
-    chip = sc[sc.shape[0] - 2]
-    core = sc[sc.shape[0] - 1]
-    for k, ref in enumerate(pieces):
-        at = lax.bitwise_xor(chip, k) * rows
-        acc[pl.ds(pl.multiple_of(core * half + at, 16), rows)] = ref[...].astype(F32)
-        acc[pl.ds(pl.multiple_of((1 - core) * half + at, 16), rows)] = other[
-            k * rows : (k + 1) * rows
-        ].astype(F32)
+def _final_kernel(sc, mine, other, got, grad, cw, sw, cb, sb, fg, acc):
+    c = mine.shape[1]
+    half = acc.shape[0] // 2
+    z, x, core = _place(sc)
+    blocks = 4
+    rows = half // (2 * blocks)
+    for ref, at_core in ((mine, core), (other, 1 - core)):
+        for k in range(2 * blocks):
+            side = x if k < blocks else 1 - x
+            chip = 2 * lax.bitwise_xor(z, k % blocks) + side
+            at = pl.multiple_of(at_core * half + chip * rows, 16)
+            acc[pl.ds(at, rows)] = ref[k * rows : (k + 1) * rows].astype(F32)
     n27, n29 = 27 * c, 29 * c
     cw[...] = acc[:n27]
     sw[...] = acc[n27:n29]
     cb[...] = acc[n29 : n29 + 1]
     sb[...] = acc[n29 + 1 : n29 + 2]
+    slots, frames, h, w, _ = grad.shape
+    part = mine.shape[0] - half
+    for s in range(slots):
+        here = sc[0] - 1 == s
+        for f in range(frames):
+            low = f == 0
+            a, b = mine[half:].astype(F32), other[half:].astype(F32)
+            beyond = jnp.where(core == 0, a, b) if low else jnp.where(core == 0, b, a)
+            beside = got[half + f * part : half + (f + 1) * part].astype(F32)
+            came = jnp.where(core == 0, _first_live(beside, beyond), beyond)
+            came = jnp.where(came < EMPTY_GRAD / 2, came, jnp.zeros_like(came)).reshape(h, w, c)
+            fg[s, f] = (grad[s, f] + jnp.where(here, came, jnp.zeros_like(came))).astype(BF)
 
 
 def _xor(x, k, n, axis):
     return lax.ppermute(x, axis, [(i, i ^ k) for i in range(n)])
 
 
-def _latest_before(x, empty, axis, n, reverse=False, beside_first=None, beside_second=None):
+def _latest_before(x, empty, axis, n, beside_x, beside_z):
     index = lax.axis_index(axis)
-    index = n - 1 - index if reverse else index
     core, pair = index & 1, (index >> 1) & 1
 
     def shift(v, k):
-        pairs = [(i, i + k) for i in range(n - k)]
-        return lax.ppermute(v, axis, [(b, a) for a, b in pairs] if reverse else pairs)
+        return lax.ppermute(v, axis, [(i, i + k) for i in range(n - k)])
 
     def newest(early, late):
         return jnp.where(late > empty / 2, early, late)
 
-    def part(v, at):
-        half = v.shape[0] // 2
-        return jnp.where(at == 0, v[:half], v[half:])
-
-    def join(mine, other, at):
-        return jnp.concatenate(
-            [jnp.where(at == 0, mine, other), jnp.where(at == 0, other, mine)], axis=0
-        )
+    def half(v):
+        rows = v.shape[0] // 2
+        return jnp.where(core == 0, v[:rows], v[rows:])
 
     other = _xor(x, 1, n, axis)
-    chip = part(jnp.where(core == 0, newest(x, other), newest(other, x)), core)
+    a, b = half(x), half(other)
+    chip = jnp.where(core == 0, newest(a, b), newest(b, a))
     beside = _xor(chip, 2, n, axis)
-    quad = part(jnp.where(pair == 0, newest(chip, beside), newest(beside, chip)), pair)
-    if beside_first is not None:
-        quad = beside_first(chip, quad)
-    blocks = n // 4
-    before = None
-    for k in range(min(3, blocks - 1), 0, -1):
-        came = shift(quad, 4 * k)
-        before = came if before is None else newest(before, came)
-    reach = min(3, blocks - 1)
-    while reach < blocks - 1:
-        before = newest(shift(before, 4 * reach), before)
-        reach *= 2
-    first = before
-    before = join(before, _xor(before, 2, n, axis), pair)
+    quad = jnp.where(pair == 0, newest(chip, beside), newest(beside, chip))
+    quad = beside_x(chip, quad)
+    before, reach = None, 0
+    while reach < n // 4 - 1:
+        start = quad if before is None else newest(before, quad)
+        came = shift(start, 4 * (reach + 1))
+        before = came if before is None else newest(came, before)
+        reach = 2 * reach + 1
+        if reach == 3:
+            before = beside_z(start, before)
     before = jnp.where(pair == 0, before, newest(before, beside))
-    if beside_second is not None:
-        before = beside_second(first, before)
-    before = join(before, _xor(before, 1, n, axis), core)
+    across = _xor(before, 1, n, axis)
+    before = jnp.concatenate(
+        [jnp.where(core == 0, before, across), jnp.where(core == 0, across, before)], axis=0
+    )
     before = jnp.where(core == 0, before, newest(before, other))
     return jnp.where(before > empty / 2, jnp.zeros_like(before), before)
 
@@ -360,7 +434,8 @@
     slots, _, h, w, c = frames.shape
     count = slab_counts[0]
     index = lax.axis_index(axis)
-    chips = min(8, n // 2)
+    chips = 8
+    assert n % (2 * chips) == 0
     sc = jnp.concatenate(
         [
             slab_counts,
@@ -395,49 +470,53 @@
     )(slab_counts, frames, row_halo)
 
     held = {}
+    wide = ((slots - 1) * m, 2 * c)
+    windows = (3, slots - 1, 4, h + 2, w, c)
 
     def early_forward(start, follow):
         held["early"] = _call(
             _early_kernel,
             [
                 jax.ShapeDtypeStruct((slots - 1, h, w, c), BF),
-                jax.ShapeDtypeStruct(((slots - 1) * m, 2 * c), BF),
-                jax.ShapeDtypeStruct(((slots - 1) * m, 2 * c), BF),
+                jax.ShapeDtypeStruct(wide, BF),
+                jax.ShapeDtypeStruct(wide, BF),
+                jax.ShapeDtypeStruct((wide[0], c), BF),
+                jax.ShapeDtypeStruct(windows, BF),
             ],
-            [_SMEM] + [_VMEM] * 7,
-            [pltpu.VMEM((3, slots - 1, 4, h + 2, w, c), BF)],
+            [_SMEM] + [_HBM] * 4 + [_VMEM] * 3,
+            [pltpu.VMEM(v.shape, BF) for v in (frames, row_halo, cotangent, wt)]
+            + [pltpu.SemaphoreType.DMA((4,))],
             flops=(slots - 1) * conv_flops,
             moved=4 << 20,
         )(_after(sc, start), frames, row_halo, cotangent, wt, cb, stride_weight, sb)
         return _after(follow, held["early"][1])
 
     def early_sums(start, follow):
-        _, g1, hid1 = held["early"]
+        _, g1, hid1, gout1, xk1 = held["early"]
         held["sums"] = _call(
             _early_sums_kernel,
             jax.ShapeDtypeStruct((rows, c), F32),
-            [_SMEM] + [_VMEM] * 5,
-            [pltpu.VMEM((3, slots - 1, 4, h + 2, w, c), BF)],
+            [_SMEM] + [_VMEM] * 4,
             flops=(slots - 1) * conv_flops,
             moved=4 << 20,
-        )(_after(sc, start), frames, row_halo, cotangent, g1, hid1)
+        )(_after(sc, start), g1, hid1, gout1, xk1)
         return _after(follow, held["sums"])
 
-    arrived = _latest_before(
-        tail, EMPTY_FRAME, axis, n, beside_first=early_forward, beside_second=early_sums
-    )
-    lat1, g1, _ = held["early"]
+    arrived = _latest_before(tail, EMPTY_FRAME, axis, n, early_forward, early_sums)
+    lat1, g1 = held["early"][:2]
 
     def first(*shape):
         return pl.BlockSpec((1, *shape), lambda i: (0,) * (len(shape) + 1))
 
-    lat0, g0, send, keep = _call(
+    half, carried = rows // 2, 2 * m
+    lat0, g0, send, keep, cache = _call(
         _late_kernel,
         [
             jax.ShapeDtypeStruct((h, w, c), BF),
             jax.ShapeDtypeStruct((m, 2 * c), BF),
-            jax.ShapeDtypeStruct((rows // 2, c), BF),
-            jax.ShapeDtypeStruct((rows // 2, c), F32),
+            jax.ShapeDtypeStruct((half + carried, c), BF),
+            jax.ShapeDtypeStruct((half, c), F32),
+            jax.ShapeDtypeStruct((carried, c), BF),
         ],
         [_SMEM, first(2, h, w, c), first(2, 2, w, c), _VMEM, first(1, h, w, c)] + [_VMEM] * 5,
         [pltpu.VMEM((3, 1, 4, h + 2, w, c), BF), pltpu.VMEM((rows, c), F32)],
@@ -446,56 +525,85 @@
         grid=(1,),
     )(sc, frames, row_halo, arrived, cotangent, wt, cb, stride_weight, sb, held["sums"])
 
+    blocks = chips // 2
+    piece = half // chips
     got = _xor(send, 1, n, axis)
-    piece = rows // 2 // chips
-    own, *outs = _call(
-        _cut_kernel,
-        [jax.ShapeDtypeStruct((piece, c), F32)]
-        + [jax.ShapeDtypeStruct((piece, c), BF)] * (chips - 1),
-        [_SMEM, _VMEM, _VMEM],
-        room=12,
-    )(sc, keep, got)
-
-    grad, cache = _call(
-        _back_kernel,
+    send_x, keep_x = _call(
+        _across_x_kernel,
         [
-            jax.ShapeDtypeStruct((slots, 2, h, w, c), F32),
-            jax.ShapeDtypeStruct((2 * h, w, c), BF),
+            jax.ShapeDtypeStruct((blocks * piece + carried // 2, c), BF),
+            jax.ShapeDtypeStruct((blocks * piece, c), F32),
         ],
         [_SMEM] + [_VMEM] * 3,
-        [pltpu.VMEM((3, slots + 1, 4, h + 2, w, c), BF)],
-        flops=(slots + 1) * conv_flops,
+        room=8,
+    )(sc, keep, got, cache)
+    got_x = _xor(send_x, 2, n, axis)
+    grad = _call(
+        _back_kernel,
+        jax.ShapeDtypeStruct((slots, 2, h, w, c), F32),
+        [_SMEM] + [_VMEM] * 3,
+        [pltpu.VMEM((3, slots, 4, h + 2, w, c), BF)],
+        flops=slots * conv_flops,
         moved=6 << 20,
         room=24,
-    )(_after(sc, own), g0, g1, wt)
-
-    total = _after(own, cache)
-    for k in range(1, chips):
-        total = total + _xor(outs[k - 1], 2 * k, n, axis).astype(F32)
-    mine = total.astype(BF)
+    )(_after(sc, keep_x), g0, g1, wt)
+    own, *sends = _call(
+        _across_z_kernel,
+        [jax.ShapeDtypeStruct((piece, c), F32)]
+        + [jax.ShapeDtypeStruct((piece + carried // 4, c), BF)] * (blocks - 1),
+        [_SMEM] + [_VMEM] * 3,
+        room=8,
+    )(_after(sc, grad), keep_x, got_x, send_x)
+    gots = [_xor(v, 4 * (j + 1), n, axis) for j, v in enumerate(sends)]
+    mine, after = _call(
+        _sum_kernel,
+        [jax.ShapeDtypeStruct((piece, c), BF), jax.ShapeDtypeStruct((carried // 4, c), BF)],
+        [_SMEM] + [_VMEM] * blocks,
+        room=8,
+    )(sc, own, *gots)
     k = 2 * chips
+    if k < n:
+        z = (index >> 2) & (blocks - 1)
+        lead = sends[0][piece:]
+        for target in range(blocks - 1, -1, -1):
+            for j, v in enumerate(gots):
+                lead = jnp.where((z ^ (j + 1)) == target, _first_live(v[piece:], lead), lead)
+            lead = jnp.where(z == target, _first_live(sends[0][piece:], lead), lead)
+        beyond, reach = None, 0
+        while reach < n // k - 1:
+            start = lead if beyond is None else _first_live(lead, beyond)
+            step = k * (reach + 1)
+            came = lax.ppermute(start, axis, [(i + step, i) for i in range(n - step)])
+            beyond = came if beyond is None else _first_live(beyond, came)
+            reach = 2 * reach + 1
+        after = _first_live(after, beyond)
     while k < n:
         mine = (mine.astype(F32) + _xor(mine, k, n, axis).astype(F32)).astype(BF)
         k *= 2
-    pieces = [mine] + [_xor(mine, 2 * k, n, axis) for k in range(1, chips)]
-    other = _xor(jnp.concatenate(pieces, axis=0), 1, n, axis)
-    cwg, swg, cbg, sbg = _call(
+    pieces = [mine] + [_xor(mine, 4 * (j + 1), n, axis) for j in range(blocks - 1)]
+    back_x = jnp.concatenate(pieces + [after], axis=0)
+    got_back = _xor(back_x, 2, n, axis)
+    pair, below = (index >> 1) & 1, blocks * piece
+    theirs = got_back[below:]
+    beyond = jnp.concatenate(
+        [jnp.where(pair == 0, after, theirs), jnp.where(pair == 0, theirs, after)], axis=0
+    )
+    beyond = jnp.where(pair == 0, _first_live(got_x[below:], beyond), beyond)
+    ours = jnp.concatenate([*pieces, got_back[:below], beyond], axis=0)
+    other = _xor(ours, 1, n, axis)
+    cwg, swg, cbg, sbg, frames_grad = _call(
         _final_kernel,
         [
             jax.ShapeDtypeStruct((27 * c, c), F32),
             jax.ShapeDtypeStruct((2 * c, c), F32),
             jax.ShapeDtypeStruct((1, c), F32),
             jax.ShapeDtypeStruct((1, c), F32),
+            jax.ShapeDtypeStruct((slots, 2, h, w, c), BF),
         ],
-        [_SMEM] + [_VMEM] * (chips + 1),
+        [_SMEM] + [_VMEM] * 4,
         [pltpu.VMEM((rows, c), F32)],
         room=12,
-    )(sc, *pieces, other)
-
-    returned = _latest_before(cache, EMPTY_GRAD, axis, n, reverse=True)
-    newest = (jnp.arange(slots, dtype=jnp.int32) == count - 1)[:, None, None, None, None]
-    back = returned.reshape(1, 2, h, w, c).astype(F32)
-    frames_grad = (grad + jnp.where(newest, back, jnp.zeros_like(back))).astype(BF)
+    )(sc, ours, other, got, grad)
     latents = jnp.concatenate([lat0[None], lat1], axis=0)[:, None]
     return (
         latents,

time: 94.2 us -> 83.7 us (0.89)
  starting transfers between devices: 43.3 us -> 23.5 us
  waiting for transfers between devices: 20.2 us -> 30.1 us
  Pallas kernels: 17.3 us -> 19.1 us
  other arithmetic: 3.84 us -> 2.62 us
  local copies, waits for them, and re-layouts: 7.36 us -> 6.41 us
    ppermute x24 -> x13, starting transfers between devices: 30.8 us -> 14.7 us  [_xor(): return lax.ppermute(x, axis, [(i, i ^ k) for i in range(n)])]
    ppermute x24 -> x13, waiting for transfers between devices: 12.8 us -> 27.9 us  [_xor(): return lax.ppermute(x, axis, [(i, i ^ k) for i in range(n)])]
    ppermute x6 -> x2, waiting for transfers between devices: 7.39 us -> 2.19 us  [shift(): return lax.ppermute(v, axis, [(i, i + k) for i in range(n - k)])]
    ppermute x6 -> x2, starting transfers between devices: 12.5 us -> 8.81 us  [shift(): return lax.ppermute(v, axis, [(i, i + k) for i in range(n - k)])]
    convert_element_type x2 -> x0, other arithmetic: 1.02 us -> none  [the longest x1 1 us: body(): (grad + jnp.where(newest, back, jnp.zeros_like(back))).astype(BF)]
    unnamed x30 -> x31, local copies, waits for them, and re-layouts: 7.35 us -> 6.4 us
    pallas_call x2 -> x4, Pallas kernels: 4.8 us -> 5.38 us  [the longest x1 3.44 us: body(): _call(_back_kernel, jax.ShapeDtypeStruct((slots, 2, h, w, c), F32), [_SME...]
  transfers between devices with their start and end apart: 30 -> 15, of which waited for: 11 -> 11; matrix products, arithmetic and copies ran while one was open for 3% -> 2% of each run, Pallas kernels for 11% -> 12%
where the time goes in v3:
time: 83.7 us; the launch traced here: 83.2 us
  waiting for transfers between devices  30.1 us (36%)
  starting transfers between devices  23.5 us (28%)
  Pallas kernels  19.1 us (23%)
  local copies, waits for them, and re-layouts  6.41 us (8%)
  other arithmetic  2.62 us (3%)
  between operations  1.54 us (2%)
    ppermute x13, waiting for transfers between devices, _xor(): return lax.ppermute(x, axis, [(i, i ^ k) for i in range(n)])  27.9 us
    ppermute x13, starting transfers between devices, _xor(): return lax.ppermute(x, axis, [(i, i ^ k) for i in range(n)])  14.7 us
    ppermute x2, starting transfers between devices, shift(): return lax.ppermute(v, axis, [(i, i + k) for i in range(n - k)])  8.81 us
    unnamed x31, local copies, waits for them, and re-layouts  6.4 us
    pallas_call x1, Pallas kernels, early_forward(): _call(_early_kernel, [jax.ShapeDtypeStruct((slots - 1, h, w, c), BF), jax...  4.1 us
    pallas_call x1, Pallas kernels, body(): _call(_back_kernel, jax.ShapeDtypeStruct((slots, 2, h, w, c), F32), [_SME...  3.44 us
    pallas_call x1, Pallas kernels, body(): _call(_late_kernel, [jax.ShapeDtypeStruct((h, w, c), BF), jax.ShapeDtypeS...  3.08 us
    pallas_call x1, Pallas kernels, early_sums(): _call(_early_sums_kernel, jax.ShapeDtypeStruct((rows, c), F32), [_SMEM] +...  2.7 us
  transfers between devices with their start and end apart: 15, of which 11 were waited for; matrix products, arithmetic and copies ran while one was open for 2% of the time, Pallas kernels for 12%

profile of v3, /device:TPU:0, one launch (start us, length us, event | category | flops | bytes accessed | tf_op | source)
XLA Modules:
  0.0 83.2 jit_solution(14625156623761220110)
XLA Ops:
  1.3 1.6 %shard_map.136 = bf16[12,64,128]{2,1,0:T(8,128)(2,1)} custom-call(s32[1]{0:T(128)S(6)} %copy.25.sc, bf16[4,2,4,64,128]{4,3,2,1,0:T(8,128)(2,1)} %frs.1, bf16[4,2,2,64,128]{4,3,2,1,0:T(8,128)(2,1)} %has.1), custom_call_target="tpu_custom_call" | custom-call | tf_op jit(solution)/shard_map/pallas_call | solution.py:457
  2.9 0.5 collective-permute-start
  3.4 0.7 pad_add_fusion.sc
  4.1 0.5 collective-permute-done
  4.7 1.0 %fusion.4 = bf16[6,64,128]{2,1,0:T(8,128)(2,1)S(1)} fusion(bf16[12,64,128]{2,1,0:T(8,128)(2,1)} %shard_map.136, bf16[12,64,128]{2,1,0:T(8,128)(2,1)S(1)} %collective-permute-done, pred[]{:T(512)S(6)} %eq.4), kind=kLoop, calls=%fused_computation.16 | loop fusion | flops 344064 | bytes 491521 | tf_op jit(solution)/shard_map/jit(_where)/select_n | solution.py:396
  5.6 2.9 %collective-permute-start.1 = (bf16[6,64,128]{2,1,0:T(8,128)(2,1)S(1)}, bf16[6,64,128]{2,1,0:T(8,128)(2,1)S(1)}, u32[]{:S(2)}, u32[]{:S(2)}) collective-permute-start(bf16[6,64,128]{2,1,0:T(8,128)(2,1)S(1)} %fusion.4), channel_id=1, source_target_pairs={{0,2},{1,3},{2,0},{3,1},{4,6},{5,7},{6,4},{7,5},{8,10},{9,11},{10,... | collective-permute-start | bytes 294920 | tf_op jit(solution)/shard_map/ppermute | solution.py:377
  8.5 0.0 copy-start
  8.5 1.0 %copy-done = bf16[4,2,4,64,128]{4,3,2,1,0:T(8,128)(2,1)S(1)} copy-done((bf16[4,2,4,64,128]{4,3,2,1,0:T(8,128)(2,1)S(1)}, bf16[4,2,4,64,128]{4,3,2,1,0:T(8,128)(2,1)}, u32[]{:S(2)}) %copy-start) | copy-done | bytes 524312
  9.6 0.0 copy-start.2
  9.6 0.9 %copy-done.2 = bf16[4,2,2,64,128]{4,3,2,1,0:T(8,128)(2,1)S(1)} copy-done((bf16[4,2,2,64,128]{4,3,2,1,0:T(8,128)(2,1)S(1)}, bf16[4,2,2,64,128]{4,3,2,1,0:T(8,128)(2,1)}, u32[]{:S(2)}) %copy-start.2) | copy-done | bytes 262168
  10.5 1.2 %copy-done.4 = bf16[3,3,3,128,128]{4,3,2,1,0:T(8,128)(2,1)S(1)} copy-done((bf16[3,3,3,128,128]{4,3,2,1,0:T(8,128)(2,1)S(1)}, bf16[3,3,3,128,128]{4,3,2,1,0:T(8,128)(2,1)}, u32[]{:S(2)}) %copy-start.4) | copy-done | bytes 884760
  11.7 0.9 %copy-done.6 = bf16[4,1,4,64,128]{4,3,2,1,0:T(8,128)(2,1)S(1)} copy-done((bf16[4,1,4,64,128]{4,3,2,1,0:T(8,128)(2,1)S(1)}, bf16[4,1,4,64,128]{4,3,2,1,0:T(8,128)(2,1)}, u32[]{:S(2)}) %copy-start.6) | copy-done | bytes 262168
  12.7 0.8 %copy-done.8 = bf16[2,128,128]{2,1,0:T(8,128)(2,1)S(1)} copy-done((bf16[2,128,128]{2,1,0:T(8,128)(2,1)S(1)}, bf16[2,128,128]{2,1,0:T(8,128)(2,1)}, u32[]{:S(2)}) %copy-start.8) | copy-done | bytes 65560
  13.5 0.7 copy-done.10
  14.2 0.7 copy-done.11
  14.8 4.1 %shard_map.137 = (bf16[3,4,64,128]{3,2,1,0:T(8,128)(2,1)S(1)}, bf16[768,256]{1,0:T(8,128)(2,1)S(1)}, bf16[768,256]{1,0:T(8,128)(2,1)S(1)}, bf16[768,128]{1,0:T(8...) custom-call(s32[7]{0:T(128)S(1)} %pad_add_fusion.sc, bf16[4,2,4,64,128]{4,3,2,1,0:T(8,128)(2,1)S(1)} %copy-done, ...), custom_call_target="tpu_custom_call" | custom-call | flops 1811939328 | bytes 4194304 | tf_op jit(solution)/shard_map/pallas_call | solution.py:477
  18.9 0.0 collective-permute-done.1
  19.0 3.5 %collective-permute-start.2 = (bf16[6,64,128]{2,1,0:T(8,128)(2,1)S(1)}, bf16[6,64,128]{2,1,0:T(8,128)(2,1)S(1)}, u32[]{:S(2)}, u32[]{:S(2)}) collective-permute-start(bf16[6,64,128]{2,1,0:T(8,128)(2,1)S(1)} %fusion.5), channel_id=1, source_target_pairs={{0,4},{1,5},{2,6},{3,7},{4,8},{5,9},{6,10},{7,11},{8,12},{9,13},{1... | collective-permute-start | bytes 294920 | tf_op jit(solution)/shard_map/ppermute | solution.py:385
  22.5 2.2 %collective-permute-done.2 = bf16[6,64,128]{2,1,0:T(8,128)(2,1)S(1)} collective-permute-done((bf16[6,64,128]{2,1,0:T(8,128)(2,1)S(1)}, bf16[6,64,128]{2,1,0:T(8,128)(2,1)S(1)}, u32[]{:S(2)}, u32[]{:S(2)}) %collective-permute-start.2) | collective-permute-done | bytes 98336 | tf_op jit(solution)/shard_map/ppermute | solution.py:385
  24.7 5.3 %collective-permute-start.3 = (bf16[6,64,128]{2,1,0:T(8,128)(2,1)S(1)}, bf16[6,64,128]{2,1,0:T(8,128)(2,1)S(1)}, u32[]{:S(2)}, u32[]{:S(2)}) collective-permute-start(bf16[6,64,128]{2,1,0:T(8,128)(2,1)S(1)} %compare_select_fusion.4), channel_id=1, source_target_pairs={{0,8},{1,9},{2,10},{3,11},{4,12},{5,13},{6,14},{7,15},{16,24},{17,... | collective-permute-start | bytes 294920 | tf_op jit(solution)/shard_map/ppermute | solution.py:385
  30.0 0.0 copy-start.1
  30.0 0.0 copy-start.3
  30.0 0.0 copy-start.5
  30.0 0.0 copy-start.7
  30.0 0.0 copy-start.9
  30.0 0.0 copy-start.12
  30.1 2.7 %shard_map.138.early = f32[3840,128]{1,0:T(8,128)S(1)} custom-call(s32[7]{0:T(128)S(1)} %pad_add_fusion.sc, bf16[768,256]{1,0:T(8,128)(2,1)S(1)} %get-tuple-element.36.g_ref.g1, bf16[768,256]{1,0:T(8,128)(2,1)S(1)} %get-tuple-element.39.hid_ref, bf16[768,128]{1,0:T(8,128)(2,1)S(1)} %get-tuple-element.40.gout_ref, ...), custom_call_target="tpu_custom_call" | custom-call | flops 1811939328 | bytes 4194304 | tf_op jit(solution)/shard_map/pallas_call | solution.py:496
  32.8 0.0 collective-permute-done.3
  32.8 0.1 collective-permute-start.4
  32.9 1.3 %collective-permute-done.4 = bf16[6,64,128]{2,1,0:T(8,128)(2,1)S(1)} collective-permute-done((bf16[6,64,128]{2,1,0:T(8,128)(2,1)S(1)}, bf16[6,64,128]{2,1,0:T(8,128)(2,1)S(1)}, u32[]{:S(2)}, u32[]{:S(2)}) %collective-permute-start.4) | collective-permute-done | bytes 98336 | tf_op jit(solution)/shard_map/ppermute | solution.py:377
  34.2 0.1 compare_select_fusion.tail
  34.3 0.0 copy-done.1
  34.3 0.0 copy-done.3
  34.3 0.0 copy-done.5
  34.3 0.0 copy-done.7
  34.3 0.0 copy-done.9
  34.3 0.0 copy-done.12
  34.3 3.1 %shard_map.139 = (bf16[4,64,128]{2,1,0:T(8,128)(2,1)S(1)}, bf16[256,256]{1,0:T(8,128)(2,1)S(1)}, bf16[2432,128]{1,0:T(8,128)(2,1)S(1)}, f32[1920,128]{1,0:T(8,128)S(1)}, bf16[512,128]{1,0:T(8,128)(2,1)S(1)}) custom-call(s32[7]{0:T(128)S(1)} %pad_add_fusion.sc, bf16[4,2,4,64,128]{4,3,2,1,0:T(8,128)(2,1)S(1)} %copy-done.1, ...), custom_call_target="tpu_custom_call" | custom-call | flops 1207959552 | bytes 6291456 | tf_op jit(solution)/shard_map/pallas_call | solution.py:512
  37.4 0.2 collective-permute-start.5
  37.6 1.9 %collective-permute-done.5.got = bf16[2432,128]{1,0:T(8,128)(2,1)S(1)} collective-permute-done((bf16[2432,128]{1,0:T(8,128)(2,1)S(1)}, bf16[2432,128]{1,0:T(8,128)(2,1)S(1)}, u32[]{:S(2)}, u32[]{:S(2)}) %collective-permute-start.5) | collective-permute-done | bytes 622624 | tf_op jit(solution)/shard_map/ppermute | solution.py:377
  39.5 0.7 shard_map.140
  40.2 0.6 collective-permute-start.6
  40.8 3.4 %shard_map.141.grad = f32[4,2,4,64,128]{4,3,2,1,0:T(8,128)S(1)} custom-call(s32[7]{0:T(128)S(1)} %pad_add_fusion.sc, bf16[256,256]{1,0:T(8,128)(2,1)S(1)} %get-tuple-element.50.g0, bf16[768,256]{1,0:T(8,128)(2,1)S(1)} %get-tuple-element.36.g_ref.g1, bf16[27,128,128]{2,1,0:T(8,128)(2,1)S(1)} %bitcast.17), custom_call_target="tpu_custom_call" | custom-call | flops 2415919104 | bytes 6291456 | tf_op jit(solution)/shard_map/pallas_call | solution.py:541
  44.3 5.4 %collective-permute-done.6.got = bf16[1216,128]{1,0:T(8,128)(2,1)S(1)} collective-permute-done((bf16[1216,128]{1,0:T(8,128)(2,1)S(1)}, bf16[1216,128]{1,0:T(8,128)(2,1)S(1)}, u32[]{:S(2)}, u32[]{:S(2)}) %collective-permute-start.6) | collective-permute-done | bytes 311328 | tf_op jit(solution)/shard_map/ppermute | solution.py:377
  49.7 0.6 shard_map.142
  50.3 1.9 %collective-permute-start.7 = (bf16[368,128]{1,0:T(8,128)(2,1)S(1)}, bf16[368,128]{1,0:T(8,128)(2,1)S(1)}, u32[]{:S(2)}, u32[]{:S(2)}) collective-permute-start(bf16[368,128]{1,0:T(8,128)(2,1)S(1)} %get-tuple-element.54), channel_id=1, source_target_pairs={{0,4},{1,5},{2,6},{3,7},{4,0},{5,1},{6,2},{7,3},{8,12},{9,13},{10,... | collective-permute-start | bytes 282632 | tf_op jit(solution)/shard_map/ppermute | solution.py:377
  52.2 3.4 %collective-permute-start.8 = (bf16[368,128]{1,0:T(8,128)(2,1)S(1)}, bf16[368,128]{1,0:T(8,128)(2,1)S(1)}, u32[]{:S(2)}, u32[]{:S(2)}) collective-permute-start(bf16[368,128]{1,0:T(8,128)(2,1)S(1)} %get-tuple-element.55), channel_id=1, source_target_pairs={{0,8},{1,9},{2,10},{3,11},{4,12},{5,13},{6,14},{7,15},{8,0},{9,1},... | collective-permute-start | bytes 282632 | tf_op jit(solution)/shard_map/ppermute | solution.py:377
  55.6 0.0 collective-permute-start.9
  55.6 0.0 collective-permute-done.7.refs_0_
  55.6 6.9 %collective-permute-done.8.refs_1_ = bf16[368,128]{1,0:T(8,128)(2,1)S(1)} collective-permute-done((bf16[368,128]{1,0:T(8,128)(2,1)S(1)}, bf16[368,128]{1,0:T(8,128)(2,1)S(1)}, u32[]{:S(2)}, u32[]{:S(2)}) %collective-permute-start.8) | collective-permute-done | bytes 94240 | tf_op jit(solution)/shard_map/ppermute | solution.py:377
  62.6 0.0 collective-permute-done.9.refs_2_
  62.6 0.6 shard_map.143
  63.2 1.6 %collective-permute-start.10 = (bf16[240,128]{1,0:T(8,128)(2,1)S(1)}, bf16[240,128]{1,0:T(8,128)(2,1)S(1)}, u32[]{:S(2)}, u32[]{:S(2)}) collective-permute-start(bf16[240,128]{1,0:T(8,128)(2,1)S(1)} %get-tuple-element.57), channel_id=1, source_target_pairs={{0,4},{1,5},{2,6},{3,7},{4,0},{5,1},{6,2},{7,3},{8,12},{9,13},{10,... | collective-permute-start | bytes 184328 | tf_op jit(solution)/shard_map/ppermute | solution.py:377
  64.8 1.4 %collective-permute-start.11 = (bf16[240,128]{1,0:T(8,128)(2,1)S(1)}, bf16[240,128]{1,0:T(8,128)(2,1)S(1)}, u32[]{:S(2)}, u32[]{:S(2)}) collective-permute-start(bf16[240,128]{1,0:T(8,128)(2,1)S(1)} %get-tuple-element.57), channel_id=1, source_target_pairs={{0,8},{1,9},{2,10},{3,11},{4,12},{5,13},{6,14},{7,15},{8,0},{9,1},... | collective-permute-start | bytes 184328 | tf_op jit(solution)/shard_map/ppermute | solution.py:377
  66.3 1.4 %collective-permute-start.12 = (bf16[240,128]{1,0:T(8,128)(2,1)S(1)}, bf16[240,128]{1,0:T(8,128)(2,1)S(1)}, u32[]{:S(2)}, u32[]{:S(2)}) collective-permute-start(bf16[240,128]{1,0:T(8,128)(2,1)S(1)} %get-tuple-element.57), channel_id=1, source_target_pairs={{0,12},{1,13},{2,14},{3,15},{4,8},{5,9},{6,10},{7,11},{8,4},{9,5},... | collective-permute-start | bytes 184328 | tf_op jit(solution)/shard_map/ppermute | solution.py:377
  67.7 0.1 collective-permute-done.10
  67.8 2.9 %collective-permute-done.11 = bf16[240,128]{1,0:T(8,128)(2,1)S(1)} collective-permute-done((bf16[240,128]{1,0:T(8,128)(2,1)S(1)}, bf16[240,128]{1,0:T(8,128)(2,1)S(1)}, u32[]{:S(2)}, u32[]{:S(2)}) %collective-permute-start.11) | collective-permute-done | bytes 61472 | tf_op jit(solution)/shard_map/ppermute | solution.py:377
  70.8 1.5 %collective-permute-done.12 = bf16[240,128]{1,0:T(8,128)(2,1)S(1)} collective-permute-done((bf16[240,128]{1,0:T(8,128)(2,1)S(1)}, bf16[240,128]{1,0:T(8,128)(2,1)S(1)}, u32[]{:S(2)}, u32[]{:S(2)}) %collective-permute-start.12) | collective-permute-done | bytes 61472 | tf_op jit(solution)/shard_map/ppermute | solution.py:377
  72.3 0.6 collective-permute-start.13
  72.9 6.0 %collective-permute-done.13 = bf16[1088,128]{1,0:T(8,128)(2,1)S(1)} collective-permute-done((bf16[1088,128]{1,0:T(8,128)(2,1)S(1)}, bf16[1088,128]{1,0:T(8,128)(2,1)S(1)}, u32[]{:S(2)}, u32[]{:S(2)}) %collective-permute-start.13) | collective-permute-done | bytes 278560 | tf_op jit(solution)/shard_map/ppermute | solution.py:377
  79.0 0.1 collective-permute-start.14
  79.1 0.7 maximum_bitcast_fusion
  79.8 1.2 %collective-permute-done.14.other = bf16[2176,128]{1,0:T(8,128)(2,1)S(1)} collective-permute-done((bf16[2176,128]{1,0:T(8,128)(2,1)S(1)}, bf16[2176,128]{1,0:T(8,128)(2,1)S(1)}, u32[]{:S(2)}, u32[]{:S(2)}) %collective-permute-start.14) | collective-permute-done | bytes 557088 | tf_op jit(solution)/shard_map/ppermute | solution.py:377
  81.1 2.2 %shard_map.144 = (f32[3456,128]{1,0:T(8,128)}, f32[256,128]{1,0:T(8,128)}, f32[1,128]{1,0:T(1,128)}, f32[1,128]{1,0:T(1,128)}, bf16[4,2,4,64,128]{4,3,2,1,0:T(8,128)(2,1)}) custom-call(s32[7]{0:T(128)S(1)} %pad_add_fusion.sc, bf16[2176,128]{1,0:T(8,128)(2,1)S(1)} %fusion.6.mine, bf16[2176,128]{1,0:T(8,128)(2,1)S(1)} %collective-permute-done.14.other, ...), custom_call_target="tpu_custom_call" | custom-call | tf_op jit(solution)/shard_map/pallas_call | solution.py:594
  (18 shorter events, 0.3 us)
Async XLA Ops:
  2.9 1.7 %collective-permute-start = (bf16[12,64,128]{2,1,0:T(8,128)(2,1)}, bf16[12,64,128]{2,1,0:T(8,128)(2,1)S(1)}, u32[]{:S(2)}, u32[]{:S(2)}) collective-permute-start(bf16[12,64,128]{2,1,0:T(8,128)(2,1)} %shard_map.136), channel_id=1, source_target_pairs={{0,1},{1,0},{2,3},{3,2},{4,5},{5,4},{6,7},{7,6},{8,9},{9,8},{10,11... | collective-permute-start | bytes 589832 | tf_op jit(solution)/shard_map/ppermute | solution.py:377
  5.6 13.3 %collective-permute-start.1 = (bf16[6,64,128]{2,1,0:T(8,128)(2,1)S(1)}, bf16[6,64,128]{2,1,0:T(8,128)(2,1)S(1)}, u32[]{:S(2)}, u32[]{:S(2)}) collective-permute-start(bf16[6,64,128]{2,1,0:T(8,128)(2,1)S(1)} %fusion.4), channel_id=1, source_target_pairs={{0,2},{1,3},{2,0},{3,1},{4,6},{5,7},{6,4},{7,5},{8,10},{9,11},{10,... | collective-permute-start | bytes 294920 | tf_op jit(solution)/shard_map/ppermute | solution.py:377
  8.5 1.0 %copy-start = (bf16[4,2,4,64,128]{4,3,2,1,0:T(8,128)(2,1)S(1)}, bf16[4,2,4,64,128]{4,3,2,1,0:T(8,128)(2,1)}, u32[]{:S(2)}) copy-start(bf16[4,2,4,64,128]{4,3,2,1,0:T(8,128)(2,1)} %frs.1) | copy-start | bytes 1572868
  9.6 0.9 %copy-start.2 = (bf16[4,2,2,64,128]{4,3,2,1,0:T(8,128)(2,1)S(1)}, bf16[4,2,2,64,128]{4,3,2,1,0:T(8,128)(2,1)}, u32[]{:S(2)}) copy-start(bf16[4,2,2,64,128]{4,3,2,1,0:T(8,128)(2,1)} %has.1) | copy-start | bytes 786436
  10.5 1.2 %copy-start.4 = (bf16[3,3,3,128,128]{4,3,2,1,0:T(8,128)(2,1)S(1)}, bf16[3,3,3,128,128]{4,3,2,1,0:T(8,128)(2,1)}, u32[]{:S(2)}) copy-start(bf16[3,3,3,128,128]{4,3,2,1,0:T(8,128)(2,1)} %param.13) | copy-start | bytes 2654212
  11.7 0.9 %copy-start.6 = (bf16[4,1,4,64,128]{4,3,2,1,0:T(8,128)(2,1)S(1)}, bf16[4,1,4,64,128]{4,3,2,1,0:T(8,128)(2,1)}, u32[]{:S(2)}) copy-start(bf16[4,1,4,64,128]{4,3,2,1,0:T(8,128)(2,1)} %cos.1) | copy-start | bytes 786436
  12.7 0.8 %copy-start.8 = (bf16[2,128,128]{2,1,0:T(8,128)(2,1)S(1)}, bf16[2,128,128]{2,1,0:T(8,128)(2,1)}, u32[]{:S(2)}) copy-start(bf16[2,128,128]{2,1,0:T(8,128)(2,1)} %sw.3) | copy-start | bytes 196612
  13.5 0.7 copy-start.10
  14.2 0.7 copy-start.11
  19.0 5.7 %collective-permute-start.2 = (bf16[6,64,128]{2,1,0:T(8,128)(2,1)S(1)}, bf16[6,64,128]{2,1,0:T(8,128)(2,1)S(1)}, u32[]{:S(2)}, u32[]{:S(2)}) collective-permute-start(bf16[6,64,128]{2,1,0:T(8,128)(2,1)S(1)} %fusion.5), channel_id=1, source_target_pairs={{0,4},{1,5},{2,6},{3,7},{4,8},{5,9},{6,10},{7,11},{8,12},{9,13},{1... | collective-permute-start | bytes 294920 | tf_op jit(solution)/shard_map/ppermute | solution.py:385
  24.7 8.1 %collective-permute-start.3 = (bf16[6,64,128]{2,1,0:T(8,128)(2,1)S(1)}, bf16[6,64,128]{2,1,0:T(8,128)(2,1)S(1)}, u32[]{:S(2)}, u32[]{:S(2)}) collective-permute-start(bf16[6,64,128]{2,1,0:T(8,128)(2,1)S(1)} %compare_select_fusion.4), channel_id=1, source_target_pairs={{0,8},{1,9},{2,10},{3,11},{4,12},{5,13},{6,14},{7,15},{16,24},{17,... | collective-permute-start | bytes 294920 | tf_op jit(solution)/shard_map/ppermute | solution.py:385
  30.0 4.3 %copy-start.1 = (bf16[4,2,4,64,128]{4,3,2,1,0:T(8,128)(2,1)S(1)}, bf16[4,2,4,64,128]{4,3,2,1,0:T(8,128)(2,1)}, u32[]{:S(2)}) copy-start(bf16[4,2,4,64,128]{4,3,2,1,0:T(8,128)(2,1)} %frs.1) | copy-start | bytes 1572868
  30.0 4.3 %copy-start.3 = (bf16[4,2,2,64,128]{4,3,2,1,0:T(8,128)(2,1)S(1)}, bf16[4,2,2,64,128]{4,3,2,1,0:T(8,128)(2,1)}, u32[]{:S(2)}) copy-start(bf16[4,2,2,64,128]{4,3,2,1,0:T(8,128)(2,1)} %has.1) | copy-start | bytes 786436
  30.0 4.3 %copy-start.5 = (bf16[3,3,3,128,128]{4,3,2,1,0:T(8,128)(2,1)S(1)}, bf16[3,3,3,128,128]{4,3,2,1,0:T(8,128)(2,1)}, u32[]{:S(2)}) copy-start(bf16[3,3,3,128,128]{4,3,2,1,0:T(8,128)(2,1)} %param.13) | copy-start | bytes 2654212
  30.0 4.3 %copy-start.7 = (bf16[4,1,4,64,128]{4,3,2,1,0:T(8,128)(2,1)S(1)}, bf16[4,1,4,64,128]{4,3,2,1,0:T(8,128)(2,1)}, u32[]{:S(2)}) copy-start(bf16[4,1,4,64,128]{4,3,2,1,0:T(8,128)(2,1)} %cos.1) | copy-start | bytes 786436
  30.0 4.3 %copy-start.9 = (bf16[2,128,128]{2,1,0:T(8,128)(2,1)S(1)}, bf16[2,128,128]{2,1,0:T(8,128)(2,1)}, u32[]{:S(2)}) copy-start(bf16[2,128,128]{2,1,0:T(8,128)(2,1)} %sw.3) | copy-start | bytes 196612
  30.0 4.3 %copy-start.12 = (f32[128]{0:T(128)S(1)}, f32[128]{0:T(128)}, u32[]{:S(2)}) copy-start(f32[128]{0:T(128)} %param.16) | copy-start | bytes 1540
  32.8 1.4 %collective-permute-start.4 = (bf16[6,64,128]{2,1,0:T(8,128)(2,1)S(1)}, bf16[6,64,128]{2,1,0:T(8,128)(2,1)S(1)}, u32[]{:S(2)}, u32[]{:S(2)}) collective-permute-start(bf16[6,64,128]{2,1,0:T(8,128)(2,1)S(1)} %fusion.1), channel_id=1, source_target_pairs={{0,1},{1,0},{2,3},{3,2},{4,5},{5,4},{6,7},{7,6},{8,9},{9,8},{10,11... | collective-permute-start | bytes 294920 | tf_op jit(solution)/shard_map/ppermute | solution.py:377
  37.4 2.1 %collective-permute-start.5 = (bf16[2432,128]{1,0:T(8,128)(2,1)S(1)}, bf16[2432,128]{1,0:T(8,128)(2,1)S(1)}, u32[]{:S(2)}, u32[]{:S(2)}) collective-permute-start(bf16[2432,128]{1,0:T(8,128)(2,1)S(1)} %get-tuple-element.46), channel_id=1, source_target_pairs={{0,1},{1,0},{2,3},{3,2},{4,5},{5,4},{6,7},{7,6},{8,9},{9,8},{10,11... | collective-permute-start | bytes 1867784 | tf_op jit(solution)/shard_map/ppermute | solution.py:377
  40.2 9.5 %collective-permute-start.6 = (bf16[1216,128]{1,0:T(8,128)(2,1)S(1)}, bf16[1216,128]{1,0:T(8,128)(2,1)S(1)}, u32[]{:S(2)}, u32[]{:S(2)}) collective-permute-start(bf16[1216,128]{1,0:T(8,128)(2,1)S(1)} %get-tuple-element.52.sent), channel_id=1, source_target_pairs={{0,2},{1,3},{2,0},{3,1},{4,6},{5,7},{6,4},{7,5},{8,10},{9,11},{10,... | collective-permute-start | bytes 933896 | tf_op jit(solution)/shard_map/ppermute | solution.py:377
  50.3 5.3 %collective-permute-start.7 = (bf16[368,128]{1,0:T(8,128)(2,1)S(1)}, bf16[368,128]{1,0:T(8,128)(2,1)S(1)}, u32[]{:S(2)}, u32[]{:S(2)}) collective-permute-start(bf16[368,128]{1,0:T(8,128)(2,1)S(1)} %get-tuple-element.54), channel_id=1, source_target_pairs={{0,4},{1,5},{2,6},{3,7},{4,0},{5,1},{6,2},{7,3},{8,12},{9,13},{10,... | collective-permute-start | bytes 282632 | tf_op jit(solution)/shard_map/ppermute | solution.py:377
  52.2 10.3 %collective-permute-start.8 = (bf16[368,128]{1,0:T(8,128)(2,1)S(1)}, bf16[368,128]{1,0:T(8,128)(2,1)S(1)}, u32[]{:S(2)}, u32[]{:S(2)}) collective-permute-start(bf16[368,128]{1,0:T(8,128)(2,1)S(1)} %get-tuple-element.55), channel_id=1, source_target_pairs={{0,8},{1,9},{2,10},{3,11},{4,12},{5,13},{6,14},{7,15},{8,0},{9,1},... | collective-permute-start | bytes 282632 | tf_op jit(solution)/shard_map/ppermute | solution.py:377
  55.6 7.0 %collective-permute-start.9 = (bf16[368,128]{1,0:T(8,128)(2,1)S(1)}, bf16[368,128]{1,0:T(8,128)(2,1)S(1)}, u32[]{:S(2)}, u32[]{:S(2)}) collective-permute-start(bf16[368,128]{1,0:T(8,128)(2,1)S(1)} %get-tuple-element.56), channel_id=1, source_target_pairs={{0,12},{1,13},{2,14},{3,15},{4,8},{5,9},{6,10},{7,11},{8,4},{9,5},... | collective-permute-start | bytes 282632 | tf_op jit(solution)/shard_map/ppermute | solution.py:377
  63.2 4.6 %collective-permute-start.10 = (bf16[240,128]{1,0:T(8,128)(2,1)S(1)}, bf16[240,128]{1,0:T(8,128)(2,1)S(1)}, u32[]{:S(2)}, u32[]{:S(2)}) collective-permute-start(bf16[240,128]{1,0:T(8,128)(2,1)S(1)} %get-tuple-element.57), channel_id=1, source_target_pairs={{0,4},{1,5},{2,6},{3,7},{4,0},{5,1},{6,2},{7,3},{8,12},{9,13},{10,... | collective-permute-start | bytes 184328 | tf_op jit(solution)/shard_map/ppermute | solution.py:377
  64.8 5.9 %collective-permute-start.11 = (bf16[240,128]{1,0:T(8,128)(2,1)S(1)}, bf16[240,128]{1,0:T(8,128)(2,1)S(1)}, u32[]{:S(2)}, u32[]{:S(2)}) collective-permute-start(bf16[240,128]{1,0:T(8,128)(2,1)S(1)} %get-tuple-element.57), channel_id=1, source_target_pairs={{0,8},{1,9},{2,10},{3,11},{4,12},{5,13},{6,14},{7,15},{8,0},{9,1},... | collective-permute-start | bytes 184328 | tf_op jit(solution)/shard_map/ppermute | solution.py:377
  66.3 6.0 %collective-permute-start.12 = (bf16[240,128]{1,0:T(8,128)(2,1)S(1)}, bf16[240,128]{1,0:T(8,128)(2,1)S(1)}, u32[]{:S(2)}, u32[]{:S(2)}) collective-permute-start(bf16[240,128]{1,0:T(8,128)(2,1)S(1)} %get-tuple-element.57), channel_id=1, source_target_pairs={{0,12},{1,13},{2,14},{3,15},{4,8},{5,9},{6,10},{7,11},{8,4},{9,5},... | collective-permute-start | bytes 184328 | tf_op jit(solution)/shard_map/ppermute | solution.py:377
  72.3 6.6 %collective-permute-start.13 = (bf16[1088,128]{1,0:T(8,128)(2,1)S(1)}, bf16[1088,128]{1,0:T(8,128)(2,1)S(1)}, u32[]{:S(2)}, u32[]{:S(2)}) collective-permute-start(bf16[1088,128]{1,0:T(8,128)(2,1)S(1)} %constant_dynamic-update-slice_fusion), channel_id=1, source_target_pairs={{0,2},{1,3},{2,0},{3,1},{4,6},{5,7},{6,4},{7,5},{8,10},{9,11},{10,... | collective-permute-start | bytes 835592 | tf_op jit(solution)/shard_map/ppermute | solution.py:377
  79.0 2.0 %collective-permute-start.14 = (bf16[2176,128]{1,0:T(8,128)(2,1)S(1)}, bf16[2176,128]{1,0:T(8,128)(2,1)S(1)}, u32[]{:S(2)}, u32[]{:S(2)}) collective-permute-start(bf16[2176,128]{1,0:T(8,128)(2,1)S(1)} %fusion.6.mine), channel_id=1, source_target_pairs={{0,1},{1,0},{2,3},{3,2},{4,5},{5,4},{6,7},{7,6},{8,9},{9,8},{10,11... | collective-permute-start | bytes 1671176 | tf_op jit(solution)/shard_map/ppermute | solution.py:377

commit v4 on v3

--- a/solution.py
+++ b/solution.py
@@ -141,10 +141,30 @@
 
 
 def _early_kernel(
-    sc, frh, hah, coh, wh, cb, sw, sb, lat_ref, g_ref, hid_ref, gout_ref, xk, fr, ha, co, w_ref, sems
+    sc,
+    frh,
+    hah,
+    coh,
+    wh,
+    cbh,
+    swh,
+    sbh,
+    lat_ref,
+    g_ref,
+    hid_ref,
+    gout_ref,
+    xk,
+    fr,
+    ha,
+    co,
+    w_ref,
+    cb,
+    sw,
+    sb,
+    sems,
 ):
     slots, _, h, w, c = fr.shape
-    pairs = ((frh, fr), (hah, ha), (coh, co), (wh, w_ref))
+    pairs = ((frh, fr), (hah, ha), (coh, co), (wh, w_ref), (cbh, cb), (swh, sw), (sbh, sb))
     copies = [pltpu.make_async_copy(a, b, sems.at[i]) for i, (a, b) in enumerate(pairs)]
     for copy in copies:
         copy.start()
@@ -154,7 +174,8 @@
     copies[2].wait()
     gout = _early_gout(sc, co)
     gout_ref[...] = gout
-    copies[3].wait()
+    for copy in copies[3:]:
+        copy.wait()
     lat, g, hidden = _head(xk, gout, w_ref, cb, sw, sb, h)
     for s in range(1, slots):
         part = lat[(s - 1) * h * w : s * h * w]
@@ -466,11 +487,15 @@
             ],
             out_specs=pl.BlockSpec((2 * h + 4, w, c), lambda i, sc: (0, 0, 0)),
         ),
-        compiler_params=pltpu.CompilerParams(vmem_limit_bytes=60 << 20),
-    )(slab_counts, frames, row_halo)
+        compiler_params=pltpu.CompilerParams(vmem_limit_bytes=8 << 20),
+    )(
+        slab_counts,
+        *(pltpu.with_memory_space_constraint(v, pltpu.HBM) for v in (frames, row_halo)),
+    )
 
     held = {}
     wide = ((slots - 1) * m, 2 * c)
+    raw = (frames, row_halo, cotangent, wt, cb, stride_weight, sb)
     windows = (3, slots - 1, 4, h + 2, w, c)
 
     def early_forward(start, follow):
@@ -483,12 +508,11 @@
                 jax.ShapeDtypeStruct((wide[0], c), BF),
                 jax.ShapeDtypeStruct(windows, BF),
             ],
-            [_SMEM] + [_HBM] * 4 + [_VMEM] * 3,
-            [pltpu.VMEM(v.shape, BF) for v in (frames, row_halo, cotangent, wt)]
-            + [pltpu.SemaphoreType.DMA((4,))],
+            [_SMEM] + [_HBM] * len(raw),
+            [pltpu.VMEM(v.shape, v.dtype) for v in raw] + [pltpu.SemaphoreType.DMA((len(raw),))],
             flops=(slots - 1) * conv_flops,
             moved=4 << 20,
-        )(_after(sc, start), frames, row_halo, cotangent, wt, cb, stride_weight, sb)
+        )(_after(sc, start), *(pltpu.with_memory_space_constraint(v, pltpu.HBM) for v in raw))
         return _after(follow, held["early"][1])
 
     def early_sums(start, follow):

time: 83.7 us -> 76.4 us (0.913)
  local copies, waits for them, and re-layouts: 6.41 us -> 0.17 us
  other arithmetic: 2.62 us -> 1.67 us
    unnamed x31 -> x19, local copies, waits for them, and re-layouts: 6.4 us -> 0.15 us
    select_n x1, other arithmetic: 0.97 us -> 0.03 us  [_latest_before(): chip = jnp.where(core == 0, newest(a, b), newest(b, a))]
    pallas_call x1, Pallas kernels: 4.1 us -> 5 us  [early_forward(): _call(_early_kernel, [jax.ShapeDtypeStruct((slots - 1, h, w, c), BF), jax...]
  transfers between devices with their start and end apart: 15 -> 15, of which waited for: 11 -> 11; matrix products, arithmetic and copies ran while one was open for 2% -> 2% of each run, Pallas kernels for 12% -> 15%
where the time goes in v4:
time: 76.4 us; the launch traced here: 76.2 us
  waiting for transfers between devices  29.9 us (39%)
  starting transfers between devices  23.5 us (31%)
  Pallas kernels  19.3 us (25%)
  other arithmetic  1.67 us (2%)
  between operations  1.55 us (2%)
    ppermute x13, waiting for transfers between devices, _xor(): return lax.ppermute(x, axis, [(i, i ^ k) for i in range(n)])  27.7 us
    ppermute x13, starting transfers between devices, _xor(): return lax.ppermute(x, axis, [(i, i ^ k) for i in range(n)])  14.7 us
    ppermute x2, starting transfers between devices, shift(): return lax.ppermute(v, axis, [(i, i + k) for i in range(n - k)])  8.81 us
    pallas_call x1, Pallas kernels, early_forward(): _call(_early_kernel, [jax.ShapeDtypeStruct((slots - 1, h, w, c), BF), jax...  5 us
    pallas_call x1, Pallas kernels, body(): _call(_back_kernel, jax.ShapeDtypeStruct((slots, 2, h, w, c), F32), [_SME...  3.43 us
    pallas_call x1, Pallas kernels, body(): _call(_late_kernel, [jax.ShapeDtypeStruct((h, w, c), BF), jax.ShapeDtypeS...  3.12 us
    pallas_call x1, Pallas kernels, early_sums(): _call(_early_sums_kernel, jax.ShapeDtypeStruct((rows, c), F32), [_SMEM] +...  2.71 us
    ppermute x2, waiting for transfers between devices, shift(): return lax.ppermute(v, axis, [(i, i + k) for i in range(n - k)])  2.19 us
  transfers between devices with their start and end apart: 15, of which 11 were waited for; matrix products, arithmetic and copies ran while one was open for 2% of the time, Pallas kernels for 15%

profile of v4, /device:TPU:0, one launch (start us, length us, event | category | flops | bytes accessed | tf_op | source)
XLA Modules:
  0.0 76.2 jit_solution(2362826662972565855)
XLA Ops:
  1.3 1.0 %shard_map.136 = bf16[12,64,128]{2,1,0:T(8,128)(2,1)S(1)} custom-call(s32[1]{0:T(128)S(6)} %copy.25.sc, bf16[4,2,4,64,128]{4,3,2,1,0:T(8,128)(2,1)} %frs.1, bf16[4,2,2,64,128]{4,3,2,1,0:T(8,128)(2,1)} %has.1), custom_call_target="tpu_custom_call" | custom-call | tf_op jit(solution)/shard_map/pallas_call | solution.py:478
  2.2 0.5 collective-permute-start
  2.8 0.7 pad_add_fusion.sc
  3.5 0.3 collective-permute-done
  3.9 2.9 %collective-permute-start.1 = (bf16[6,64,128]{2,1,0:T(8,128)(2,1)S(1)}, bf16[6,64,128]{2,1,0:T(8,128)(2,1)S(1)}, u32[]{:S(2)}, u32[]{:S(2)}) collective-permute-start(bf16[6,64,128]{2,1,0:T(8,128)(2,1)S(1)} %fusion.4), channel_id=1, source_target_pairs={{0,2},{1,3},{2,0},{3,1},{4,6},{5,7},{6,4},{7,5},{8,10},{9,11},{10,... | collective-permute-start | bytes 294920 | tf_op jit(solution)/shard_map/ppermute | solution.py:398
  6.8 5.0 %shard_map.137 = (bf16[3,4,64,128]{3,2,1,0:T(8,128)(2,1)S(1)}, bf16[768,256]{1,0:T(8,128)(2,1)S(1)}, bf16[768,256]{1,0:T(8,128)(2,1)S(1)}, bf16[768,128]{1,0:T(8...) custom-call(s32[7]{0:T(128)S(1)} %pad_add_fusion.sc, bf16[4,2,4,64,128]{4,3,2,1,0:T(8,128)(2,1)} %frs.1, ...), custom_call_target="tpu_custom_call" | custom-call | flops 1811939328 | bytes 4194304 | tf_op jit(solution)/shard_map/pallas_call | solution.py:502
  11.8 0.0 collective-permute-done.1
  11.8 3.5 %collective-permute-start.2 = (bf16[6,64,128]{2,1,0:T(8,128)(2,1)S(1)}, bf16[6,64,128]{2,1,0:T(8,128)(2,1)S(1)}, u32[]{:S(2)}, u32[]{:S(2)}) collective-permute-start(bf16[6,64,128]{2,1,0:T(8,128)(2,1)S(1)} %fusion.5), channel_id=1, source_target_pairs={{0,4},{1,5},{2,6},{3,7},{4,8},{5,9},{6,10},{7,11},{8,12},{9,13},{1... | collective-permute-start | bytes 294920 | tf_op jit(solution)/shard_map/ppermute | solution.py:406
  15.3 2.2 %collective-permute-done.2 = bf16[6,64,128]{2,1,0:T(8,128)(2,1)S(1)} collective-permute-done((bf16[6,64,128]{2,1,0:T(8,128)(2,1)S(1)}, bf16[6,64,128]{2,1,0:T(8,128)(2,1)S(1)}, u32[]{:S(2)}, u32[]{:S(2)}) %collective-permute-start.2) | collective-permute-done | bytes 98336 | tf_op jit(solution)/shard_map/ppermute | solution.py:406
  17.5 5.3 %collective-permute-start.3 = (bf16[6,64,128]{2,1,0:T(8,128)(2,1)S(1)}, bf16[6,64,128]{2,1,0:T(8,128)(2,1)S(1)}, u32[]{:S(2)}, u32[]{:S(2)}) collective-permute-start(bf16[6,64,128]{2,1,0:T(8,128)(2,1)S(1)} %compare_select_fusion.4), channel_id=1, source_target_pairs={{0,8},{1,9},{2,10},{3,11},{4,12},{5,13},{6,14},{7,15},{16,24},{17,... | collective-permute-start | bytes 294920 | tf_op jit(solution)/shard_map/ppermute | solution.py:406
  22.9 0.0 copy-start
  22.9 0.0 copy-start.1
  22.9 0.0 copy-start.2
  22.9 0.0 copy-start.3
  22.9 0.0 copy-start.4
  22.9 0.0 copy-start.5
  22.9 0.0 copy-start.6
  23.0 2.7 %shard_map.138.early = f32[3840,128]{1,0:T(8,128)S(1)} custom-call(s32[7]{0:T(128)S(1)} %pad_add_fusion.sc, bf16[768,256]{1,0:T(8,128)(2,1)S(1)} %get-tuple-element.36.g_ref.g1, bf16[768,256]{1,0:T(8,128)(2,1)S(1)} %get-tuple-element.39.hid_ref, bf16[768,128]{1,0:T(8,128)(2,1)S(1)} %get-tuple-element.40.gout_ref, ...), custom_call_target="tpu_custom_call" | custom-call | flops 1811939328 | bytes 4194304 | tf_op jit(solution)/shard_map/pallas_call | solution.py:520
  25.7 0.0 collective-permute-done.3
  25.7 0.1 collective-permute-start.4
  25.8 1.3 %collective-permute-done.4 = bf16[6,64,128]{2,1,0:T(8,128)(2,1)S(1)} collective-permute-done((bf16[6,64,128]{2,1,0:T(8,128)(2,1)S(1)}, bf16[6,64,128]{2,1,0:T(8,128)(2,1)S(1)}, u32[]{:S(2)}, u32[]{:S(2)}) %collective-permute-start.4) | collective-permute-done | bytes 98336 | tf_op jit(solution)/shard_map/ppermute | solution.py:398
  27.1 0.1 compare_select_fusion.tail
  27.2 0.0 copy-done
  27.2 0.0 copy-done.1
  27.2 0.0 copy-done.2
  27.2 0.0 copy-done.3
  27.2 0.0 copy-done.4
  27.2 0.0 copy-done.5
  27.2 0.0 copy-done.6
  27.2 3.1 %shard_map.139 = (bf16[4,64,128]{2,1,0:T(8,128)(2,1)S(1)}, bf16[256,256]{1,0:T(8,128)(2,1)S(1)}, bf16[2432,128]{1,0:T(8,128)(2,1)S(1)}, f32[1920,128]{1,0:T(8,128)S(1)}, bf16[512,128]{1,0:T(8,128)(2,1)S(1)}) custom-call(s32[7]{0:T(128)S(1)} %pad_add_fusion.sc, bf16[4,2,4,64,128]{4,3,2,1,0:T(8,128)(2,1)S(1)} %copy-done, ...), custom_call_target="tpu_custom_call" | custom-call | flops 1207959552 | bytes 6291456 | tf_op jit(solution)/shard_map/pallas_call | solution.py:536
  30.4 0.2 collective-permute-start.5
  30.6 1.9 %collective-permute-done.5.got = bf16[2432,128]{1,0:T(8,128)(2,1)S(1)} collective-permute-done((bf16[2432,128]{1,0:T(8,128)(2,1)S(1)}, bf16[2432,128]{1,0:T(8,128)(2,1)S(1)}, u32[]{:S(2)}, u32[]{:S(2)}) %collective-permute-start.5) | collective-permute-done | bytes 622624 | tf_op jit(solution)/shard_map/ppermute | solution.py:398
  32.5 0.7 shard_map.140
  33.2 0.6 collective-permute-start.6
  33.8 3.4 %shard_map.141.grad = f32[4,2,4,64,128]{4,3,2,1,0:T(8,128)S(1)} custom-call(s32[7]{0:T(128)S(1)} %pad_add_fusion.sc, bf16[256,256]{1,0:T(8,128)(2,1)S(1)} %get-tuple-element.50.g0, bf16[768,256]{1,0:T(8,128)(2,1)S(1)} %get-tuple-element.36.g_ref.g1, bf16[27,128,128]{2,1,0:T(8,128)(2,1)S(1)} %bitcast.17), custom_call_target="tpu_custom_call" | custom-call | flops 2415919104 | bytes 6291456 | tf_op jit(solution)/shard_map/pallas_call | solution.py:565
  37.2 5.4 %collective-permute-done.6.got = bf16[1216,128]{1,0:T(8,128)(2,1)S(1)} collective-permute-done((bf16[1216,128]{1,0:T(8,128)(2,1)S(1)}, bf16[1216,128]{1,0:T(8,128)(2,1)S(1)}, u32[]{:S(2)}, u32[]{:S(2)}) %collective-permute-start.6) | collective-permute-done | bytes 311328 | tf_op jit(solution)/shard_map/ppermute | solution.py:398
  42.6 0.6 shard_map.142
  43.3 1.9 %collective-permute-start.7 = (bf16[368,128]{1,0:T(8,128)(2,1)S(1)}, bf16[368,128]{1,0:T(8,128)(2,1)S(1)}, u32[]{:S(2)}, u32[]{:S(2)}) collective-permute-start(bf16[368,128]{1,0:T(8,128)(2,1)S(1)} %get-tuple-element.54), channel_id=1, source_target_pairs={{0,4},{1,5},{2,6},{3,7},{4,0},{5,1},{6,2},{7,3},{8,12},{9,13},{10,... | collective-permute-start | bytes 282632 | tf_op jit(solution)/shard_map/ppermute | solution.py:398
  45.1 3.4 %collective-permute-start.8 = (bf16[368,128]{1,0:T(8,128)(2,1)S(1)}, bf16[368,128]{1,0:T(8,128)(2,1)S(1)}, u32[]{:S(2)}, u32[]{:S(2)}) collective-permute-start(bf16[368,128]{1,0:T(8,128)(2,1)S(1)} %get-tuple-element.55), channel_id=1, source_target_pairs={{0,8},{1,9},{2,10},{3,11},{4,12},{5,13},{6,14},{7,15},{8,0},{9,1},... | collective-permute-start | bytes 282632 | tf_op jit(solution)/shard_map/ppermute | solution.py:398
  48.5 0.0 collective-permute-start.9
  48.5 0.0 collective-permute-done.7.refs_0_
  48.5 7.0 %collective-permute-done.8.refs_1_ = bf16[368,128]{1,0:T(8,128)(2,1)S(1)} collective-permute-done((bf16[368,128]{1,0:T(8,128)(2,1)S(1)}, bf16[368,128]{1,0:T(8,128)(2,1)S(1)}, u32[]{:S(2)}, u32[]{:S(2)}) %collective-permute-start.8) | collective-permute-done | bytes 94240 | tf_op jit(solution)/shard_map/ppermute | solution.py:398
  55.5 0.0 collective-permute-done.9.refs_2_
  55.5 0.6 shard_map.143
  56.1 1.6 %collective-permute-start.10 = (bf16[240,128]{1,0:T(8,128)(2,1)S(1)}, bf16[240,128]{1,0:T(8,128)(2,1)S(1)}, u32[]{:S(2)}, u32[]{:S(2)}) collective-permute-start(bf16[240,128]{1,0:T(8,128)(2,1)S(1)} %get-tuple-element.57), channel_id=1, source_target_pairs={{0,4},{1,5},{2,6},{3,7},{4,0},{5,1},{6,2},{7,3},{8,12},{9,13},{10,... | collective-permute-start | bytes 184328 | tf_op jit(solution)/shard_map/ppermute | solution.py:398
  57.8 1.4 %collective-permute-start.11 = (bf16[240,128]{1,0:T(8,128)(2,1)S(1)}, bf16[240,128]{1,0:T(8,128)(2,1)S(1)}, u32[]{:S(2)}, u32[]{:S(2)}) collective-permute-start(bf16[240,128]{1,0:T(8,128)(2,1)S(1)} %get-tuple-element.57), channel_id=1, source_target_pairs={{0,8},{1,9},{2,10},{3,11},{4,12},{5,13},{6,14},{7,15},{8,0},{9,1},... | collective-permute-start | bytes 184328 | tf_op jit(solution)/shard_map/ppermute | solution.py:398
  59.2 1.4 %collective-permute-start.12 = (bf16[240,128]{1,0:T(8,128)(2,1)S(1)}, bf16[240,128]{1,0:T(8,128)(2,1)S(1)}, u32[]{:S(2)}, u32[]{:S(2)}) collective-permute-start(bf16[240,128]{1,0:T(8,128)(2,1)S(1)} %get-tuple-element.57), channel_id=1, source_target_pairs={{0,12},{1,13},{2,14},{3,15},{4,8},{5,9},{6,10},{7,11},{8,4},{9,5},... | collective-permute-start | bytes 184328 | tf_op jit(solution)/shard_map/ppermute | solution.py:398
  60.6 0.1 collective-permute-done.10
  60.8 2.9 %collective-permute-done.11 = bf16[240,128]{1,0:T(8,128)(2,1)S(1)} collective-permute-done((bf16[240,128]{1,0:T(8,128)(2,1)S(1)}, bf16[240,128]{1,0:T(8,128)(2,1)S(1)}, u32[]{:S(2)}, u32[]{:S(2)}) %collective-permute-start.11) | collective-permute-done | bytes 61472 | tf_op jit(solution)/shard_map/ppermute | solution.py:398
  63.7 1.5 %collective-permute-done.12 = bf16[240,128]{1,0:T(8,128)(2,1)S(1)} collective-permute-done((bf16[240,128]{1,0:T(8,128)(2,1)S(1)}, bf16[240,128]{1,0:T(8,128)(2,1)S(1)}, u32[]{:S(2)}, u32[]{:S(2)}) %collective-permute-start.12) | collective-permute-done | bytes 61472 | tf_op jit(solution)/shard_map/ppermute | solution.py:398
  65.3 0.6 collective-permute-start.13
  65.9 6.0 %collective-permute-done.13 = bf16[1088,128]{1,0:T(8,128)(2,1)S(1)} collective-permute-done((bf16[1088,128]{1,0:T(8,128)(2,1)S(1)}, bf16[1088,128]{1,0:T(8,128)(2,1)S(1)}, u32[]{:S(2)}, u32[]{:S(2)}) %collective-permute-start.13) | collective-permute-done | bytes 278560 | tf_op jit(solution)/shard_map/ppermute | solution.py:398
  72.0 0.1 collective-permute-start.14
  72.1 0.7 maximum_bitcast_fusion
  72.8 1.2 %collective-permute-done.14.other = bf16[2176,128]{1,0:T(8,128)(2,1)S(1)} collective-permute-done((bf16[2176,128]{1,0:T(8,128)(2,1)S(1)}, bf16[2176,128]{1,0:T(8,128)(2,1)S(1)}, u32[]{:S(2)}, u32[]{:S(2)}) %collective-permute-start.14) | collective-permute-done | bytes 557088 | tf_op jit(solution)/shard_map/ppermute | solution.py:398
  74.0 2.2 %shard_map.144 = (f32[3456,128]{1,0:T(8,128)}, f32[256,128]{1,0:T(8,128)}, f32[1,128]{1,0:T(1,128)}, f32[1,128]{1,0:T(1,128)}, bf16[4,2,4,64,128]{4,3,2,1,0:T(8,128)(2,1)}) custom-call(s32[7]{0:T(128)S(1)} %pad_add_fusion.sc, bf16[2176,128]{1,0:T(8,128)(2,1)S(1)} %fusion.6.mine, bf16[2176,128]{1,0:T(8,128)(2,1)S(1)} %collective-permute-done.14.other, ...), custom_call_target="tpu_custom_call" | custom-call | tf_op jit(solution)/shard_map/pallas_call | solution.py:618
  (14 shorter events, 0.3 us)
Async XLA Ops:
  2.2 1.6 %collective-permute-start = (bf16[12,64,128]{2,1,0:T(8,128)(2,1)S(1)}, bf16[12,64,128]{2,1,0:T(8,128)(2,1)S(1)}, u32[]{:S(2)}, u32[]{:S(2)}) collective-permute-start(bf16[12,64,128]{2,1,0:T(8,128)(2,1)S(1)} %shard_map.136), channel_id=1, source_target_pairs={{0,1},{1,0},{2,3},{3,2},{4,5},{5,4},{6,7},{7,6},{8,9},{9,8},{10,11... | collective-permute-start | bytes 589832 | tf_op jit(solution)/shard_map/ppermute | solution.py:398
  3.9 7.9 %collective-permute-start.1 = (bf16[6,64,128]{2,1,0:T(8,128)(2,1)S(1)}, bf16[6,64,128]{2,1,0:T(8,128)(2,1)S(1)}, u32[]{:S(2)}, u32[]{:S(2)}) collective-permute-start(bf16[6,64,128]{2,1,0:T(8,128)(2,1)S(1)} %fusion.4), channel_id=1, source_target_pairs={{0,2},{1,3},{2,0},{3,1},{4,6},{5,7},{6,4},{7,5},{8,10},{9,11},{10,... | collective-permute-start | bytes 294920 | tf_op jit(solution)/shard_map/ppermute | solution.py:398
  11.8 5.7 %collective-permute-start.2 = (bf16[6,64,128]{2,1,0:T(8,128)(2,1)S(1)}, bf16[6,64,128]{2,1,0:T(8,128)(2,1)S(1)}, u32[]{:S(2)}, u32[]{:S(2)}) collective-permute-start(bf16[6,64,128]{2,1,0:T(8,128)(2,1)S(1)} %fusion.5), channel_id=1, source_target_pairs={{0,4},{1,5},{2,6},{3,7},{4,8},{5,9},{6,10},{7,11},{8,12},{9,13},{1... | collective-permute-start | bytes 294920 | tf_op jit(solution)/shard_map/ppermute | solution.py:406
  17.5 8.1 %collective-permute-start.3 = (bf16[6,64,128]{2,1,0:T(8,128)(2,1)S(1)}, bf16[6,64,128]{2,1,0:T(8,128)(2,1)S(1)}, u32[]{:S(2)}, u32[]{:S(2)}) collective-permute-start(bf16[6,64,128]{2,1,0:T(8,128)(2,1)S(1)} %compare_select_fusion.4), channel_id=1, source_target_pairs={{0,8},{1,9},{2,10},{3,11},{4,12},{5,13},{6,14},{7,15},{16,24},{17,... | collective-permute-start | bytes 294920 | tf_op jit(solution)/shard_map/ppermute | solution.py:406
  22.9 4.3 %copy-start = (bf16[4,2,4,64,128]{4,3,2,1,0:T(8,128)(2,1)S(1)}, bf16[4,2,4,64,128]{4,3,2,1,0:T(8,128)(2,1)}, u32[]{:S(2)}) copy-start(bf16[4,2,4,64,128]{4,3,2,1,0:T(8,128)(2,1)} %frs.1) | copy-start | bytes 1572868
  22.9 4.3 %copy-start.1 = (bf16[4,2,2,64,128]{4,3,2,1,0:T(8,128)(2,1)S(1)}, bf16[4,2,2,64,128]{4,3,2,1,0:T(8,128)(2,1)}, u32[]{:S(2)}) copy-start(bf16[4,2,2,64,128]{4,3,2,1,0:T(8,128)(2,1)} %has.1) | copy-start | bytes 786436
  22.9 4.3 %copy-start.2 = (bf16[3,3,3,128,128]{4,3,2,1,0:T(8,128)(2,1)S(1)}, bf16[3,3,3,128,128]{4,3,2,1,0:T(8,128)(2,1)}, u32[]{:S(2)}) copy-start(bf16[3,3,3,128,128]{4,3,2,1,0:T(8,128)(2,1)} %param.13) | copy-start | bytes 2654212
  22.9 4.3 %copy-start.3 = (bf16[4,1,4,64,128]{4,3,2,1,0:T(8,128)(2,1)S(1)}, bf16[4,1,4,64,128]{4,3,2,1,0:T(8,128)(2,1)}, u32[]{:S(2)}) copy-start(bf16[4,1,4,64,128]{4,3,2,1,0:T(8,128)(2,1)} %cos.1) | copy-start | bytes 786436
  22.9 4.3 %copy-start.4 = (bf16[2,128,128]{2,1,0:T(8,128)(2,1)S(1)}, bf16[2,128,128]{2,1,0:T(8,128)(2,1)}, u32[]{:S(2)}) copy-start(bf16[2,128,128]{2,1,0:T(8,128)(2,1)} %sw.1) | copy-start | bytes 196612
  22.9 4.3 %copy-start.5 = (f32[128]{0:T(128)S(1)}, f32[128]{0:T(128)}, u32[]{:S(2)}) copy-start(f32[128]{0:T(128)} %param.14) | copy-start | bytes 1540
  22.9 4.3 %copy-start.6 = (f32[128]{0:T(128)S(1)}, f32[128]{0:T(128)}, u32[]{:S(2)}) copy-start(f32[128]{0:T(128)} %param.16) | copy-start | bytes 1540
  25.7 1.4 %collective-permute-start.4 = (bf16[6,64,128]{2,1,0:T(8,128)(2,1)S(1)}, bf16[6,64,128]{2,1,0:T(8,128)(2,1)S(1)}, u32[]{:S(2)}, u32[]{:S(2)}) collective-permute-start(bf16[6,64,128]{2,1,0:T(8,128)(2,1)S(1)} %fusion.1), channel_id=1, source_target_pairs={{0,1},{1,0},{2,3},{3,2},{4,5},{5,4},{6,7},{7,6},{8,9},{9,8},{10,11... | collective-permute-start | bytes 294920 | tf_op jit(solution)/shard_map/ppermute | solution.py:398
  30.4 2.1 %collective-permute-start.5 = (bf16[2432,128]{1,0:T(8,128)(2,1)S(1)}, bf16[2432,128]{1,0:T(8,128)(2,1)S(1)}, u32[]{:S(2)}, u32[]{:S(2)}) collective-permute-start(bf16[2432,128]{1,0:T(8,128)(2,1)S(1)} %get-tuple-element.46), channel_id=1, source_target_pairs={{0,1},{1,0},{2,3},{3,2},{4,5},{5,4},{6,7},{7,6},{8,9},{9,8},{10,11... | collective-permute-start | bytes 1867784 | tf_op jit(solution)/shard_map/ppermute | solution.py:398
  33.2 9.5 %collective-permute-start.6 = (bf16[1216,128]{1,0:T(8,128)(2,1)S(1)}, bf16[1216,128]{1,0:T(8,128)(2,1)S(1)}, u32[]{:S(2)}, u32[]{:S(2)}) collective-permute-start(bf16[1216,128]{1,0:T(8,128)(2,1)S(1)} %get-tuple-element.52.sent), channel_id=1, source_target_pairs={{0,2},{1,3},{2,0},{3,1},{4,6},{5,7},{6,4},{7,5},{8,10},{9,11},{10,... | collective-permute-start | bytes 933896 | tf_op jit(solution)/shard_map/ppermute | solution.py:398
  43.3 5.3 %collective-permute-start.7 = (bf16[368,128]{1,0:T(8,128)(2,1)S(1)}, bf16[368,128]{1,0:T(8,128)(2,1)S(1)}, u32[]{:S(2)}, u32[]{:S(2)}) collective-permute-start(bf16[368,128]{1,0:T(8,128)(2,1)S(1)} %get-tuple-element.54), channel_id=1, source_target_pairs={{0,4},{1,5},{2,6},{3,7},{4,0},{5,1},{6,2},{7,3},{8,12},{9,13},{10,... | collective-permute-start | bytes 282632 | tf_op jit(solution)/shard_map/ppermute | solution.py:398
  45.1 10.3 %collective-permute-start.8 = (bf16[368,128]{1,0:T(8,128)(2,1)S(1)}, bf16[368,128]{1,0:T(8,128)(2,1)S(1)}, u32[]{:S(2)}, u32[]{:S(2)}) collective-permute-start(bf16[368,128]{1,0:T(8,128)(2,1)S(1)} %get-tuple-element.55), channel_id=1, source_target_pairs={{0,8},{1,9},{2,10},{3,11},{4,12},{5,13},{6,14},{7,15},{8,0},{9,1},... | collective-permute-start | bytes 282632 | tf_op jit(solution)/shard_map/ppermute | solution.py:398
  48.5 7.0 %collective-permute-start.9 = (bf16[368,128]{1,0:T(8,128)(2,1)S(1)}, bf16[368,128]{1,0:T(8,128)(2,1)S(1)}, u32[]{:S(2)}, u32[]{:S(2)}) collective-permute-start(bf16[368,128]{1,0:T(8,128)(2,1)S(1)} %get-tuple-element.56), channel_id=1, source_target_pairs={{0,12},{1,13},{2,14},{3,15},{4,8},{5,9},{6,10},{7,11},{8,4},{9,5},... | collective-permute-start | bytes 282632 | tf_op jit(solution)/shard_map/ppermute | solution.py:398
  56.1 4.6 %collective-permute-start.10 = (bf16[240,128]{1,0:T(8,128)(2,1)S(1)}, bf16[240,128]{1,0:T(8,128)(2,1)S(1)}, u32[]{:S(2)}, u32[]{:S(2)}) collective-permute-start(bf16[240,128]{1,0:T(8,128)(2,1)S(1)} %get-tuple-element.57), channel_id=1, source_target_pairs={{0,4},{1,5},{2,6},{3,7},{4,0},{5,1},{6,2},{7,3},{8,12},{9,13},{10,... | collective-permute-start | bytes 184328 | tf_op jit(solution)/shard_map/ppermute | solution.py:398
  57.8 5.9 %collective-permute-start.11 = (bf16[240,128]{1,0:T(8,128)(2,1)S(1)}, bf16[240,128]{1,0:T(8,128)(2,1)S(1)}, u32[]{:S(2)}, u32[]{:S(2)}) collective-permute-start(bf16[240,128]{1,0:T(8,128)(2,1)S(1)} %get-tuple-element.57), channel_id=1, source_target_pairs={{0,8},{1,9},{2,10},{3,11},{4,12},{5,13},{6,14},{7,15},{8,0},{9,1},... | collective-permute-start | bytes 184328 | tf_op jit(solution)/shard_map/ppermute | solution.py:398
  59.2 6.0 %collective-permute-start.12 = (bf16[240,128]{1,0:T(8,128)(2,1)S(1)}, bf16[240,128]{1,0:T(8,128)(2,1)S(1)}, u32[]{:S(2)}, u32[]{:S(2)}) collective-permute-start(bf16[240,128]{1,0:T(8,128)(2,1)S(1)} %get-tuple-element.57), channel_id=1, source_target_pairs={{0,12},{1,13},{2,14},{3,15},{4,8},{5,9},{6,10},{7,11},{8,4},{9,5},... | collective-permute-start | bytes 184328 | tf_op jit(solution)/shard_map/ppermute | solution.py:398
  65.3 6.6 %collective-permute-start.13 = (bf16[1088,128]{1,0:T(8,128)(2,1)S(1)}, bf16[1088,128]{1,0:T(8,128)(2,1)S(1)}, u32[]{:S(2)}, u32[]{:S(2)}) collective-permute-start(bf16[1088,128]{1,0:T(8,128)(2,1)S(1)} %constant_dynamic-update-slice_fusion), channel_id=1, source_target_pairs={{0,2},{1,3},{2,0},{3,1},{4,6},{5,7},{6,4},{7,5},{8,10},{9,11},{10,... | collective-permute-start | bytes 835592 | tf_op jit(solution)/shard_map/ppermute | solution.py:398
  72.0 2.0 %collective-permute-start.14 = (bf16[2176,128]{1,0:T(8,128)(2,1)S(1)}, bf16[2176,128]{1,0:T(8,128)(2,1)S(1)}, u32[]{:S(2)}, u32[]{:S(2)}) collective-permute-start(bf16[2176,128]{1,0:T(8,128)(2,1)S(1)} %fusion.6.mine), channel_id=1, source_target_pairs={{0,1},{1,0},{2,3},{3,2},{4,5},{5,4},{6,7},{7,6},{8,9},{9,8},{10,11... | collective-permute-start | bytes 1671176 | tf_op jit(solution)/shard_map/ppermute | solution.py:398

commit v5 on v3

--- a/solution.py
+++ b/solution.py
@@ -84,8 +84,7 @@
     )
 
 
-def _head(xk, gout, w_ref, cb_ref, sw_ref, sb_ref, h):
-    pre = _conv(xk, w_ref, h) + jnp.concatenate([cb_ref[...], cb_ref[...]], axis=1)
+def _activate(pre, gout, sw_ref, sb_ref):
     s = 1.0 / (1.0 + jnp.exp(-pre))
     hidden = (pre * s).astype(BF)
     sw = jnp.concatenate([sw_ref[0], sw_ref[1]], axis=0)
@@ -93,6 +92,10 @@
     gh = lax.dot_general(gout, sw, (((1,), (1,)), ((), ())), preferred_element_type=F32)
     g = (gh * s * (1.0 + pre * (1.0 - s))).astype(BF)
     return lat, g, hidden
+
+
+def _conv_bias(xk, w_ref, cb_ref, h):
+    return _conv(xk, w_ref, h) + jnp.concatenate([cb_ref[...], cb_ref[...]], axis=1)
 
 
 def _weight_grads(xk, g, hidden, gout, h, add):
@@ -140,11 +143,11 @@
     )
 
 
-def _early_kernel(
-    sc, frh, hah, coh, wh, cb, sw, sb, lat_ref, g_ref, hid_ref, gout_ref, xk, fr, ha, co, w_ref, sems
+def _early_conv_kernel(
+    sc, frh, hah, coh, wh, cbh, swh, sbh, pre_ref, gout_ref, sw, sb, xk, fr, ha, co, w_ref, cb, sems
 ):
-    slots, _, h, w, c = fr.shape
-    pairs = ((frh, fr), (hah, ha), (coh, co), (wh, w_ref))
+    h = fr.shape[2]
+    pairs = ((frh, fr), (hah, ha), (coh, co), (wh, w_ref), (cbh, cb), (swh, sw), (sbh, sb))
     copies = [pltpu.make_async_copy(a, b, sems.at[i]) for i, (a, b) in enumerate(pairs)]
     for copy in copies:
         copy.start()
@@ -152,15 +155,19 @@
     copies[1].wait()
     _fill_early(sc, fr, ha, xk)
     copies[2].wait()
-    gout = _early_gout(sc, co)
-    gout_ref[...] = gout
-    copies[3].wait()
-    lat, g, hidden = _head(xk, gout, w_ref, cb, sw, sb, h)
-    for s in range(1, slots):
-        part = lat[(s - 1) * h * w : s * h * w]
-        lat_ref[s - 1] = (
-            jnp.where(s < sc[0], part, jnp.zeros_like(part)).astype(BF).reshape(h, w, c)
-        )
+    gout_ref[...] = _early_gout(sc, co)
+    for copy in copies[3:]:
+        copy.wait()
+    pre_ref[...] = _conv_bias(xk, w_ref, cb, h)
+
+
+def _early_act_kernel(sc, pre_ref, gout_ref, sw, sb, lat_ref, g_ref, hid_ref):
+    slots, h, w, c = lat_ref.shape
+    lat, g, hidden = _activate(pre_ref[...], gout_ref[...], sw, sb)
+    for s in range(slots):
+        part = lat[s * h * w : (s + 1) * h * w]
+        filled = s + 1 < sc[0]
+        lat_ref[s] = jnp.where(filled, part, jnp.zeros_like(part)).astype(BF).reshape(h, w, c)
     g_ref[...] = g
     hid_ref[...] = hidden
 
@@ -202,7 +209,7 @@
         _put(xk, (0, f), slice(h + 1, h + 2), b[1:])
     filled = sc[0] > 0
     gout = jnp.where(filled, co[0], jnp.zeros_like(co[0])).reshape(h * w, c)
-    lat, g, hidden = _head(xk, gout, w_ref, cb, sw, sb, h)
+    lat, g, hidden = _activate(_conv_bias(xk, w_ref, cb, h), gout, sw, sb)
     lat_ref[...] = jnp.where(filled, lat, jnp.zeros_like(lat)).astype(BF).reshape(h, w, c)
     g_ref[...] = g
     n9 = 9 * c
@@ -276,62 +283,26 @@
     return lax.shift_right_logical(chip, 1), lax.bitwise_and(chip, 1), core
 
 
-def _across_x_kernel(sc, keep, got, cache, send, kept):
+def _across_x_kernel(sc, keep, got, cache, send_far, send_near, kept):
     z, x, core = _place(sc)
-    del z
     half = keep.shape[0]
     blocks = 4
     rows = half // (2 * blocks)
 
-    def piece(p):
+    def piece(j, side):
+        p = 2 * lax.bitwise_xor(z, j) + side
         at = pl.ds(pl.multiple_of(p * rows, 16), rows)
         return keep[at] + got[at].astype(F32)
 
-    for b in range(blocks):
-        kept[b * rows : (b + 1) * rows] = piece(2 * b + x)
-        send[b * rows : (b + 1) * rows] = piece(2 * b + 1 - x).astype(BF)
+    for j in range(blocks):
+        kept[j * rows : (j + 1) * rows] = piece(j, x)
+        send, i = (send_near, j) if j < 2 else (send_far, j - 2)
+        send[i * rows : (i + 1) * rows] = piece(j, 1 - x).astype(BF)
     part = cache.shape[0] // 2
     at = pl.multiple_of(core * part, 16)
     mine, theirs = cache[pl.ds(at, part)], got[pl.ds(half + at, part)]
     first = jnp.where(core == 0, _first_live(mine, theirs), _first_live(theirs, mine))
-    send[blocks * rows :] = first
-
-
-def _across_z_kernel(sc, kept, got, sent, own, *sends):
-    z, x, core = _place(sc)
-    del core
-    rows = own.shape[0]
-    below = kept.shape[0]
-    part = (sent.shape[0] - below) // 2
-
-    def piece(b):
-        at = pl.ds(pl.multiple_of(b * rows, 16), rows)
-        return kept[at] + got[at].astype(F32)
-
-    at = pl.ds(pl.multiple_of(below + x * part, 16), part)
-    first = jnp.where(x == 0, _first_live(sent[at], got[at]), _first_live(got[at], sent[at]))
-    own[...] = piece(z)
-    for j, ref in enumerate(sends):
-        ref[:rows] = piece(lax.bitwise_xor(z, j + 1)).astype(BF)
-        ref[rows:] = first
-
-
-def _sum_kernel(sc, own, *refs):
-    gots, (mine, after) = refs[:-2], refs[-2:]
-    z, _, _ = _place(sc)
-    rows = own.shape[0]
-    total = own[...]
-    for ref in gots:
-        total = total + ref[:rows].astype(F32)
-    mine[...] = total.astype(BF)
-    best = jnp.full(after.shape, EMPTY_GRAD, F32)
-    for target in range(len(gots), 0, -1):
-        for j, ref in enumerate(gots):
-            here = jnp.logical_and(lax.bitwise_xor(z, j + 1) == target, target > z)
-            value = ref[rows:].astype(F32)
-            use = jnp.where(here, value, jnp.full_like(value, EMPTY_GRAD))
-            best = _first_live(use, best)
-    after[...] = best.astype(BF)
+    send_far[2 * rows :] = first
 
 
 def _tail_kernel(sc, fr, ha, out):
@@ -377,7 +348,7 @@
     return lax.ppermute(x, axis, [(i, i ^ k) for i in range(n)])
 
 
-def _latest_before(x, empty, axis, n, beside_x, beside_z):
+def _latest_before(x, empty, axis, n, beside_x, beside_near, beside_far):
     index = lax.axis_index(axis)
     core, pair = index & 1, (index >> 1) & 1
 
@@ -401,10 +372,12 @@
     while reach < n // 4 - 1:
         start = quad if before is None else newest(before, quad)
         came = shift(start, 4 * (reach + 1))
+        if reach == 0:
+            came = beside_near(start, came)
         before = came if before is None else newest(came, before)
         reach = 2 * reach + 1
         if reach == 3:
-            before = beside_z(start, before)
+            before = beside_far(start, before)
     before = jnp.where(pair == 0, before, newest(before, beside))
     across = _xor(before, 1, n, axis)
     before = jnp.concatenate(
@@ -466,33 +439,52 @@
             ],
             out_specs=pl.BlockSpec((2 * h + 4, w, c), lambda i, sc: (0, 0, 0)),
         ),
-        compiler_params=pltpu.CompilerParams(vmem_limit_bytes=60 << 20),
-    )(slab_counts, frames, row_halo)
+        compiler_params=pltpu.CompilerParams(vmem_limit_bytes=8 << 20),
+    )(
+        slab_counts,
+        *(pltpu.with_memory_space_constraint(v, pltpu.HBM) for v in (frames, row_halo)),
+    )
 
     held = {}
     wide = ((slots - 1) * m, 2 * c)
+    raw = (frames, row_halo, cotangent, wt, cb, stride_weight, sb)
     windows = (3, slots - 1, 4, h + 2, w, c)
 
-    def early_forward(start, follow):
+    def early_conv(start, follow):
+        held["conv"] = _call(
+            _early_conv_kernel,
+            [
+                jax.ShapeDtypeStruct(wide, F32),
+                jax.ShapeDtypeStruct((wide[0], c), BF),
+                jax.ShapeDtypeStruct(stride_weight.shape, BF),
+                jax.ShapeDtypeStruct(sb.shape, F32),
+                jax.ShapeDtypeStruct(windows, BF),
+            ],
+            [_SMEM] + [_HBM] * len(raw),
+            [pltpu.VMEM(v.shape, v.dtype) for v in raw[:5]]
+            + [pltpu.SemaphoreType.DMA((len(raw),))],
+            flops=(slots - 1) * conv_flops,
+            moved=4 << 20,
+        )(_after(sc, start), *(pltpu.with_memory_space_constraint(v, pltpu.HBM) for v in raw))
+        return _after(follow, held["conv"][0])
+
+    def early_act(start, follow):
+        pre, gout1, sw1, sb1, _ = held["conv"]
         held["early"] = _call(
-            _early_kernel,
+            _early_act_kernel,
             [
                 jax.ShapeDtypeStruct((slots - 1, h, w, c), BF),
                 jax.ShapeDtypeStruct(wide, BF),
                 jax.ShapeDtypeStruct(wide, BF),
-                jax.ShapeDtypeStruct((wide[0], c), BF),
-                jax.ShapeDtypeStruct(windows, BF),
             ],
-            [_SMEM] + [_HBM] * 4 + [_VMEM] * 3,
-            [pltpu.VMEM(v.shape, BF) for v in (frames, row_halo, cotangent, wt)]
-            + [pltpu.SemaphoreType.DMA((4,))],
-            flops=(slots - 1) * conv_flops,
-            moved=4 << 20,
-        )(_after(sc, start), frames, row_halo, cotangent, wt, cb, stride_weight, sb)
+            [_SMEM] + [_VMEM] * 4,
+            moved=2 << 20,
+        )(_after(sc, start), pre, gout1, sw1, sb1)
         return _after(follow, held["early"][1])
 
     def early_sums(start, follow):
-        _, g1, hid1, gout1, xk1 = held["early"]
+        _, gout1, _, _, xk1 = held["conv"]
+        _, g1, hid1 = held["early"]
         held["sums"] = _call(
             _early_sums_kernel,
             jax.ShapeDtypeStruct((rows, c), F32),
@@ -502,8 +494,8 @@
         )(_after(sc, start), g1, hid1, gout1, xk1)
         return _after(follow, held["sums"])
 
-    arrived = _latest_before(tail, EMPTY_FRAME, axis, n, early_forward, early_sums)
-    lat1, g1 = held["early"][:2]
+    arrived = _latest_before(tail, EMPTY_FRAME, axis, n, early_conv, early_act, early_sums)
+    lat1, g1, _ = held["early"]
 
     def first(*shape):
         return pl.BlockSpec((1, *shape), lambda i: (0,) * (len(shape) + 1))
@@ -528,47 +520,68 @@
     blocks = chips // 2
     piece = half // chips
     got = _xor(send, 1, n, axis)
-    send_x, keep_x = _call(
+    send_far, send_near, kept = _call(
         _across_x_kernel,
         [
-            jax.ShapeDtypeStruct((blocks * piece + carried // 2, c), BF),
+            jax.ShapeDtypeStruct((2 * piece + carried // 2, c), BF),
+            jax.ShapeDtypeStruct((2 * piece, c), BF),
             jax.ShapeDtypeStruct((blocks * piece, c), F32),
         ],
         [_SMEM] + [_VMEM] * 3,
         room=8,
     )(sc, keep, got, cache)
-    got_x = _xor(send_x, 2, n, axis)
+    got_far = _xor(send_far, 2, n, axis)
+    got_near = _xor(send_near, 2, n, axis)
     grad = _call(
         _back_kernel,
         jax.ShapeDtypeStruct((slots, 2, h, w, c), F32),
         [_SMEM] + [_VMEM] * 3,
         [pltpu.VMEM((3, slots, 4, h + 2, w, c), BF)],
-        flops=slots * conv_flops,
-        moved=6 << 20,
+        flops=1,
+        moved=1,
         room=24,
-    )(_after(sc, keep_x), g0, g1, wt)
-    own, *sends = _call(
-        _across_z_kernel,
-        [jax.ShapeDtypeStruct((piece, c), F32)]
-        + [jax.ShapeDtypeStruct((piece + carried // 4, c), BF)] * (blocks - 1),
-        [_SMEM] + [_VMEM] * 3,
-        room=8,
-    )(_after(sc, grad), keep_x, got_x, send_x)
-    gots = [_xor(v, 4 * (j + 1), n, axis) for j, v in enumerate(sends)]
-    mine, after = _call(
-        _sum_kernel,
-        [jax.ShapeDtypeStruct((piece, c), BF), jax.ShapeDtypeStruct((carried // 4, c), BF)],
-        [_SMEM] + [_VMEM] * blocks,
-        room=8,
-    )(sc, own, *gots)
+    )(_after(sc, kept), g0, g1, wt)
+    kept, send_far = _after(kept, grad), _after(send_far, grad)
+    core, pair, z = index & 1, (index >> 1) & 1, (index >> 2) & (blocks - 1)
+    below, quarter = 2 * piece, carried // 4
+
+    def by_pair(a, b):
+        return jnp.where(pair == 0, a, b)
+
+    chip_first, beside_first = send_far[below:], got_far[below:]
+    quad_first = by_pair(
+        _first_live(chip_first[:quarter], beside_first[:quarter]),
+        _first_live(beside_first[quarter:], chip_first[quarter:]),
+    )
+
+    def summed(j, came):
+        i = j % 2
+        return kept[j * piece : (j + 1) * piece] + came[i * piece : (i + 1) * piece].astype(F32)
+
+    outs = {
+        j: jnp.concatenate([summed(j, got_far).astype(BF), quad_first], axis=0) for j in (3, 2)
+    }
+    got_near = _after(got_near, outs[3], outs[2])
+    outs[1] = jnp.concatenate([summed(1, got_near).astype(BF), quad_first], axis=0)
+    gots = {j: _xor(outs[j], 4 * j, n, axis) for j in (3, 2, 1)}
+    mine = summed(0, got_near)
+    for j in (1, 2, 3):
+        mine = mine + gots[j][:piece].astype(F32)
+    mine = mine.astype(BF)
+    after = jnp.full((quarter, c), EMPTY_GRAD, BF)
+    for target in range(blocks - 1, 0, -1):
+        value = gots[3][piece:]
+        for j in (1, 2):
+            value = jnp.where((z ^ j) == target, gots[j][piece:], value)
+        after = jnp.where(target > z, _first_live(value, after), after)
     k = 2 * chips
     if k < n:
-        z = (index >> 2) & (blocks - 1)
-        lead = sends[0][piece:]
+        lead = jnp.full((quarter, c), EMPTY_GRAD, BF)
         for target in range(blocks - 1, -1, -1):
-            for j, v in enumerate(gots):
-                lead = jnp.where((z ^ (j + 1)) == target, _first_live(v[piece:], lead), lead)
-            lead = jnp.where(z == target, _first_live(sends[0][piece:], lead), lead)
+            value = quad_first
+            for j in (1, 2, 3):
+                value = jnp.where((z ^ j) == target, gots[j][piece:], value)
+            lead = _first_live(value, lead)
         beyond, reach = None, 0
         while reach < n // k - 1:
             start = lead if beyond is None else _first_live(lead, beyond)
@@ -580,16 +593,16 @@
     while k < n:
         mine = (mine.astype(F32) + _xor(mine, k, n, axis).astype(F32)).astype(BF)
         k *= 2
-    pieces = [mine] + [_xor(mine, 4 * (j + 1), n, axis) for j in range(blocks - 1)]
-    back_x = jnp.concatenate(pieces + [after], axis=0)
-    got_back = _xor(back_x, 2, n, axis)
-    pair, below = (index >> 1) & 1, blocks * piece
-    theirs = got_back[below:]
-    beyond = jnp.concatenate(
-        [jnp.where(pair == 0, after, theirs), jnp.where(pair == 0, theirs, after)], axis=0
-    )
-    beyond = jnp.where(pair == 0, _first_live(got_x[below:], beyond), beyond)
-    ours = jnp.concatenate([*pieces, got_back[:below], beyond], axis=0)
+    others = {j: _xor(mine, 4 * j, n, axis) for j in (3, 2, 1)}
+    x_own = _xor(jnp.concatenate([mine, after], axis=0), 2, n, axis)
+    x_near = _xor(others[1], 2, n, axis)
+    x_far = _xor(jnp.concatenate([others[2], others[3]], axis=0), 2, n, axis)
+    theirs = x_own[piece:]
+    beyond = jnp.concatenate([by_pair(after, theirs), by_pair(theirs, after)], axis=0)
+    beyond = by_pair(_first_live(beside_first, beyond), beyond)
+    ours = jnp.concatenate(
+        [mine, others[1], others[2], others[3], x_own[:piece], x_near, x_far, beyond], axis=0
+    )
     other = _xor(ours, 1, n, axis)
     cwg, swg, cbg, sbg, frames_grad = _call(
         _final_kernel,

time: 83.7 us -> 70.9 us (0.85)
  waiting for transfers between devices: 30.1 us -> 21.3 us
  local copies, waits for them, and re-layouts: 6.41 us -> 0.13 us
  starting transfers between devices: 23.5 us -> 27.3 us
    ppermute x13 -> x16, waiting for transfers between devices: 27.9 us -> 20.1 us  [_xor(): return lax.ppermute(x, axis, [(i, i ^ k) for i in range(n)])]
    unnamed x31 -> x20, local copies, waits for them, and re-layouts: 6.4 us -> 0.13 us
    ppermute x13 -> x16, starting transfers between devices: 14.7 us -> 18.5 us  [_xor(): return lax.ppermute(x, axis, [(i, i ^ k) for i in range(n)])]
    ppermute x2, waiting for transfers between devices: 2.19 us -> 1.21 us  [shift(): return lax.ppermute(v, axis, [(i, i + k) for i in range(n - k)])]
    select_n x1, other arithmetic: 0.97 us -> 0.03 us  [_latest_before(): chip = jnp.where(core == 0, newest(a, b), newest(b, a))]
    pallas_call x4 -> x3, Pallas kernels: 6.04 us -> 6.07 us  [the longest x1 4.41 us: early_conv(): _call(_early_conv_kernel, [jax.ShapeDtypeStruct(wide, F32), jax.ShapeDtyp...]
  transfers between devices with their start and end apart: 15 -> 18, of which waited for: 11 -> 11; matrix products, arithmetic and copies ran while one was open for 2% -> 2% of each run, Pallas kernels for 12% -> 16%
where the time goes in v5:
time: 70.9 us; the launch traced here: 70.7 us
  starting transfers between devices  27.3 us (39%)
  waiting for transfers between devices  21.3 us (30%)
  Pallas kernels  18.4 us (26%)
  other arithmetic  1.9 us (3%)
  between operations  1.63 us (2%)
    ppermute x16, waiting for transfers between devices, _xor(): return lax.ppermute(x, axis, [(i, i ^ k) for i in range(n)])  20.1 us
    ppermute x16, starting transfers between devices, _xor(): return lax.ppermute(x, axis, [(i, i ^ k) for i in range(n)])  18.5 us
    ppermute x2, starting transfers between devices, shift(): return lax.ppermute(v, axis, [(i, i + k) for i in range(n - k)])  8.81 us
    pallas_call x1, Pallas kernels, early_conv(): _call(_early_conv_kernel, [jax.ShapeDtypeStruct(wide, F32), jax.ShapeDtyp...  4.41 us
    pallas_call x1, Pallas kernels, body(): _call(_back_kernel, jax.ShapeDtypeStruct((slots, 2, h, w, c), F32), [_SME...  3.44 us
    pallas_call x1, Pallas kernels, body(): _call(_late_kernel, [jax.ShapeDtypeStruct((h, w, c), BF), jax.ShapeDtypeS...  3.09 us
    pallas_call x1, Pallas kernels, early_sums(): _call(_early_sums_kernel, jax.ShapeDtypeStruct((rows, c), F32), [_SMEM] +...  2.7 us
    pallas_call x1, Pallas kernels, body(): _call(_final_kernel, [jax.ShapeDtypeStruct((27 * c, c), F32), jax.ShapeDt...  2.18 us
  transfers between devices with their start and end apart: 18, of which 11 were waited for; matrix products, arithmetic and copies ran while one was open for 2% of the time, Pallas kernels for 16%

profile of v5, /device:TPU:0, one launch (start us, length us, event | category | flops | bytes accessed | tf_op | source)
XLA Modules:
  0.0 70.7 jit_solution(1637213230296309383)
XLA Ops:
  1.3 1.0 %shard_map.136 = bf16[12,64,128]{2,1,0:T(8,128)(2,1)S(1)} custom-call(s32[1]{0:T(128)S(6)} %copy.23.sc, bf16[4,2,4,64,128]{4,3,2,1,0:T(8,128)(2,1)} %frs.1, bf16[4,2,2,64,128]{4,3,2,1,0:T(8,128)(2,1)} %has.1), custom_call_target="tpu_custom_call" | custom-call | tf_op jit(solution)/shard_map/pallas_call | solution.py:430
  2.2 0.5 collective-permute-start
  2.8 0.7 %pad_add_fusion.sc = s32[7]{0:T(128)S(1)} fusion(s32[1]{0:T(128)} %bitcast.1, s32[1]{0:T(128)} %bitcast, s32[4]{0:T(128)} %param.11, s32[1]{0:T(128)S(6)} %copy.23.sc), kind=kLoop, calls=%fused_computation.54 | loop fusion | flops 21 | bytes 56 | tf_op jit(solution)/shard_map/concatenate | solution.py:412
  3.5 0.3 collective-permute-done
  3.9 2.9 %collective-permute-start.1 = (bf16[6,64,128]{2,1,0:T(8,128)(2,1)S(1)}, bf16[6,64,128]{2,1,0:T(8,128)(2,1)S(1)}, u32[]{:S(2)}, u32[]{:S(2)}) collective-permute-start(bf16[6,64,128]{2,1,0:T(8,128)(2,1)S(1)} %fusion.4), channel_id=1, source_target_pairs={{0,2},{1,3},{2,0},{3,1},{4,6},{5,7},{6,4},{7,5},{8,10},{9,11},{10,... | collective-permute-start | bytes 294920 | tf_op jit(solution)/shard_map/ppermute | solution.py:348
  6.8 4.4 %shard_map.137 = (f32[768,256]{1,0:T(8,128)S(1)}, bf16[768,128]{1,0:T(8,128)(2,1)S(1)}, bf16[2,128,128]{2,1,0:T(8,128)(2,1)S(1)}, f32[1,128]{1,0:T(1,128)S(1)}, bf16[3,3,4,6,64,128]{5,4,3,2,1,0:T(8,128)(2,1)S(1)}) custom-call(s32[7]{0:T(128)S(1)} %pad_add_fusion.sc, bf16[4,2,4,64,128]{4,3,2,1,0:T(8,128)(2,1)} %frs.1, bf16[4,2,2,64,128]{4,3,2,1,0:T(8,128)(2,1)} %has.1, ...), custom_call_target="tpu_custom_call" | custom-call | flops 1811939328 | bytes 4194304 | tf_op jit(solution)/shard_map/pallas_call | solution.py:454
  11.2 0.0 collective-permute-done.1
  11.2 3.5 %collective-permute-start.2 = (bf16[6,64,128]{2,1,0:T(8,128)(2,1)S(1)}, bf16[6,64,128]{2,1,0:T(8,128)(2,1)S(1)}, u32[]{:S(2)}, u32[]{:S(2)}) collective-permute-start(bf16[6,64,128]{2,1,0:T(8,128)(2,1)S(1)} %fusion.5), channel_id=1, source_target_pairs={{0,4},{1,5},{2,6},{3,7},{4,8},{5,9},{6,10},{7,11},{8,12},{9,13},{1... | collective-permute-start | bytes 294920 | tf_op jit(solution)/shard_map/ppermute | solution.py:356
  14.7 1.0 %shard_map.138 = (bf16[3,4,64,128]{3,2,1,0:T(8,128)(2,1)S(1)}, bf16[768,256]{1,0:T(8,128)(2,1)S(1)}, bf16[768,256]{1,0:T(8,128)(2,1)S(1)}) custom-call(s32[7]{0:T(128)S(1)} %pad_add_fusion.sc, f32[768,256]{1,0:T(8,128)S(1)} %get-tuple-element.38.pre_ref, bf16[768,128]{1,0:T(8,128)(2,1)S(1)} %get-tuple-element.41.gout_ref, ...), custom_call_target="tpu_custom_call" | custom-call | bytes 2097152 | tf_op jit(solution)/shard_map/pallas_call | solution.py:473
  15.7 1.2 %collective-permute-done.2 = bf16[6,64,128]{2,1,0:T(8,128)(2,1)S(1)} collective-permute-done((bf16[6,64,128]{2,1,0:T(8,128)(2,1)S(1)}, bf16[6,64,128]{2,1,0:T(8,128)(2,1)S(1)}, u32[]{:S(2)}, u32[]{:S(2)}) %collective-permute-start.2) | collective-permute-done | bytes 98336 | tf_op jit(solution)/shard_map/ppermute | solution.py:356
  16.9 5.3 %collective-permute-start.3 = (bf16[6,64,128]{2,1,0:T(8,128)(2,1)S(1)}, bf16[6,64,128]{2,1,0:T(8,128)(2,1)S(1)}, u32[]{:S(2)}, u32[]{:S(2)}) collective-permute-start(bf16[6,64,128]{2,1,0:T(8,128)(2,1)S(1)} %compare_select_fusion.4), channel_id=1, source_target_pairs={{0,8},{1,9},{2,10},{3,11},{4,12},{5,13},{6,14},{7,15},{16,24},{17,... | collective-permute-start | bytes 294920 | tf_op jit(solution)/shard_map/ppermute | solution.py:356
  22.3 0.0 copy-start
  22.3 0.0 copy-start.1
  22.3 0.0 copy-start.2
  22.3 0.0 copy-start.3
  22.3 0.0 copy-start.4
  22.3 0.0 copy-start.5
  22.3 0.0 copy-start.6
  22.4 2.7 %shard_map.139.early = f32[3840,128]{1,0:T(8,128)S(1)} custom-call(s32[7]{0:T(128)S(1)} %pad_add_fusion.sc, bf16[768,256]{1,0:T(8,128)(2,1)S(1)} %get-tuple-element.44.g_ref.g1, bf16[768,256]{1,0:T(8,128)(2,1)S(1)} %get-tuple-element.47.hid_ref, bf16[768,128]{1,0:T(8,128)(2,1)S(1)} %get-tuple-element.41.gout_ref, ...), custom_call_target="tpu_custom_call" | custom-call | flops 1811939328 | bytes 4194304 | tf_op jit(solution)/shard_map/pallas_call | solution.py:488
  25.1 0.0 collective-permute-done.3
  25.1 0.1 collective-permute-start.4
  25.2 1.3 %collective-permute-done.4 = bf16[6,64,128]{2,1,0:T(8,128)(2,1)S(1)} collective-permute-done((bf16[6,64,128]{2,1,0:T(8,128)(2,1)S(1)}, bf16[6,64,128]{2,1,0:T(8,128)(2,1)S(1)}, u32[]{:S(2)}, u32[]{:S(2)}) %collective-permute-start.4) | collective-permute-done | bytes 98336 | tf_op jit(solution)/shard_map/ppermute | solution.py:348
  26.6 0.0 copy-done
  26.6 0.0 copy-done.1
  26.6 0.0 copy-done.2
  26.6 0.0 copy-done.3
  26.6 0.0 copy-done.4
  26.6 0.0 copy-done.5
  26.6 0.0 copy-done.6
  26.6 3.1 %shard_map.140 = (bf16[4,64,128]{2,1,0:T(8,128)(2,1)S(1)}, bf16[256,256]{1,0:T(8,128)(2,1)S(1)}, bf16[2432,128]{1,0:T(8,128)(2,1)S(1)}, f32[1920,128]{1,0:T(8,128)S(1)}, bf16[512,128]{1,0:T(8,128)(2,1)S(1)}) custom-call(s32[7]{0:T(128)S(1)} %pad_add_fusion.sc, bf16[4,2,4,64,128]{4,3,2,1,0:T(8,128)(2,1)S(1)} %copy-done.1, ...), custom_call_target="tpu_custom_call" | custom-call | flops 1207959552 | bytes 6291456 | tf_op jit(solution)/shard_map/pallas_call | solution.py:504
  29.7 0.2 collective-permute-start.5
  29.9 1.9 %collective-permute-done.5.got = bf16[2432,128]{1,0:T(8,128)(2,1)S(1)} collective-permute-done((bf16[2432,128]{1,0:T(8,128)(2,1)S(1)}, bf16[2432,128]{1,0:T(8,128)(2,1)S(1)}, u32[]{:S(2)}, u32[]{:S(2)}) %collective-permute-start.5) | collective-permute-done | bytes 622624 | tf_op jit(solution)/shard_map/ppermute | solution.py:348
  31.9 0.7 shard_map.141
  32.5 0.6 collective-permute-start.7
  33.1 3.4 %shard_map.142.grad = f32[4,2,4,64,128]{4,3,2,1,0:T(8,128)S(1)} custom-call(s32[7]{0:T(128)S(1)} %pad_add_fusion.sc, bf16[256,256]{1,0:T(8,128)(2,1)S(1)} %get-tuple-element.57.g0, bf16[768,256]{1,0:T(8,128)(2,1)S(1)} %get-tuple-element.44.g_ref.g1, bf16[27,128,128]{2,1,0:T(8,128)(2,1)S(1)} %bitcast.16), custom_call_target="tpu_custom_call" | custom-call | flops 1 | bytes 1 | tf_op jit(solution)/shard_map/pallas_call | solution.py:535
  36.6 1.6 %collective-permute-start.6 = (bf16[480,128]{1,0:T(8,128)(2,1)S(1)}, bf16[480,128]{1,0:T(8,128)(2,1)S(1)}, u32[]{:S(2)}, u32[]{:S(2)}) collective-permute-start(bf16[480,128]{1,0:T(8,128)(2,1)S(1)} %get-tuple-element.59), channel_id=1, source_target_pairs={{0,2},{1,3},{2,0},{3,1},{4,6},{5,7},{6,4},{7,5},{8,10},{9,11},{10,... | collective-permute-start | bytes 368648 | tf_op jit(solution)/shard_map/ppermute | solution.py:348
  38.1 1.4 %collective-permute-done.7 = bf16[736,128]{1,0:T(8,128)(2,1)S(1)} collective-permute-done((bf16[736,128]{1,0:T(8,128)(2,1)S(1)}, bf16[736,128]{1,0:T(8,128)(2,1)S(1)}, u32[]{:S(2)}, u32[]{:S(2)}) %collective-permute-start.7) | collective-permute-done | bytes 188448 | tf_op jit(solution)/shard_map/ppermute | solution.py:348
  39.7 4.7 %collective-permute-start.10 = (bf16[368,128]{1,0:T(8,128)(2,1)S(1)}, bf16[368,128]{1,0:T(8,128)(2,1)S(1)}, u32[]{:S(2)}, u32[]{:S(2)}) collective-permute-start(bf16[368,128]{1,0:T(8,128)(2,1)S(1)} %get-tuple-element.83), channel_id=1, source_target_pairs={{0,12},{1,13},{2,14},{3,15},{4,8},{5,9},{6,10},{7,11},{8,4},{9,5},... | collective-permute-start | bytes 282632 | tf_op jit(solution)/shard_map/ppermute | solution.py:348
  44.4 0.0 collective-permute-start.9
  44.4 0.0 collective-permute-done.6
  44.4 0.7 collective-permute-start.8
  45.1 2.5 %collective-permute-done.10 = bf16[368,128]{1,0:T(8,128)(2,1)S(1)} collective-permute-done((bf16[368,128]{1,0:T(8,128)(2,1)S(1)}, bf16[368,128]{1,0:T(8,128)(2,1)S(1)}, u32[]{:S(2)}, u32[]{:S(2)}) %collective-permute-start.10) | collective-permute-done | bytes 94240 | tf_op jit(solution)/shard_map/ppermute | solution.py:348
  47.6 3.8 %collective-permute-done.9 = bf16[368,128]{1,0:T(8,128)(2,1)S(1)} collective-permute-done((bf16[368,128]{1,0:T(8,128)(2,1)S(1)}, bf16[368,128]{1,0:T(8,128)(2,1)S(1)}, u32[]{:S(2)}, u32[]{:S(2)}) %collective-permute-start.9) | collective-permute-done | bytes 94240 | tf_op jit(solution)/shard_map/ppermute | solution.py:348
  51.4 0.0 collective-permute-done.8
  51.5 0.8 %collective-permute-start.11 = (bf16[240,128]{1,0:T(8,128)(2,1)S(1)}, bf16[240,128]{1,0:T(8,128)(2,1)S(1)}, u32[]{:S(2)}, u32[]{:S(2)}) collective-permute-start(bf16[240,128]{1,0:T(8,128)(2,1)S(1)} %get-tuple-element.75), channel_id=1, source_target_pairs={{0,4},{1,5},{2,6},{3,7},{4,0},{5,1},{6,2},{7,3},{8,12},{9,13},{10,... | collective-permute-start | bytes 184328 | tf_op jit(solution)/shard_map/ppermute | solution.py:348
  52.3 2.4 %collective-permute-start.12 = (bf16[240,128]{1,0:T(8,128)(2,1)S(1)}, bf16[240,128]{1,0:T(8,128)(2,1)S(1)}, u32[]{:S(2)}, u32[]{:S(2)}) collective-permute-start(bf16[240,128]{1,0:T(8,128)(2,1)S(1)} %get-tuple-element.75), channel_id=1, source_target_pairs={{0,8},{1,9},{2,10},{3,11},{4,12},{5,13},{6,14},{7,15},{8,0},{9,1},... | collective-permute-start | bytes 184328 | tf_op jit(solution)/shard_map/ppermute | solution.py:348
  54.7 1.2 %collective-permute-start.13 = (bf16[240,128]{1,0:T(8,128)(2,1)S(1)}, bf16[240,128]{1,0:T(8,128)(2,1)S(1)}, u32[]{:S(2)}, u32[]{:S(2)}) collective-permute-start(bf16[240,128]{1,0:T(8,128)(2,1)S(1)} %get-tuple-element.75), channel_id=1, source_target_pairs={{0,12},{1,13},{2,14},{3,15},{4,8},{5,9},{6,10},{7,11},{8,4},{9,5},... | collective-permute-start | bytes 184328 | tf_op jit(solution)/shard_map/ppermute | solution.py:348
  56.0 0.6 collective-permute-start.14
  56.6 0.8 %collective-permute-done.12 = bf16[240,128]{1,0:T(8,128)(2,1)S(1)} collective-permute-done((bf16[240,128]{1,0:T(8,128)(2,1)S(1)}, bf16[240,128]{1,0:T(8,128)(2,1)S(1)}, u32[]{:S(2)}, u32[]{:S(2)}) %collective-permute-start.12) | collective-permute-done | bytes 61472 | tf_op jit(solution)/shard_map/ppermute | solution.py:348
  57.4 3.3 %collective-permute-done.13 = bf16[240,128]{1,0:T(8,128)(2,1)S(1)} collective-permute-done((bf16[240,128]{1,0:T(8,128)(2,1)S(1)}, bf16[240,128]{1,0:T(8,128)(2,1)S(1)}, u32[]{:S(2)}, u32[]{:S(2)}) %collective-permute-start.13) | collective-permute-done | bytes 61472 | tf_op jit(solution)/shard_map/ppermute | solution.py:348
  60.8 0.4 collective-permute-start.16
  61.2 0.0 collective-permute-done.11
  61.2 1.7 %collective-permute-start.15 = (bf16[240,128]{1,0:T(8,128)(2,1)S(1)}, bf16[240,128]{1,0:T(8,128)(2,1)S(1)}, u32[]{:S(2)}, u32[]{:S(2)}) collective-permute-start(bf16[240,128]{1,0:T(8,128)(2,1)S(1)} %collective-permute-done.11), channel_id=1, source_target_pairs={{0,2},{1,3},{2,0},{3,1},{4,6},{5,7},{6,4},{7,5},{8,10},{9,11},{10,... | collective-permute-start | bytes 184328 | tf_op jit(solution)/shard_map/ppermute | solution.py:348
  62.9 0.0 collective-permute-done.14
  63.0 3.4 %collective-permute-done.15 = bf16[240,128]{1,0:T(8,128)(2,1)S(1)} collective-permute-done((bf16[240,128]{1,0:T(8,128)(2,1)S(1)}, bf16[240,128]{1,0:T(8,128)(2,1)S(1)}, u32[]{:S(2)}, u32[]{:S(2)}) %collective-permute-start.15) | collective-permute-done | bytes 61472 | tf_op jit(solution)/shard_map/ppermute | solution.py:348
  66.4 0.0 collective-permute-done.16
  66.5 0.1 collective-permute-start.17
  66.6 0.7 %maximum_bitcast_fusion = bf16[4,1,4,64,128]{4,3,2,1,0:T(8,128)(2,1)} fusion(bf16[3,4,64,128]{3,2,1,0:T(8,128)(2,1)S(1)} %get-tuple-element.51, bf16[1,4,64,128]{3,2,1,0:T(8,128)(2,1)S(1)} %bitcast.17), kind=kLoop, calls=%fused_computation.10 | loop fusion | flops 131072 | bytes 524288
  67.3 1.2 %collective-permute-done.17.other = bf16[2176,128]{1,0:T(8,128)(2,1)S(1)} collective-permute-done((bf16[2176,128]{1,0:T(8,128)(2,1)S(1)}, bf16[2176,128]{1,0:T(8,128)(2,1)S(1)}, u32[]{:S(2)}, u32[]{:S(2)}) %collective-permute-start.17) | collective-permute-done | bytes 557088 | tf_op jit(solution)/shard_map/ppermute | solution.py:348
  68.5 2.2 %shard_map.143 = (f32[3456,128]{1,0:T(8,128)}, f32[256,128]{1,0:T(8,128)}, f32[1,128]{1,0:T(1,128)}, f32[1,128]{1,0:T(1,128)}, bf16[4,2,4,64,128]{4,3,2,1,0:T(8,128)(2,1)}) custom-call(s32[7]{0:T(128)S(1)} %pad_add_fusion.sc, bf16[2176,128]{1,0:T(8,128)(2,1)S(1)} %fusion.6.mine, bf16[2176,128]{1,0:T(8,128)(2,1)S(1)} %collective-permute-done.17.other, ...), custom_call_target="tpu_custom_call" | custom-call | tf_op jit(solution)/shard_map/pallas_call | solution.py:607
  (24 shorter events, 0.5 us)
Async XLA Ops:
  2.2 1.6 %collective-permute-start = (bf16[12,64,128]{2,1,0:T(8,128)(2,1)S(1)}, bf16[12,64,128]{2,1,0:T(8,128)(2,1)S(1)}, u32[]{:S(2)}, u32[]{:S(2)}) collective-permute-start(bf16[12,64,128]{2,1,0:T(8,128)(2,1)S(1)} %shard_map.136), channel_id=1, source_target_pairs={{0,1},{1,0},{2,3},{3,2},{4,5},{5,4},{6,7},{7,6},{8,9},{9,8},{10,11... | collective-permute-start | bytes 589832 | tf_op jit(solution)/shard_map/ppermute | solution.py:348
  3.9 7.3 %collective-permute-start.1 = (bf16[6,64,128]{2,1,0:T(8,128)(2,1)S(1)}, bf16[6,64,128]{2,1,0:T(8,128)(2,1)S(1)}, u32[]{:S(2)}, u32[]{:S(2)}) collective-permute-start(bf16[6,64,128]{2,1,0:T(8,128)(2,1)S(1)} %fusion.4), channel_id=1, source_target_pairs={{0,2},{1,3},{2,0},{3,1},{4,6},{5,7},{6,4},{7,5},{8,10},{9,11},{10,... | collective-permute-start | bytes 294920 | tf_op jit(solution)/shard_map/ppermute | solution.py:348
  11.2 5.7 %collective-permute-start.2 = (bf16[6,64,128]{2,1,0:T(8,128)(2,1)S(1)}, bf16[6,64,128]{2,1,0:T(8,128)(2,1)S(1)}, u32[]{:S(2)}, u32[]{:S(2)}) collective-permute-start(bf16[6,64,128]{2,1,0:T(8,128)(2,1)S(1)} %fusion.5), channel_id=1, source_target_pairs={{0,4},{1,5},{2,6},{3,7},{4,8},{5,9},{6,10},{7,11},{8,12},{9,13},{1... | collective-permute-start | bytes 294920 | tf_op jit(solution)/shard_map/ppermute | solution.py:356
  16.9 8.1 %collective-permute-start.3 = (bf16[6,64,128]{2,1,0:T(8,128)(2,1)S(1)}, bf16[6,64,128]{2,1,0:T(8,128)(2,1)S(1)}, u32[]{:S(2)}, u32[]{:S(2)}) collective-permute-start(bf16[6,64,128]{2,1,0:T(8,128)(2,1)S(1)} %compare_select_fusion.4), channel_id=1, source_target_pairs={{0,8},{1,9},{2,10},{3,11},{4,12},{5,13},{6,14},{7,15},{16,24},{17,... | collective-permute-start | bytes 294920 | tf_op jit(solution)/shard_map/ppermute | solution.py:356
  22.3 4.3 %copy-start = (bf16[3,3,3,128,128]{4,3,2,1,0:T(8,128)(2,1)S(1)}, bf16[3,3,3,128,128]{4,3,2,1,0:T(8,128)(2,1)}, u32[]{:S(2)}) copy-start(bf16[3,3,3,128,128]{4,3,2,1,0:T(8,128)(2,1)} %param.13) | copy-start | bytes 2654212
  22.3 4.3 %copy-start.1 = (bf16[4,2,4,64,128]{4,3,2,1,0:T(8,128)(2,1)S(1)}, bf16[4,2,4,64,128]{4,3,2,1,0:T(8,128)(2,1)}, u32[]{:S(2)}) copy-start(bf16[4,2,4,64,128]{4,3,2,1,0:T(8,128)(2,1)} %frs.1) | copy-start | bytes 1572868
  22.3 4.3 %copy-start.2 = (bf16[4,2,2,64,128]{4,3,2,1,0:T(8,128)(2,1)S(1)}, bf16[4,2,2,64,128]{4,3,2,1,0:T(8,128)(2,1)}, u32[]{:S(2)}) copy-start(bf16[4,2,2,64,128]{4,3,2,1,0:T(8,128)(2,1)} %has.1) | copy-start | bytes 786436
  22.3 4.3 %copy-start.3 = (bf16[4,1,4,64,128]{4,3,2,1,0:T(8,128)(2,1)S(1)}, bf16[4,1,4,64,128]{4,3,2,1,0:T(8,128)(2,1)}, u32[]{:S(2)}) copy-start(bf16[4,1,4,64,128]{4,3,2,1,0:T(8,128)(2,1)} %cos.1) | copy-start | bytes 786436
  22.3 4.3 %copy-start.4 = (bf16[2,128,128]{2,1,0:T(8,128)(2,1)S(1)}, bf16[2,128,128]{2,1,0:T(8,128)(2,1)}, u32[]{:S(2)}) copy-start(bf16[2,128,128]{2,1,0:T(8,128)(2,1)} %sw.1) | copy-start | bytes 196612
  22.3 4.3 %copy-start.5 = (f32[128]{0:T(128)S(1)}, f32[128]{0:T(128)}, u32[]{:S(2)}) copy-start(f32[128]{0:T(128)} %param.14) | copy-start | bytes 1540
  22.3 4.3 %copy-start.6 = (f32[128]{0:T(128)S(1)}, f32[128]{0:T(128)}, u32[]{:S(2)}) copy-start(f32[128]{0:T(128)} %param.16) | copy-start | bytes 1540
  25.1 1.4 %collective-permute-start.4 = (bf16[6,64,128]{2,1,0:T(8,128)(2,1)S(1)}, bf16[6,64,128]{2,1,0:T(8,128)(2,1)S(1)}, u32[]{:S(2)}, u32[]{:S(2)}) collective-permute-start(bf16[6,64,128]{2,1,0:T(8,128)(2,1)S(1)} %fusion.1), channel_id=1, source_target_pairs={{0,1},{1,0},{2,3},{3,2},{4,5},{5,4},{6,7},{7,6},{8,9},{9,8},{10,11... | collective-permute-start | bytes 294920 | tf_op jit(solution)/shard_map/ppermute | solution.py:348
  29.7 2.1 %collective-permute-start.5 = (bf16[2432,128]{1,0:T(8,128)(2,1)S(1)}, bf16[2432,128]{1,0:T(8,128)(2,1)S(1)}, u32[]{:S(2)}, u32[]{:S(2)}) collective-permute-start(bf16[2432,128]{1,0:T(8,128)(2,1)S(1)} %get-tuple-element.53), channel_id=1, source_target_pairs={{0,1},{1,0},{2,3},{3,2},{4,5},{5,4},{6,7},{7,6},{8,9},{9,8},{10,11... | collective-permute-start | bytes 1867784 | tf_op jit(solution)/shard_map/ppermute | solution.py:348
  32.5 7.0 %collective-permute-start.7 = (bf16[736,128]{1,0:T(8,128)(2,1)S(1)}, bf16[736,128]{1,0:T(8,128)(2,1)S(1)}, u32[]{:S(2)}, u32[]{:S(2)}) collective-permute-start(bf16[736,128]{1,0:T(8,128)(2,1)S(1)} %get-tuple-element.61), channel_id=1, source_target_pairs={{0,2},{1,3},{2,0},{3,1},{4,6},{5,7},{6,4},{7,5},{8,10},{9,11},{10,... | collective-permute-start | bytes 565256 | tf_op jit(solution)/shard_map/ppermute | solution.py:348
  36.6 7.8 %collective-permute-start.6 = (bf16[480,128]{1,0:T(8,128)(2,1)S(1)}, bf16[480,128]{1,0:T(8,128)(2,1)S(1)}, u32[]{:S(2)}, u32[]{:S(2)}) collective-permute-start(bf16[480,128]{1,0:T(8,128)(2,1)S(1)} %get-tuple-element.59), channel_id=1, source_target_pairs={{0,2},{1,3},{2,0},{3,1},{4,6},{5,7},{6,4},{7,5},{8,10},{9,11},{10,... | collective-permute-start | bytes 368648 | tf_op jit(solution)/shard_map/ppermute | solution.py:348
  39.7 7.9 %collective-permute-start.10 = (bf16[368,128]{1,0:T(8,128)(2,1)S(1)}, bf16[368,128]{1,0:T(8,128)(2,1)S(1)}, u32[]{:S(2)}, u32[]{:S(2)}) collective-permute-start(bf16[368,128]{1,0:T(8,128)(2,1)S(1)} %get-tuple-element.83), channel_id=1, source_target_pairs={{0,12},{1,13},{2,14},{3,15},{4,8},{5,9},{6,10},{7,11},{8,4},{9,5},... | collective-permute-start | bytes 282632 | tf_op jit(solution)/shard_map/ppermute | solution.py:348
  44.4 7.0 %collective-permute-start.9 = (bf16[368,128]{1,0:T(8,128)(2,1)S(1)}, bf16[368,128]{1,0:T(8,128)(2,1)S(1)}, u32[]{:S(2)}, u32[]{:S(2)}) collective-permute-start(bf16[368,128]{1,0:T(8,128)(2,1)S(1)} %get-tuple-element.82), channel_id=1, source_target_pairs={{0,8},{1,9},{2,10},{3,11},{4,12},{5,13},{6,14},{7,15},{8,0},{9,1},... | collective-permute-start | bytes 282632 | tf_op jit(solution)/shard_map/ppermute | solution.py:348
  44.4 7.0 %collective-permute-start.8 = (bf16[368,128]{1,0:T(8,128)(2,1)S(1)}, bf16[368,128]{1,0:T(8,128)(2,1)S(1)}, u32[]{:S(2)}, u32[]{:S(2)}) collective-permute-start(bf16[368,128]{1,0:T(8,128)(2,1)S(1)} %pad_maximum_fusion), channel_id=1, source_target_pairs={{0,4},{1,5},{2,6},{3,7},{4,0},{5,1},{6,2},{7,3},{8,12},{9,13},{10,... | collective-permute-start | bytes 282632 | tf_op jit(solution)/shard_map/ppermute | solution.py:348
  51.5 9.7 %collective-permute-start.11 = (bf16[240,128]{1,0:T(8,128)(2,1)S(1)}, bf16[240,128]{1,0:T(8,128)(2,1)S(1)}, u32[]{:S(2)}, u32[]{:S(2)}) collective-permute-start(bf16[240,128]{1,0:T(8,128)(2,1)S(1)} %get-tuple-element.75), channel_id=1, source_target_pairs={{0,4},{1,5},{2,6},{3,7},{4,0},{5,1},{6,2},{7,3},{8,12},{9,13},{10,... | collective-permute-start | bytes 184328 | tf_op jit(solution)/shard_map/ppermute | solution.py:348
  52.3 5.1 %collective-permute-start.12 = (bf16[240,128]{1,0:T(8,128)(2,1)S(1)}, bf16[240,128]{1,0:T(8,128)(2,1)S(1)}, u32[]{:S(2)}, u32[]{:S(2)}) collective-permute-start(bf16[240,128]{1,0:T(8,128)(2,1)S(1)} %get-tuple-element.75), channel_id=1, source_target_pairs={{0,8},{1,9},{2,10},{3,11},{4,12},{5,13},{6,14},{7,15},{8,0},{9,1},... | collective-permute-start | bytes 184328 | tf_op jit(solution)/shard_map/ppermute | solution.py:348
  54.7 6.0 %collective-permute-start.13 = (bf16[240,128]{1,0:T(8,128)(2,1)S(1)}, bf16[240,128]{1,0:T(8,128)(2,1)S(1)}, u32[]{:S(2)}, u32[]{:S(2)}) collective-permute-start(bf16[240,128]{1,0:T(8,128)(2,1)S(1)} %get-tuple-element.75), channel_id=1, source_target_pairs={{0,12},{1,13},{2,14},{3,15},{4,8},{5,9},{6,10},{7,11},{8,4},{9,5},... | collective-permute-start | bytes 184328 | tf_op jit(solution)/shard_map/ppermute | solution.py:348
  56.0 6.9 %collective-permute-start.14 = (bf16[368,128]{1,0:T(8,128)(2,1)S(1)}, bf16[368,128]{1,0:T(8,128)(2,1)S(1)}, u32[]{:S(2)}, u32[]{:S(2)}) collective-permute-start(bf16[368,128]{1,0:T(8,128)(2,1)S(1)} %pad_maximum_fusion.4), channel_id=1, source_target_pairs={{0,2},{1,3},{2,0},{3,1},{4,6},{5,7},{6,4},{7,5},{8,10},{9,11},{10,... | collective-permute-start | bytes 282632 | tf_op jit(solution)/shard_map/ppermute | solution.py:348
  60.8 5.6 %collective-permute-start.16 = (bf16[480,128]{1,0:T(8,128)(2,1)S(1)}, bf16[480,128]{1,0:T(8,128)(2,1)S(1)}, u32[]{:S(2)}, u32[]{:S(2)}) collective-permute-start(bf16[480,128]{1,0:T(8,128)(2,1)S(1)} %pad_maximum_fusion.3), channel_id=1, source_target_pairs={{0,2},{1,3},{2,0},{3,1},{4,6},{5,7},{6,4},{7,5},{8,10},{9,11},{10,... | collective-permute-start | bytes 368648 | tf_op jit(solution)/shard_map/ppermute | solution.py:348
  61.2 5.2 %collective-permute-start.15 = (bf16[240,128]{1,0:T(8,128)(2,1)S(1)}, bf16[240,128]{1,0:T(8,128)(2,1)S(1)}, u32[]{:S(2)}, u32[]{:S(2)}) collective-permute-start(bf16[240,128]{1,0:T(8,128)(2,1)S(1)} %collective-permute-done.11), channel_id=1, source_target_pairs={{0,2},{1,3},{2,0},{3,1},{4,6},{5,7},{6,4},{7,5},{8,10},{9,11},{10,... | collective-permute-start | bytes 184328 | tf_op jit(solution)/shard_map/ppermute | solution.py:348
  66.5 2.0 %collective-permute-start.17 = (bf16[2176,128]{1,0:T(8,128)(2,1)S(1)}, bf16[2176,128]{1,0:T(8,128)(2,1)S(1)}, u32[]{:S(2)}, u32[]{:S(2)}) collective-permute-start(bf16[2176,128]{1,0:T(8,128)(2,1)S(1)} %fusion.6.mine), channel_id=1, source_target_pairs={{0,1},{1,0},{2,3},{3,2},{4,5},{5,4},{6,7},{7,6},{8,9},{9,8},{10,11... | collective-permute-start | bytes 1671176 | tf_op jit(solution)/shard_map/ppermute | solution.py:348

commit v6 on v5

--- a/solution.py
+++ b/solution.py
@@ -144,7 +144,7 @@
 
 
 def _early_conv_kernel(
-    sc, frh, hah, coh, wh, cbh, swh, sbh, pre_ref, gout_ref, sw, sb, xk, fr, ha, co, w_ref, cb, sems
+    sc, frh, hah, coh, wh, cbh, swh, sbh, pre_ref, gout_ref, sw, sb, fr, ha, co, w_ref, cb, xk, sems
 ):
     h = fr.shape[2]
     pairs = ((frh, fr), (hah, ha), (coh, co), (wh, w_ref), (cbh, cb), (swh, sw), (sbh, sb))
@@ -172,9 +172,16 @@
     hid_ref[...] = hidden
 
 
-def _early_sums_kernel(sc, g_ref, hid_ref, gout_ref, xk, acc):
-    c = gout_ref.shape[-1]
-    h = xk.shape[3] - 2
+def _early_sums_kernel(sc, frh, hah, g_ref, hid_ref, gout_ref, acc, xk, fr, ha, sems):
+    copies = [
+        pltpu.make_async_copy(a, b, sems.at[i]) for i, (a, b) in enumerate(((frh, fr), (hah, ha)))
+    ]
+    for copy in copies:
+        copy.start()
+    for copy in copies:
+        copy.wait()
+    _fill_early(sc, fr, ha, xk)
+    _, _, h, _, c = fr.shape
     n9 = 9 * c
 
     def add(kind, value):
@@ -352,9 +359,6 @@
     index = lax.axis_index(axis)
     core, pair = index & 1, (index >> 1) & 1
 
-    def shift(v, k):
-        return lax.ppermute(v, axis, [(i, i + k) for i in range(n - k)])
-
     def newest(early, late):
         return jnp.where(late > empty / 2, early, late)
 
@@ -368,16 +372,18 @@
     beside = _xor(chip, 2, n, axis)
     quad = jnp.where(pair == 0, newest(chip, beside), newest(beside, chip))
     quad = beside_x(chip, quad)
-    before, reach = None, 0
-    while reach < n // 4 - 1:
-        start = quad if before is None else newest(before, quad)
-        came = shift(start, 4 * (reach + 1))
-        if reach == 0:
-            came = beside_near(start, came)
-        before = came if before is None else newest(came, before)
-        reach = 2 * reach + 1
-        if reach == 3:
-            before = beside_far(start, before)
+    block, before, k = quad, jnp.full_like(quad, empty), 4
+    while k < n:
+        late = (index & k) > 0
+        came = _xor(block, k, n, axis)
+        if k == 4:
+            came = beside_near(block, came)
+        before = jnp.where(late, newest(came, before), before)
+        if k == 8:
+            before = beside_far(block, before)
+        if 2 * k < n:
+            block = jnp.where(late, newest(came, block), newest(block, came))
+        k *= 2
     before = jnp.where(pair == 0, before, newest(before, beside))
     across = _xor(before, 1, n, axis)
     before = jnp.concatenate(
@@ -447,7 +453,10 @@
 
     held = {}
     wide = ((slots - 1) * m, 2 * c)
-    raw = (frames, row_halo, cotangent, wt, cb, stride_weight, sb)
+    raw = [
+        pltpu.with_memory_space_constraint(v, pltpu.HBM)
+        for v in (frames, row_halo, cotangent, wt, cb, stride_weight, sb)
+    ]
     windows = (3, slots - 1, 4, h + 2, w, c)
 
     def early_conv(start, follow):
@@ -458,18 +467,17 @@
                 jax.ShapeDtypeStruct((wide[0], c), BF),
                 jax.ShapeDtypeStruct(stride_weight.shape, BF),
                 jax.ShapeDtypeStruct(sb.shape, F32),
-                jax.ShapeDtypeStruct(windows, BF),
             ],
             [_SMEM] + [_HBM] * len(raw),
             [pltpu.VMEM(v.shape, v.dtype) for v in raw[:5]]
-            + [pltpu.SemaphoreType.DMA((len(raw),))],
+            + [pltpu.VMEM(windows, BF), pltpu.SemaphoreType.DMA((len(raw),))],
             flops=(slots - 1) * conv_flops,
             moved=4 << 20,
-        )(_after(sc, start), *(pltpu.with_memory_space_constraint(v, pltpu.HBM) for v in raw))
+        )(_after(sc, start), *raw)
         return _after(follow, held["conv"][0])
 
     def early_act(start, follow):
-        pre, gout1, sw1, sb1, _ = held["conv"]
+        pre, gout1, sw1, sb1 = held["conv"]
         held["early"] = _call(
             _early_act_kernel,
             [
@@ -479,19 +487,23 @@
             ],
             [_SMEM] + [_VMEM] * 4,
             moved=2 << 20,
+            room=6,
         )(_after(sc, start), pre, gout1, sw1, sb1)
         return _after(follow, held["early"][1])
 
     def early_sums(start, follow):
-        _, gout1, _, _, xk1 = held["conv"]
+        gout1 = held["conv"][1]
         _, g1, hid1 = held["early"]
         held["sums"] = _call(
             _early_sums_kernel,
             jax.ShapeDtypeStruct((rows, c), F32),
-            [_SMEM] + [_VMEM] * 4,
+            [_SMEM, _HBM, _HBM] + [_VMEM] * 3,
+            [pltpu.VMEM(windows, BF)]
+            + [pltpu.VMEM(v.shape, BF) for v in raw[:2]]
+            + [pltpu.SemaphoreType.DMA((2,))],
             flops=(slots - 1) * conv_flops,
             moved=4 << 20,
-        )(_after(sc, start), g1, hid1, gout1, xk1)
+        )(_after(sc, start), raw[0], raw[1], g1, hid1, gout1)
         return _after(follow, held["sums"])
 
     arrived = _latest_before(tail, EMPTY_FRAME, axis, n, early_conv, early_act, early_sums)
@@ -564,10 +576,11 @@
     got_near = _after(got_near, outs[3], outs[2])
     outs[1] = jnp.concatenate([summed(1, got_near).astype(BF), quad_first], axis=0)
     gots = {j: _xor(outs[j], 4 * j, n, axis) for j in (3, 2, 1)}
-    mine = summed(0, got_near)
-    for j in (1, 2, 3):
+    mine = summed(0, _after(got_near, outs[1]))
+    for j in (3, 2):
         mine = mine + gots[j][:piece].astype(F32)
-    mine = mine.astype(BF)
+    gots[1] = _after(gots[1], mine)
+    mine = (mine + gots[1][:piece].astype(F32)).astype(BF)
     after = jnp.full((quarter, c), EMPTY_GRAD, BF)
     for target in range(blocks - 1, 0, -1):
         value = gots[3][piece:]
@@ -593,9 +606,10 @@
     while k < n:
         mine = (mine.astype(F32) + _xor(mine, k, n, axis).astype(F32)).astype(BF)
         k *= 2
-    others = {j: _xor(mine, 4 * j, n, axis) for j in (3, 2, 1)}
+    others = {j: _xor(mine, 4 * j, n, axis) for j in (1, 3, 2)}
     x_own = _xor(jnp.concatenate([mine, after], axis=0), 2, n, axis)
     x_near = _xor(others[1], 2, n, axis)
+    others[2] = _after(others[2], x_near)
     x_far = _xor(jnp.concatenate([others[2], others[3]], axis=0), 2, n, axis)
     theirs = x_own[piece:]
     beyond = jnp.concatenate([by_pair(after, theirs), by_pair(theirs, after)], axis=0)

time: 70.9 us -> 69.5 us (0.980)
  starting transfers between devices: 27.3 us -> 20.9 us
  waiting for transfers between devices: 21.3 us -> 25.1 us
  Pallas kernels: 18.4 us -> 19.6 us
    ppermute x2 -> x0, starting transfers between devices: 8.81 us -> none  [shift(): return lax.ppermute(v, axis, [(i, i + k) for i in range(n - k)])]
    ppermute x16 -> x18, waiting for transfers between devices: 20.1 us -> 25.1 us  [_xor(): return lax.ppermute(x, axis, [(i, i ^ k) for i in range(n)])]
    ppermute x16 -> x18, starting transfers between devices: 18.5 us -> 20.9 us  [_xor(): return lax.ppermute(x, axis, [(i, i ^ k) for i in range(n)])]
    pallas_call x1, Pallas kernels: 2.7 us -> 3.94 us  [early_sums(): _call(_early_sums_kernel, jax.ShapeDtypeStruct((rows, c), F32), [_SMEM, _...]
    ppermute x2 -> x0, waiting for transfers between devices: 1.21 us -> none  [shift(): return lax.ppermute(v, axis, [(i, i + k) for i in range(n - k)])]
  transfers between devices with their start and end apart: 18 -> 18, of which waited for: 11 -> 12; matrix products, arithmetic and copies ran while one was open for 2% -> 2% of each run, Pallas kernels for 16% -> 18%
where the time goes in v6:
time: 69.5 us; the launch traced here: 69.3 us
  waiting for transfers between devices  25.1 us (36%)
  starting transfers between devices  20.9 us (30%)
  Pallas kernels  19.6 us (28%)
  other arithmetic  1.93 us (3%)
  between operations  1.58 us (2%)
    ppermute x18, waiting for transfers between devices, _xor(): return lax.ppermute(x, axis, [(i, i ^ k) for i in range(n)])  25.1 us
    ppermute x18, starting transfers between devices, _xor(): return lax.ppermute(x, axis, [(i, i ^ k) for i in range(n)])  20.9 us
    pallas_call x1, Pallas kernels, early_conv(): _call(_early_conv_kernel, [jax.ShapeDtypeStruct(wide, F32), jax.ShapeDtyp...  4.41 us
    pallas_call x1, Pallas kernels, early_sums(): _call(_early_sums_kernel, jax.ShapeDtypeStruct((rows, c), F32), [_SMEM, _...  3.94 us
    pallas_call x1, Pallas kernels, body(): _call(_back_kernel, jax.ShapeDtypeStruct((slots, 2, h, w, c), F32), [_SME...  3.39 us
    pallas_call x1, Pallas kernels, body(): _call(_late_kernel, [jax.ShapeDtypeStruct((h, w, c), BF), jax.ShapeDtypeS...  3.1 us
    pallas_call x1, Pallas kernels, body(): _call(_final_kernel, [jax.ShapeDtypeStruct((27 * c, c), F32), jax.ShapeDt...  2.18 us
  transfers between devices with their start and end apart: 18, of which 12 were waited for; matrix products, arithmetic and copies ran while one was open for 2% of the time, Pallas kernels for 18%

profile of v6, /device:TPU:0, one launch (start us, length us, event | category | flops | bytes accessed | tf_op | source)
XLA Modules:
  0.0 69.3 jit_solution(8244146304224138622)
XLA Ops:
  1.3 1.0 %shard_map.136 = bf16[12,64,128]{2,1,0:T(8,128)(2,1)S(1)} custom-call(s32[1]{0:T(128)S(6)} %copy.23.sc, bf16[4,2,4,64,128]{4,3,2,1,0:T(8,128)(2,1)} %frs.1, bf16[4,2,2,64,128]{4,3,2,1,0:T(8,128)(2,1)} %has.1), custom_call_target="tpu_custom_call" | custom-call | tf_op jit(solution)/shard_map/pallas_call | solution.py:436
  2.2 0.5 collective-permute-start
  2.8 0.7 %pad_add_fusion.sc = s32[7]{0:T(128)S(1)} fusion(s32[1]{0:T(128)} %bitcast.1, s32[1]{0:T(128)} %bitcast, s32[4]{0:T(128)} %param.11, s32[1]{0:T(128)S(6)} %copy.23.sc), kind=kLoop, calls=%fused_computation.58 | loop fusion | flops 21 | bytes 56 | tf_op jit(solution)/shard_map/concatenate | solution.py:418
  3.5 0.3 collective-permute-done
  3.9 2.9 %collective-permute-start.1 = (bf16[6,64,128]{2,1,0:T(8,128)(2,1)S(1)}, bf16[6,64,128]{2,1,0:T(8,128)(2,1)S(1)}, u32[]{:S(2)}, u32[]{:S(2)}) collective-permute-start(bf16[6,64,128]{2,1,0:T(8,128)(2,1)S(1)} %fusion.5), channel_id=1, source_target_pairs={{0,2},{1,3},{2,0},{3,1},{4,6},{5,7},{6,4},{7,5},{8,10},{9,11},{10,... | collective-permute-start | bytes 294920 | tf_op jit(solution)/shard_map/ppermute | solution.py:355
  6.8 4.4 %shard_map.137 = (f32[768,256]{1,0:T(8,128)S(1)}, bf16[768,128]{1,0:T(8,128)(2,1)S(1)}, bf16[2,128,128]{2,1,0:T(8,128)(2,1)S(1)}, f32[1,128]{1,0:T(1,128)S(1)}) custom-call(s32[7]{0:T(128)S(1)} %pad_add_fusion.sc, bf16[4,2,4,64,128]{4,3,2,1,0:T(8,128)(2,1)} %frs.1, bf16[4,2,2,64,128]{4,3,2,1,0:T(8,128)(2,1)} %has.1, bf16[4,1,4,64,128]{4,3,2,1,0:T(8,128)(2,1)} %cos.1, ...), custom_call_target="tpu_custom_call" | custom-call | flops 1811939328 | bytes 4194304 | tf_op jit(solution)/shard_map/pallas_call | solution.py:463
  11.2 0.0 collective-permute-done.1
  11.2 1.6 %collective-permute-start.2 = (bf16[6,64,128]{2,1,0:T(8,128)(2,1)S(1)}, bf16[6,64,128]{2,1,0:T(8,128)(2,1)S(1)}, u32[]{:S(2)}, u32[]{:S(2)}) collective-permute-start(bf16[6,64,128]{2,1,0:T(8,128)(2,1)S(1)} %fusion.6), channel_id=1, source_target_pairs={{0,4},{1,5},{2,6},{3,7},{4,0},{5,1},{6,2},{7,3},{8,12},{9,13},{10,... | collective-permute-start | bytes 294920 | tf_op jit(solution)/shard_map/ppermute | solution.py:355
  12.9 1.0 %shard_map.138 = (bf16[3,4,64,128]{3,2,1,0:T(8,128)(2,1)S(1)}, bf16[768,256]{1,0:T(8,128)(2,1)S(1)}, bf16[768,256]{1,0:T(8,128)(2,1)S(1)}) custom-call(s32[7]{0:T(128)S(1)} %pad_add_fusion.sc, f32[768,256]{1,0:T(8,128)S(1)} %get-tuple-element.40.pre_ref, bf16[768,128]{1,0:T(8,128)(2,1)S(1)} %get-tuple-element.43.gout_ref, ...), custom_call_target="tpu_custom_call" | custom-call | bytes 2097152 | tf_op jit(solution)/shard_map/pallas_call | solution.py:481
  13.8 2.1 %collective-permute-done.2 = bf16[6,64,128]{2,1,0:T(8,128)(2,1)S(1)} collective-permute-done((bf16[6,64,128]{2,1,0:T(8,128)(2,1)S(1)}, bf16[6,64,128]{2,1,0:T(8,128)(2,1)S(1)}, u32[]{:S(2)}, u32[]{:S(2)}) %collective-permute-start.2) | collective-permute-done | bytes 98336 | tf_op jit(solution)/shard_map/ppermute | solution.py:355
  15.9 2.7 %collective-permute-start.3 = (bf16[6,64,128]{2,1,0:T(8,128)(2,1)S(1)}, bf16[6,64,128]{2,1,0:T(8,128)(2,1)S(1)}, u32[]{:S(2)}, u32[]{:S(2)}) collective-permute-start(bf16[6,64,128]{2,1,0:T(8,128)(2,1)S(1)} %fusion.7), channel_id=1, source_target_pairs={{0,8},{1,9},{2,10},{3,11},{4,12},{5,13},{6,14},{7,15},{8,0},{9,1},... | collective-permute-start | bytes 294920 | tf_op jit(solution)/shard_map/ppermute | solution.py:355
  18.6 0.0 copy-start
  18.6 0.0 copy-start.1
  18.6 0.0 copy-start.2
  18.6 0.0 copy-start.3
  18.6 0.0 copy-start.4
  18.6 0.0 copy-start.5
  18.6 0.0 copy-start.6
  18.6 3.9 %shard_map.139.early = f32[3840,128]{1,0:T(8,128)S(1)} custom-call(s32[7]{0:T(128)S(1)} %pad_add_fusion.sc, bf16[4,2,4,64,128]{4,3,2,1,0:T(8,128)(2,1)} %frs.1, bf16[4,2,2,64,128]{4,3,2,1,0:T(8,128)(2,1)} %has.1, bf16[768,256]{1,0:T(8,128)(2,1)S(1)} %get-tuple-element.46.g_ref.g1, bf16[768,256]{1,0:T(8,128)(2,1)S(1)} %get-tuple-element.49.hid_ref, ...), custom_call_target="tpu_custom_call" | custom-call | flops 1811939328 | bytes 4194304 | tf_op jit(solution)/shard_map/pallas_call | solution.py:497
  22.6 0.0 collective-permute-done.3
  22.7 0.1 collective-permute-start.4
  22.7 1.3 %collective-permute-done.4 = bf16[6,64,128]{2,1,0:T(8,128)(2,1)S(1)} collective-permute-done((bf16[6,64,128]{2,1,0:T(8,128)(2,1)S(1)}, bf16[6,64,128]{2,1,0:T(8,128)(2,1)S(1)}, u32[]{:S(2)}, u32[]{:S(2)}) %collective-permute-start.4) | collective-permute-done | bytes 98336 | tf_op jit(solution)/shard_map/ppermute | solution.py:355
  24.1 0.0 copy-done
  24.1 0.0 copy-done.1
  24.1 0.0 copy-done.2
  24.1 0.0 copy-done.3
  24.2 0.0 copy-done.4
  24.2 0.0 copy-done.5
  24.2 0.0 copy-done.6
  24.2 3.1 %shard_map.140 = (bf16[4,64,128]{2,1,0:T(8,128)(2,1)S(1)}, bf16[256,256]{1,0:T(8,128)(2,1)S(1)}, bf16[2432,128]{1,0:T(8,128)(2,1)S(1)}, f32[1920,128]{1,0:T(8,128)S(1)}, bf16[512,128]{1,0:T(8,128)(2,1)S(1)}) custom-call(s32[7]{0:T(128)S(1)} %pad_add_fusion.sc, bf16[4,2,4,64,128]{4,3,2,1,0:T(8,128)(2,1)S(1)} %copy-done.1, ...), custom_call_target="tpu_custom_call" | custom-call | flops 1207959552 | bytes 6291456 | tf_op jit(solution)/shard_map/pallas_call | solution.py:516
  27.3 0.2 collective-permute-start.5
  27.5 1.9 %collective-permute-done.5.got = bf16[2432,128]{1,0:T(8,128)(2,1)S(1)} collective-permute-done((bf16[2432,128]{1,0:T(8,128)(2,1)S(1)}, bf16[2432,128]{1,0:T(8,128)(2,1)S(1)}, u32[]{:S(2)}, u32[]{:S(2)}) %collective-permute-start.5) | collective-permute-done | bytes 622624 | tf_op jit(solution)/shard_map/ppermute | solution.py:355
  29.4 0.7 shard_map.141
  30.1 0.6 collective-permute-start.7
  30.7 3.4 %shard_map.142.grad = f32[4,2,4,64,128]{4,3,2,1,0:T(8,128)S(1)} custom-call(s32[7]{0:T(128)S(1)} %pad_add_fusion.sc, bf16[256,256]{1,0:T(8,128)(2,1)S(1)} %get-tuple-element.58.g0, bf16[768,256]{1,0:T(8,128)(2,1)S(1)} %get-tuple-element.46.g_ref.g1, bf16[27,128,128]{2,1,0:T(8,128)(2,1)S(1)} %bitcast.16), custom_call_target="tpu_custom_call" | custom-call | flops 1 | bytes 1 | tf_op jit(solution)/shard_map/pallas_call | solution.py:547
  34.1 1.6 %collective-permute-start.6 = (bf16[480,128]{1,0:T(8,128)(2,1)S(1)}, bf16[480,128]{1,0:T(8,128)(2,1)S(1)}, u32[]{:S(2)}, u32[]{:S(2)}) collective-permute-start(bf16[480,128]{1,0:T(8,128)(2,1)S(1)} %get-tuple-element.60), channel_id=1, source_target_pairs={{0,2},{1,3},{2,0},{3,1},{4,6},{5,7},{6,4},{7,5},{8,10},{9,11},{10,... | collective-permute-start | bytes 368648 | tf_op jit(solution)/shard_map/ppermute | solution.py:355
  35.6 1.5 %collective-permute-done.7 = bf16[736,128]{1,0:T(8,128)(2,1)S(1)} collective-permute-done((bf16[736,128]{1,0:T(8,128)(2,1)S(1)}, bf16[736,128]{1,0:T(8,128)(2,1)S(1)}, u32[]{:S(2)}, u32[]{:S(2)}) %collective-permute-start.7) | collective-permute-done | bytes 188448 | tf_op jit(solution)/shard_map/ppermute | solution.py:355
  37.3 3.5 %collective-permute-start.8 = (bf16[368,128]{1,0:T(8,128)(2,1)S(1)}, bf16[368,128]{1,0:T(8,128)(2,1)S(1)}, u32[]{:S(2)}, u32[]{:S(2)}) collective-permute-start(bf16[368,128]{1,0:T(8,128)(2,1)S(1)} %get-tuple-element.86), channel_id=1, source_target_pairs={{0,12},{1,13},{2,14},{3,15},{4,8},{5,9},{6,10},{7,11},{8,4},{9,5},... | collective-permute-start | bytes 282632 | tf_op jit(solution)/shard_map/ppermute | solution.py:355
  40.8 0.0 collective-permute-start.9
  40.8 0.0 collective-permute-done.6
  40.8 1.0 %collective-permute-start.10 = (bf16[368,128]{1,0:T(8,128)(2,1)S(1)}, bf16[368,128]{1,0:T(8,128)(2,1)S(1)}, u32[]{:S(2)}, u32[]{:S(2)}) collective-permute-start(bf16[368,128]{1,0:T(8,128)(2,1)S(1)} %pad_maximum_fusion), channel_id=1, source_target_pairs={{0,4},{1,5},{2,6},{3,7},{4,0},{5,1},{6,2},{7,3},{8,12},{9,13},{10,... | collective-permute-start | bytes 282632 | tf_op jit(solution)/shard_map/ppermute | solution.py:355
  41.8 2.2 %collective-permute-done.8 = bf16[368,128]{1,0:T(8,128)(2,1)S(1)} collective-permute-done((bf16[368,128]{1,0:T(8,128)(2,1)S(1)}, bf16[368,128]{1,0:T(8,128)(2,1)S(1)}, u32[]{:S(2)}, u32[]{:S(2)}) %collective-permute-start.8) | collective-permute-done | bytes 94240 | tf_op jit(solution)/shard_map/ppermute | solution.py:355
  44.0 4.1 %collective-permute-done.9 = bf16[368,128]{1,0:T(8,128)(2,1)S(1)} collective-permute-done((bf16[368,128]{1,0:T(8,128)(2,1)S(1)}, bf16[368,128]{1,0:T(8,128)(2,1)S(1)}, u32[]{:S(2)}, u32[]{:S(2)}) %collective-permute-start.9) | collective-permute-done | bytes 94240 | tf_op jit(solution)/shard_map/ppermute | solution.py:355
  48.1 0.0 collective-permute-done.10
  48.2 2.4 %collective-permute-start.14 = (bf16[240,128]{1,0:T(8,128)(2,1)S(1)}, bf16[240,128]{1,0:T(8,128)(2,1)S(1)}, u32[]{:S(2)}, u32[]{:S(2)}) collective-permute-start(bf16[240,128]{1,0:T(8,128)(2,1)S(1)} %get-tuple-element.79), channel_id=1, source_target_pairs={{0,12},{1,13},{2,14},{3,15},{4,8},{5,9},{6,10},{7,11},{8,4},{9,5},... | collective-permute-start | bytes 184328 | tf_op jit(solution)/shard_map/ppermute | solution.py:355
  50.6 0.0 collective-permute-start.12
  50.6 2.0 %collective-permute-start.11 = (bf16[240,128]{1,0:T(8,128)(2,1)S(1)}, bf16[240,128]{1,0:T(8,128)(2,1)S(1)}, u32[]{:S(2)}, u32[]{:S(2)}) collective-permute-start(bf16[240,128]{1,0:T(8,128)(2,1)S(1)} %get-tuple-element.79), channel_id=1, source_target_pairs={{0,4},{1,5},{2,6},{3,7},{4,0},{5,1},{6,2},{7,3},{8,12},{9,13},{10,... | collective-permute-start | bytes 184328 | tf_op jit(solution)/shard_map/ppermute | solution.py:355
  52.7 0.6 collective-permute-start.15
  53.3 2.0 %collective-permute-done.11 = bf16[240,128]{1,0:T(8,128)(2,1)S(1)} collective-permute-done((bf16[240,128]{1,0:T(8,128)(2,1)S(1)}, bf16[240,128]{1,0:T(8,128)(2,1)S(1)}, u32[]{:S(2)}, u32[]{:S(2)}) %collective-permute-start.11) | collective-permute-done | bytes 61472 | tf_op jit(solution)/shard_map/ppermute | solution.py:355
  55.3 0.5 collective-permute-start.13
  55.9 1.5 %collective-permute-done.15 = bf16[368,128]{1,0:T(8,128)(2,1)S(1)} collective-permute-done((bf16[368,128]{1,0:T(8,128)(2,1)S(1)}, bf16[368,128]{1,0:T(8,128)(2,1)S(1)}, u32[]{:S(2)}, u32[]{:S(2)}) %collective-permute-start.15) | collective-permute-done | bytes 94240 | tf_op jit(solution)/shard_map/ppermute | solution.py:355
  57.3 0.0 collective-permute-done.12
  57.4 2.6 %collective-permute-done.13 = bf16[240,128]{1,0:T(8,128)(2,1)S(1)} collective-permute-done((bf16[240,128]{1,0:T(8,128)(2,1)S(1)}, bf16[240,128]{1,0:T(8,128)(2,1)S(1)}, u32[]{:S(2)}, u32[]{:S(2)}) %collective-permute-start.13) | collective-permute-done | bytes 61472 | tf_op jit(solution)/shard_map/ppermute | solution.py:355
  60.0 0.0 collective-permute-done.14
  60.0 0.6 collective-permute-start.16
  60.7 4.3 %collective-permute-done.16 = bf16[480,128]{1,0:T(8,128)(2,1)S(1)} collective-permute-done((bf16[480,128]{1,0:T(8,128)(2,1)S(1)}, bf16[480,128]{1,0:T(8,128)(2,1)S(1)}, u32[]{:S(2)}, u32[]{:S(2)}) %collective-permute-start.16) | collective-permute-done | bytes 122912 | tf_op jit(solution)/shard_map/ppermute | solution.py:355
  65.1 0.1 collective-permute-start.17
  65.1 0.7 %maximum_bitcast_fusion = bf16[4,1,4,64,128]{4,3,2,1,0:T(8,128)(2,1)} fusion(bf16[3,4,64,128]{3,2,1,0:T(8,128)(2,1)S(1)} %get-tuple-element.52, bf16[1,4,64,128]{3,2,1,0:T(8,128)(2,1)S(1)} %bitcast.17), kind=kLoop, calls=%fused_computation.11 | loop fusion | flops 131072 | bytes 524288
  65.9 1.2 %collective-permute-done.17.other = bf16[2176,128]{1,0:T(8,128)(2,1)S(1)} collective-permute-done((bf16[2176,128]{1,0:T(8,128)(2,1)S(1)}, bf16[2176,128]{1,0:T(8,128)(2,1)S(1)}, u32[]{:S(2)}, u32[]{:S(2)}) %collective-permute-start.17) | collective-permute-done | bytes 557088 | tf_op jit(solution)/shard_map/ppermute | solution.py:355
  67.1 2.2 %shard_map.143 = (f32[3456,128]{1,0:T(8,128)}, f32[256,128]{1,0:T(8,128)}, f32[1,128]{1,0:T(1,128)}, f32[1,128]{1,0:T(1,128)}, bf16[4,2,4,64,128]{4,3,2,1,0:T(8,128)(2,1)}) custom-call(s32[7]{0:T(128)S(1)} %pad_add_fusion.sc, bf16[2176,128]{1,0:T(8,128)(2,1)S(1)} %fusion.8.mine, bf16[2176,128]{1,0:T(8,128)(2,1)S(1)} %collective-permute-done.17.other, ...), custom_call_target="tpu_custom_call" | custom-call | tf_op jit(solution)/shard_map/pallas_call | solution.py:621
  (25 shorter events, 0.6 us)
Async XLA Ops:
  2.2 1.6 %collective-permute-start = (bf16[12,64,128]{2,1,0:T(8,128)(2,1)S(1)}, bf16[12,64,128]{2,1,0:T(8,128)(2,1)S(1)}, u32[]{:S(2)}, u32[]{:S(2)}) collective-permute-start(bf16[12,64,128]{2,1,0:T(8,128)(2,1)S(1)} %shard_map.136), channel_id=1, source_target_pairs={{0,1},{1,0},{2,3},{3,2},{4,5},{5,4},{6,7},{7,6},{8,9},{9,8},{10,11... | collective-permute-start | bytes 589832 | tf_op jit(solution)/shard_map/ppermute | solution.py:355
  3.9 7.3 %collective-permute-start.1 = (bf16[6,64,128]{2,1,0:T(8,128)(2,1)S(1)}, bf16[6,64,128]{2,1,0:T(8,128)(2,1)S(1)}, u32[]{:S(2)}, u32[]{:S(2)}) collective-permute-start(bf16[6,64,128]{2,1,0:T(8,128)(2,1)S(1)} %fusion.5), channel_id=1, source_target_pairs={{0,2},{1,3},{2,0},{3,1},{4,6},{5,7},{6,4},{7,5},{8,10},{9,11},{10,... | collective-permute-start | bytes 294920 | tf_op jit(solution)/shard_map/ppermute | solution.py:355
  11.2 4.7 %collective-permute-start.2 = (bf16[6,64,128]{2,1,0:T(8,128)(2,1)S(1)}, bf16[6,64,128]{2,1,0:T(8,128)(2,1)S(1)}, u32[]{:S(2)}, u32[]{:S(2)}) collective-permute-start(bf16[6,64,128]{2,1,0:T(8,128)(2,1)S(1)} %fusion.6), channel_id=1, source_target_pairs={{0,4},{1,5},{2,6},{3,7},{4,0},{5,1},{6,2},{7,3},{8,12},{9,13},{10,... | collective-permute-start | bytes 294920 | tf_op jit(solution)/shard_map/ppermute | solution.py:355
  15.9 6.7 %collective-permute-start.3 = (bf16[6,64,128]{2,1,0:T(8,128)(2,1)S(1)}, bf16[6,64,128]{2,1,0:T(8,128)(2,1)S(1)}, u32[]{:S(2)}, u32[]{:S(2)}) collective-permute-start(bf16[6,64,128]{2,1,0:T(8,128)(2,1)S(1)} %fusion.7), channel_id=1, source_target_pairs={{0,8},{1,9},{2,10},{3,11},{4,12},{5,13},{6,14},{7,15},{8,0},{9,1},... | collective-permute-start | bytes 294920 | tf_op jit(solution)/shard_map/ppermute | solution.py:355
  18.6 5.5 %copy-start = (bf16[3,3,3,128,128]{4,3,2,1,0:T(8,128)(2,1)S(1)}, bf16[3,3,3,128,128]{4,3,2,1,0:T(8,128)(2,1)}, u32[]{:S(2)}) copy-start(bf16[3,3,3,128,128]{4,3,2,1,0:T(8,128)(2,1)} %param.13) | copy-start | bytes 2654212
  18.6 5.5 %copy-start.1 = (bf16[4,2,4,64,128]{4,3,2,1,0:T(8,128)(2,1)S(1)}, bf16[4,2,4,64,128]{4,3,2,1,0:T(8,128)(2,1)}, u32[]{:S(2)}) copy-start(bf16[4,2,4,64,128]{4,3,2,1,0:T(8,128)(2,1)} %frs.1) | copy-start | bytes 1572868
  18.6 5.5 %copy-start.2 = (bf16[4,2,2,64,128]{4,3,2,1,0:T(8,128)(2,1)S(1)}, bf16[4,2,2,64,128]{4,3,2,1,0:T(8,128)(2,1)}, u32[]{:S(2)}) copy-start(bf16[4,2,2,64,128]{4,3,2,1,0:T(8,128)(2,1)} %has.1) | copy-start | bytes 786436
  18.6 5.5 %copy-start.3 = (bf16[4,1,4,64,128]{4,3,2,1,0:T(8,128)(2,1)S(1)}, bf16[4,1,4,64,128]{4,3,2,1,0:T(8,128)(2,1)}, u32[]{:S(2)}) copy-start(bf16[4,1,4,64,128]{4,3,2,1,0:T(8,128)(2,1)} %cos.1) | copy-start | bytes 786436
  18.6 5.5 %copy-start.4 = (bf16[2,128,128]{2,1,0:T(8,128)(2,1)S(1)}, bf16[2,128,128]{2,1,0:T(8,128)(2,1)}, u32[]{:S(2)}) copy-start(bf16[2,128,128]{2,1,0:T(8,128)(2,1)} %sw.1) | copy-start | bytes 196612
  18.6 5.5 %copy-start.5 = (f32[128]{0:T(128)S(1)}, f32[128]{0:T(128)}, u32[]{:S(2)}) copy-start(f32[128]{0:T(128)} %param.14) | copy-start | bytes 1540
  18.6 5.5 %copy-start.6 = (f32[128]{0:T(128)S(1)}, f32[128]{0:T(128)}, u32[]{:S(2)}) copy-start(f32[128]{0:T(128)} %param.16) | copy-start | bytes 1540
  22.7 1.4 %collective-permute-start.4 = (bf16[6,64,128]{2,1,0:T(8,128)(2,1)S(1)}, bf16[6,64,128]{2,1,0:T(8,128)(2,1)S(1)}, u32[]{:S(2)}, u32[]{:S(2)}) collective-permute-start(bf16[6,64,128]{2,1,0:T(8,128)(2,1)S(1)} %fusion.2), channel_id=1, source_target_pairs={{0,1},{1,0},{2,3},{3,2},{4,5},{5,4},{6,7},{7,6},{8,9},{9,8},{10,11... | collective-permute-start | bytes 294920 | tf_op jit(solution)/shard_map/ppermute | solution.py:355
  27.3 2.1 %collective-permute-start.5 = (bf16[2432,128]{1,0:T(8,128)(2,1)S(1)}, bf16[2432,128]{1,0:T(8,128)(2,1)S(1)}, u32[]{:S(2)}, u32[]{:S(2)}) collective-permute-start(bf16[2432,128]{1,0:T(8,128)(2,1)S(1)} %get-tuple-element.54), channel_id=1, source_target_pairs={{0,1},{1,0},{2,3},{3,2},{4,5},{5,4},{6,7},{7,6},{8,9},{9,8},{10,11... | collective-permute-start | bytes 1867784 | tf_op jit(solution)/shard_map/ppermute | solution.py:355
  30.1 7.1 %collective-permute-start.7 = (bf16[736,128]{1,0:T(8,128)(2,1)S(1)}, bf16[736,128]{1,0:T(8,128)(2,1)S(1)}, u32[]{:S(2)}, u32[]{:S(2)}) collective-permute-start(bf16[736,128]{1,0:T(8,128)(2,1)S(1)} %get-tuple-element.62), channel_id=1, source_target_pairs={{0,2},{1,3},{2,0},{3,1},{4,6},{5,7},{6,4},{7,5},{8,10},{9,11},{10,... | collective-permute-start | bytes 565256 | tf_op jit(solution)/shard_map/ppermute | solution.py:355
  34.1 6.7 %collective-permute-start.6 = (bf16[480,128]{1,0:T(8,128)(2,1)S(1)}, bf16[480,128]{1,0:T(8,128)(2,1)S(1)}, u32[]{:S(2)}, u32[]{:S(2)}) collective-permute-start(bf16[480,128]{1,0:T(8,128)(2,1)S(1)} %get-tuple-element.60), channel_id=1, source_target_pairs={{0,2},{1,3},{2,0},{3,1},{4,6},{5,7},{6,4},{7,5},{8,10},{9,11},{10,... | collective-permute-start | bytes 368648 | tf_op jit(solution)/shard_map/ppermute | solution.py:355
  37.3 6.8 %collective-permute-start.8 = (bf16[368,128]{1,0:T(8,128)(2,1)S(1)}, bf16[368,128]{1,0:T(8,128)(2,1)S(1)}, u32[]{:S(2)}, u32[]{:S(2)}) collective-permute-start(bf16[368,128]{1,0:T(8,128)(2,1)S(1)} %get-tuple-element.86), channel_id=1, source_target_pairs={{0,12},{1,13},{2,14},{3,15},{4,8},{5,9},{6,10},{7,11},{8,4},{9,5},... | collective-permute-start | bytes 282632 | tf_op jit(solution)/shard_map/ppermute | solution.py:355
  40.8 7.3 %collective-permute-start.9 = (bf16[368,128]{1,0:T(8,128)(2,1)S(1)}, bf16[368,128]{1,0:T(8,128)(2,1)S(1)}, u32[]{:S(2)}, u32[]{:S(2)}) collective-permute-start(bf16[368,128]{1,0:T(8,128)(2,1)S(1)} %get-tuple-element.87), channel_id=1, source_target_pairs={{0,8},{1,9},{2,10},{3,11},{4,12},{5,13},{6,14},{7,15},{8,0},{9,1},... | collective-permute-start | bytes 282632 | tf_op jit(solution)/shard_map/ppermute | solution.py:355
  40.8 7.3 %collective-permute-start.10 = (bf16[368,128]{1,0:T(8,128)(2,1)S(1)}, bf16[368,128]{1,0:T(8,128)(2,1)S(1)}, u32[]{:S(2)}, u32[]{:S(2)}) collective-permute-start(bf16[368,128]{1,0:T(8,128)(2,1)S(1)} %pad_maximum_fusion), channel_id=1, source_target_pairs={{0,4},{1,5},{2,6},{3,7},{4,0},{5,1},{6,2},{7,3},{8,12},{9,13},{10,... | collective-permute-start | bytes 282632 | tf_op jit(solution)/shard_map/ppermute | solution.py:355
  48.2 11.8 %collective-permute-start.14 = (bf16[240,128]{1,0:T(8,128)(2,1)S(1)}, bf16[240,128]{1,0:T(8,128)(2,1)S(1)}, u32[]{:S(2)}, u32[]{:S(2)}) collective-permute-start(bf16[240,128]{1,0:T(8,128)(2,1)S(1)} %get-tuple-element.79), channel_id=1, source_target_pairs={{0,12},{1,13},{2,14},{3,15},{4,8},{5,9},{6,10},{7,11},{8,4},{9,5},... | collective-permute-start | bytes 184328 | tf_op jit(solution)/shard_map/ppermute | solution.py:355
  50.6 6.7 %collective-permute-start.12 = (bf16[240,128]{1,0:T(8,128)(2,1)S(1)}, bf16[240,128]{1,0:T(8,128)(2,1)S(1)}, u32[]{:S(2)}, u32[]{:S(2)}) collective-permute-start(bf16[240,128]{1,0:T(8,128)(2,1)S(1)} %get-tuple-element.79), channel_id=1, source_target_pairs={{0,8},{1,9},{2,10},{3,11},{4,12},{5,13},{6,14},{7,15},{8,0},{9,1},... | collective-permute-start | bytes 184328 | tf_op jit(solution)/shard_map/ppermute | solution.py:355
  50.6 4.7 %collective-permute-start.11 = (bf16[240,128]{1,0:T(8,128)(2,1)S(1)}, bf16[240,128]{1,0:T(8,128)(2,1)S(1)}, u32[]{:S(2)}, u32[]{:S(2)}) collective-permute-start(bf16[240,128]{1,0:T(8,128)(2,1)S(1)} %get-tuple-element.79), channel_id=1, source_target_pairs={{0,4},{1,5},{2,6},{3,7},{4,0},{5,1},{6,2},{7,3},{8,12},{9,13},{10,... | collective-permute-start | bytes 184328 | tf_op jit(solution)/shard_map/ppermute | solution.py:355
  52.7 4.6 %collective-permute-start.15 = (bf16[368,128]{1,0:T(8,128)(2,1)S(1)}, bf16[368,128]{1,0:T(8,128)(2,1)S(1)}, u32[]{:S(2)}, u32[]{:S(2)}) collective-permute-start(bf16[368,128]{1,0:T(8,128)(2,1)S(1)} %pad_maximum_fusion.4), channel_id=1, source_target_pairs={{0,2},{1,3},{2,0},{3,1},{4,6},{5,7},{6,4},{7,5},{8,10},{9,11},{10,... | collective-permute-start | bytes 282632 | tf_op jit(solution)/shard_map/ppermute | solution.py:355
  55.3 4.7 %collective-permute-start.13 = (bf16[240,128]{1,0:T(8,128)(2,1)S(1)}, bf16[240,128]{1,0:T(8,128)(2,1)S(1)}, u32[]{:S(2)}, u32[]{:S(2)}) collective-permute-start(bf16[240,128]{1,0:T(8,128)(2,1)S(1)} %collective-permute-done.11), channel_id=1, source_target_pairs={{0,2},{1,3},{2,0},{3,1},{4,6},{5,7},{6,4},{7,5},{8,10},{9,11},{10,... | collective-permute-start | bytes 184328 | tf_op jit(solution)/shard_map/ppermute | solution.py:355
  60.0 4.9 %collective-permute-start.16 = (bf16[480,128]{1,0:T(8,128)(2,1)S(1)}, bf16[480,128]{1,0:T(8,128)(2,1)S(1)}, u32[]{:S(2)}, u32[]{:S(2)}) collective-permute-start(bf16[480,128]{1,0:T(8,128)(2,1)S(1)} %pad_maximum_fusion.3), channel_id=1, source_target_pairs={{0,2},{1,3},{2,0},{3,1},{4,6},{5,7},{6,4},{7,5},{8,10},{9,11},{10,... | collective-permute-start | bytes 368648 | tf_op jit(solution)/shard_map/ppermute | solution.py:355
  65.1 2.0 %collective-permute-start.17 = (bf16[2176,128]{1,0:T(8,128)(2,1)S(1)}, bf16[2176,128]{1,0:T(8,128)(2,1)S(1)}, u32[]{:S(2)}, u32[]{:S(2)}) collective-permute-start(bf16[2176,128]{1,0:T(8,128)(2,1)S(1)} %fusion.8.mine), channel_id=1, source_target_pairs={{0,1},{1,0},{2,3},{3,2},{4,5},{5,4},{6,7},{7,6},{8,9},{9,8},{10,11... | collective-permute-start | bytes 1671176 | tf_op jit(solution)/shard_map/ppermute | solution.py:355

commit v7 on v6

--- a/solution.py
+++ b/solution.py
@@ -67,10 +67,10 @@
     return jnp.dot(lhs, jnp.concatenate(rhs, axis=0), preferred_element_type=F32)
 
 
-def _conv_back(xk, w_ref, h, frames=range(4)):
+def _conv_back(xk, w_ref, h, frames=range(4), base=0):
     c = w_ref.shape[-1]
     zero = jnp.zeros((c, c), BF)
-    lhs = jnp.concatenate([_wide(xk, j, h) for j in frames], axis=1)
+    lhs = jnp.concatenate([_wide(xk, j - base, h) for j in frames], axis=1)
     rhs = []
     for f in range(2):
         row = []
@@ -198,7 +198,7 @@
 
 
 def _late_kernel(
-    sc, frs, has, tail, cos, w_ref, cb, sw, sb, early, lat_ref, g_ref, send, keep, cache_ref, xk, acc
+    sc, frs, has, tail, cos, w_ref, cb, sw, sb, early, lat_ref, g_ref, send, keep, xk, acc
 ):
     fr, ha, co = frs.at[0], has.at[0], cos.at[0]
     _, h, w, c = fr.shape
@@ -238,22 +238,26 @@
     def _():
         _weight_grads(xk, g, hidden, gout, h, add)
 
-        for t in range(2):
-            for kw in range(3):
-                xk[kw, 0, 2 + t, 0:1] = jnp.zeros((1, w, c), BF)
-                xk[kw, 0, 2 + t, h + 1 : h + 2] = jnp.zeros((1, w, c), BF)
-            v = g[:, t * c : (t + 1) * c].reshape(h, w, c)
-            _put(xk, (0, 2 + t), slice(1, 1 + h), jnp.where(on, v, jnp.zeros_like(v)))
-        back = _conv_back(xk, w_ref, h, (2, 3))
-        back = jnp.where(filled, back, jnp.full_like(back, EMPTY_GRAD)).astype(BF)
         half = keep.shape[0]
-        for t in range(2):
-            lanes = slice(t * c, (t + 1) * c)
-            cache_ref[t * h * w : (t + 1) * h * w] = back[:, lanes]
-            send[half + t * h * w : half + (t + 1) * h * w] = back[:, lanes]
         core = sc[sc.shape[0] - 1]
-        send[:half] = acc[pl.ds(pl.multiple_of((1 - core) * half, 16), half)].astype(BF)
+        send[...] = acc[pl.ds(pl.multiple_of((1 - core) * half, 16), half)].astype(BF)
         keep[...] = acc[pl.ds(pl.multiple_of(core * half, 16), half)]
+
+
+def _carried_kernel(sc, g_ref, w_ref, out, xk):
+    _, _, _, h, w, c = xk.shape
+    h = h - 2
+    on = sc[1] == 0
+    for t in range(2):
+        for kw in range(3):
+            xk[kw, 0, t, 0:1] = jnp.zeros((1, w, c), BF)
+            xk[kw, 0, t, h + 1 : h + 2] = jnp.zeros((1, w, c), BF)
+        v = g_ref[:, t * c : (t + 1) * c].reshape(h, w, c)
+        _put(xk, (0, t), slice(1, 1 + h), jnp.where(on, v, jnp.zeros_like(v)))
+    back = _conv_back(xk, w_ref, h, (2, 3), 2)
+    back = jnp.where(sc[0] > 0, back, jnp.full_like(back, EMPTY_GRAD)).astype(BF)
+    for t in range(2):
+        out[t * h * w : (t + 1) * h * w] = back[:, t * c : (t + 1) * c]
 
 
 def _back_kernel(sc, g0, g1, w_ref, out_ref, xk):
@@ -290,8 +294,8 @@
     return lax.shift_right_logical(chip, 1), lax.bitwise_and(chip, 1), core
 
 
-def _across_x_kernel(sc, keep, got, cache, send_far, send_near, kept):
-    z, x, core = _place(sc)
+def _across_x_kernel(sc, keep, got, send_far, send_near, kept):
+    z, x, _ = _place(sc)
     half = keep.shape[0]
     blocks = 4
     rows = half // (2 * blocks)
@@ -305,11 +309,6 @@
         kept[j * rows : (j + 1) * rows] = piece(j, x)
         send, i = (send_near, j) if j < 2 else (send_far, j - 2)
         send[i * rows : (i + 1) * rows] = piece(j, 1 - x).astype(BF)
-    part = cache.shape[0] // 2
-    at = pl.multiple_of(core * part, 16)
-    mine, theirs = cache[pl.ds(at, part)], got[pl.ds(half + at, part)]
-    first = jnp.where(core == 0, _first_live(mine, theirs), _first_live(theirs, mine))
-    send_far[2 * rows :] = first
 
 
 def _tail_kernel(sc, fr, ha, out):
@@ -345,7 +344,7 @@
             low = f == 0
             a, b = mine[half:].astype(F32), other[half:].astype(F32)
             beyond = jnp.where(core == 0, a, b) if low else jnp.where(core == 0, b, a)
-            beside = got[half + f * part : half + (f + 1) * part].astype(F32)
+            beside = got[f * part : (f + 1) * part].astype(F32)
             came = jnp.where(core == 0, _first_live(beside, beyond), beyond)
             came = jnp.where(came < EMPTY_GRAD / 2, came, jnp.zeros_like(came)).reshape(h, w, c)
             fg[s, f] = (grad[s, f] + jnp.where(here, came, jnp.zeros_like(came))).astype(BF)
@@ -513,14 +512,13 @@
         return pl.BlockSpec((1, *shape), lambda i: (0,) * (len(shape) + 1))
 
     half, carried = rows // 2, 2 * m
-    lat0, g0, send, keep, cache = _call(
+    lat0, g0, send, keep = _call(
         _late_kernel,
         [
             jax.ShapeDtypeStruct((h, w, c), BF),
             jax.ShapeDtypeStruct((m, 2 * c), BF),
-            jax.ShapeDtypeStruct((half + carried, c), BF),
+            jax.ShapeDtypeStruct((half, c), BF),
             jax.ShapeDtypeStruct((half, c), F32),
-            jax.ShapeDtypeStruct((carried, c), BF),
         ],
         [_SMEM, first(2, h, w, c), first(2, 2, w, c), _VMEM, first(1, h, w, c)] + [_VMEM] * 5,
         [pltpu.VMEM((3, 1, 4, h + 2, w, c), BF), pltpu.VMEM((rows, c), F32)],
@@ -532,18 +530,28 @@
     blocks = chips // 2
     piece = half // chips
     got = _xor(send, 1, n, axis)
+    first_grad = _call(
+        _carried_kernel,
+        jax.ShapeDtypeStruct((carried, c), BF),
+        [_SMEM, _VMEM, _VMEM],
+        [pltpu.VMEM((3, 1, 2, h + 2, w, c), BF)],
+        flops=conv_flops // 2,
+        moved=1 << 20,
+        room=8,
+    )(sc, g0, wt)
+    keep = _after(keep, first_grad)
     send_far, send_near, kept = _call(
         _across_x_kernel,
         [
-            jax.ShapeDtypeStruct((2 * piece + carried // 2, c), BF),
+            jax.ShapeDtypeStruct((2 * piece, c), BF),
             jax.ShapeDtypeStruct((2 * piece, c), BF),
             jax.ShapeDtypeStruct((blocks * piece, c), F32),
         ],
-        [_SMEM] + [_VMEM] * 3,
+        [_SMEM] + [_VMEM] * 2,
         room=8,
-    )(sc, keep, got, cache)
+    )(sc, keep, got)
     got_far = _xor(send_far, 2, n, axis)
-    got_near = _xor(send_near, 2, n, axis)
+    got_first = _xor(_after(first_grad, kept), 1, n, axis)
     grad = _call(
         _back_kernel,
         jax.ShapeDtypeStruct((slots, 2, h, w, c), F32),
@@ -553,69 +561,59 @@
         moved=1,
         room=24,
     )(_after(sc, kept), g0, g1, wt)
-    kept, send_far = _after(kept, grad), _after(send_far, grad)
-    core, pair, z = index & 1, (index >> 1) & 1, (index >> 2) & (blocks - 1)
+    kept, got_first = _after(kept, grad), _after(got_first, grad)
+    core, pair = index & 1, (index >> 1) & 1
     below, quarter = 2 * piece, carried // 4
 
-    def by_pair(a, b):
-        return jnp.where(pair == 0, a, b)
-
-    chip_first, beside_first = send_far[below:], got_far[below:]
-    quad_first = by_pair(
-        _first_live(chip_first[:quarter], beside_first[:quarter]),
-        _first_live(beside_first[quarter:], chip_first[quarter:]),
-    )
+    def by(bit, a, b):
+        return jnp.where(bit == 0, a, b)
+
+    def by_half(bit, v):
+        rows = v.shape[0] // 2
+        return by(bit, v[:rows], v[rows:])
+
+    def ordered(bit, ours, theirs):
+        return by(bit, _first_live(ours, theirs), _first_live(theirs, ours))
+
+    chip_first = ordered(core, by_half(core, first_grad), by_half(core, got_first))
+    got_near = _xor(jnp.concatenate([send_near, chip_first], axis=0), 2, n, axis)
 
     def summed(j, came):
         i = j % 2
         return kept[j * piece : (j + 1) * piece] + came[i * piece : (i + 1) * piece].astype(F32)
 
-    outs = {
-        j: jnp.concatenate([summed(j, got_far).astype(BF), quad_first], axis=0) for j in (3, 2)
-    }
+    outs = {j: summed(j, got_far).astype(BF) for j in (3, 2)}
     got_near = _after(got_near, outs[3], outs[2])
-    outs[1] = jnp.concatenate([summed(1, got_near).astype(BF), quad_first], axis=0)
+    beside_first = got_near[below:]
+    outs[1] = summed(1, got_near).astype(BF)
     gots = {j: _xor(outs[j], 4 * j, n, axis) for j in (3, 2, 1)}
-    mine = summed(0, _after(got_near, outs[1]))
+    near_again = _after(got_near, outs[1])
+    mine = summed(0, near_again)
+    lead = ordered(pair, by_half(pair, chip_first), by_half(pair, near_again[below:]))
+    beyond, k = jnp.full_like(lead, EMPTY_GRAD), 4
+    while k < n:
+        came = _xor(lead, k, n, axis)
+        beyond = by(index & k, _first_live(beyond, came), beyond)
+        if 2 * k < n:
+            lead = ordered(index & k, lead, came)
+        k *= 2
     for j in (3, 2):
-        mine = mine + gots[j][:piece].astype(F32)
+        mine = mine + gots[j].astype(F32)
     gots[1] = _after(gots[1], mine)
-    mine = (mine + gots[1][:piece].astype(F32)).astype(BF)
-    after = jnp.full((quarter, c), EMPTY_GRAD, BF)
-    for target in range(blocks - 1, 0, -1):
-        value = gots[3][piece:]
-        for j in (1, 2):
-            value = jnp.where((z ^ j) == target, gots[j][piece:], value)
-        after = jnp.where(target > z, _first_live(value, after), after)
+    mine = (mine + gots[1].astype(F32)).astype(BF)
     k = 2 * chips
-    if k < n:
-        lead = jnp.full((quarter, c), EMPTY_GRAD, BF)
-        for target in range(blocks - 1, -1, -1):
-            value = quad_first
-            for j in (1, 2, 3):
-                value = jnp.where((z ^ j) == target, gots[j][piece:], value)
-            lead = _first_live(value, lead)
-        beyond, reach = None, 0
-        while reach < n // k - 1:
-            start = lead if beyond is None else _first_live(lead, beyond)
-            step = k * (reach + 1)
-            came = lax.ppermute(start, axis, [(i + step, i) for i in range(n - step)])
-            beyond = came if beyond is None else _first_live(beyond, came)
-            reach = 2 * reach + 1
-        after = _first_live(after, beyond)
     while k < n:
         mine = (mine.astype(F32) + _xor(mine, k, n, axis).astype(F32)).astype(BF)
         k *= 2
-    others = {j: _xor(mine, 4 * j, n, axis) for j in (1, 3, 2)}
-    x_own = _xor(jnp.concatenate([mine, after], axis=0), 2, n, axis)
+    others = {j: _xor(mine, 4 * j, n, axis) for j in (3, 2, 1)}
+    x_own = _xor(mine, 2, n, axis)
     x_near = _xor(others[1], 2, n, axis)
-    others[2] = _after(others[2], x_near)
-    x_far = _xor(jnp.concatenate([others[2], others[3]], axis=0), 2, n, axis)
-    theirs = x_own[piece:]
-    beyond = jnp.concatenate([by_pair(after, theirs), by_pair(theirs, after)], axis=0)
-    beyond = by_pair(_first_live(beside_first, beyond), beyond)
+    x_far = _xor(jnp.concatenate([others[2], others[3], beyond], axis=0), 2, n, axis)
+    theirs = x_far[below:]
+    beyond = jnp.concatenate([by(pair, beyond, theirs), by(pair, theirs, beyond)], axis=0)
+    beyond = by(pair, _first_live(beside_first, beyond), beyond)
     ours = jnp.concatenate(
-        [mine, others[1], others[2], others[3], x_own[:piece], x_near, x_far, beyond], axis=0
+        [mine, others[1], others[2], others[3], x_own, x_near, x_far[:below], beyond], axis=0
     )
     other = _xor(ours, 1, n, axis)
     cwg, swg, cbg, sbg, frames_grad = _call(
@@ -630,7 +628,7 @@
         [_SMEM] + [_VMEM] * 4,
         [pltpu.VMEM((rows, c), F32)],
         room=12,
-    )(sc, ours, other, got, grad)
+    )(sc, ours, other, got_first, grad)
     latents = jnp.concatenate([lat0[None], lat1], axis=0)[:, None]
     return (
         latents,

time: 69.5 us -> 67.1 us (0.965)
  waiting for transfers between devices: 25.1 us -> 16.1 us
  starting transfers between devices: 20.9 us -> 26.8 us
  Pallas kernels: 19.6 us -> 20.3 us
    ppermute x18 -> x21, waiting for transfers between devices: 25.1 us -> 16.1 us  [_xor(): return lax.ppermute(x, axis, [(i, i ^ k) for i in range(n)])]
    ppermute x18 -> x21, starting transfers between devices: 20.9 us -> 26.8 us  [_xor(): return lax.ppermute(x, axis, [(i, i ^ k) for i in range(n)])]
    pallas_call x1 -> x2, Pallas kernels: 0.68 us -> 1.69 us  [the longest x1 1.05 us: body(): _call(_carried_kernel, jax.ShapeDtypeStruct((carried, c), BF), [_SMEM, _V...]
  transfers between devices with their start and end apart: 18 -> 21, of which waited for: 12 -> 10; matrix products, arithmetic and copies ran while one was open for 2% -> 3% of each run, Pallas kernels for 18% -> 21%
where the time goes in v7:
time: 67.1 us; the launch traced here: 66.9 us
  starting transfers between devices  26.8 us (40%)
  Pallas kernels  20.3 us (30%)
  waiting for transfers between devices  16.1 us (24%)
  other arithmetic  1.96 us (3%)
  between operations  1.59 us (2%)
    ppermute x21, starting transfers between devices, _xor(): return lax.ppermute(x, axis, [(i, i ^ k) for i in range(n)])  26.8 us
    ppermute x21, waiting for transfers between devices, _xor(): return lax.ppermute(x, axis, [(i, i ^ k) for i in range(n)])  16.1 us
    pallas_call x1, Pallas kernels, early_conv(): _call(_early_conv_kernel, [jax.ShapeDtypeStruct(wide, F32), jax.ShapeDtyp...  4.4 us
    pallas_call x1, Pallas kernels, early_sums(): _call(_early_sums_kernel, jax.ShapeDtypeStruct((rows, c), F32), [_SMEM, _...  3.94 us
    pallas_call x1, Pallas kernels, body(): _call(_back_kernel, jax.ShapeDtypeStruct((slots, 2, h, w, c), F32), [_SME...  3.39 us
    pallas_call x1, Pallas kernels, body(): _call(_late_kernel, [jax.ShapeDtypeStruct((h, w, c), BF), jax.ShapeDtypeS...  2.78 us
    pallas_call x1, Pallas kernels, body(): _call(_final_kernel, [jax.ShapeDtypeStruct((27 * c, c), F32), jax.ShapeDt...  2.18 us
  transfers between devices with their start and end apart: 21, of which 10 were waited for; matrix products, arithmetic and copies ran while one was open for 3% of the time, Pallas kernels for 21%

profile of v7, /device:TPU:0, one launch (start us, length us, event | category | flops | bytes accessed | tf_op | source)
XLA Modules:
  0.0 66.9 jit_solution(10586684103287981073)
XLA Ops:
  1.3 1.0 %shard_map.136 = bf16[12,64,128]{2,1,0:T(8,128)(2,1)S(1)} custom-call(s32[1]{0:T(128)S(6)} %copy.23.sc, bf16[4,2,4,64,128]{4,3,2,1,0:T(8,128)(2,1)} %frs.1, bf16[4,2,2,64,128]{4,3,2,1,0:T(8,128)(2,1)} %has.1), custom_call_target="tpu_custom_call" | custom-call | tf_op jit(solution)/shard_map/pallas_call | solution.py:435
  2.2 0.5 collective-permute-start
  2.8 0.7 %pad_add_fusion.sc = s32[7]{0:T(128)S(1)} fusion(s32[1]{0:T(128)} %bitcast.1, s32[1]{0:T(128)} %bitcast, s32[4]{0:T(128)} %param.11, s32[1]{0:T(128)S(6)} %copy.23.sc), kind=kLoop, calls=%fused_computation.61 | loop fusion | flops 21 | bytes 56 | tf_op jit(solution)/shard_map/concatenate | solution.py:417
  3.5 0.3 collective-permute-done
  3.9 2.9 %collective-permute-start.1 = (bf16[6,64,128]{2,1,0:T(8,128)(2,1)S(1)}, bf16[6,64,128]{2,1,0:T(8,128)(2,1)S(1)}, u32[]{:S(2)}, u32[]{:S(2)}) collective-permute-start(bf16[6,64,128]{2,1,0:T(8,128)(2,1)S(1)} %fusion.7), channel_id=1, source_target_pairs={{0,2},{1,3},{2,0},{3,1},{4,6},{5,7},{6,4},{7,5},{8,10},{9,11},{10,... | collective-permute-start | bytes 294920 | tf_op jit(solution)/shard_map/ppermute | solution.py:354
  6.8 4.4 %shard_map.137 = (f32[768,256]{1,0:T(8,128)S(1)}, bf16[768,128]{1,0:T(8,128)(2,1)S(1)}, bf16[2,128,128]{2,1,0:T(8,128)(2,1)S(1)}, f32[1,128]{1,0:T(1,128)S(1)}) custom-call(s32[7]{0:T(128)S(1)} %pad_add_fusion.sc, bf16[4,2,4,64,128]{4,3,2,1,0:T(8,128)(2,1)} %frs.1, bf16[4,2,2,64,128]{4,3,2,1,0:T(8,128)(2,1)} %has.1, bf16[4,1,4,64,128]{4,3,2,1,0:T(8,128)(2,1)} %cos.1, ...), custom_call_target="tpu_custom_call" | custom-call | flops 1811939328 | bytes 4194304 | tf_op jit(solution)/shard_map/pallas_call | solution.py:462
  11.2 0.0 collective-permute-done.1
  11.2 1.6 %collective-permute-start.2 = (bf16[6,64,128]{2,1,0:T(8,128)(2,1)S(1)}, bf16[6,64,128]{2,1,0:T(8,128)(2,1)S(1)}, u32[]{:S(2)}, u32[]{:S(2)}) collective-permute-start(bf16[6,64,128]{2,1,0:T(8,128)(2,1)S(1)} %fusion.8), channel_id=1, source_target_pairs={{0,4},{1,5},{2,6},{3,7},{4,0},{5,1},{6,2},{7,3},{8,12},{9,13},{10,... | collective-permute-start | bytes 294920 | tf_op jit(solution)/shard_map/ppermute | solution.py:354
  12.9 1.0 %shard_map.138 = (bf16[3,4,64,128]{3,2,1,0:T(8,128)(2,1)S(1)}, bf16[768,256]{1,0:T(8,128)(2,1)S(1)}, bf16[768,256]{1,0:T(8,128)(2,1)S(1)}) custom-call(s32[7]{0:T(128)S(1)} %pad_add_fusion.sc, f32[768,256]{1,0:T(8,128)S(1)} %get-tuple-element.40.pre_ref, bf16[768,128]{1,0:T(8,128)(2,1)S(1)} %get-tuple-element.43.gout_ref, ...), custom_call_target="tpu_custom_call" | custom-call | bytes 2097152 | tf_op jit(solution)/shard_map/pallas_call | solution.py:480
  13.9 2.1 %collective-permute-done.2 = bf16[6,64,128]{2,1,0:T(8,128)(2,1)S(1)} collective-permute-done((bf16[6,64,128]{2,1,0:T(8,128)(2,1)S(1)}, bf16[6,64,128]{2,1,0:T(8,128)(2,1)S(1)}, u32[]{:S(2)}, u32[]{:S(2)}) %collective-permute-start.2) | collective-permute-done | bytes 98336 | tf_op jit(solution)/shard_map/ppermute | solution.py:354
  16.0 2.7 %collective-permute-start.3 = (bf16[6,64,128]{2,1,0:T(8,128)(2,1)S(1)}, bf16[6,64,128]{2,1,0:T(8,128)(2,1)S(1)}, u32[]{:S(2)}, u32[]{:S(2)}) collective-permute-start(bf16[6,64,128]{2,1,0:T(8,128)(2,1)S(1)} %fusion.9), channel_id=1, source_target_pairs={{0,8},{1,9},{2,10},{3,11},{4,12},{5,13},{6,14},{7,15},{8,0},{9,1},... | collective-permute-start | bytes 294920 | tf_op jit(solution)/shard_map/ppermute | solution.py:354
  18.6 0.0 copy-start.4
  18.6 0.0 copy-start.5
  18.6 0.0 copy-start.6
  18.7 3.9 %shard_map.139.early = f32[3840,128]{1,0:T(8,128)S(1)} custom-call(s32[7]{0:T(128)S(1)} %pad_add_fusion.sc, bf16[4,2,4,64,128]{4,3,2,1,0:T(8,128)(2,1)} %frs.1, bf16[4,2,2,64,128]{4,3,2,1,0:T(8,128)(2,1)} %has.1, bf16[768,256]{1,0:T(8,128)(2,1)S(1)} %get-tuple-element.46.g_ref.g1, bf16[768,256]{1,0:T(8,128)(2,1)S(1)} %get-tuple-element.49.hid_ref, ...), custom_call_target="tpu_custom_call" | custom-call | flops 1811939328 | bytes 4194304 | tf_op jit(solution)/shard_map/pallas_call | solution.py:496
  22.6 0.0 collective-permute-done.3
  22.7 0.1 collective-permute-start.4
  22.7 1.3 %collective-permute-done.4 = bf16[6,64,128]{2,1,0:T(8,128)(2,1)S(1)} collective-permute-done((bf16[6,64,128]{2,1,0:T(8,128)(2,1)S(1)}, bf16[6,64,128]{2,1,0:T(8,128)(2,1)S(1)}, u32[]{:S(2)}, u32[]{:S(2)}) %collective-permute-start.4) | collective-permute-done | bytes 98336 | tf_op jit(solution)/shard_map/ppermute | solution.py:354
  24.1 0.1 compare_select_fusion.tail
  24.1 0.0 copy-done
  24.1 0.0 copy-done.1
  24.1 0.0 copy-done.2
  24.1 0.0 copy-done.3
  24.2 0.0 copy-done.4
  24.2 0.0 copy-done.5
  24.2 2.8 %shard_map.140 = (bf16[4,64,128]{2,1,0:T(8,128)(2,1)S(1)}, bf16[256,256]{1,0:T(8,128)(2,1)S(1)}, bf16[1920,128]{1,0:T(8,128)(2,1)S(1)}, f32[1920,128]{1,0:T(8,128)S(1)}) custom-call(s32[7]{0:T(128)S(1)} %pad_add_fusion.sc, bf16[4,2,4,64,128]{4,3,2,1,0:T(8,128)(2,1)S(1)} %copy-done.1, bf16[4,2,2,64,128]{4,3,2,1,0:T(8,128)(2,1)S(1)} %copy-done.2, ...), custom_call_target="tpu_custom_call" | custom-call | flops 1207959552 | bytes 6291456 | tf_op jit(solution)/shard_map/pallas_call | solution.py:515
  27.0 0.2 collective-permute-start.5
  27.2 1.1 %shard_map.141 = bf16[512,128]{1,0:T(8,128)(2,1)S(1)} custom-call(s32[7]{0:T(128)S(1)} %pad_add_fusion.sc, bf16[256,256]{1,0:T(8,128)(2,1)S(1)} %get-tuple-element.54.g_ref.g0, bf16[27,128,128]{2,1,0:T(8,128)(2,1)S(1)} %bitcast.16), custom_call_target="tpu_custom_call" | custom-call | flops 301989888 | bytes 1048576 | tf_op jit(solution)/shard_map/pallas_call | solution.py:533
  28.2 0.6 collective-permute-done.5.got
  28.9 0.6 shard_map.142
  29.5 0.2 collective-permute-start.6
  29.8 0.6 collective-permute-start.8
  30.3 3.4 %shard_map.143.grad = f32[4,2,4,64,128]{4,3,2,1,0:T(8,128)S(1)} custom-call(s32[7]{0:T(128)S(1)} %pad_add_fusion.sc, bf16[256,256]{1,0:T(8,128)(2,1)S(1)} %get-tuple-element.54.g_ref.g0, bf16[768,256]{1,0:T(8,128)(2,1)S(1)} %get-tuple-element.46.g_ref.g1, bf16[27,128,128]{2,1,0:T(8,128)(2,1)S(1)} %bitcast.17), custom_call_target="tpu_custom_call" | custom-call | flops 1 | bytes 1 | tf_op jit(solution)/shard_map/pallas_call | solution.py:555
  33.7 0.0 collective-permute-done.6.got
  33.7 0.1 fusion.11
  33.8 1.5 %collective-permute-start.7 = (bf16[736,128]{1,0:T(8,128)(2,1)S(1)}, bf16[736,128]{1,0:T(8,128)(2,1)S(1)}, u32[]{:S(2)}, u32[]{:S(2)}) collective-permute-start(bf16[736,128]{1,0:T(8,128)(2,1)S(1)} %pad_maximum_fusion), channel_id=1, source_target_pairs={{0,2},{1,3},{2,0},{3,1},{4,6},{5,7},{6,4},{7,5},{8,10},{9,11},{10,... | collective-permute-start | bytes 565256 | tf_op jit(solution)/shard_map/ppermute | solution.py:354
  35.3 0.0 collective-permute-done.8
  35.4 3.5 %collective-permute-start.9 = (bf16[240,128]{1,0:T(8,128)(2,1)S(1)}, bf16[240,128]{1,0:T(8,128)(2,1)S(1)}, u32[]{:S(2)}, u32[]{:S(2)}) collective-permute-start(bf16[240,128]{1,0:T(8,128)(2,1)S(1)} %get-tuple-element.80), channel_id=1, source_target_pairs={{0,12},{1,13},{2,14},{3,15},{4,8},{5,9},{6,10},{7,11},{8,4},{9,5},... | collective-permute-start | bytes 184328 | tf_op jit(solution)/shard_map/ppermute | solution.py:354
  38.9 0.0 collective-permute-start.10
  38.9 1.7 %collective-permute-done.7 = bf16[736,128]{1,0:T(8,128)(2,1)S(1)} collective-permute-done((bf16[736,128]{1,0:T(8,128)(2,1)S(1)}, bf16[736,128]{1,0:T(8,128)(2,1)S(1)}, u32[]{:S(2)}, u32[]{:S(2)}) %collective-permute-start.7) | collective-permute-done | bytes 188448 | tf_op jit(solution)/shard_map/ppermute | solution.py:354
  40.6 1.6 %collective-permute-start.11 = (bf16[240,128]{1,0:T(8,128)(2,1)S(1)}, bf16[240,128]{1,0:T(8,128)(2,1)S(1)}, u32[]{:S(2)}, u32[]{:S(2)}) collective-permute-start(bf16[240,128]{1,0:T(8,128)(2,1)S(1)} %add_convert_fusion.1), channel_id=1, source_target_pairs={{0,4},{1,5},{2,6},{3,7},{4,0},{5,1},{6,2},{7,3},{8,12},{9,13},{10,... | collective-permute-start | bytes 184328 | tf_op jit(solution)/shard_map/ppermute | solution.py:354
  42.3 0.5 collective-permute-start.17
  42.8 0.0 collective-permute-done.9
  42.8 1.6 %collective-permute-done.10 = bf16[240,128]{1,0:T(8,128)(2,1)S(1)} collective-permute-done((bf16[240,128]{1,0:T(8,128)(2,1)S(1)}, bf16[240,128]{1,0:T(8,128)(2,1)S(1)}, u32[]{:S(2)}, u32[]{:S(2)}) %collective-permute-start.10) | collective-permute-done | bytes 61472 | tf_op jit(solution)/shard_map/ppermute | solution.py:354
  44.4 1.9 %collective-permute-done.17 = bf16[128,128]{1,0:T(8,128)(2,1)S(1)} collective-permute-done((bf16[128,128]{1,0:T(8,128)(2,1)S(1)}, bf16[128,128]{1,0:T(8,128)(2,1)S(1)}, u32[]{:S(2)}, u32[]{:S(2)}) %collective-permute-start.17) | collective-permute-done | bytes 32800 | tf_op jit(solution)/shard_map/ppermute | solution.py:354
  46.3 2.5 %collective-permute-start.18 = (bf16[128,128]{1,0:T(8,128)(2,1)S(1)}, bf16[128,128]{1,0:T(8,128)(2,1)S(1)}, u32[]{:S(2)}, u32[]{:S(2)}) collective-permute-start(bf16[128,128]{1,0:T(8,128)(2,1)S(1)} %fusion.19), channel_id=1, source_target_pairs={{0,8},{1,9},{2,10},{3,11},{4,12},{5,13},{6,14},{7,15},{8,0},{9,1},... | collective-permute-start | bytes 98312 | tf_op jit(solution)/shard_map/ppermute | solution.py:354
  48.8 0.0 collective-permute-done.11
  48.8 1.8 %collective-permute-start.15 = (bf16[240,128]{1,0:T(8,128)(2,1)S(1)}, bf16[240,128]{1,0:T(8,128)(2,1)S(1)}, u32[]{:S(2)}, u32[]{:S(2)}) collective-permute-start(bf16[240,128]{1,0:T(8,128)(2,1)S(1)} %get-tuple-element.79), channel_id=1, source_target_pairs={{0,2},{1,3},{2,0},{3,1},{4,6},{5,7},{6,4},{7,5},{8,10},{9,11},{10,... | collective-permute-start | bytes 184328 | tf_op jit(solution)/shard_map/ppermute | solution.py:354
  50.6 0.3 collective-permute-start.14
  50.8 1.5 %collective-permute-start.13 = (bf16[240,128]{1,0:T(8,128)(2,1)S(1)}, bf16[240,128]{1,0:T(8,128)(2,1)S(1)}, u32[]{:S(2)}, u32[]{:S(2)}) collective-permute-start(bf16[240,128]{1,0:T(8,128)(2,1)S(1)} %get-tuple-element.79), channel_id=1, source_target_pairs={{0,8},{1,9},{2,10},{3,11},{4,12},{5,13},{6,14},{7,15},{8,0},{9,1},... | collective-permute-start | bytes 184328 | tf_op jit(solution)/shard_map/ppermute | solution.py:354
  52.4 2.6 %collective-permute-start.12 = (bf16[240,128]{1,0:T(8,128)(2,1)S(1)}, bf16[240,128]{1,0:T(8,128)(2,1)S(1)}, u32[]{:S(2)}, u32[]{:S(2)}) collective-permute-start(bf16[240,128]{1,0:T(8,128)(2,1)S(1)} %get-tuple-element.79), channel_id=1, source_target_pairs={{0,4},{1,5},{2,6},{3,7},{4,0},{5,1},{6,2},{7,3},{8,12},{9,13},{10,... | collective-permute-start | bytes 184328 | tf_op jit(solution)/shard_map/ppermute | solution.py:354
  55.0 0.0 collective-permute-done.18
  55.0 1.6 %collective-permute-done.14 = bf16[240,128]{1,0:T(8,128)(2,1)S(1)} collective-permute-done((bf16[240,128]{1,0:T(8,128)(2,1)S(1)}, bf16[240,128]{1,0:T(8,128)(2,1)S(1)}, u32[]{:S(2)}, u32[]{:S(2)}) %collective-permute-start.14) | collective-permute-done | bytes 61472 | tf_op jit(solution)/shard_map/ppermute | solution.py:354
  56.6 0.0 collective-permute-done.13
  56.6 1.3 %collective-permute-start.19 = (bf16[608,128]{1,0:T(8,128)(2,1)S(1)}, bf16[608,128]{1,0:T(8,128)(2,1)S(1)}, u32[]{:S(2)}, u32[]{:S(2)}) collective-permute-start(bf16[608,128]{1,0:T(8,128)(2,1)S(1)} %pad_maximum_fusion.1), channel_id=1, source_target_pairs={{0,2},{1,3},{2,0},{3,1},{4,6},{5,7},{6,4},{7,5},{8,10},{9,11},{10,... | collective-permute-start | bytes 466952 | tf_op jit(solution)/shard_map/ppermute | solution.py:354
  57.9 0.0 collective-permute-done.12
  57.9 0.8 %collective-permute-start.16 = (bf16[240,128]{1,0:T(8,128)(2,1)S(1)}, bf16[240,128]{1,0:T(8,128)(2,1)S(1)}, u32[]{:S(2)}, u32[]{:S(2)}) collective-permute-start(bf16[240,128]{1,0:T(8,128)(2,1)S(1)} %collective-permute-done.12), channel_id=1, source_target_pairs={{0,2},{1,3},{2,0},{3,1},{4,6},{5,7},{6,4},{7,5},{8,10},{9,11},{10,... | collective-permute-start | bytes 184328 | tf_op jit(solution)/shard_map/ppermute | solution.py:354
  58.8 0.0 collective-permute-done.15
  58.8 3.8 %collective-permute-done.16 = bf16[240,128]{1,0:T(8,128)(2,1)S(1)} collective-permute-done((bf16[240,128]{1,0:T(8,128)(2,1)S(1)}, bf16[240,128]{1,0:T(8,128)(2,1)S(1)}, u32[]{:S(2)}, u32[]{:S(2)}) %collective-permute-start.16) | collective-permute-done | bytes 61472 | tf_op jit(solution)/shard_map/ppermute | solution.py:354
  62.6 0.0 collective-permute-done.19
  62.7 0.1 collective-permute-start.20
  62.8 0.7 %maximum_bitcast_fusion = bf16[4,1,4,64,128]{4,3,2,1,0:T(8,128)(2,1)} fusion(bf16[3,4,64,128]{3,2,1,0:T(8,128)(2,1)S(1)} %get-tuple-element.52, bf16[1,4,64,128]{3,2,1,0:T(8,128)(2,1)S(1)} %bitcast.18), kind=kLoop, calls=%fused_computation.11 | loop fusion | flops 131072 | bytes 524288
  63.5 1.2 %collective-permute-done.20.other = bf16[2176,128]{1,0:T(8,128)(2,1)S(1)} collective-permute-done((bf16[2176,128]{1,0:T(8,128)(2,1)S(1)}, bf16[2176,128]{1,0:T(8,128)(2,1)S(1)}, u32[]{:S(2)}, u32[]{:S(2)}) %collective-permute-start.20) | collective-permute-done | bytes 557088 | tf_op jit(solution)/shard_map/ppermute | solution.py:354
  64.7 2.2 %shard_map.144 = (f32[3456,128]{1,0:T(8,128)}, f32[256,128]{1,0:T(8,128)}, f32[1,128]{1,0:T(1,128)}, f32[1,128]{1,0:T(1,128)}, bf16[4,2,4,64,128]{4,3,2,1,0:T(8,128)(2,1)}) custom-call(s32[7]{0:T(128)S(1)} %pad_add_fusion.sc, bf16[2176,128]{1,0:T(8,128)(2,1)S(1)} %fusion.10.mine, bf16[2176,128]{1,0:T(8,128)(2,1)S(1)} %collective-permute-done.20.other, ...), custom_call_target="tpu_custom_call" | custom-call | tf_op jit(solution)/shard_map/pallas_call | solution.py:619
  (28 shorter events, 0.5 us)
Async XLA Ops:
  2.2 1.6 %collective-permute-start = (bf16[12,64,128]{2,1,0:T(8,128)(2,1)S(1)}, bf16[12,64,128]{2,1,0:T(8,128)(2,1)S(1)}, u32[]{:S(2)}, u32[]{:S(2)}) collective-permute-start(bf16[12,64,128]{2,1,0:T(8,128)(2,1)S(1)} %shard_map.136), channel_id=1, source_target_pairs={{0,1},{1,0},{2,3},{3,2},{4,5},{5,4},{6,7},{7,6},{8,9},{9,8},{10,11... | collective-permute-start | bytes 589832 | tf_op jit(solution)/shard_map/ppermute | solution.py:354
  3.9 7.3 %collective-permute-start.1 = (bf16[6,64,128]{2,1,0:T(8,128)(2,1)S(1)}, bf16[6,64,128]{2,1,0:T(8,128)(2,1)S(1)}, u32[]{:S(2)}, u32[]{:S(2)}) collective-permute-start(bf16[6,64,128]{2,1,0:T(8,128)(2,1)S(1)} %fusion.7), channel_id=1, source_target_pairs={{0,2},{1,3},{2,0},{3,1},{4,6},{5,7},{6,4},{7,5},{8,10},{9,11},{10,... | collective-permute-start | bytes 294920 | tf_op jit(solution)/shard_map/ppermute | solution.py:354
  11.2 4.7 %collective-permute-start.2 = (bf16[6,64,128]{2,1,0:T(8,128)(2,1)S(1)}, bf16[6,64,128]{2,1,0:T(8,128)(2,1)S(1)}, u32[]{:S(2)}, u32[]{:S(2)}) collective-permute-start(bf16[6,64,128]{2,1,0:T(8,128)(2,1)S(1)} %fusion.8), channel_id=1, source_target_pairs={{0,4},{1,5},{2,6},{3,7},{4,0},{5,1},{6,2},{7,3},{8,12},{9,13},{10,... | collective-permute-start | bytes 294920 | tf_op jit(solution)/shard_map/ppermute | solution.py:354
  16.0 6.7 %collective-permute-start.3 = (bf16[6,64,128]{2,1,0:T(8,128)(2,1)S(1)}, bf16[6,64,128]{2,1,0:T(8,128)(2,1)S(1)}, u32[]{:S(2)}, u32[]{:S(2)}) collective-permute-start(bf16[6,64,128]{2,1,0:T(8,128)(2,1)S(1)} %fusion.9), channel_id=1, source_target_pairs={{0,8},{1,9},{2,10},{3,11},{4,12},{5,13},{6,14},{7,15},{8,0},{9,1},... | collective-permute-start | bytes 294920 | tf_op jit(solution)/shard_map/ppermute | solution.py:354
  18.6 5.5 %copy-start = (bf16[3,3,3,128,128]{4,3,2,1,0:T(8,128)(2,1)S(1)}, bf16[3,3,3,128,128]{4,3,2,1,0:T(8,128)(2,1)}, u32[]{:S(2)}) copy-start(bf16[3,3,3,128,128]{4,3,2,1,0:T(8,128)(2,1)} %param.13) | copy-start | bytes 2654212
  18.6 5.5 %copy-start.1 = (bf16[4,2,4,64,128]{4,3,2,1,0:T(8,128)(2,1)S(1)}, bf16[4,2,4,64,128]{4,3,2,1,0:T(8,128)(2,1)}, u32[]{:S(2)}) copy-start(bf16[4,2,4,64,128]{4,3,2,1,0:T(8,128)(2,1)} %frs.1) | copy-start | bytes 1572868
  18.6 5.5 %copy-start.2 = (bf16[4,2,2,64,128]{4,3,2,1,0:T(8,128)(2,1)S(1)}, bf16[4,2,2,64,128]{4,3,2,1,0:T(8,128)(2,1)}, u32[]{:S(2)}) copy-start(bf16[4,2,2,64,128]{4,3,2,1,0:T(8,128)(2,1)} %has.1) | copy-start | bytes 786436
  18.6 5.5 %copy-start.3 = (bf16[4,1,4,64,128]{4,3,2,1,0:T(8,128)(2,1)S(1)}, bf16[4,1,4,64,128]{4,3,2,1,0:T(8,128)(2,1)}, u32[]{:S(2)}) copy-start(bf16[4,1,4,64,128]{4,3,2,1,0:T(8,128)(2,1)} %cos.1) | copy-start | bytes 786436
  18.6 5.5 %copy-start.4 = (bf16[2,128,128]{2,1,0:T(8,128)(2,1)S(1)}, bf16[2,128,128]{2,1,0:T(8,128)(2,1)}, u32[]{:S(2)}) copy-start(bf16[2,128,128]{2,1,0:T(8,128)(2,1)} %sw.1) | copy-start | bytes 196612
  18.6 5.5 %copy-start.5 = (f32[128]{0:T(128)S(1)}, f32[128]{0:T(128)}, u32[]{:S(2)}) copy-start(f32[128]{0:T(128)} %param.14) | copy-start | bytes 1540
  18.6 5.5 %copy-start.6 = (f32[128]{0:T(128)S(1)}, f32[128]{0:T(128)}, u32[]{:S(2)}) copy-start(f32[128]{0:T(128)} %param.16) | copy-start | bytes 1540
  22.7 1.4 %collective-permute-start.4 = (bf16[6,64,128]{2,1,0:T(8,128)(2,1)S(1)}, bf16[6,64,128]{2,1,0:T(8,128)(2,1)S(1)}, u32[]{:S(2)}, u32[]{:S(2)}) collective-permute-start(bf16[6,64,128]{2,1,0:T(8,128)(2,1)S(1)} %fusion.2), channel_id=1, source_target_pairs={{0,1},{1,0},{2,3},{3,2},{4,5},{5,4},{6,7},{7,6},{8,9},{9,8},{10,11... | collective-permute-start | bytes 294920 | tf_op jit(solution)/shard_map/ppermute | solution.py:354
  27.0 1.9 %collective-permute-start.5 = (bf16[1920,128]{1,0:T(8,128)(2,1)S(1)}, bf16[1920,128]{1,0:T(8,128)(2,1)S(1)}, u32[]{:S(2)}, u32[]{:S(2)}) collective-permute-start(bf16[1920,128]{1,0:T(8,128)(2,1)S(1)} %get-tuple-element.56), channel_id=1, source_target_pairs={{0,1},{1,0},{2,3},{3,2},{4,5},{5,4},{6,7},{7,6},{8,9},{9,8},{10,11... | collective-permute-start | bytes 1474568 | tf_op jit(solution)/shard_map/ppermute | solution.py:354
  29.5 4.2 %collective-permute-start.6 = (bf16[512,128]{1,0:T(8,128)(2,1)S(1)}, bf16[512,128]{1,0:T(8,128)(2,1)S(1)}, u32[]{:S(2)}, u32[]{:S(2)}) collective-permute-start(bf16[512,128]{1,0:T(8,128)(2,1)S(1)} %shard_map.141), channel_id=1, source_target_pairs={{0,1},{1,0},{2,3},{3,2},{4,5},{5,4},{6,7},{7,6},{8,9},{9,8},{10,11... | collective-permute-start | bytes 393224 | tf_op jit(solution)/shard_map/ppermute | solution.py:354
  29.8 5.6 %collective-permute-start.8 = (bf16[480,128]{1,0:T(8,128)(2,1)S(1)}, bf16[480,128]{1,0:T(8,128)(2,1)S(1)}, u32[]{:S(2)}, u32[]{:S(2)}) collective-permute-start(bf16[480,128]{1,0:T(8,128)(2,1)S(1)} %get-tuple-element.63), channel_id=1, source_target_pairs={{0,2},{1,3},{2,0},{3,1},{4,6},{5,7},{6,4},{7,5},{8,10},{9,11},{10,... | collective-permute-start | bytes 368648 | tf_op jit(solution)/shard_map/ppermute | solution.py:354
  33.8 6.8 %collective-permute-start.7 = (bf16[736,128]{1,0:T(8,128)(2,1)S(1)}, bf16[736,128]{1,0:T(8,128)(2,1)S(1)}, u32[]{:S(2)}, u32[]{:S(2)}) collective-permute-start(bf16[736,128]{1,0:T(8,128)(2,1)S(1)} %pad_maximum_fusion), channel_id=1, source_target_pairs={{0,2},{1,3},{2,0},{3,1},{4,6},{5,7},{6,4},{7,5},{8,10},{9,11},{10,... | collective-permute-start | bytes 565256 | tf_op jit(solution)/shard_map/ppermute | solution.py:354
  35.4 7.4 %collective-permute-start.9 = (bf16[240,128]{1,0:T(8,128)(2,1)S(1)}, bf16[240,128]{1,0:T(8,128)(2,1)S(1)}, u32[]{:S(2)}, u32[]{:S(2)}) collective-permute-start(bf16[240,128]{1,0:T(8,128)(2,1)S(1)} %get-tuple-element.80), channel_id=1, source_target_pairs={{0,12},{1,13},{2,14},{3,15},{4,8},{5,9},{6,10},{7,11},{8,4},{9,5},... | collective-permute-start | bytes 184328 | tf_op jit(solution)/shard_map/ppermute | solution.py:354
  38.9 5.4 %collective-permute-start.10 = (bf16[240,128]{1,0:T(8,128)(2,1)S(1)}, bf16[240,128]{1,0:T(8,128)(2,1)S(1)}, u32[]{:S(2)}, u32[]{:S(2)}) collective-permute-start(bf16[240,128]{1,0:T(8,128)(2,1)S(1)} %get-tuple-element.81), channel_id=1, source_target_pairs={{0,8},{1,9},{2,10},{3,11},{4,12},{5,13},{6,14},{7,15},{8,0},{9,1},... | collective-permute-start | bytes 184328 | tf_op jit(solution)/shard_map/ppermute | solution.py:354
  40.6 8.2 %collective-permute-start.11 = (bf16[240,128]{1,0:T(8,128)(2,1)S(1)}, bf16[240,128]{1,0:T(8,128)(2,1)S(1)}, u32[]{:S(2)}, u32[]{:S(2)}) collective-permute-start(bf16[240,128]{1,0:T(8,128)(2,1)S(1)} %add_convert_fusion.1), channel_id=1, source_target_pairs={{0,4},{1,5},{2,6},{3,7},{4,0},{5,1},{6,2},{7,3},{8,12},{9,13},{10,... | collective-permute-start | bytes 184328 | tf_op jit(solution)/shard_map/ppermute | solution.py:354
  42.3 4.0 %collective-permute-start.17 = (bf16[128,128]{1,0:T(8,128)(2,1)S(1)}, bf16[128,128]{1,0:T(8,128)(2,1)S(1)}, u32[]{:S(2)}, u32[]{:S(2)}) collective-permute-start(bf16[128,128]{1,0:T(8,128)(2,1)S(1)} %fusion.18), channel_id=1, source_target_pairs={{0,4},{1,5},{2,6},{3,7},{4,0},{5,1},{6,2},{7,3},{8,12},{9,13},{10,... | collective-permute-start | bytes 98312 | tf_op jit(solution)/shard_map/ppermute | solution.py:354
  46.3 8.7 %collective-permute-start.18 = (bf16[128,128]{1,0:T(8,128)(2,1)S(1)}, bf16[128,128]{1,0:T(8,128)(2,1)S(1)}, u32[]{:S(2)}, u32[]{:S(2)}) collective-permute-start(bf16[128,128]{1,0:T(8,128)(2,1)S(1)} %fusion.19), channel_id=1, source_target_pairs={{0,8},{1,9},{2,10},{3,11},{4,12},{5,13},{6,14},{7,15},{8,0},{9,1},... | collective-permute-start | bytes 98312 | tf_op jit(solution)/shard_map/ppermute | solution.py:354
  48.8 10.0 %collective-permute-start.15 = (bf16[240,128]{1,0:T(8,128)(2,1)S(1)}, bf16[240,128]{1,0:T(8,128)(2,1)S(1)}, u32[]{:S(2)}, u32[]{:S(2)}) collective-permute-start(bf16[240,128]{1,0:T(8,128)(2,1)S(1)} %get-tuple-element.79), channel_id=1, source_target_pairs={{0,2},{1,3},{2,0},{3,1},{4,6},{5,7},{6,4},{7,5},{8,10},{9,11},{10,... | collective-permute-start | bytes 184328 | tf_op jit(solution)/shard_map/ppermute | solution.py:354
  50.6 6.0 %collective-permute-start.14 = (bf16[240,128]{1,0:T(8,128)(2,1)S(1)}, bf16[240,128]{1,0:T(8,128)(2,1)S(1)}, u32[]{:S(2)}, u32[]{:S(2)}) collective-permute-start(bf16[240,128]{1,0:T(8,128)(2,1)S(1)} %get-tuple-element.79), channel_id=1, source_target_pairs={{0,12},{1,13},{2,14},{3,15},{4,8},{5,9},{6,10},{7,11},{8,4},{9,5},... | collective-permute-start | bytes 184328 | tf_op jit(solution)/shard_map/ppermute | solution.py:354
  50.8 5.8 %collective-permute-start.13 = (bf16[240,128]{1,0:T(8,128)(2,1)S(1)}, bf16[240,128]{1,0:T(8,128)(2,1)S(1)}, u32[]{:S(2)}, u32[]{:S(2)}) collective-permute-start(bf16[240,128]{1,0:T(8,128)(2,1)S(1)} %get-tuple-element.79), channel_id=1, source_target_pairs={{0,8},{1,9},{2,10},{3,11},{4,12},{5,13},{6,14},{7,15},{8,0},{9,1},... | collective-permute-start | bytes 184328 | tf_op jit(solution)/shard_map/ppermute | solution.py:354
  52.4 5.5 %collective-permute-start.12 = (bf16[240,128]{1,0:T(8,128)(2,1)S(1)}, bf16[240,128]{1,0:T(8,128)(2,1)S(1)}, u32[]{:S(2)}, u32[]{:S(2)}) collective-permute-start(bf16[240,128]{1,0:T(8,128)(2,1)S(1)} %get-tuple-element.79), channel_id=1, source_target_pairs={{0,4},{1,5},{2,6},{3,7},{4,0},{5,1},{6,2},{7,3},{8,12},{9,13},{10,... | collective-permute-start | bytes 184328 | tf_op jit(solution)/shard_map/ppermute | solution.py:354
  56.6 6.0 %collective-permute-start.19 = (bf16[608,128]{1,0:T(8,128)(2,1)S(1)}, bf16[608,128]{1,0:T(8,128)(2,1)S(1)}, u32[]{:S(2)}, u32[]{:S(2)}) collective-permute-start(bf16[608,128]{1,0:T(8,128)(2,1)S(1)} %pad_maximum_fusion.1), channel_id=1, source_target_pairs={{0,2},{1,3},{2,0},{3,1},{4,6},{5,7},{6,4},{7,5},{8,10},{9,11},{10,... | collective-permute-start | bytes 466952 | tf_op jit(solution)/shard_map/ppermute | solution.py:354
  57.9 4.7 %collective-permute-start.16 = (bf16[240,128]{1,0:T(8,128)(2,1)S(1)}, bf16[240,128]{1,0:T(8,128)(2,1)S(1)}, u32[]{:S(2)}, u32[]{:S(2)}) collective-permute-start(bf16[240,128]{1,0:T(8,128)(2,1)S(1)} %collective-permute-done.12), channel_id=1, source_target_pairs={{0,2},{1,3},{2,0},{3,1},{4,6},{5,7},{6,4},{7,5},{8,10},{9,11},{10,... | collective-permute-start | bytes 184328 | tf_op jit(solution)/shard_map/ppermute | solution.py:354
  62.7 2.0 %collective-permute-start.20 = (bf16[2176,128]{1,0:T(8,128)(2,1)S(1)}, bf16[2176,128]{1,0:T(8,128)(2,1)S(1)}, u32[]{:S(2)}, u32[]{:S(2)}) collective-permute-start(bf16[2176,128]{1,0:T(8,128)(2,1)S(1)} %fusion.10.mine), channel_id=1, source_target_pairs={{0,1},{1,0},{2,3},{3,2},{4,5},{5,4},{6,7},{7,6},{8,9},{9,8},{10,11... | collective-permute-start | bytes 1671176 | tf_op jit(solution)/shard_map/ppermute | solution.py:354

commit v8 on v7

--- a/solution.py
+++ b/solution.py
@@ -551,7 +551,33 @@
         room=8,
     )(sc, keep, got)
     got_far = _xor(send_far, 2, n, axis)
+    got_near = _xor(send_near, 2, n, axis)
     got_first = _xor(_after(first_grad, kept), 1, n, axis)
+    core, pair = index & 1, (index >> 1) & 1
+
+    def by(bit, a, b):
+        return jnp.where(bit == 0, a, b)
+
+    def by_half(bit, v):
+        rows = v.shape[0] // 2
+        return by(bit, v[:rows], v[rows:])
+
+    def ordered(bit, ours, theirs):
+        return by(bit, _first_live(ours, theirs), _first_live(theirs, ours))
+
+    chip_first = ordered(core, by_half(core, first_grad), by_half(core, got_first))
+    beside_first = _xor(chip_first, 2, n, axis)
+
+    def summed(j, came):
+        i = j % 2
+        return kept[j * piece : (j + 1) * piece] + came[i * piece : (i + 1) * piece].astype(F32)
+
+    outs = {j: summed(j, got_far).astype(BF) for j in (3, 2)}
+    got_near = _after(got_near, outs[3], outs[2])
+    outs[1] = summed(1, got_near).astype(BF)
+    gots = {j: _xor(outs[j], 4 * j, n, axis) for j in (3, 2, 1)}
+    beside_first = _after(beside_first, outs[1])
+    lead = ordered(pair, by_half(pair, chip_first), by_half(pair, beside_first))
     grad = _call(
         _back_kernel,
         jax.ShapeDtypeStruct((slots, 2, h, w, c), F32),
@@ -560,43 +586,8 @@
         flops=1,
         moved=1,
         room=24,
-    )(_after(sc, kept), g0, g1, wt)
-    kept, got_first = _after(kept, grad), _after(got_first, grad)
-    core, pair = index & 1, (index >> 1) & 1
-    below, quarter = 2 * piece, carried // 4
-
-    def by(bit, a, b):
-        return jnp.where(bit == 0, a, b)
-
-    def by_half(bit, v):
-        rows = v.shape[0] // 2
-        return by(bit, v[:rows], v[rows:])
-
-    def ordered(bit, ours, theirs):
-        return by(bit, _first_live(ours, theirs), _first_live(theirs, ours))
-
-    chip_first = ordered(core, by_half(core, first_grad), by_half(core, got_first))
-    got_near = _xor(jnp.concatenate([send_near, chip_first], axis=0), 2, n, axis)
-
-    def summed(j, came):
-        i = j % 2
-        return kept[j * piece : (j + 1) * piece] + came[i * piece : (i + 1) * piece].astype(F32)
-
-    outs = {j: summed(j, got_far).astype(BF) for j in (3, 2)}
-    got_near = _after(got_near, outs[3], outs[2])
-    beside_first = got_near[below:]
-    outs[1] = summed(1, got_near).astype(BF)
-    gots = {j: _xor(outs[j], 4 * j, n, axis) for j in (3, 2, 1)}
-    near_again = _after(got_near, outs[1])
-    mine = summed(0, near_again)
-    lead = ordered(pair, by_half(pair, chip_first), by_half(pair, near_again[below:]))
-    beyond, k = jnp.full_like(lead, EMPTY_GRAD), 4
-    while k < n:
-        came = _xor(lead, k, n, axis)
-        beyond = by(index & k, _first_live(beyond, came), beyond)
-        if 2 * k < n:
-            lead = ordered(index & k, lead, came)
-        k *= 2
+    )(_after(sc, outs[1], lead), g0, g1, wt)
+    mine = summed(0, _after(got_near, grad))
     for j in (3, 2):
         mine = mine + gots[j].astype(F32)
     gots[1] = _after(gots[1], mine)
@@ -608,12 +599,21 @@
     others = {j: _xor(mine, 4 * j, n, axis) for j in (3, 2, 1)}
     x_own = _xor(mine, 2, n, axis)
     x_near = _xor(others[1], 2, n, axis)
-    x_far = _xor(jnp.concatenate([others[2], others[3], beyond], axis=0), 2, n, axis)
-    theirs = x_far[below:]
+    x_far = _xor(jnp.concatenate([others[2], others[3]], axis=0), 2, n, axis)
+    beyond, k = jnp.full_like(lead, EMPTY_GRAD), 4
+    while k < n:
+        if k == 8:
+            lead = _after(lead, others[1])
+        came = _xor(lead, k, n, axis)
+        beyond = by(index & k, _first_live(beyond, came), beyond)
+        if 2 * k < n:
+            lead = ordered(index & k, lead, came)
+        k *= 2
+    theirs = _xor(beyond, 2, n, axis)
     beyond = jnp.concatenate([by(pair, beyond, theirs), by(pair, theirs, beyond)], axis=0)
     beyond = by(pair, _first_live(beside_first, beyond), beyond)
     ours = jnp.concatenate(
-        [mine, others[1], others[2], others[3], x_own, x_near, x_far[:below], beyond], axis=0
+        [mine, others[1], others[2], others[3], x_own, x_near, x_far, beyond], axis=0
     )
     other = _xor(ours, 1, n, axis)
     cwg, swg, cbg, sbg, frames_grad = _call(

time: 67.1 us -> 70.2 us (1.046)
  waiting for transfers between devices: 16.1 us -> 18.2 us
  starting transfers between devices: 26.8 us -> 27.8 us
    ppermute x21 -> x23, waiting for transfers between devices: 16.1 us -> 18.2 us  [_xor(): return lax.ppermute(x, axis, [(i, i ^ k) for i in range(n)])]
    ppermute x21 -> x23, starting transfers between devices: 26.8 us -> 27.8 us  [_xor(): return lax.ppermute(x, axis, [(i, i ^ k) for i in range(n)])]
  transfers between devices with their start and end apart: 21 -> 23, of which waited for: 10 -> 10; matrix products, arithmetic and copies ran while one was open for 3% -> 3% of each run, Pallas kernels for 21% -> 20%
where the time goes in v8:
time: 70.2 us; the launch traced here: 70 us
  starting transfers between devices  27.8 us (40%)
  Pallas kernels  20.3 us (29%)
  waiting for transfers between devices  18.2 us (26%)
  other arithmetic  1.95 us (3%)
  between operations  1.62 us (2%)
    ppermute x23, starting transfers between devices, _xor(): return lax.ppermute(x, axis, [(i, i ^ k) for i in range(n)])  27.8 us
    ppermute x23, waiting for transfers between devices, _xor(): return lax.ppermute(x, axis, [(i, i ^ k) for i in range(n)])  18.2 us
    pallas_call x1, Pallas kernels, early_conv(): _call(_early_conv_kernel, [jax.ShapeDtypeStruct(wide, F32), jax.ShapeDtyp...  4.41 us
    pallas_call x1, Pallas kernels, early_sums(): _call(_early_sums_kernel, jax.ShapeDtypeStruct((rows, c), F32), [_SMEM, _...  3.95 us
    pallas_call x1, Pallas kernels, body(): _call(_back_kernel, jax.ShapeDtypeStruct((slots, 2, h, w, c), F32), [_SME...  3.39 us
    pallas_call x1, Pallas kernels, body(): _call(_late_kernel, [jax.ShapeDtypeStruct((h, w, c), BF), jax.ShapeDtypeS...  2.79 us
    pallas_call x1, Pallas kernels, body(): _call(_final_kernel, [jax.ShapeDtypeStruct((27 * c, c), F32), jax.ShapeDt...  2.18 us
  transfers between devices with their start and end apart: 23, of which 10 were waited for; matrix products, arithmetic and copies ran while one was open for 3% of the time, Pallas kernels for 20%

profile of v8, /device:TPU:0, one launch (start us, length us, event | category | flops | bytes accessed | tf_op | source)
XLA Modules:
  0.0 70.0 jit_solution(8821200524021430021)
XLA Ops:
  1.3 1.0 %shard_map.136 = bf16[12,64,128]{2,1,0:T(8,128)(2,1)S(1)} custom-call(s32[1]{0:T(128)S(6)} %copy.23.sc, bf16[4,2,4,64,128]{4,3,2,1,0:T(8,128)(2,1)} %frs.1, bf16[4,2,2,64,128]{4,3,2,1,0:T(8,128)(2,1)} %has.1), custom_call_target="tpu_custom_call" | custom-call | tf_op jit(solution)/shard_map/pallas_call | solution.py:435
  2.2 0.5 collective-permute-start
  2.8 0.7 %pad_add_fusion.sc = s32[7]{0:T(128)S(1)} fusion(s32[1]{0:T(128)} %bitcast.1, s32[1]{0:T(128)} %bitcast, s32[4]{0:T(128)} %param.11, s32[1]{0:T(128)S(6)} %copy.23.sc), kind=kLoop, calls=%fused_computation.61 | loop fusion | flops 21 | bytes 56 | tf_op jit(solution)/shard_map/concatenate | solution.py:417
  3.5 0.3 collective-permute-done
  3.9 2.9 %collective-permute-start.1 = (bf16[6,64,128]{2,1,0:T(8,128)(2,1)S(1)}, bf16[6,64,128]{2,1,0:T(8,128)(2,1)S(1)}, u32[]{:S(2)}, u32[]{:S(2)}) collective-permute-start(bf16[6,64,128]{2,1,0:T(8,128)(2,1)S(1)} %fusion.7), channel_id=1, source_target_pairs={{0,2},{1,3},{2,0},{3,1},{4,6},{5,7},{6,4},{7,5},{8,10},{9,11},{10,... | collective-permute-start | bytes 294920 | tf_op jit(solution)/shard_map/ppermute | solution.py:354
  6.8 4.4 %shard_map.137 = (f32[768,256]{1,0:T(8,128)S(1)}, bf16[768,128]{1,0:T(8,128)(2,1)S(1)}, bf16[2,128,128]{2,1,0:T(8,128)(2,1)S(1)}, f32[1,128]{1,0:T(1,128)S(1)}) custom-call(s32[7]{0:T(128)S(1)} %pad_add_fusion.sc, bf16[4,2,4,64,128]{4,3,2,1,0:T(8,128)(2,1)} %frs.1, bf16[4,2,2,64,128]{4,3,2,1,0:T(8,128)(2,1)} %has.1, bf16[4,1,4,64,128]{4,3,2,1,0:T(8,128)(2,1)} %cos.1, ...), custom_call_target="tpu_custom_call" | custom-call | flops 1811939328 | bytes 4194304 | tf_op jit(solution)/shard_map/pallas_call | solution.py:462
  11.2 0.0 collective-permute-done.1
  11.2 1.6 %collective-permute-start.2 = (bf16[6,64,128]{2,1,0:T(8,128)(2,1)S(1)}, bf16[6,64,128]{2,1,0:T(8,128)(2,1)S(1)}, u32[]{:S(2)}, u32[]{:S(2)}) collective-permute-start(bf16[6,64,128]{2,1,0:T(8,128)(2,1)S(1)} %fusion.8), channel_id=1, source_target_pairs={{0,4},{1,5},{2,6},{3,7},{4,0},{5,1},{6,2},{7,3},{8,12},{9,13},{10,... | collective-permute-start | bytes 294920 | tf_op jit(solution)/shard_map/ppermute | solution.py:354
  12.9 1.0 %shard_map.138 = (bf16[3,4,64,128]{3,2,1,0:T(8,128)(2,1)S(1)}, bf16[768,256]{1,0:T(8,128)(2,1)S(1)}, bf16[768,256]{1,0:T(8,128)(2,1)S(1)}) custom-call(s32[7]{0:T(128)S(1)} %pad_add_fusion.sc, f32[768,256]{1,0:T(8,128)S(1)} %get-tuple-element.40.pre_ref, bf16[768,128]{1,0:T(8,128)(2,1)S(1)} %get-tuple-element.43.gout_ref, ...), custom_call_target="tpu_custom_call" | custom-call | bytes 2097152 | tf_op jit(solution)/shard_map/pallas_call | solution.py:480
  13.8 2.1 %collective-permute-done.2 = bf16[6,64,128]{2,1,0:T(8,128)(2,1)S(1)} collective-permute-done((bf16[6,64,128]{2,1,0:T(8,128)(2,1)S(1)}, bf16[6,64,128]{2,1,0:T(8,128)(2,1)S(1)}, u32[]{:S(2)}, u32[]{:S(2)}) %collective-permute-start.2) | collective-permute-done | bytes 98336 | tf_op jit(solution)/shard_map/ppermute | solution.py:354
  15.9 2.7 %collective-permute-start.3 = (bf16[6,64,128]{2,1,0:T(8,128)(2,1)S(1)}, bf16[6,64,128]{2,1,0:T(8,128)(2,1)S(1)}, u32[]{:S(2)}, u32[]{:S(2)}) collective-permute-start(bf16[6,64,128]{2,1,0:T(8,128)(2,1)S(1)} %fusion.9), channel_id=1, source_target_pairs={{0,8},{1,9},{2,10},{3,11},{4,12},{5,13},{6,14},{7,15},{8,0},{9,1},... | collective-permute-start | bytes 294920 | tf_op jit(solution)/shard_map/ppermute | solution.py:354
  18.6 0.0 copy-start.4
  18.6 0.0 copy-start.5
  18.6 0.0 copy-start.6
  18.6 3.9 %shard_map.139.early = f32[3840,128]{1,0:T(8,128)S(1)} custom-call(s32[7]{0:T(128)S(1)} %pad_add_fusion.sc, bf16[4,2,4,64,128]{4,3,2,1,0:T(8,128)(2,1)} %frs.1, bf16[4,2,2,64,128]{4,3,2,1,0:T(8,128)(2,1)} %has.1, bf16[768,256]{1,0:T(8,128)(2,1)S(1)} %get-tuple-element.46.g_ref.g1, bf16[768,256]{1,0:T(8,128)(2,1)S(1)} %get-tuple-element.49.hid_ref, ...), custom_call_target="tpu_custom_call" | custom-call | flops 1811939328 | bytes 4194304 | tf_op jit(solution)/shard_map/pallas_call | solution.py:496
  22.6 0.0 collective-permute-done.3
  22.7 0.1 collective-permute-start.4
  22.7 1.3 %collective-permute-done.4 = bf16[6,64,128]{2,1,0:T(8,128)(2,1)S(1)} collective-permute-done((bf16[6,64,128]{2,1,0:T(8,128)(2,1)S(1)}, bf16[6,64,128]{2,1,0:T(8,128)(2,1)S(1)}, u32[]{:S(2)}, u32[]{:S(2)}) %collective-permute-start.4) | collective-permute-done | bytes 98336 | tf_op jit(solution)/shard_map/ppermute | solution.py:354
  24.1 0.0 copy-done
  24.1 0.0 copy-done.1
  24.1 0.0 copy-done.2
  24.2 2.8 %shard_map.140 = (bf16[4,64,128]{2,1,0:T(8,128)(2,1)S(1)}, bf16[256,256]{1,0:T(8,128)(2,1)S(1)}, bf16[1920,128]{1,0:T(8,128)(2,1)S(1)}, f32[1920,128]{1,0:T(8,128)S(1)}) custom-call(s32[7]{0:T(128)S(1)} %pad_add_fusion.sc, bf16[4,2,4,64,128]{4,3,2,1,0:T(8,128)(2,1)S(1)} %copy-done.1, bf16[4,2,2,64,128]{4,3,2,1,0:T(8,128)(2,1)S(1)} %copy-done.2, ...), custom_call_target="tpu_custom_call" | custom-call | flops 1207959552 | bytes 6291456 | tf_op jit(solution)/shard_map/pallas_call | solution.py:515
  27.0 0.2 collective-permute-start.5
  27.2 1.1 %shard_map.141 = bf16[512,128]{1,0:T(8,128)(2,1)S(1)} custom-call(s32[7]{0:T(128)S(1)} %pad_add_fusion.sc, bf16[256,256]{1,0:T(8,128)(2,1)S(1)} %get-tuple-element.54.g_ref.g0, bf16[27,128,128]{2,1,0:T(8,128)(2,1)S(1)} %bitcast.16), custom_call_target="tpu_custom_call" | custom-call | flops 301989888 | bytes 1048576 | tf_op jit(solution)/shard_map/pallas_call | solution.py:533
  28.3 0.7 collective-permute-done.5.got
  28.9 0.6 shard_map.142
  29.6 0.6 collective-permute-start.7
  30.2 1.5 %collective-permute-start.6 = (bf16[480,128]{1,0:T(8,128)(2,1)S(1)}, bf16[480,128]{1,0:T(8,128)(2,1)S(1)}, u32[]{:S(2)}, u32[]{:S(2)}) collective-permute-start(bf16[480,128]{1,0:T(8,128)(2,1)S(1)} %get-tuple-element.58), channel_id=1, source_target_pairs={{0,2},{1,3},{2,0},{3,1},{4,6},{5,7},{6,4},{7,5},{8,10},{9,11},{10,... | collective-permute-start | bytes 368648 | tf_op jit(solution)/shard_map/ppermute | solution.py:354
  31.6 0.0 collective-permute-start.8
  31.6 4.1 %collective-permute-done.7 = bf16[480,128]{1,0:T(8,128)(2,1)S(1)} collective-permute-done((bf16[480,128]{1,0:T(8,128)(2,1)S(1)}, bf16[480,128]{1,0:T(8,128)(2,1)S(1)}, u32[]{:S(2)}, u32[]{:S(2)}) %collective-permute-start.7) | collective-permute-done | bytes 122912 | tf_op jit(solution)/shard_map/ppermute | solution.py:354
  35.8 3.5 %collective-permute-start.10 = (bf16[240,128]{1,0:T(8,128)(2,1)S(1)}, bf16[240,128]{1,0:T(8,128)(2,1)S(1)}, u32[]{:S(2)}, u32[]{:S(2)}) collective-permute-start(bf16[240,128]{1,0:T(8,128)(2,1)S(1)} %get-tuple-element.80), channel_id=1, source_target_pairs={{0,12},{1,13},{2,14},{3,15},{4,8},{5,9},{6,10},{7,11},{8,4},{9,5},... | collective-permute-start | bytes 184328 | tf_op jit(solution)/shard_map/ppermute | solution.py:354
  39.3 0.0 collective-permute-start.11
  39.3 0.0 collective-permute-done.6
  39.3 0.0 collective-permute-done.8.got
  39.4 0.1 fusion.11
  39.4 0.6 collective-permute-start.9
  40.0 1.0 %collective-permute-start.12 = (bf16[240,128]{1,0:T(8,128)(2,1)S(1)}, bf16[240,128]{1,0:T(8,128)(2,1)S(1)}, u32[]{:S(2)}, u32[]{:S(2)}) collective-permute-start(bf16[240,128]{1,0:T(8,128)(2,1)S(1)} %add_convert_fusion.1), channel_id=1, source_target_pairs={{0,4},{1,5},{2,6},{3,7},{4,0},{5,1},{6,2},{7,3},{8,12},{9,13},{10,... | collective-permute-start | bytes 184328 | tf_op jit(solution)/shard_map/ppermute | solution.py:354
  41.0 2.7 %collective-permute-done.9 = bf16[256,128]{1,0:T(8,128)(2,1)S(1)} collective-permute-done((bf16[256,128]{1,0:T(8,128)(2,1)S(1)}, bf16[256,128]{1,0:T(8,128)(2,1)S(1)}, u32[]{:S(2)}, u32[]{:S(2)}) %collective-permute-start.9) | collective-permute-done | bytes 65568 | tf_op jit(solution)/shard_map/ppermute | solution.py:354
  43.8 1.0 %collective-permute-start.19 = (bf16[128,128]{1,0:T(8,128)(2,1)S(1)}, bf16[128,128]{1,0:T(8,128)(2,1)S(1)}, u32[]{:S(2)}, u32[]{:S(2)}) collective-permute-start(bf16[128,128]{1,0:T(8,128)(2,1)S(1)} %fusion.18), channel_id=1, source_target_pairs={{0,4},{1,5},{2,6},{3,7},{4,0},{5,1},{6,2},{7,3},{8,12},{9,13},{10,... | collective-permute-start | bytes 98312 | tf_op jit(solution)/shard_map/ppermute | solution.py:354
  44.8 3.4 %shard_map.143.grad = f32[4,2,4,64,128]{4,3,2,1,0:T(8,128)S(1)} custom-call(s32[7]{0:T(128)S(1)} %pad_add_fusion.sc, bf16[256,256]{1,0:T(8,128)(2,1)S(1)} %get-tuple-element.54.g_ref.g0, bf16[768,256]{1,0:T(8,128)(2,1)S(1)} %get-tuple-element.46.g_ref.g1, bf16[27,128,128]{2,1,0:T(8,128)(2,1)S(1)} %bitcast.17), custom_call_target="tpu_custom_call" | custom-call | flops 1 | bytes 1 | tf_op jit(solution)/shard_map/pallas_call | solution.py:581
  48.2 0.0 collective-permute-done.10
  48.2 0.0 collective-permute-done.11
  48.2 0.0 collective-permute-done.12
  48.3 0.6 collective-permute-start.16
  48.9 3.4 %collective-permute-start.15 = (bf16[240,128]{1,0:T(8,128)(2,1)S(1)}, bf16[240,128]{1,0:T(8,128)(2,1)S(1)}, u32[]{:S(2)}, u32[]{:S(2)}) collective-permute-start(bf16[240,128]{1,0:T(8,128)(2,1)S(1)} %get-tuple-element.79), channel_id=1, source_target_pairs={{0,12},{1,13},{2,14},{3,15},{4,8},{5,9},{6,10},{7,11},{8,4},{9,5},... | collective-permute-start | bytes 184328 | tf_op jit(solution)/shard_map/ppermute | solution.py:354
  52.3 0.0 collective-permute-start.14
  52.3 0.9 %collective-permute-start.13 = (bf16[240,128]{1,0:T(8,128)(2,1)S(1)}, bf16[240,128]{1,0:T(8,128)(2,1)S(1)}, u32[]{:S(2)}, u32[]{:S(2)}) collective-permute-start(bf16[240,128]{1,0:T(8,128)(2,1)S(1)} %get-tuple-element.79), channel_id=1, source_target_pairs={{0,4},{1,5},{2,6},{3,7},{4,0},{5,1},{6,2},{7,3},{8,12},{9,13},{10,... | collective-permute-start | bytes 184328 | tf_op jit(solution)/shard_map/ppermute | solution.py:354
  53.3 0.0 collective-permute-done.19
  53.3 3.3 %collective-permute-done.13 = bf16[240,128]{1,0:T(8,128)(2,1)S(1)} collective-permute-done((bf16[240,128]{1,0:T(8,128)(2,1)S(1)}, bf16[240,128]{1,0:T(8,128)(2,1)S(1)}, u32[]{:S(2)}, u32[]{:S(2)}) %collective-permute-start.13) | collective-permute-done | bytes 61472 | tf_op jit(solution)/shard_map/ppermute | solution.py:354
  56.6 2.8 %collective-permute-start.20 = (bf16[128,128]{1,0:T(8,128)(2,1)S(1)}, bf16[128,128]{1,0:T(8,128)(2,1)S(1)}, u32[]{:S(2)}, u32[]{:S(2)}) collective-permute-start(bf16[128,128]{1,0:T(8,128)(2,1)S(1)} %fusion.19), channel_id=1, source_target_pairs={{0,8},{1,9},{2,10},{3,11},{4,12},{5,13},{6,14},{7,15},{8,0},{9,1},... | collective-permute-start | bytes 98312 | tf_op jit(solution)/shard_map/ppermute | solution.py:354
  59.5 0.0 collective-permute-done.15
  59.5 0.0 collective-permute-done.14
  59.5 1.5 %collective-permute-start.18 = (bf16[480,128]{1,0:T(8,128)(2,1)S(1)}, bf16[480,128]{1,0:T(8,128)(2,1)S(1)}, u32[]{:S(2)}, u32[]{:S(2)}) collective-permute-start(bf16[480,128]{1,0:T(8,128)(2,1)S(1)} %pad_maximum_fusion), channel_id=1, source_target_pairs={{0,2},{1,3},{2,0},{3,1},{4,6},{5,7},{6,4},{7,5},{8,10},{9,11},{10,... | collective-permute-start | bytes 368648 | tf_op jit(solution)/shard_map/ppermute | solution.py:354
  61.0 0.5 collective-permute-start.17
  61.6 0.0 collective-permute-done.16
  61.7 0.0 collective-permute-done.20
  61.7 1.5 %collective-permute-start.21 = (bf16[128,128]{1,0:T(8,128)(2,1)S(1)}, bf16[128,128]{1,0:T(8,128)(2,1)S(1)}, u32[]{:S(2)}, u32[]{:S(2)}) collective-permute-start(bf16[128,128]{1,0:T(8,128)(2,1)S(1)} %fusion.17), channel_id=1, source_target_pairs={{0,2},{1,3},{2,0},{3,1},{4,6},{5,7},{6,4},{7,5},{8,10},{9,11},{10,... | collective-permute-start | bytes 98312 | tf_op jit(solution)/shard_map/ppermute | solution.py:354
  63.3 2.0 %collective-permute-done.17 = bf16[240,128]{1,0:T(8,128)(2,1)S(1)} collective-permute-done((bf16[240,128]{1,0:T(8,128)(2,1)S(1)}, bf16[240,128]{1,0:T(8,128)(2,1)S(1)}, u32[]{:S(2)}, u32[]{:S(2)}) %collective-permute-start.17) | collective-permute-done | bytes 61472 | tf_op jit(solution)/shard_map/ppermute | solution.py:354
  65.3 0.4 collective-permute-done.21
  65.7 0.0 collective-permute-done.18
  65.8 0.1 collective-permute-start.22
  65.9 0.7 %maximum_bitcast_fusion = bf16[4,1,4,64,128]{4,3,2,1,0:T(8,128)(2,1)} fusion(bf16[3,4,64,128]{3,2,1,0:T(8,128)(2,1)S(1)} %get-tuple-element.52, bf16[1,4,64,128]{3,2,1,0:T(8,128)(2,1)S(1)} %bitcast.18), kind=kLoop, calls=%fused_computation.11 | loop fusion | flops 131072 | bytes 524288
  66.6 1.2 %collective-permute-done.22.other = bf16[2176,128]{1,0:T(8,128)(2,1)S(1)} collective-permute-done((bf16[2176,128]{1,0:T(8,128)(2,1)S(1)}, bf16[2176,128]{1,0:T(8,128)(2,1)S(1)}, u32[]{:S(2)}, u32[]{:S(2)}) %collective-permute-start.22) | collective-permute-done | bytes 557088 | tf_op jit(solution)/shard_map/ppermute | solution.py:354
  67.8 2.2 %shard_map.144 = (f32[3456,128]{1,0:T(8,128)}, f32[256,128]{1,0:T(8,128)}, f32[1,128]{1,0:T(1,128)}, f32[1,128]{1,0:T(1,128)}, bf16[4,2,4,64,128]{4,3,2,1,0:T(8,128)(2,1)}) custom-call(s32[7]{0:T(128)S(1)} %pad_add_fusion.sc, bf16[2176,128]{1,0:T(8,128)(2,1)S(1)} %fusion.10.mine, bf16[2176,128]{1,0:T(8,128)(2,1)S(1)} %collective-permute-done.22.other, ...), custom_call_target="tpu_custom_call" | custom-call | tf_op jit(solution)/shard_map/pallas_call | solution.py:619
  (31 shorter events, 0.5 us)
Async XLA Ops:
  2.2 1.6 %collective-permute-start = (bf16[12,64,128]{2,1,0:T(8,128)(2,1)S(1)}, bf16[12,64,128]{2,1,0:T(8,128)(2,1)S(1)}, u32[]{:S(2)}, u32[]{:S(2)}) collective-permute-start(bf16[12,64,128]{2,1,0:T(8,128)(2,1)S(1)} %shard_map.136), channel_id=1, source_target_pairs={{0,1},{1,0},{2,3},{3,2},{4,5},{5,4},{6,7},{7,6},{8,9},{9,8},{10,11... | collective-permute-start | bytes 589832 | tf_op jit(solution)/shard_map/ppermute | solution.py:354
  3.9 7.3 %collective-permute-start.1 = (bf16[6,64,128]{2,1,0:T(8,128)(2,1)S(1)}, bf16[6,64,128]{2,1,0:T(8,128)(2,1)S(1)}, u32[]{:S(2)}, u32[]{:S(2)}) collective-permute-start(bf16[6,64,128]{2,1,0:T(8,128)(2,1)S(1)} %fusion.7), channel_id=1, source_target_pairs={{0,2},{1,3},{2,0},{3,1},{4,6},{5,7},{6,4},{7,5},{8,10},{9,11},{10,... | collective-permute-start | bytes 294920 | tf_op jit(solution)/shard_map/ppermute | solution.py:354
  11.2 4.7 %collective-permute-start.2 = (bf16[6,64,128]{2,1,0:T(8,128)(2,1)S(1)}, bf16[6,64,128]{2,1,0:T(8,128)(2,1)S(1)}, u32[]{:S(2)}, u32[]{:S(2)}) collective-permute-start(bf16[6,64,128]{2,1,0:T(8,128)(2,1)S(1)} %fusion.8), channel_id=1, source_target_pairs={{0,4},{1,5},{2,6},{3,7},{4,0},{5,1},{6,2},{7,3},{8,12},{9,13},{10,... | collective-permute-start | bytes 294920 | tf_op jit(solution)/shard_map/ppermute | solution.py:354
  15.9 6.7 %collective-permute-start.3 = (bf16[6,64,128]{2,1,0:T(8,128)(2,1)S(1)}, bf16[6,64,128]{2,1,0:T(8,128)(2,1)S(1)}, u32[]{:S(2)}, u32[]{:S(2)}) collective-permute-start(bf16[6,64,128]{2,1,0:T(8,128)(2,1)S(1)} %fusion.9), channel_id=1, source_target_pairs={{0,8},{1,9},{2,10},{3,11},{4,12},{5,13},{6,14},{7,15},{8,0},{9,1},... | collective-permute-start | bytes 294920 | tf_op jit(solution)/shard_map/ppermute | solution.py:354
  18.6 5.5 %copy-start = (bf16[3,3,3,128,128]{4,3,2,1,0:T(8,128)(2,1)S(1)}, bf16[3,3,3,128,128]{4,3,2,1,0:T(8,128)(2,1)}, u32[]{:S(2)}) copy-start(bf16[3,3,3,128,128]{4,3,2,1,0:T(8,128)(2,1)} %param.13) | copy-start | bytes 2654212
  18.6 5.5 %copy-start.1 = (bf16[4,2,4,64,128]{4,3,2,1,0:T(8,128)(2,1)S(1)}, bf16[4,2,4,64,128]{4,3,2,1,0:T(8,128)(2,1)}, u32[]{:S(2)}) copy-start(bf16[4,2,4,64,128]{4,3,2,1,0:T(8,128)(2,1)} %frs.1) | copy-start | bytes 1572868
  18.6 5.5 %copy-start.2 = (bf16[4,2,2,64,128]{4,3,2,1,0:T(8,128)(2,1)S(1)}, bf16[4,2,2,64,128]{4,3,2,1,0:T(8,128)(2,1)}, u32[]{:S(2)}) copy-start(bf16[4,2,2,64,128]{4,3,2,1,0:T(8,128)(2,1)} %has.1) | copy-start | bytes 786436
  18.6 5.5 %copy-start.3 = (bf16[4,1,4,64,128]{4,3,2,1,0:T(8,128)(2,1)S(1)}, bf16[4,1,4,64,128]{4,3,2,1,0:T(8,128)(2,1)}, u32[]{:S(2)}) copy-start(bf16[4,1,4,64,128]{4,3,2,1,0:T(8,128)(2,1)} %cos.1) | copy-start | bytes 786436
  18.6 5.5 %copy-start.4 = (bf16[2,128,128]{2,1,0:T(8,128)(2,1)S(1)}, bf16[2,128,128]{2,1,0:T(8,128)(2,1)}, u32[]{:S(2)}) copy-start(bf16[2,128,128]{2,1,0:T(8,128)(2,1)} %sw.1) | copy-start | bytes 196612
  18.6 5.5 %copy-start.5 = (f32[128]{0:T(128)S(1)}, f32[128]{0:T(128)}, u32[]{:S(2)}) copy-start(f32[128]{0:T(128)} %param.14) | copy-start | bytes 1540
  18.6 5.5 %copy-start.6 = (f32[128]{0:T(128)S(1)}, f32[128]{0:T(128)}, u32[]{:S(2)}) copy-start(f32[128]{0:T(128)} %param.16) | copy-start | bytes 1540
  22.7 1.4 %collective-permute-start.4 = (bf16[6,64,128]{2,1,0:T(8,128)(2,1)S(1)}, bf16[6,64,128]{2,1,0:T(8,128)(2,1)S(1)}, u32[]{:S(2)}, u32[]{:S(2)}) collective-permute-start(bf16[6,64,128]{2,1,0:T(8,128)(2,1)S(1)} %fusion.2), channel_id=1, source_target_pairs={{0,1},{1,0},{2,3},{3,2},{4,5},{5,4},{6,7},{7,6},{8,9},{9,8},{10,11... | collective-permute-start | bytes 294920 | tf_op jit(solution)/shard_map/ppermute | solution.py:354
  27.0 1.9 %collective-permute-start.5 = (bf16[1920,128]{1,0:T(8,128)(2,1)S(1)}, bf16[1920,128]{1,0:T(8,128)(2,1)S(1)}, u32[]{:S(2)}, u32[]{:S(2)}) collective-permute-start(bf16[1920,128]{1,0:T(8,128)(2,1)S(1)} %get-tuple-element.56), channel_id=1, source_target_pairs={{0,1},{1,0},{2,3},{3,2},{4,5},{5,4},{6,7},{7,6},{8,9},{9,8},{10,11... | collective-permute-start | bytes 1474568 | tf_op jit(solution)/shard_map/ppermute | solution.py:354
  29.6 6.2 %collective-permute-start.7 = (bf16[480,128]{1,0:T(8,128)(2,1)S(1)}, bf16[480,128]{1,0:T(8,128)(2,1)S(1)}, u32[]{:S(2)}, u32[]{:S(2)}) collective-permute-start(bf16[480,128]{1,0:T(8,128)(2,1)S(1)} %get-tuple-element.59), channel_id=1, source_target_pairs={{0,2},{1,3},{2,0},{3,1},{4,6},{5,7},{6,4},{7,5},{8,10},{9,11},{10,... | collective-permute-start | bytes 368648 | tf_op jit(solution)/shard_map/ppermute | solution.py:354
  30.2 9.2 %collective-permute-start.6 = (bf16[480,128]{1,0:T(8,128)(2,1)S(1)}, bf16[480,128]{1,0:T(8,128)(2,1)S(1)}, u32[]{:S(2)}, u32[]{:S(2)}) collective-permute-start(bf16[480,128]{1,0:T(8,128)(2,1)S(1)} %get-tuple-element.58), channel_id=1, source_target_pairs={{0,2},{1,3},{2,0},{3,1},{4,6},{5,7},{6,4},{7,5},{8,10},{9,11},{10,... | collective-permute-start | bytes 368648 | tf_op jit(solution)/shard_map/ppermute | solution.py:354
  31.6 7.7 %collective-permute-start.8 = (bf16[512,128]{1,0:T(8,128)(2,1)S(1)}, bf16[512,128]{1,0:T(8,128)(2,1)S(1)}, u32[]{:S(2)}, u32[]{:S(2)}) collective-permute-start(bf16[512,128]{1,0:T(8,128)(2,1)S(1)} %shard_map.141), channel_id=1, source_target_pairs={{0,1},{1,0},{2,3},{3,2},{4,5},{5,4},{6,7},{7,6},{8,9},{9,8},{10,11... | collective-permute-start | bytes 393224 | tf_op jit(solution)/shard_map/ppermute | solution.py:354
  35.8 12.4 %collective-permute-start.10 = (bf16[240,128]{1,0:T(8,128)(2,1)S(1)}, bf16[240,128]{1,0:T(8,128)(2,1)S(1)}, u32[]{:S(2)}, u32[]{:S(2)}) collective-permute-start(bf16[240,128]{1,0:T(8,128)(2,1)S(1)} %get-tuple-element.80), channel_id=1, source_target_pairs={{0,12},{1,13},{2,14},{3,15},{4,8},{5,9},{6,10},{7,11},{8,4},{9,5},... | collective-permute-start | bytes 184328 | tf_op jit(solution)/shard_map/ppermute | solution.py:354
  39.3 8.8 %collective-permute-start.11 = (bf16[240,128]{1,0:T(8,128)(2,1)S(1)}, bf16[240,128]{1,0:T(8,128)(2,1)S(1)}, u32[]{:S(2)}, u32[]{:S(2)}) collective-permute-start(bf16[240,128]{1,0:T(8,128)(2,1)S(1)} %get-tuple-element.81), channel_id=1, source_target_pairs={{0,8},{1,9},{2,10},{3,11},{4,12},{5,13},{6,14},{7,15},{8,0},{9,1},... | collective-permute-start | bytes 184328 | tf_op jit(solution)/shard_map/ppermute | solution.py:354
  39.4 4.3 %collective-permute-start.9 = (bf16[256,128]{1,0:T(8,128)(2,1)S(1)}, bf16[256,128]{1,0:T(8,128)(2,1)S(1)}, u32[]{:S(2)}, u32[]{:S(2)}) collective-permute-start(bf16[256,128]{1,0:T(8,128)(2,1)S(1)} %fusion.11), channel_id=1, source_target_pairs={{0,2},{1,3},{2,0},{3,1},{4,6},{5,7},{6,4},{7,5},{8,10},{9,11},{10,... | collective-permute-start | bytes 196616 | tf_op jit(solution)/shard_map/ppermute | solution.py:354
  40.0 8.2 %collective-permute-start.12 = (bf16[240,128]{1,0:T(8,128)(2,1)S(1)}, bf16[240,128]{1,0:T(8,128)(2,1)S(1)}, u32[]{:S(2)}, u32[]{:S(2)}) collective-permute-start(bf16[240,128]{1,0:T(8,128)(2,1)S(1)} %add_convert_fusion.1), channel_id=1, source_target_pairs={{0,4},{1,5},{2,6},{3,7},{4,0},{5,1},{6,2},{7,3},{8,12},{9,13},{10,... | collective-permute-start | bytes 184328 | tf_op jit(solution)/shard_map/ppermute | solution.py:354
  43.8 9.5 %collective-permute-start.19 = (bf16[128,128]{1,0:T(8,128)(2,1)S(1)}, bf16[128,128]{1,0:T(8,128)(2,1)S(1)}, u32[]{:S(2)}, u32[]{:S(2)}) collective-permute-start(bf16[128,128]{1,0:T(8,128)(2,1)S(1)} %fusion.18), channel_id=1, source_target_pairs={{0,4},{1,5},{2,6},{3,7},{4,0},{5,1},{6,2},{7,3},{8,12},{9,13},{10,... | collective-permute-start | bytes 98312 | tf_op jit(solution)/shard_map/ppermute | solution.py:354
  48.3 13.4 %collective-permute-start.16 = (bf16[240,128]{1,0:T(8,128)(2,1)S(1)}, bf16[240,128]{1,0:T(8,128)(2,1)S(1)}, u32[]{:S(2)}, u32[]{:S(2)}) collective-permute-start(bf16[240,128]{1,0:T(8,128)(2,1)S(1)} %get-tuple-element.79), channel_id=1, source_target_pairs={{0,2},{1,3},{2,0},{3,1},{4,6},{5,7},{6,4},{7,5},{8,10},{9,11},{10,... | collective-permute-start | bytes 184328 | tf_op jit(solution)/shard_map/ppermute | solution.py:354
  48.9 10.6 %collective-permute-start.15 = (bf16[240,128]{1,0:T(8,128)(2,1)S(1)}, bf16[240,128]{1,0:T(8,128)(2,1)S(1)}, u32[]{:S(2)}, u32[]{:S(2)}) collective-permute-start(bf16[240,128]{1,0:T(8,128)(2,1)S(1)} %get-tuple-element.79), channel_id=1, source_target_pairs={{0,12},{1,13},{2,14},{3,15},{4,8},{5,9},{6,10},{7,11},{8,4},{9,5},... | collective-permute-start | bytes 184328 | tf_op jit(solution)/shard_map/ppermute | solution.py:354
  52.3 7.2 %collective-permute-start.14 = (bf16[240,128]{1,0:T(8,128)(2,1)S(1)}, bf16[240,128]{1,0:T(8,128)(2,1)S(1)}, u32[]{:S(2)}, u32[]{:S(2)}) collective-permute-start(bf16[240,128]{1,0:T(8,128)(2,1)S(1)} %get-tuple-element.79), channel_id=1, source_target_pairs={{0,8},{1,9},{2,10},{3,11},{4,12},{5,13},{6,14},{7,15},{8,0},{9,1},... | collective-permute-start | bytes 184328 | tf_op jit(solution)/shard_map/ppermute | solution.py:354
  52.3 4.3 %collective-permute-start.13 = (bf16[240,128]{1,0:T(8,128)(2,1)S(1)}, bf16[240,128]{1,0:T(8,128)(2,1)S(1)}, u32[]{:S(2)}, u32[]{:S(2)}) collective-permute-start(bf16[240,128]{1,0:T(8,128)(2,1)S(1)} %get-tuple-element.79), channel_id=1, source_target_pairs={{0,4},{1,5},{2,6},{3,7},{4,0},{5,1},{6,2},{7,3},{8,12},{9,13},{10,... | collective-permute-start | bytes 184328 | tf_op jit(solution)/shard_map/ppermute | solution.py:354
  56.6 5.0 %collective-permute-start.20 = (bf16[128,128]{1,0:T(8,128)(2,1)S(1)}, bf16[128,128]{1,0:T(8,128)(2,1)S(1)}, u32[]{:S(2)}, u32[]{:S(2)}) collective-permute-start(bf16[128,128]{1,0:T(8,128)(2,1)S(1)} %fusion.19), channel_id=1, source_target_pairs={{0,8},{1,9},{2,10},{3,11},{4,12},{5,13},{6,14},{7,15},{8,0},{9,1},... | collective-permute-start | bytes 98312 | tf_op jit(solution)/shard_map/ppermute | solution.py:354
  59.5 6.2 %collective-permute-start.18 = (bf16[480,128]{1,0:T(8,128)(2,1)S(1)}, bf16[480,128]{1,0:T(8,128)(2,1)S(1)}, u32[]{:S(2)}, u32[]{:S(2)}) collective-permute-start(bf16[480,128]{1,0:T(8,128)(2,1)S(1)} %pad_maximum_fusion), channel_id=1, source_target_pairs={{0,2},{1,3},{2,0},{3,1},{4,6},{5,7},{6,4},{7,5},{8,10},{9,11},{10,... | collective-permute-start | bytes 368648 | tf_op jit(solution)/shard_map/ppermute | solution.py:354
  61.0 4.2 %collective-permute-start.17 = (bf16[240,128]{1,0:T(8,128)(2,1)S(1)}, bf16[240,128]{1,0:T(8,128)(2,1)S(1)}, u32[]{:S(2)}, u32[]{:S(2)}) collective-permute-start(bf16[240,128]{1,0:T(8,128)(2,1)S(1)} %collective-permute-done.13), channel_id=1, source_target_pairs={{0,2},{1,3},{2,0},{3,1},{4,6},{5,7},{6,4},{7,5},{8,10},{9,11},{10,... | collective-permute-start | bytes 184328 | tf_op jit(solution)/shard_map/ppermute | solution.py:354
  61.7 4.0 %collective-permute-start.21 = (bf16[128,128]{1,0:T(8,128)(2,1)S(1)}, bf16[128,128]{1,0:T(8,128)(2,1)S(1)}, u32[]{:S(2)}, u32[]{:S(2)}) collective-permute-start(bf16[128,128]{1,0:T(8,128)(2,1)S(1)} %fusion.17), channel_id=1, source_target_pairs={{0,2},{1,3},{2,0},{3,1},{4,6},{5,7},{6,4},{7,5},{8,10},{9,11},{10,... | collective-permute-start | bytes 98312 | tf_op jit(solution)/shard_map/ppermute | solution.py:354
  65.8 2.0 %collective-permute-start.22 = (bf16[2176,128]{1,0:T(8,128)(2,1)S(1)}, bf16[2176,128]{1,0:T(8,128)(2,1)S(1)}, u32[]{:S(2)}, u32[]{:S(2)}) collective-permute-start(bf16[2176,128]{1,0:T(8,128)(2,1)S(1)} %fusion.10.mine), channel_id=1, source_target_pairs={{0,1},{1,0},{2,3},{3,2},{4,5},{5,4},{6,7},{7,6},{8,9},{9,8},{10,11... | collective-permute-start | bytes 1671176 | tf_op jit(solution)/shard_map/ppermute | solution.py:354

commit v9 on v8

--- a/solution.py
+++ b/solution.py
@@ -567,6 +567,7 @@
 
     chip_first = ordered(core, by_half(core, first_grad), by_half(core, got_first))
     beside_first = _xor(chip_first, 2, n, axis)
+    got_far = _after(got_far, chip_first)
 
     def summed(j, came):
         i = j % 2
@@ -576,8 +577,8 @@
     got_near = _after(got_near, outs[3], outs[2])
     outs[1] = summed(1, got_near).astype(BF)
     gots = {j: _xor(outs[j], 4 * j, n, axis) for j in (3, 2, 1)}
-    beside_first = _after(beside_first, outs[1])
     lead = ordered(pair, by_half(pair, chip_first), by_half(pair, beside_first))
+    near_lead = _xor(lead, 4, n, axis)
     grad = _call(
         _back_kernel,
         jax.ShapeDtypeStruct((slots, 2, h, w, c), F32),
@@ -586,7 +587,7 @@
         flops=1,
         moved=1,
         room=24,
-    )(_after(sc, outs[1], lead), g0, g1, wt)
+    )(_after(sc, outs[1]), g0, g1, wt)
     mine = summed(0, _after(got_near, grad))
     for j in (3, 2):
         mine = mine + gots[j].astype(F32)
@@ -600,10 +601,9 @@
     x_own = _xor(mine, 2, n, axis)
     x_near = _xor(others[1], 2, n, axis)
     x_far = _xor(jnp.concatenate([others[2], others[3]], axis=0), 2, n, axis)
-    beyond, k = jnp.full_like(lead, EMPTY_GRAD), 4
+    beyond = by(index & 4, near_lead, jnp.full_like(lead, EMPTY_GRAD))
+    lead, k = _after(ordered(index & 4, lead, near_lead), mine), 8
     while k < n:
-        if k == 8:
-            lead = _after(lead, others[1])
         came = _xor(lead, k, n, axis)
         beyond = by(index & k, _first_live(beyond, came), beyond)
         if 2 * k < n:

time: 70.2 us -> 68.5 us (0.976)
  starting transfers between devices: 27.8 us -> 26.9 us
  waiting for transfers between devices: 18.2 us -> 17.4 us
    ppermute x23, starting transfers between devices: 27.8 us -> 26.9 us  [_xor(): return lax.ppermute(x, axis, [(i, i ^ k) for i in range(n)])]
    ppermute x23, waiting for transfers between devices: 18.2 us -> 17.4 us  [_xor(): return lax.ppermute(x, axis, [(i, i ^ k) for i in range(n)])]
  transfers between devices with their start and end apart: 23 -> 23, of which waited for: 10 -> 11; matrix products, arithmetic and copies ran while one was open for 3% -> 3% of each run, Pallas kernels for 20% -> 20%
where the time goes in v9:
time: 68.5 us; the launch traced here: 68.3 us
  starting transfers between devices  26.9 us (39%)
  Pallas kernels  20.3 us (30%)
  waiting for transfers between devices  17.4 us (25%)
  other arithmetic  1.94 us (3%)
  between operations  1.59 us (2%)
    ppermute x23, starting transfers between devices, _xor(): return lax.ppermute(x, axis, [(i, i ^ k) for i in range(n)])  26.9 us
    ppermute x23, waiting for transfers between devices, _xor(): return lax.ppermute(x, axis, [(i, i ^ k) for i in range(n)])  17.4 us
    pallas_call x1, Pallas kernels, early_conv(): _call(_early_conv_kernel, [jax.ShapeDtypeStruct(wide, F32), jax.ShapeDtyp...  4.41 us
    pallas_call x1, Pallas kernels, early_sums(): _call(_early_sums_kernel, jax.ShapeDtypeStruct((rows, c), F32), [_SMEM, _...  3.94 us
    pallas_call x1, Pallas kernels, body(): _call(_back_kernel, jax.ShapeDtypeStruct((slots, 2, h, w, c), F32), [_SME...  3.39 us
    pallas_call x1, Pallas kernels, body(): _call(_late_kernel, [jax.ShapeDtypeStruct((h, w, c), BF), jax.ShapeDtypeS...  2.78 us
    pallas_call x1, Pallas kernels, body(): _call(_final_kernel, [jax.ShapeDtypeStruct((27 * c, c), F32), jax.ShapeDt...  2.18 us
  transfers between devices with their start and end apart: 23, of which 11 were waited for; matrix products, arithmetic and copies ran while one was open for 3% of the time, Pallas kernels for 20%

profile of v9, /device:TPU:0, one launch (start us, length us, event | category | flops | bytes accessed | tf_op | source)
XLA Modules:
  0.0 68.3 jit_solution(14930243456526837452)
XLA Ops:
  1.3 1.0 %shard_map.136 = bf16[12,64,128]{2,1,0:T(8,128)(2,1)S(1)} custom-call(s32[1]{0:T(128)S(6)} %copy.23.sc, bf16[4,2,4,64,128]{4,3,2,1,0:T(8,128)(2,1)} %frs.1, bf16[4,2,2,64,128]{4,3,2,1,0:T(8,128)(2,1)} %has.1), custom_call_target="tpu_custom_call" | custom-call | tf_op jit(solution)/shard_map/pallas_call | solution.py:435
  2.2 0.5 collective-permute-start
  2.8 0.7 %pad_add_fusion.sc = s32[7]{0:T(128)S(1)} fusion(s32[1]{0:T(128)} %bitcast.1, s32[1]{0:T(128)} %bitcast, s32[4]{0:T(128)} %param.11, s32[1]{0:T(128)S(6)} %copy.23.sc), kind=kLoop, calls=%fused_computation.62 | loop fusion | flops 21 | bytes 56 | tf_op jit(solution)/shard_map/concatenate | solution.py:417
  3.5 0.3 collective-permute-done
  3.9 2.9 %collective-permute-start.1 = (bf16[6,64,128]{2,1,0:T(8,128)(2,1)S(1)}, bf16[6,64,128]{2,1,0:T(8,128)(2,1)S(1)}, u32[]{:S(2)}, u32[]{:S(2)}) collective-permute-start(bf16[6,64,128]{2,1,0:T(8,128)(2,1)S(1)} %fusion.7), channel_id=1, source_target_pairs={{0,2},{1,3},{2,0},{3,1},{4,6},{5,7},{6,4},{7,5},{8,10},{9,11},{10,... | collective-permute-start | bytes 294920 | tf_op jit(solution)/shard_map/ppermute | solution.py:354
  6.8 4.4 %shard_map.137 = (f32[768,256]{1,0:T(8,128)S(1)}, bf16[768,128]{1,0:T(8,128)(2,1)S(1)}, bf16[2,128,128]{2,1,0:T(8,128)(2,1)S(1)}, f32[1,128]{1,0:T(1,128)S(1)}) custom-call(s32[7]{0:T(128)S(1)} %pad_add_fusion.sc, bf16[4,2,4,64,128]{4,3,2,1,0:T(8,128)(2,1)} %frs.1, bf16[4,2,2,64,128]{4,3,2,1,0:T(8,128)(2,1)} %has.1, bf16[4,1,4,64,128]{4,3,2,1,0:T(8,128)(2,1)} %cos.1, ...), custom_call_target="tpu_custom_call" | custom-call | flops 1811939328 | bytes 4194304 | tf_op jit(solution)/shard_map/pallas_call | solution.py:462
  11.2 0.0 collective-permute-done.1
  11.2 1.6 %collective-permute-start.2 = (bf16[6,64,128]{2,1,0:T(8,128)(2,1)S(1)}, bf16[6,64,128]{2,1,0:T(8,128)(2,1)S(1)}, u32[]{:S(2)}, u32[]{:S(2)}) collective-permute-start(bf16[6,64,128]{2,1,0:T(8,128)(2,1)S(1)} %fusion.8), channel_id=1, source_target_pairs={{0,4},{1,5},{2,6},{3,7},{4,0},{5,1},{6,2},{7,3},{8,12},{9,13},{10,... | collective-permute-start | bytes 294920 | tf_op jit(solution)/shard_map/ppermute | solution.py:354
  12.9 1.0 %shard_map.138 = (bf16[3,4,64,128]{3,2,1,0:T(8,128)(2,1)S(1)}, bf16[768,256]{1,0:T(8,128)(2,1)S(1)}, bf16[768,256]{1,0:T(8,128)(2,1)S(1)}) custom-call(s32[7]{0:T(128)S(1)} %pad_add_fusion.sc, f32[768,256]{1,0:T(8,128)S(1)} %get-tuple-element.40.pre_ref, bf16[768,128]{1,0:T(8,128)(2,1)S(1)} %get-tuple-element.43.gout_ref, ...), custom_call_target="tpu_custom_call" | custom-call | bytes 2097152 | tf_op jit(solution)/shard_map/pallas_call | solution.py:480
  13.9 2.1 %collective-permute-done.2 = bf16[6,64,128]{2,1,0:T(8,128)(2,1)S(1)} collective-permute-done((bf16[6,64,128]{2,1,0:T(8,128)(2,1)S(1)}, bf16[6,64,128]{2,1,0:T(8,128)(2,1)S(1)}, u32[]{:S(2)}, u32[]{:S(2)}) %collective-permute-start.2) | collective-permute-done | bytes 98336 | tf_op jit(solution)/shard_map/ppermute | solution.py:354
  16.0 2.7 %collective-permute-start.3 = (bf16[6,64,128]{2,1,0:T(8,128)(2,1)S(1)}, bf16[6,64,128]{2,1,0:T(8,128)(2,1)S(1)}, u32[]{:S(2)}, u32[]{:S(2)}) collective-permute-start(bf16[6,64,128]{2,1,0:T(8,128)(2,1)S(1)} %fusion.9), channel_id=1, source_target_pairs={{0,8},{1,9},{2,10},{3,11},{4,12},{5,13},{6,14},{7,15},{8,0},{9,1},... | collective-permute-start | bytes 294920 | tf_op jit(solution)/shard_map/ppermute | solution.py:354
  18.6 0.0 copy-start.4
  18.6 0.0 copy-start.5
  18.6 0.0 copy-start.6
  18.7 3.9 %shard_map.139.early = f32[3840,128]{1,0:T(8,128)S(1)} custom-call(s32[7]{0:T(128)S(1)} %pad_add_fusion.sc, bf16[4,2,4,64,128]{4,3,2,1,0:T(8,128)(2,1)} %frs.1, bf16[4,2,2,64,128]{4,3,2,1,0:T(8,128)(2,1)} %has.1, bf16[768,256]{1,0:T(8,128)(2,1)S(1)} %get-tuple-element.46.g_ref.g1, bf16[768,256]{1,0:T(8,128)(2,1)S(1)} %get-tuple-element.49.hid_ref, ...), custom_call_target="tpu_custom_call" | custom-call | flops 1811939328 | bytes 4194304 | tf_op jit(solution)/shard_map/pallas_call | solution.py:496
  22.6 0.0 collective-permute-done.3
  22.7 0.1 collective-permute-start.4
  22.8 1.3 %collective-permute-done.4 = bf16[6,64,128]{2,1,0:T(8,128)(2,1)S(1)} collective-permute-done((bf16[6,64,128]{2,1,0:T(8,128)(2,1)S(1)}, bf16[6,64,128]{2,1,0:T(8,128)(2,1)S(1)}, u32[]{:S(2)}, u32[]{:S(2)}) %collective-permute-start.4) | collective-permute-done | bytes 98336 | tf_op jit(solution)/shard_map/ppermute | solution.py:354
  24.1 0.1 compare_select_fusion.tail
  24.1 0.0 copy-done
  24.1 0.0 copy-done.1
  24.2 2.8 %shard_map.140 = (bf16[4,64,128]{2,1,0:T(8,128)(2,1)S(1)}, bf16[256,256]{1,0:T(8,128)(2,1)S(1)}, bf16[1920,128]{1,0:T(8,128)(2,1)S(1)}, f32[1920,128]{1,0:T(8,128)S(1)}) custom-call(s32[7]{0:T(128)S(1)} %pad_add_fusion.sc, bf16[4,2,4,64,128]{4,3,2,1,0:T(8,128)(2,1)S(1)} %copy-done.1, bf16[4,2,2,64,128]{4,3,2,1,0:T(8,128)(2,1)S(1)} %copy-done.2, ...), custom_call_target="tpu_custom_call" | custom-call | flops 1207959552 | bytes 6291456 | tf_op jit(solution)/shard_map/pallas_call | solution.py:515
  27.0 0.2 collective-permute-start.5
  27.2 1.1 %shard_map.141 = bf16[512,128]{1,0:T(8,128)(2,1)S(1)} custom-call(s32[7]{0:T(128)S(1)} %pad_add_fusion.sc, bf16[256,256]{1,0:T(8,128)(2,1)S(1)} %get-tuple-element.54.g_ref.g0, bf16[27,128,128]{2,1,0:T(8,128)(2,1)S(1)} %bitcast.16), custom_call_target="tpu_custom_call" | custom-call | flops 301989888 | bytes 1048576 | tf_op jit(solution)/shard_map/pallas_call | solution.py:533
  28.3 0.7 collective-permute-done.5.got
  28.9 0.6 shard_map.142
  29.5 0.2 collective-permute-start.8
  29.8 0.6 collective-permute-start.6
  30.3 1.5 %collective-permute-start.7 = (bf16[480,128]{1,0:T(8,128)(2,1)S(1)}, bf16[480,128]{1,0:T(8,128)(2,1)S(1)}, u32[]{:S(2)}, u32[]{:S(2)}) collective-permute-start(bf16[480,128]{1,0:T(8,128)(2,1)S(1)} %get-tuple-element.59), channel_id=1, source_target_pairs={{0,2},{1,3},{2,0},{3,1},{4,6},{5,7},{6,4},{7,5},{8,10},{9,11},{10,... | collective-permute-start | bytes 368648 | tf_op jit(solution)/shard_map/ppermute | solution.py:354
  31.8 0.0 collective-permute-done.8.got
  31.8 0.1 fusion.11
  31.9 6.1 %collective-permute-done.7 = bf16[480,128]{1,0:T(8,128)(2,1)S(1)} collective-permute-done((bf16[480,128]{1,0:T(8,128)(2,1)S(1)}, bf16[480,128]{1,0:T(8,128)(2,1)S(1)}, u32[]{:S(2)}, u32[]{:S(2)}) %collective-permute-start.7) | collective-permute-done | bytes 122912 | tf_op jit(solution)/shard_map/ppermute | solution.py:354
  38.0 3.5 %collective-permute-start.9 = (bf16[240,128]{1,0:T(8,128)(2,1)S(1)}, bf16[240,128]{1,0:T(8,128)(2,1)S(1)}, u32[]{:S(2)}, u32[]{:S(2)}) collective-permute-start(bf16[240,128]{1,0:T(8,128)(2,1)S(1)} %get-tuple-element.80), channel_id=1, source_target_pairs={{0,12},{1,13},{2,14},{3,15},{4,8},{5,9},{6,10},{7,11},{8,4},{9,5},... | collective-permute-start | bytes 184328 | tf_op jit(solution)/shard_map/ppermute | solution.py:354
  41.5 0.0 collective-permute-start.10
  41.5 0.0 collective-permute-done.6
  41.6 1.0 %collective-permute-start.11 = (bf16[240,128]{1,0:T(8,128)(2,1)S(1)}, bf16[240,128]{1,0:T(8,128)(2,1)S(1)}, u32[]{:S(2)}, u32[]{:S(2)}) collective-permute-start(bf16[240,128]{1,0:T(8,128)(2,1)S(1)} %add_convert_fusion.1), channel_id=1, source_target_pairs={{0,4},{1,5},{2,6},{3,7},{4,0},{5,1},{6,2},{7,3},{8,12},{9,13},{10,... | collective-permute-start | bytes 184328 | tf_op jit(solution)/shard_map/ppermute | solution.py:354
  42.6 0.5 collective-permute-start.18
  43.1 3.4 %shard_map.143.grad = f32[4,2,4,64,128]{4,3,2,1,0:T(8,128)S(1)} custom-call(s32[7]{0:T(128)S(1)} %pad_add_fusion.sc, bf16[256,256]{1,0:T(8,128)(2,1)S(1)} %get-tuple-element.54.g_ref.g0, bf16[768,256]{1,0:T(8,128)(2,1)S(1)} %get-tuple-element.46.g_ref.g1, bf16[27,128,128]{2,1,0:T(8,128)(2,1)S(1)} %bitcast.17), custom_call_target="tpu_custom_call" | custom-call | flops 1 | bytes 1 | tf_op jit(solution)/shard_map/pallas_call | solution.py:582
  46.5 0.0 collective-permute-done.9
  46.5 0.2 collective-permute-done.10
  46.8 0.2 collective-permute-done.11
  47.0 0.0 collective-permute-done.18
  47.0 1.0 %collective-permute-start.19 = (bf16[128,128]{1,0:T(8,128)(2,1)S(1)}, bf16[128,128]{1,0:T(8,128)(2,1)S(1)}, u32[]{:S(2)}, u32[]{:S(2)}) collective-permute-start(bf16[128,128]{1,0:T(8,128)(2,1)S(1)} %fusion.18), channel_id=1, source_target_pairs={{0,4},{1,5},{2,6},{3,7},{4,0},{5,1},{6,2},{7,3},{8,12},{9,13},{10,... | collective-permute-start | bytes 98312 | tf_op jit(solution)/shard_map/ppermute | solution.py:354
  48.0 1.3 %collective-permute-start.15 = (bf16[240,128]{1,0:T(8,128)(2,1)S(1)}, bf16[240,128]{1,0:T(8,128)(2,1)S(1)}, u32[]{:S(2)}, u32[]{:S(2)}) collective-permute-start(bf16[240,128]{1,0:T(8,128)(2,1)S(1)} %get-tuple-element.79), channel_id=1, source_target_pairs={{0,2},{1,3},{2,0},{3,1},{4,6},{5,7},{6,4},{7,5},{8,10},{9,11},{10,... | collective-permute-start | bytes 184328 | tf_op jit(solution)/shard_map/ppermute | solution.py:354
  49.4 2.4 %collective-permute-start.14 = (bf16[240,128]{1,0:T(8,128)(2,1)S(1)}, bf16[240,128]{1,0:T(8,128)(2,1)S(1)}, u32[]{:S(2)}, u32[]{:S(2)}) collective-permute-start(bf16[240,128]{1,0:T(8,128)(2,1)S(1)} %get-tuple-element.79), channel_id=1, source_target_pairs={{0,12},{1,13},{2,14},{3,15},{4,8},{5,9},{6,10},{7,11},{8,4},{9,5},... | collective-permute-start | bytes 184328 | tf_op jit(solution)/shard_map/ppermute | solution.py:354
  51.8 0.5 collective-permute-start.13
  52.3 1.5 %collective-permute-start.12 = (bf16[240,128]{1,0:T(8,128)(2,1)S(1)}, bf16[240,128]{1,0:T(8,128)(2,1)S(1)}, u32[]{:S(2)}, u32[]{:S(2)}) collective-permute-start(bf16[240,128]{1,0:T(8,128)(2,1)S(1)} %get-tuple-element.79), channel_id=1, source_target_pairs={{0,4},{1,5},{2,6},{3,7},{4,0},{5,1},{6,2},{7,3},{8,12},{9,13},{10,... | collective-permute-start | bytes 184328 | tf_op jit(solution)/shard_map/ppermute | solution.py:354
  53.8 0.0 collective-permute-done.19
  53.8 2.1 %collective-permute-start.20 = (bf16[128,128]{1,0:T(8,128)(2,1)S(1)}, bf16[128,128]{1,0:T(8,128)(2,1)S(1)}, u32[]{:S(2)}, u32[]{:S(2)}) collective-permute-start(bf16[128,128]{1,0:T(8,128)(2,1)S(1)} %fusion.19), channel_id=1, source_target_pairs={{0,8},{1,9},{2,10},{3,11},{4,12},{5,13},{6,14},{7,15},{8,0},{9,1},... | collective-permute-start | bytes 98312 | tf_op jit(solution)/shard_map/ppermute | solution.py:354
  55.9 0.1 collective-permute-done.14
  55.9 1.8 %collective-permute-done.13 = bf16[240,128]{1,0:T(8,128)(2,1)S(1)} collective-permute-done((bf16[240,128]{1,0:T(8,128)(2,1)S(1)}, bf16[240,128]{1,0:T(8,128)(2,1)S(1)}, u32[]{:S(2)}, u32[]{:S(2)}) %collective-permute-start.13) | collective-permute-done | bytes 61472 | tf_op jit(solution)/shard_map/ppermute | solution.py:354
  57.8 0.6 collective-permute-start.17
  58.4 0.0 collective-permute-done.12
  58.4 1.5 %collective-permute-start.16 = (bf16[240,128]{1,0:T(8,128)(2,1)S(1)}, bf16[240,128]{1,0:T(8,128)(2,1)S(1)}, u32[]{:S(2)}, u32[]{:S(2)}) collective-permute-start(bf16[240,128]{1,0:T(8,128)(2,1)S(1)} %collective-permute-done.12), channel_id=1, source_target_pairs={{0,2},{1,3},{2,0},{3,1},{4,6},{5,7},{6,4},{7,5},{8,10},{9,11},{10,... | collective-permute-start | bytes 184328 | tf_op jit(solution)/shard_map/ppermute | solution.py:354
  60.0 0.0 collective-permute-done.20
  60.0 0.6 collective-permute-start.21
  60.6 0.0 collective-permute-done.15
  60.6 3.3 %collective-permute-done.21 = bf16[128,128]{1,0:T(8,128)(2,1)S(1)} collective-permute-done((bf16[128,128]{1,0:T(8,128)(2,1)S(1)}, bf16[128,128]{1,0:T(8,128)(2,1)S(1)}, u32[]{:S(2)}, u32[]{:S(2)}) %collective-permute-start.21) | collective-permute-done | bytes 32800 | tf_op jit(solution)/shard_map/ppermute | solution.py:354
  64.0 0.0 collective-permute-done.16
  64.0 0.0 collective-permute-done.17
  64.1 0.1 collective-permute-start.22
  64.2 0.7 %maximum_bitcast_fusion = bf16[4,1,4,64,128]{4,3,2,1,0:T(8,128)(2,1)} fusion(bf16[3,4,64,128]{3,2,1,0:T(8,128)(2,1)S(1)} %get-tuple-element.52, bf16[1,4,64,128]{3,2,1,0:T(8,128)(2,1)S(1)} %bitcast.18), kind=kLoop, calls=%fused_computation.11 | loop fusion | flops 131072 | bytes 524288
  64.9 1.2 %collective-permute-done.22.other = bf16[2176,128]{1,0:T(8,128)(2,1)S(1)} collective-permute-done((bf16[2176,128]{1,0:T(8,128)(2,1)S(1)}, bf16[2176,128]{1,0:T(8,128)(2,1)S(1)}, u32[]{:S(2)}, u32[]{:S(2)}) %collective-permute-start.22) | collective-permute-done | bytes 557088 | tf_op jit(solution)/shard_map/ppermute | solution.py:354
  66.1 2.2 %shard_map.144 = (f32[3456,128]{1,0:T(8,128)}, f32[256,128]{1,0:T(8,128)}, f32[1,128]{1,0:T(1,128)}, f32[1,128]{1,0:T(1,128)}, bf16[4,2,4,64,128]{4,3,2,1,0:T(8,128)(2,1)}) custom-call(s32[7]{0:T(128)S(1)} %pad_add_fusion.sc, bf16[2176,128]{1,0:T(8,128)(2,1)S(1)} %fusion.10.mine, bf16[2176,128]{1,0:T(8,128)(2,1)S(1)} %collective-permute-done.22.other, ...), custom_call_target="tpu_custom_call" | custom-call | tf_op jit(solution)/shard_map/pallas_call | solution.py:619
  (31 shorter events, 0.5 us)
Async XLA Ops:
  2.2 1.6 %collective-permute-start = (bf16[12,64,128]{2,1,0:T(8,128)(2,1)S(1)}, bf16[12,64,128]{2,1,0:T(8,128)(2,1)S(1)}, u32[]{:S(2)}, u32[]{:S(2)}) collective-permute-start(bf16[12,64,128]{2,1,0:T(8,128)(2,1)S(1)} %shard_map.136), channel_id=1, source_target_pairs={{0,1},{1,0},{2,3},{3,2},{4,5},{5,4},{6,7},{7,6},{8,9},{9,8},{10,11... | collective-permute-start | bytes 589832 | tf_op jit(solution)/shard_map/ppermute | solution.py:354
  3.9 7.3 %collective-permute-start.1 = (bf16[6,64,128]{2,1,0:T(8,128)(2,1)S(1)}, bf16[6,64,128]{2,1,0:T(8,128)(2,1)S(1)}, u32[]{:S(2)}, u32[]{:S(2)}) collective-permute-start(bf16[6,64,128]{2,1,0:T(8,128)(2,1)S(1)} %fusion.7), channel_id=1, source_target_pairs={{0,2},{1,3},{2,0},{3,1},{4,6},{5,7},{6,4},{7,5},{8,10},{9,11},{10,... | collective-permute-start | bytes 294920 | tf_op jit(solution)/shard_map/ppermute | solution.py:354
  11.2 4.7 %collective-permute-start.2 = (bf16[6,64,128]{2,1,0:T(8,128)(2,1)S(1)}, bf16[6,64,128]{2,1,0:T(8,128)(2,1)S(1)}, u32[]{:S(2)}, u32[]{:S(2)}) collective-permute-start(bf16[6,64,128]{2,1,0:T(8,128)(2,1)S(1)} %fusion.8), channel_id=1, source_target_pairs={{0,4},{1,5},{2,6},{3,7},{4,0},{5,1},{6,2},{7,3},{8,12},{9,13},{10,... | collective-permute-start | bytes 294920 | tf_op jit(solution)/shard_map/ppermute | solution.py:354
  16.0 6.7 %collective-permute-start.3 = (bf16[6,64,128]{2,1,0:T(8,128)(2,1)S(1)}, bf16[6,64,128]{2,1,0:T(8,128)(2,1)S(1)}, u32[]{:S(2)}, u32[]{:S(2)}) collective-permute-start(bf16[6,64,128]{2,1,0:T(8,128)(2,1)S(1)} %fusion.9), channel_id=1, source_target_pairs={{0,8},{1,9},{2,10},{3,11},{4,12},{5,13},{6,14},{7,15},{8,0},{9,1},... | collective-permute-start | bytes 294920 | tf_op jit(solution)/shard_map/ppermute | solution.py:354
  18.6 5.5 %copy-start = (bf16[3,3,3,128,128]{4,3,2,1,0:T(8,128)(2,1)S(1)}, bf16[3,3,3,128,128]{4,3,2,1,0:T(8,128)(2,1)}, u32[]{:S(2)}) copy-start(bf16[3,3,3,128,128]{4,3,2,1,0:T(8,128)(2,1)} %param.13) | copy-start | bytes 2654212
  18.6 5.5 %copy-start.1 = (bf16[4,2,4,64,128]{4,3,2,1,0:T(8,128)(2,1)S(1)}, bf16[4,2,4,64,128]{4,3,2,1,0:T(8,128)(2,1)}, u32[]{:S(2)}) copy-start(bf16[4,2,4,64,128]{4,3,2,1,0:T(8,128)(2,1)} %frs.1) | copy-start | bytes 1572868
  18.6 5.5 %copy-start.2 = (bf16[4,2,2,64,128]{4,3,2,1,0:T(8,128)(2,1)S(1)}, bf16[4,2,2,64,128]{4,3,2,1,0:T(8,128)(2,1)}, u32[]{:S(2)}) copy-start(bf16[4,2,2,64,128]{4,3,2,1,0:T(8,128)(2,1)} %has.1) | copy-start | bytes 786436
  18.6 5.5 %copy-start.3 = (bf16[4,1,4,64,128]{4,3,2,1,0:T(8,128)(2,1)S(1)}, bf16[4,1,4,64,128]{4,3,2,1,0:T(8,128)(2,1)}, u32[]{:S(2)}) copy-start(bf16[4,1,4,64,128]{4,3,2,1,0:T(8,128)(2,1)} %cos.1) | copy-start | bytes 786436
  18.6 5.5 %copy-start.4 = (bf16[2,128,128]{2,1,0:T(8,128)(2,1)S(1)}, bf16[2,128,128]{2,1,0:T(8,128)(2,1)}, u32[]{:S(2)}) copy-start(bf16[2,128,128]{2,1,0:T(8,128)(2,1)} %sw.1) | copy-start | bytes 196612
  18.6 5.5 %copy-start.5 = (f32[128]{0:T(128)S(1)}, f32[128]{0:T(128)}, u32[]{:S(2)}) copy-start(f32[128]{0:T(128)} %param.14) | copy-start | bytes 1540
  18.6 5.5 %copy-start.6 = (f32[128]{0:T(128)S(1)}, f32[128]{0:T(128)}, u32[]{:S(2)}) copy-start(f32[128]{0:T(128)} %param.16) | copy-start | bytes 1540
  22.7 1.4 %collective-permute-start.4 = (bf16[6,64,128]{2,1,0:T(8,128)(2,1)S(1)}, bf16[6,64,128]{2,1,0:T(8,128)(2,1)S(1)}, u32[]{:S(2)}, u32[]{:S(2)}) collective-permute-start(bf16[6,64,128]{2,1,0:T(8,128)(2,1)S(1)} %fusion.2), channel_id=1, source_target_pairs={{0,1},{1,0},{2,3},{3,2},{4,5},{5,4},{6,7},{7,6},{8,9},{9,8},{10,11... | collective-permute-start | bytes 294920 | tf_op jit(solution)/shard_map/ppermute | solution.py:354
  27.0 1.9 %collective-permute-start.5 = (bf16[1920,128]{1,0:T(8,128)(2,1)S(1)}, bf16[1920,128]{1,0:T(8,128)(2,1)S(1)}, u32[]{:S(2)}, u32[]{:S(2)}) collective-permute-start(bf16[1920,128]{1,0:T(8,128)(2,1)S(1)} %get-tuple-element.56), channel_id=1, source_target_pairs={{0,1},{1,0},{2,3},{3,2},{4,5},{5,4},{6,7},{7,6},{8,9},{9,8},{10,11... | collective-permute-start | bytes 1474568 | tf_op jit(solution)/shard_map/ppermute | solution.py:354
  29.5 2.3 %collective-permute-start.8 = (bf16[512,128]{1,0:T(8,128)(2,1)S(1)}, bf16[512,128]{1,0:T(8,128)(2,1)S(1)}, u32[]{:S(2)}, u32[]{:S(2)}) collective-permute-start(bf16[512,128]{1,0:T(8,128)(2,1)S(1)} %shard_map.141), channel_id=1, source_target_pairs={{0,1},{1,0},{2,3},{3,2},{4,5},{5,4},{6,7},{7,6},{8,9},{9,8},{10,11... | collective-permute-start | bytes 393224 | tf_op jit(solution)/shard_map/ppermute | solution.py:354
  29.8 11.8 %collective-permute-start.6 = (bf16[480,128]{1,0:T(8,128)(2,1)S(1)}, bf16[480,128]{1,0:T(8,128)(2,1)S(1)}, u32[]{:S(2)}, u32[]{:S(2)}) collective-permute-start(bf16[480,128]{1,0:T(8,128)(2,1)S(1)} %get-tuple-element.58), channel_id=1, source_target_pairs={{0,2},{1,3},{2,0},{3,1},{4,6},{5,7},{6,4},{7,5},{8,10},{9,11},{10,... | collective-permute-start | bytes 368648 | tf_op jit(solution)/shard_map/ppermute | solution.py:354
  30.3 7.7 %collective-permute-start.7 = (bf16[480,128]{1,0:T(8,128)(2,1)S(1)}, bf16[480,128]{1,0:T(8,128)(2,1)S(1)}, u32[]{:S(2)}, u32[]{:S(2)}) collective-permute-start(bf16[480,128]{1,0:T(8,128)(2,1)S(1)} %get-tuple-element.59), channel_id=1, source_target_pairs={{0,2},{1,3},{2,0},{3,1},{4,6},{5,7},{6,4},{7,5},{8,10},{9,11},{10,... | collective-permute-start | bytes 368648 | tf_op jit(solution)/shard_map/ppermute | solution.py:354
  38.0 8.5 %collective-permute-start.9 = (bf16[240,128]{1,0:T(8,128)(2,1)S(1)}, bf16[240,128]{1,0:T(8,128)(2,1)S(1)}, u32[]{:S(2)}, u32[]{:S(2)}) collective-permute-start(bf16[240,128]{1,0:T(8,128)(2,1)S(1)} %get-tuple-element.80), channel_id=1, source_target_pairs={{0,12},{1,13},{2,14},{3,15},{4,8},{5,9},{6,10},{7,11},{8,4},{9,5},... | collective-permute-start | bytes 184328 | tf_op jit(solution)/shard_map/ppermute | solution.py:354
  41.5 5.2 %collective-permute-start.10 = (bf16[240,128]{1,0:T(8,128)(2,1)S(1)}, bf16[240,128]{1,0:T(8,128)(2,1)S(1)}, u32[]{:S(2)}, u32[]{:S(2)}) collective-permute-start(bf16[240,128]{1,0:T(8,128)(2,1)S(1)} %get-tuple-element.81), channel_id=1, source_target_pairs={{0,8},{1,9},{2,10},{3,11},{4,12},{5,13},{6,14},{7,15},{8,0},{9,1},... | collective-permute-start | bytes 184328 | tf_op jit(solution)/shard_map/ppermute | solution.py:354
  41.6 5.4 %collective-permute-start.11 = (bf16[240,128]{1,0:T(8,128)(2,1)S(1)}, bf16[240,128]{1,0:T(8,128)(2,1)S(1)}, u32[]{:S(2)}, u32[]{:S(2)}) collective-permute-start(bf16[240,128]{1,0:T(8,128)(2,1)S(1)} %add_convert_fusion.1), channel_id=1, source_target_pairs={{0,4},{1,5},{2,6},{3,7},{4,0},{5,1},{6,2},{7,3},{8,12},{9,13},{10,... | collective-permute-start | bytes 184328 | tf_op jit(solution)/shard_map/ppermute | solution.py:354
  42.6 4.4 %collective-permute-start.18 = (bf16[256,128]{1,0:T(8,128)(2,1)S(1)}, bf16[256,128]{1,0:T(8,128)(2,1)S(1)}, u32[]{:S(2)}, u32[]{:S(2)}) collective-permute-start(bf16[256,128]{1,0:T(8,128)(2,1)S(1)} %fusion.11), channel_id=1, source_target_pairs={{0,2},{1,3},{2,0},{3,1},{4,6},{5,7},{6,4},{7,5},{8,10},{9,11},{10,... | collective-permute-start | bytes 196616 | tf_op jit(solution)/shard_map/ppermute | solution.py:354
  47.0 6.8 %collective-permute-start.19 = (bf16[128,128]{1,0:T(8,128)(2,1)S(1)}, bf16[128,128]{1,0:T(8,128)(2,1)S(1)}, u32[]{:S(2)}, u32[]{:S(2)}) collective-permute-start(bf16[128,128]{1,0:T(8,128)(2,1)S(1)} %fusion.18), channel_id=1, source_target_pairs={{0,4},{1,5},{2,6},{3,7},{4,0},{5,1},{6,2},{7,3},{8,12},{9,13},{10,... | collective-permute-start | bytes 98312 | tf_op jit(solution)/shard_map/ppermute | solution.py:354
  48.0 12.6 %collective-permute-start.15 = (bf16[240,128]{1,0:T(8,128)(2,1)S(1)}, bf16[240,128]{1,0:T(8,128)(2,1)S(1)}, u32[]{:S(2)}, u32[]{:S(2)}) collective-permute-start(bf16[240,128]{1,0:T(8,128)(2,1)S(1)} %get-tuple-element.79), channel_id=1, source_target_pairs={{0,2},{1,3},{2,0},{3,1},{4,6},{5,7},{6,4},{7,5},{8,10},{9,11},{10,... | collective-permute-start | bytes 184328 | tf_op jit(solution)/shard_map/ppermute | solution.py:354
  49.4 6.6 %collective-permute-start.14 = (bf16[240,128]{1,0:T(8,128)(2,1)S(1)}, bf16[240,128]{1,0:T(8,128)(2,1)S(1)}, u32[]{:S(2)}, u32[]{:S(2)}) collective-permute-start(bf16[240,128]{1,0:T(8,128)(2,1)S(1)} %get-tuple-element.79), channel_id=1, source_target_pairs={{0,12},{1,13},{2,14},{3,15},{4,8},{5,9},{6,10},{7,11},{8,4},{9,5},... | collective-permute-start | bytes 184328 | tf_op jit(solution)/shard_map/ppermute | solution.py:354
  51.8 6.0 %collective-permute-start.13 = (bf16[240,128]{1,0:T(8,128)(2,1)S(1)}, bf16[240,128]{1,0:T(8,128)(2,1)S(1)}, u32[]{:S(2)}, u32[]{:S(2)}) collective-permute-start(bf16[240,128]{1,0:T(8,128)(2,1)S(1)} %get-tuple-element.79), channel_id=1, source_target_pairs={{0,8},{1,9},{2,10},{3,11},{4,12},{5,13},{6,14},{7,15},{8,0},{9,1},... | collective-permute-start | bytes 184328 | tf_op jit(solution)/shard_map/ppermute | solution.py:354
  52.3 6.2 %collective-permute-start.12 = (bf16[240,128]{1,0:T(8,128)(2,1)S(1)}, bf16[240,128]{1,0:T(8,128)(2,1)S(1)}, u32[]{:S(2)}, u32[]{:S(2)}) collective-permute-start(bf16[240,128]{1,0:T(8,128)(2,1)S(1)} %get-tuple-element.79), channel_id=1, source_target_pairs={{0,4},{1,5},{2,6},{3,7},{4,0},{5,1},{6,2},{7,3},{8,12},{9,13},{10,... | collective-permute-start | bytes 184328 | tf_op jit(solution)/shard_map/ppermute | solution.py:354
  53.8 6.2 %collective-permute-start.20 = (bf16[128,128]{1,0:T(8,128)(2,1)S(1)}, bf16[128,128]{1,0:T(8,128)(2,1)S(1)}, u32[]{:S(2)}, u32[]{:S(2)}) collective-permute-start(bf16[128,128]{1,0:T(8,128)(2,1)S(1)} %fusion.19), channel_id=1, source_target_pairs={{0,8},{1,9},{2,10},{3,11},{4,12},{5,13},{6,14},{7,15},{8,0},{9,1},... | collective-permute-start | bytes 98312 | tf_op jit(solution)/shard_map/ppermute | solution.py:354
  57.8 6.2 %collective-permute-start.17 = (bf16[480,128]{1,0:T(8,128)(2,1)S(1)}, bf16[480,128]{1,0:T(8,128)(2,1)S(1)}, u32[]{:S(2)}, u32[]{:S(2)}) collective-permute-start(bf16[480,128]{1,0:T(8,128)(2,1)S(1)} %pad_maximum_fusion), channel_id=1, source_target_pairs={{0,2},{1,3},{2,0},{3,1},{4,6},{5,7},{6,4},{7,5},{8,10},{9,11},{10,... | collective-permute-start | bytes 368648 | tf_op jit(solution)/shard_map/ppermute | solution.py:354
  58.4 5.6 %collective-permute-start.16 = (bf16[240,128]{1,0:T(8,128)(2,1)S(1)}, bf16[240,128]{1,0:T(8,128)(2,1)S(1)}, u32[]{:S(2)}, u32[]{:S(2)}) collective-permute-start(bf16[240,128]{1,0:T(8,128)(2,1)S(1)} %collective-permute-done.12), channel_id=1, source_target_pairs={{0,2},{1,3},{2,0},{3,1},{4,6},{5,7},{6,4},{7,5},{8,10},{9,11},{10,... | collective-permute-start | bytes 184328 | tf_op jit(solution)/shard_map/ppermute | solution.py:354
  60.0 4.0 %collective-permute-start.21 = (bf16[128,128]{1,0:T(8,128)(2,1)S(1)}, bf16[128,128]{1,0:T(8,128)(2,1)S(1)}, u32[]{:S(2)}, u32[]{:S(2)}) collective-permute-start(bf16[128,128]{1,0:T(8,128)(2,1)S(1)} %fusion.17), channel_id=1, source_target_pairs={{0,2},{1,3},{2,0},{3,1},{4,6},{5,7},{6,4},{7,5},{8,10},{9,11},{10,... | collective-permute-start | bytes 98312 | tf_op jit(solution)/shard_map/ppermute | solution.py:354
  64.1 2.0 %collective-permute-start.22 = (bf16[2176,128]{1,0:T(8,128)(2,1)S(1)}, bf16[2176,128]{1,0:T(8,128)(2,1)S(1)}, u32[]{:S(2)}, u32[]{:S(2)}) collective-permute-start(bf16[2176,128]{1,0:T(8,128)(2,1)S(1)} %fusion.10.mine), channel_id=1, source_target_pairs={{0,1},{1,0},{2,3},{3,2},{4,5},{5,4},{6,7},{7,6},{8,9},{9,8},{10,11... | collective-permute-start | bytes 1671176 | tf_op jit(solution)/shard_map/ppermute | solution.py:354

commit v10 on v9

--- a/solution.py
+++ b/solution.py
@@ -17,13 +17,14 @@
 _HBM = pl.BlockSpec(memory_space=pltpu.HBM)
 
 
-def _call(kernel, out_shape, in_specs, scratch=(), flops=0, moved=0, room=16, grid=()):
+def _call(kernel, out_shape, in_specs, scratch=(), flops=0, moved=0, room=16, grid=(), outs=None, alias=None):
     return pl.pallas_call(
         kernel,
         out_shape=out_shape,
         grid=grid,
         in_specs=in_specs,
-        out_specs=jax.tree.map(lambda _: _VMEM, out_shape),
+        out_specs=jax.tree.map(lambda _: _VMEM, out_shape) if outs is None else outs,
+        input_output_aliases=alias or {},
         scratch_shapes=list(scratch),
         compiler_params=pltpu.CompilerParams(vmem_limit_bytes=room << 20),
         cost_estimate=pl.CostEstimate(flops=flops, bytes_accessed=moved, transcendentals=0),
@@ -260,7 +261,7 @@
         out[t * h * w : (t + 1) * h * w] = back[:, t * c : (t + 1) * c]
 
 
-def _back_kernel(sc, g0, g1, w_ref, out_ref, xk):
+def _back_kernel(sc, g0, g1, w_ref, out_ref, last_ref, xk, all_ref):
     slots, _, h, w, c = out_ref.shape
     m = h * w
     zero = jnp.zeros((1, w, c), BF)
@@ -282,7 +283,10 @@
                 _put(xk, (s - 1, f + 2), slice(1, 1 + h), jnp.where(on, v, jnp.zeros_like(v)))
     out = _conv_back(xk, w_ref, h)
     for f in range(2):
-        out_ref[:, f] = out[:, f * c : (f + 1) * c].reshape(slots, h, w, c)
+        lanes = slice(f * c, (f + 1) * c)
+        out_ref[:, f] = out[:, lanes].astype(BF).reshape(slots, h, w, c)
+        all_ref[:, f] = out[:, lanes].reshape(slots, h, w, c)
+    last_ref[...] = all_ref[jnp.maximum(sc[0] - 1, 0)]
 
 
 def _first_live(a, b):
@@ -294,21 +298,34 @@
     return lax.shift_right_logical(chip, 1), lax.bitwise_and(chip, 1), core
 
 
-def _across_x_kernel(sc, keep, got, send_far, send_near, kept):
-    z, x, _ = _place(sc)
-    half = keep.shape[0]
+def _piece(sc, keep, got, j, side):
     blocks = 4
-    rows = half // (2 * blocks)
-
-    def piece(j, side):
-        p = 2 * lax.bitwise_xor(z, j) + side
-        at = pl.ds(pl.multiple_of(p * rows, 16), rows)
-        return keep[at] + got[at].astype(F32)
-
-    for j in range(blocks):
-        kept[j * rows : (j + 1) * rows] = piece(j, x)
-        send, i = (send_near, j) if j < 2 else (send_far, j - 2)
-        send[i * rows : (i + 1) * rows] = piece(j, 1 - x).astype(BF)
+    rows = keep.shape[0] // (2 * blocks)
+    p = 2 * lax.bitwise_xor(_place(sc)[0], j) + side
+    at = pl.ds(pl.multiple_of(p * rows, 16), rows)
+    return keep[at] + got[at].astype(F32)
+
+
+def _far_kernel(sc, keep, got, send, kept):
+    x = _place(sc)[1]
+    rows = kept.shape[0] // 2
+    for i, j in enumerate((2, 3)):
+        kept[i * rows : (i + 1) * rows] = _piece(sc, keep, got, j, x)
+        send[i * rows : (i + 1) * rows] = _piece(sc, keep, got, j, 1 - x).astype(BF)
+
+
+def _near_kernel(sc, keep, got, mine, theirs, send, kept, chip_first):
+    _, x, core = _place(sc)
+    rows = kept.shape[0] // 2
+    for j in (0, 1):
+        kept[j * rows : (j + 1) * rows] = _piece(sc, keep, got, j, x)
+        send[j * rows : (j + 1) * rows] = _piece(sc, keep, got, j, 1 - x).astype(BF)
+    part = mine.shape[0] // 2
+    at = pl.ds(pl.multiple_of(core * part, 16), part)
+    a, b = mine[at], theirs[at]
+    first = jnp.where(core == 0, _first_live(a, b), _first_live(b, a))
+    chip_first[...] = first
+    send[2 * rows :] = first
 
 
 def _tail_kernel(sc, fr, ha, out):
@@ -319,35 +336,54 @@
         out[rows] = jnp.where(live, v, jnp.full_like(v, EMPTY_FRAME))
 
 
-def _final_kernel(sc, mine, other, got, grad, cw, sw, cb, sb, fg, acc):
+def _final_kernel(
+    sc, mine, other, beside, last, fg_in, cw, sw, cb, sb, fg, acc, newest, sems
+):
+    del fg_in
     c = mine.shape[1]
     half = acc.shape[0] // 2
     z, x, core = _place(sc)
     blocks = 4
     rows = half // (2 * blocks)
+    n27, n29 = 27 * c, 29 * c
+    low = [pltpu.make_async_copy(acc.at[:half], cw.at[:half], sems.at[0])]
+    high = [
+        pltpu.make_async_copy(acc.at[half:n27], cw.at[half:n27], sems.at[1]),
+        pltpu.make_async_copy(acc.at[n27:n29], sw, sems.at[2]),
+    ]
     for ref, at_core in ((mine, core), (other, 1 - core)):
         for k in range(2 * blocks):
             side = x if k < blocks else 1 - x
             chip = 2 * lax.bitwise_xor(z, k % blocks) + side
             at = pl.multiple_of(at_core * half + chip * rows, 16)
             acc[pl.ds(at, rows)] = ref[k * rows : (k + 1) * rows].astype(F32)
-    n27, n29 = 27 * c, 29 * c
-    cw[...] = acc[:n27]
-    sw[...] = acc[n27:n29]
+
+        @pl.when(at_core == 0)
+        def _():
+            for copy in low:
+                copy.start()
+
+        @pl.when(at_core != 0)
+        def _():
+            for copy in high:
+                copy.start()
+
+    frames, h, w, _ = last.shape
+    part = mine.shape[0] - half
+    for f in range(frames):
+        a, b = mine[half:].astype(F32), other[half:].astype(F32)
+        beyond = jnp.where(core == 0, a, b) if f == 0 else jnp.where(core == 0, b, a)
+        near = beside[f * part : (f + 1) * part].astype(F32)
+        came = jnp.where(core == 0, _first_live(near, beyond), beyond)
+        came = jnp.where(came < EMPTY_GRAD / 2, came, jnp.zeros_like(came)).reshape(h, w, c)
+        came = jnp.where(sc[0] > 0, came, jnp.zeros_like(came))
+        newest[f] = (last[f] + came).astype(BF)
+    slab = pltpu.make_async_copy(newest, fg.at[jnp.maximum(sc[0] - 1, 0)], sems.at[3])
+    slab.start()
     cb[...] = acc[n29 : n29 + 1]
     sb[...] = acc[n29 + 1 : n29 + 2]
-    slots, frames, h, w, _ = grad.shape
-    part = mine.shape[0] - half
-    for s in range(slots):
-        here = sc[0] - 1 == s
-        for f in range(frames):
-            low = f == 0
-            a, b = mine[half:].astype(F32), other[half:].astype(F32)
-            beyond = jnp.where(core == 0, a, b) if low else jnp.where(core == 0, b, a)
-            beside = got[f * part : (f + 1) * part].astype(F32)
-            came = jnp.where(core == 0, _first_live(beside, beyond), beyond)
-            came = jnp.where(came < EMPTY_GRAD / 2, came, jnp.zeros_like(came)).reshape(h, w, c)
-            fg[s, f] = (grad[s, f] + jnp.where(here, came, jnp.zeros_like(came))).astype(BF)
+    for copy in (*low, *high, slab):
+        copy.wait()
 
 
 def _xor(x, k, n, axis):
@@ -539,20 +575,26 @@
         moved=1 << 20,
         room=8,
     )(sc, g0, wt)
-    keep = _after(keep, first_grad)
-    send_far, send_near, kept = _call(
-        _across_x_kernel,
-        [
-            jax.ShapeDtypeStruct((2 * piece, c), BF),
-            jax.ShapeDtypeStruct((2 * piece, c), BF),
-            jax.ShapeDtypeStruct((blocks * piece, c), F32),
-        ],
-        [_SMEM] + [_VMEM] * 2,
-        room=8,
-    )(sc, keep, got)
+    got_first = _xor(first_grad, 1, n, axis)
+    pieces = (
+        jax.ShapeDtypeStruct((2 * piece, c), BF),
+        jax.ShapeDtypeStruct((2 * piece, c), F32),
+    )
+    send_far, kept_far = _call(_far_kernel, pieces, [_SMEM] + [_VMEM] * 2, room=4)(
+        sc, _after(keep, first_grad), got
+    )
     got_far = _xor(send_far, 2, n, axis)
+    send_near, kept_near, chip_first = _call(
+        _near_kernel,
+        (
+            jax.ShapeDtypeStruct((2 * piece + carried // 2, c), BF),
+            pieces[1],
+            jax.ShapeDtypeStruct((carried // 2, c), BF),
+        ),
+        [_SMEM] + [_VMEM] * 4,
+        room=4,
+    )(sc, _after(keep, kept_far), got, first_grad, got_first)
     got_near = _xor(send_near, 2, n, axis)
-    got_first = _xor(_after(first_grad, kept), 1, n, axis)
     core, pair = index & 1, (index >> 1) & 1
 
     def by(bit, a, b):
@@ -565,30 +607,34 @@
     def ordered(bit, ours, theirs):
         return by(bit, _first_live(ours, theirs), _first_live(theirs, ours))
 
-    chip_first = ordered(core, by_half(core, first_grad), by_half(core, got_first))
-    beside_first = _xor(chip_first, 2, n, axis)
-    got_far = _after(got_far, chip_first)
-
     def summed(j, came):
-        i = j % 2
-        return kept[j * piece : (j + 1) * piece] + came[i * piece : (i + 1) * piece].astype(F32)
+        kept = kept_near if j < 2 else kept_far
+        rows = slice((j % 2) * piece, (j % 2 + 1) * piece)
+        return kept[rows] + came[rows].astype(F32)
 
     outs = {j: summed(j, got_far).astype(BF) for j in (3, 2)}
     got_near = _after(got_near, outs[3], outs[2])
     outs[1] = summed(1, got_near).astype(BF)
     gots = {j: _xor(outs[j], 4 * j, n, axis) for j in (3, 2, 1)}
+    beside_first = got_near[2 * piece :]
     lead = ordered(pair, by_half(pair, chip_first), by_half(pair, beside_first))
     near_lead = _xor(lead, 4, n, axis)
-    grad = _call(
+    slabs, last = _call(
         _back_kernel,
-        jax.ShapeDtypeStruct((slots, 2, h, w, c), F32),
+        [
+            jax.ShapeDtypeStruct((slots, 2, h, w, c), BF),
+            jax.ShapeDtypeStruct((2, h, w, c), F32),
+        ],
         [_SMEM] + [_VMEM] * 3,
-        [pltpu.VMEM((3, slots, 4, h + 2, w, c), BF)],
+        [
+            pltpu.VMEM((3, slots, 4, h + 2, w, c), BF),
+            pltpu.VMEM((slots, 2, h, w, c), F32),
+        ],
         flops=1,
         moved=1,
         room=24,
-    )(_after(sc, outs[1]), g0, g1, wt)
-    mine = summed(0, _after(got_near, grad))
+    )(_after(sc, outs[1], lead), g0, g1, wt)
+    mine = summed(0, _after(got_near, last))
     for j in (3, 2):
         mine = mine + gots[j].astype(F32)
     gots[1] = _after(gots[1], mine)
@@ -602,7 +648,7 @@
     x_near = _xor(others[1], 2, n, axis)
     x_far = _xor(jnp.concatenate([others[2], others[3]], axis=0), 2, n, axis)
     beyond = by(index & 4, near_lead, jnp.full_like(lead, EMPTY_GRAD))
-    lead, k = _after(ordered(index & 4, lead, near_lead), mine), 8
+    lead, k = _after(ordered(index & 4, lead, near_lead), x_own), 8
     while k < n:
         came = _xor(lead, k, n, axis)
         beyond = by(index & k, _first_live(beyond, came), beyond)
@@ -625,10 +671,16 @@
             jax.ShapeDtypeStruct((1, c), F32),
             jax.ShapeDtypeStruct((slots, 2, h, w, c), BF),
         ],
-        [_SMEM] + [_VMEM] * 4,
-        [pltpu.VMEM((rows, c), F32)],
+        [_SMEM] + [_VMEM] * 4 + [_HBM],
+        [
+            pltpu.VMEM((rows, c), F32),
+            pltpu.VMEM((2, h, w, c), BF),
+            pltpu.SemaphoreType.DMA((4,)),
+        ],
         room=12,
-    )(sc, ours, other, got_first, grad)
+        outs=[_HBM, _HBM, _VMEM, _VMEM, _HBM],
+        alias={5: 4},
+    )(sc, ours, other, got_first, last, pltpu.with_memory_space_constraint(slabs, pltpu.HBM))
     latents = jnp.concatenate([lat0[None], lat1], axis=0)[:, None]
     return (
         latents,

time: 68.5 us -> 67.5 us (0.985)
  waiting for transfers between devices: 17.4 us -> 12.2 us
  Pallas kernels: 20.3 us -> 22.6 us
  other arithmetic: 1.94 us -> 2.74 us
    ppermute x23 -> x22, waiting for transfers between devices: 17.4 us -> 12.2 us  [_xor(): return lax.ppermute(x, axis, [(i, i ^ k) for i in range(n)])]
    pallas_call x2 -> x3, Pallas kernels: 4.03 us -> 6.06 us  [the longest x1 4.19 us: body(): _call(_back_kernel, [jax.ShapeDtypeStruct((slots, 2, h, w, c), BF), jax.S...]
    convert_element_type x1, other arithmetic: 0.03 us -> 0.89 us  [body(): outs = {j: summed(j, got_far).astype(BF) for j in (3, 2)}]
    ppermute x23 -> x22, starting transfers between devices: 26.9 us -> 27.1 us  [_xor(): return lax.ppermute(x, axis, [(i, i ^ k) for i in range(n)])]
  transfers between devices with their start and end apart: 23 -> 22, of which waited for: 11 -> 10; matrix products, arithmetic and copies ran while one was open for 3% -> 4% of each run, Pallas kernels for 20% -> 24%
where the time goes in v10:
time: 67.5 us; the launch traced here: 67.2 us
  starting transfers between devices  27.1 us (40%)
  Pallas kernels  22.6 us (33%)
  waiting for transfers between devices  12.2 us (18%)
  other arithmetic  2.74 us (4%)
  between operations  1.76 us (3%)
  local copies, waits for them, and re-layouts  0.8 us (1%)
    ppermute x22, starting transfers between devices, _xor(): return lax.ppermute(x, axis, [(i, i ^ k) for i in range(n)])  27.1 us
    ppermute x22, waiting for transfers between devices, _xor(): return lax.ppermute(x, axis, [(i, i ^ k) for i in range(n)])  12.2 us
    pallas_call x1, Pallas kernels, early_conv(): _call(_early_conv_kernel, [jax.ShapeDtypeStruct(wide, F32), jax.ShapeDtyp...  4.41 us
    pallas_call x1, Pallas kernels, body(): _call(_back_kernel, [jax.ShapeDtypeStruct((slots, 2, h, w, c), BF), jax.S...  4.19 us
    pallas_call x1, Pallas kernels, early_sums(): _call(_early_sums_kernel, jax.ShapeDtypeStruct((rows, c), F32), [_SMEM, _...  3.94 us
    pallas_call x1, Pallas kernels, body(): _call(_late_kernel, [jax.ShapeDtypeStruct((h, w, c), BF), jax.ShapeDtypeS...  2.81 us
    pallas_call x1, Pallas kernels, body(): _call(_final_kernel, [jax.ShapeDtypeStruct((27 * c, c), F32), jax.ShapeDt...  2.44 us
  transfers between devices with their start and end apart: 22, of which 10 were waited for; matrix products, arithmetic and copies ran while one was open for 4% of the time, Pallas kernels for 24%

profile of v10, /device:TPU:0, one launch (start us, length us, event | category | flops | bytes accessed | tf_op | source)
XLA Modules:
  0.0 67.2 jit_solution(1385706252078886355)
XLA Ops:
  1.3 1.0 %shard_map.136 = bf16[12,64,128]{2,1,0:T(8,128)(2,1)S(1)} custom-call(s32[1]{0:T(128)S(6)} %copy.25.sc, bf16[4,2,4,64,128]{4,3,2,1,0:T(8,128)(2,1)} %frs.1, bf16[4,2,2,64,128]{4,3,2,1,0:T(8,128)(2,1)} %has.1), custom_call_target="tpu_custom_call" | custom-call | tf_op jit(solution)/shard_map/pallas_call | solution.py:471
  2.2 0.5 collective-permute-start
  2.8 0.7 %pad_add_fusion.sc = s32[7]{0:T(128)S(1)} fusion(s32[1]{0:T(128)} %bitcast.1, s32[1]{0:T(128)} %bitcast, s32[4]{0:T(128)} %param.11, s32[1]{0:T(128)S(6)} %copy.25.sc), kind=kLoop, calls=%fused_computation.53 | loop fusion | flops 21 | bytes 56 | tf_op jit(solution)/shard_map/concatenate | solution.py:453
  3.5 0.3 collective-permute-done
  3.9 2.9 %collective-permute-start.1 = (bf16[6,64,128]{2,1,0:T(8,128)(2,1)S(1)}, bf16[6,64,128]{2,1,0:T(8,128)(2,1)S(1)}, u32[]{:S(2)}, u32[]{:S(2)}) collective-permute-start(bf16[6,64,128]{2,1,0:T(8,128)(2,1)S(1)} %fusion.5), channel_id=1, source_target_pairs={{0,2},{1,3},{2,0},{3,1},{4,6},{5,7},{6,4},{7,5},{8,10},{9,11},{10,... | collective-permute-start | bytes 294920 | tf_op jit(solution)/shard_map/ppermute | solution.py:390
  6.8 4.4 %shard_map.137 = (f32[768,256]{1,0:T(8,128)S(1)}, bf16[768,128]{1,0:T(8,128)(2,1)S(1)}, bf16[2,128,128]{2,1,0:T(8,128)(2,1)S(1)}, f32[1,128]{1,0:T(1,128)S(1)}) custom-call(s32[7]{0:T(128)S(1)} %pad_add_fusion.sc, bf16[4,2,4,64,128]{4,3,2,1,0:T(8,128)(2,1)} %frs.1, bf16[4,2,2,64,128]{4,3,2,1,0:T(8,128)(2,1)} %has.1, bf16[4,1,4,64,128]{4,3,2,1,0:T(8,128)(2,1)} %cos.1, ...), custom_call_target="tpu_custom_call" | custom-call | flops 1811939328 | bytes 4194304 | tf_op jit(solution)/shard_map/pallas_call | solution.py:498
  11.2 0.0 collective-permute-done.1
  11.2 1.6 %collective-permute-start.2 = (bf16[6,64,128]{2,1,0:T(8,128)(2,1)S(1)}, bf16[6,64,128]{2,1,0:T(8,128)(2,1)S(1)}, u32[]{:S(2)}, u32[]{:S(2)}) collective-permute-start(bf16[6,64,128]{2,1,0:T(8,128)(2,1)S(1)} %fusion.6), channel_id=1, source_target_pairs={{0,4},{1,5},{2,6},{3,7},{4,0},{5,1},{6,2},{7,3},{8,12},{9,13},{10,... | collective-permute-start | bytes 294920 | tf_op jit(solution)/shard_map/ppermute | solution.py:390
  12.9 1.0 %shard_map.138 = (bf16[3,4,64,128]{3,2,1,0:T(8,128)(2,1)S(1)}, bf16[768,256]{1,0:T(8,128)(2,1)S(1)}, bf16[768,256]{1,0:T(8,128)(2,1)S(1)}) custom-call(s32[7]{0:T(128)S(1)} %pad_add_fusion.sc, f32[768,256]{1,0:T(8,128)S(1)} %get-tuple-element.43.pre_ref, bf16[768,128]{1,0:T(8,128)(2,1)S(1)} %get-tuple-element.46.gout_ref, ...), custom_call_target="tpu_custom_call" | custom-call | bytes 2097152 | tf_op jit(solution)/shard_map/pallas_call | solution.py:516
  13.9 0.0 copy-start.3
  13.9 0.7 copy-done.3
  14.5 1.4 %collective-permute-done.2 = bf16[6,64,128]{2,1,0:T(8,128)(2,1)S(1)} collective-permute-done((bf16[6,64,128]{2,1,0:T(8,128)(2,1)S(1)}, bf16[6,64,128]{2,1,0:T(8,128)(2,1)S(1)}, u32[]{:S(2)}, u32[]{:S(2)}) %collective-permute-start.2) | collective-permute-done | bytes 98336 | tf_op jit(solution)/shard_map/ppermute | solution.py:390
  15.9 2.7 %collective-permute-start.3 = (bf16[6,64,128]{2,1,0:T(8,128)(2,1)S(1)}, bf16[6,64,128]{2,1,0:T(8,128)(2,1)S(1)}, u32[]{:S(2)}, u32[]{:S(2)}) collective-permute-start(bf16[6,64,128]{2,1,0:T(8,128)(2,1)S(1)} %fusion.7), channel_id=1, source_target_pairs={{0,8},{1,9},{2,10},{3,11},{4,12},{5,13},{6,14},{7,15},{8,0},{9,1},... | collective-permute-start | bytes 294920 | tf_op jit(solution)/shard_map/ppermute | solution.py:390
  18.6 0.0 copy-start.6
  18.6 0.0 copy-start.7
  18.6 0.0 copy-start.8
  18.7 3.9 %shard_map.139.early = f32[3840,128]{1,0:T(8,128)S(1)} custom-call(s32[7]{0:T(128)S(1)} %pad_add_fusion.sc, bf16[4,2,4,64,128]{4,3,2,1,0:T(8,128)(2,1)} %frs.1, bf16[4,2,2,64,128]{4,3,2,1,0:T(8,128)(2,1)} %has.1, bf16[768,256]{1,0:T(8,128)(2,1)S(1)} %get-tuple-element.49.g_ref.g1, bf16[768,256]{1,0:T(8,128)(2,1)S(1)} %get-tuple-element.52.hid_ref, ...), custom_call_target="tpu_custom_call" | custom-call | flops 1811939328 | bytes 4194304 | tf_op jit(solution)/shard_map/pallas_call | solution.py:532
  22.6 0.0 collective-permute-done.3
  22.7 0.1 collective-permute-start.4
  22.7 1.3 %collective-permute-done.4 = bf16[6,64,128]{2,1,0:T(8,128)(2,1)S(1)} collective-permute-done((bf16[6,64,128]{2,1,0:T(8,128)(2,1)S(1)}, bf16[6,64,128]{2,1,0:T(8,128)(2,1)S(1)}, u32[]{:S(2)}, u32[]{:S(2)}) %collective-permute-start.4) | collective-permute-done | bytes 98336 | tf_op jit(solution)/shard_map/ppermute | solution.py:390
  24.1 0.0 copy-done
  24.1 0.0 copy-done.1
  24.2 2.8 %shard_map.140 = (bf16[4,64,128]{2,1,0:T(8,128)(2,1)S(1)}, bf16[256,256]{1,0:T(8,128)(2,1)S(1)}, bf16[1920,128]{1,0:T(8,128)(2,1)S(1)}, f32[1920,128]{1,0:T(8,128)S(1)}) custom-call(s32[7]{0:T(128)S(1)} %pad_add_fusion.sc, bf16[4,2,4,64,128]{4,3,2,1,0:T(8,128)(2,1)S(1)} %copy-done.1, bf16[4,2,2,64,128]{4,3,2,1,0:T(8,128)(2,1)S(1)} %copy-done.2, ...), custom_call_target="tpu_custom_call" | custom-call | flops 1207959552 | bytes 6291456 | tf_op jit(solution)/shard_map/pallas_call | solution.py:551
  27.0 0.2 collective-permute-start.5
  27.2 1.1 %shard_map.141.mine = bf16[512,128]{1,0:T(8,128)(2,1)S(1)} custom-call(s32[7]{0:T(128)S(1)} %pad_add_fusion.sc, bf16[256,256]{1,0:T(8,128)(2,1)S(1)} %get-tuple-element.57.g_ref.g0, bf16[27,128,128]{2,1,0:T(8,128)(2,1)S(1)} %bitcast.16), custom_call_target="tpu_custom_call" | custom-call | flops 301989888 | bytes 1048576 | tf_op jit(solution)/shard_map/pallas_call | solution.py:569
  28.3 0.4 collective-permute-start.6
  28.7 0.2 collective-permute-done.5.got
  28.9 1.2 %shard_map.142 = (bf16[480,128]{1,0:T(8,128)(2,1)}, f32[480,128]{1,0:T(8,128)S(1)}) custom-call(s32[7]{0:T(128)S(1)} %pad_add_fusion.sc, f32[1920,128]{1,0:T(8,128)S(1)} %get-tuple-element.61.keep, bf16[1920,128]{1,0:T(8,128)(2,1)S(1)} %collective-permute-done.5.got), custom_call_target="tpu_custom_call" | custom-call | tf_op jit(solution)/shard_map/pallas_call | solution.py:583
  30.2 0.5 collective-permute-start.8
  30.7 0.0 collective-permute-done.6.theirs.beside
  30.7 0.6 shard_map.143
  31.3 1.6 %collective-permute-start.7 = (bf16[736,128]{1,0:T(8,128)(2,1)S(1)}, bf16[736,128]{1,0:T(8,128)(2,1)S(1)}, u32[]{:S(2)}, u32[]{:S(2)}) collective-permute-start(bf16[736,128]{1,0:T(8,128)(2,1)S(1)} %get-tuple-element.63), channel_id=1, source_target_pairs={{0,2},{1,3},{2,0},{3,1},{4,6},{5,7},{6,4},{7,5},{8,10},{9,11},{10,... | collective-permute-start | bytes 565256 | tf_op jit(solution)/shard_map/ppermute | solution.py:390
  32.9 3.7 %collective-permute-done.8 = bf16[480,128]{1,0:T(8,128)(2,1)} collective-permute-done((bf16[480,128]{1,0:T(8,128)(2,1)}, bf16[480,128]{1,0:T(8,128)(2,1)}, u32[]{:S(2)}, u32[]{:S(2)}) %collective-permute-start.8) | collective-permute-done | bytes 122912 | tf_op jit(solution)/shard_map/ppermute | solution.py:390
  36.6 0.9 %add_convert_fusion.3 = (bf16[240,128]{1,0:T(8,128)(2,1)S(1)}, bf16[240,128]{1,0:T(8,128)(2,1)S(1)}) fusion(f32[480,128]{1,0:T(8,128)S(1)} %get-tuple-element.60, bf16[480,128]{1,0:T(8,128)(2,1)} %collective-permute-done.8), kind=kLoop, calls=%fused_computation.21 | loop fusion | flops 184320 | bytes 491520 | tf_op jit(solution)/shard_map/convert_element_type | solution.py:615
  37.5 3.5 %collective-permute-start.9 = (bf16[240,128]{1,0:T(8,128)(2,1)S(1)}, bf16[240,128]{1,0:T(8,128)(2,1)S(1)}, u32[]{:S(2)}, u32[]{:S(2)}) collective-permute-start(bf16[240,128]{1,0:T(8,128)(2,1)S(1)} %get-tuple-element.86), channel_id=1, source_target_pairs={{0,12},{1,13},{2,14},{3,15},{4,8},{5,9},{6,10},{7,11},{8,4},{9,5},... | collective-permute-start | bytes 184328 | tf_op jit(solution)/shard_map/ppermute | solution.py:390
  41.1 0.0 collective-permute-start.10
  41.1 0.0 collective-permute-done.7
  41.1 1.0 %collective-permute-start.18 = (bf16[128,128]{1,0:T(8,128)(2,1)S(1)}, bf16[128,128]{1,0:T(8,128)(2,1)S(1)}, u32[]{:S(2)}, u32[]{:S(2)}) collective-permute-start(bf16[128,128]{1,0:T(8,128)(2,1)S(1)} %fusion.15), channel_id=1, source_target_pairs={{0,4},{1,5},{2,6},{3,7},{4,0},{5,1},{6,2},{7,3},{8,12},{9,13},{10,... | collective-permute-start | bytes 98312 | tf_op jit(solution)/shard_map/ppermute | solution.py:390
  42.1 1.2 %collective-permute-start.11 = (bf16[240,128]{1,0:T(8,128)(2,1)S(1)}, bf16[240,128]{1,0:T(8,128)(2,1)S(1)}, u32[]{:S(2)}, u32[]{:S(2)}) collective-permute-start(bf16[240,128]{1,0:T(8,128)(2,1)S(1)} %add_convert_fusion.1), channel_id=1, source_target_pairs={{0,4},{1,5},{2,6},{3,7},{4,0},{5,1},{6,2},{7,3},{8,12},{9,13},{10,... | collective-permute-start | bytes 184328 | tf_op jit(solution)/shard_map/ppermute | solution.py:390
  43.3 4.2 %shard_map.144 = (bf16[4,2,4,64,128]{4,3,2,1,0:T(8,128)(2,1)}, f32[2,4,64,128]{3,2,1,0:T(8,128)S(1)}) custom-call(s32[7]{0:T(128)S(1)} %pad_add_fusion.sc, bf16[256,256]{1,0:T(8,128)(2,1)S(1)} %get-tuple-element.57.g_ref.g0, bf16[768,256]{1,0:T(8,128)(2,1)S(1)} %get-tuple-element.49.g_ref.g1, bf16[27,128,128]{2,1,0:T(8,128)(2,1)S(1)} %bitcast.17), custom_call_target="tpu_custom_call" | custom-call | flops 1 | bytes 1 | tf_op jit(solution)/shard_map/pallas_call | solution.py:622
  47.5 0.0 collective-permute-done.9
  47.5 0.0 collective-permute-done.10
  47.5 0.0 collective-permute-done.11
  47.6 0.6 collective-permute-start.15
  48.1 2.4 %collective-permute-start.14 = (bf16[240,128]{1,0:T(8,128)(2,1)S(1)}, bf16[240,128]{1,0:T(8,128)(2,1)S(1)}, u32[]{:S(2)}, u32[]{:S(2)}) collective-permute-start(bf16[240,128]{1,0:T(8,128)(2,1)S(1)} %get-tuple-element.85), channel_id=1, source_target_pairs={{0,12},{1,13},{2,14},{3,15},{4,8},{5,9},{6,10},{7,11},{8,4},{9,5},... | collective-permute-start | bytes 184328 | tf_op jit(solution)/shard_map/ppermute | solution.py:390
  50.5 0.5 collective-permute-start.13
  51.1 0.0 collective-permute-done.18
  51.1 1.5 %collective-permute-start.12 = (bf16[240,128]{1,0:T(8,128)(2,1)S(1)}, bf16[240,128]{1,0:T(8,128)(2,1)S(1)}, u32[]{:S(2)}, u32[]{:S(2)}) collective-permute-start(bf16[240,128]{1,0:T(8,128)(2,1)S(1)} %get-tuple-element.85), channel_id=1, source_target_pairs={{0,4},{1,5},{2,6},{3,7},{4,0},{5,1},{6,2},{7,3},{8,12},{9,13},{10,... | collective-permute-start | bytes 184328 | tf_op jit(solution)/shard_map/ppermute | solution.py:390
  52.6 0.0 collective-permute-done.15
  52.6 2.1 %collective-permute-start.19 = (bf16[128,128]{1,0:T(8,128)(2,1)S(1)}, bf16[128,128]{1,0:T(8,128)(2,1)S(1)}, u32[]{:S(2)}, u32[]{:S(2)}) collective-permute-start(bf16[128,128]{1,0:T(8,128)(2,1)S(1)} %fusion.16), channel_id=1, source_target_pairs={{0,8},{1,9},{2,10},{3,11},{4,12},{5,13},{6,14},{7,15},{8,0},{9,1},... | collective-permute-start | bytes 98312 | tf_op jit(solution)/shard_map/ppermute | solution.py:390
  54.8 0.1 collective-permute-done.14
  54.8 1.5 %collective-permute-done.13 = bf16[240,128]{1,0:T(8,128)(2,1)S(1)} collective-permute-done((bf16[240,128]{1,0:T(8,128)(2,1)S(1)}, bf16[240,128]{1,0:T(8,128)(2,1)S(1)}, u32[]{:S(2)}, u32[]{:S(2)}) %collective-permute-start.13) | collective-permute-done | bytes 61472 | tf_op jit(solution)/shard_map/ppermute | solution.py:390
  56.3 1.6 %collective-permute-start.17 = (bf16[480,128]{1,0:T(8,128)(2,1)S(1)}, bf16[480,128]{1,0:T(8,128)(2,1)S(1)}, u32[]{:S(2)}, u32[]{:S(2)}) collective-permute-start(bf16[480,128]{1,0:T(8,128)(2,1)S(1)} %pad_maximum_fusion), channel_id=1, source_target_pairs={{0,2},{1,3},{2,0},{3,1},{4,6},{5,7},{6,4},{7,5},{8,10},{9,11},{10,... | collective-permute-start | bytes 368648 | tf_op jit(solution)/shard_map/ppermute | solution.py:390
  57.9 0.0 collective-permute-done.12
  57.9 0.5 collective-permute-start.16
  58.5 0.0 collective-permute-done.19
  58.5 1.6 %collective-permute-start.20 = (bf16[128,128]{1,0:T(8,128)(2,1)S(1)}, bf16[128,128]{1,0:T(8,128)(2,1)S(1)}, u32[]{:S(2)}, u32[]{:S(2)}) collective-permute-start(bf16[128,128]{1,0:T(8,128)(2,1)S(1)} %fusion.14), channel_id=1, source_target_pairs={{0,2},{1,3},{2,0},{3,1},{4,6},{5,7},{6,4},{7,5},{8,10},{9,11},{10,... | collective-permute-start | bytes 98312 | tf_op jit(solution)/shard_map/ppermute | solution.py:390
  60.1 2.0 %collective-permute-done.16 = bf16[240,128]{1,0:T(8,128)(2,1)S(1)} collective-permute-done((bf16[240,128]{1,0:T(8,128)(2,1)S(1)}, bf16[240,128]{1,0:T(8,128)(2,1)S(1)}, u32[]{:S(2)}, u32[]{:S(2)}) %collective-permute-start.16) | collective-permute-done | bytes 61472 | tf_op jit(solution)/shard_map/ppermute | solution.py:390
  62.1 0.4 collective-permute-done.20
  62.5 0.0 collective-permute-done.17
  62.6 0.1 collective-permute-start.21
  62.7 0.7 %maximum_bitcast_fusion = bf16[4,1,4,64,128]{4,3,2,1,0:T(8,128)(2,1)} fusion(bf16[3,4,64,128]{3,2,1,0:T(8,128)(2,1)S(1)} %copy-done.4, bf16[1,4,64,128]{3,2,1,0:T(8,128)(2,1)S(1)} %bitcast.18), kind=kLoop, calls=%fused_computation.11 | loop fusion | flops 131072 | bytes 524288
  63.4 1.2 %collective-permute-done.21.other = bf16[2176,128]{1,0:T(8,128)(2,1)S(1)} collective-permute-done((bf16[2176,128]{1,0:T(8,128)(2,1)S(1)}, bf16[2176,128]{1,0:T(8,128)(2,1)S(1)}, u32[]{:S(2)}, u32[]{:S(2)}) %collective-permute-start.21) | collective-permute-done | bytes 557088 | tf_op jit(solution)/shard_map/ppermute | solution.py:390
  64.6 2.4 %shard_map.145 = (f32[3456,128]{1,0:T(8,128)}, f32[256,128]{1,0:T(8,128)}, f32[1,128]{1,0:T(1,128)}, f32[1,128]{1,0:T(1,128)}, bf16[4,2,4,64,128]{4,3,2,1,0:T(8,128)(2,1)}) custom-call(s32[7]{0:T(128)S(1)} %pad_add_fusion.sc, bf16[2176,128]{1,0:T(8,128)(2,1)S(1)} %fusion.8.mine, ...), custom_call_target="tpu_custom_call", output_to_operand_aliasing={{4}: (5, {})} | custom-call | tf_op jit(solution)/shard_map/pallas_call | solution.py:665
  (33 shorter events, 0.5 us)
Async XLA Ops:
  2.2 1.6 %collective-permute-start = (bf16[12,64,128]{2,1,0:T(8,128)(2,1)S(1)}, bf16[12,64,128]{2,1,0:T(8,128)(2,1)S(1)}, u32[]{:S(2)}, u32[]{:S(2)}) collective-permute-start(bf16[12,64,128]{2,1,0:T(8,128)(2,1)S(1)} %shard_map.136), channel_id=1, source_target_pairs={{0,1},{1,0},{2,3},{3,2},{4,5},{5,4},{6,7},{7,6},{8,9},{9,8},{10,11... | collective-permute-start | bytes 589832 | tf_op jit(solution)/shard_map/ppermute | solution.py:390
  3.9 7.3 %collective-permute-start.1 = (bf16[6,64,128]{2,1,0:T(8,128)(2,1)S(1)}, bf16[6,64,128]{2,1,0:T(8,128)(2,1)S(1)}, u32[]{:S(2)}, u32[]{:S(2)}) collective-permute-start(bf16[6,64,128]{2,1,0:T(8,128)(2,1)S(1)} %fusion.5), channel_id=1, source_target_pairs={{0,2},{1,3},{2,0},{3,1},{4,6},{5,7},{6,4},{7,5},{8,10},{9,11},{10,... | collective-permute-start | bytes 294920 | tf_op jit(solution)/shard_map/ppermute | solution.py:390
  11.2 4.7 %collective-permute-start.2 = (bf16[6,64,128]{2,1,0:T(8,128)(2,1)S(1)}, bf16[6,64,128]{2,1,0:T(8,128)(2,1)S(1)}, u32[]{:S(2)}, u32[]{:S(2)}) collective-permute-start(bf16[6,64,128]{2,1,0:T(8,128)(2,1)S(1)} %fusion.6), channel_id=1, source_target_pairs={{0,4},{1,5},{2,6},{3,7},{4,0},{5,1},{6,2},{7,3},{8,12},{9,13},{10,... | collective-permute-start | bytes 294920 | tf_op jit(solution)/shard_map/ppermute | solution.py:390
  13.9 0.7 %copy-start.3 = (bf16[3,4,64,128]{3,2,1,0:T(8,128)(2,1)}, bf16[3,4,64,128]{3,2,1,0:T(8,128)(2,1)S(1)}, u32[]{:S(2)}) copy-start(bf16[3,4,64,128]{3,2,1,0:T(8,128)(2,1)S(1)} %get-tuple-element.55) | copy-start | bytes 589828
  15.9 6.7 %collective-permute-start.3 = (bf16[6,64,128]{2,1,0:T(8,128)(2,1)S(1)}, bf16[6,64,128]{2,1,0:T(8,128)(2,1)S(1)}, u32[]{:S(2)}, u32[]{:S(2)}) collective-permute-start(bf16[6,64,128]{2,1,0:T(8,128)(2,1)S(1)} %fusion.7), channel_id=1, source_target_pairs={{0,8},{1,9},{2,10},{3,11},{4,12},{5,13},{6,14},{7,15},{8,0},{9,1},... | collective-permute-start | bytes 294920 | tf_op jit(solution)/shard_map/ppermute | solution.py:390
  18.6 5.5 %copy-start = (bf16[3,3,3,128,128]{4,3,2,1,0:T(8,128)(2,1)S(1)}, bf16[3,3,3,128,128]{4,3,2,1,0:T(8,128)(2,1)}, u32[]{:S(2)}) copy-start(bf16[3,3,3,128,128]{4,3,2,1,0:T(8,128)(2,1)} %param.13) | copy-start | bytes 2654212
  18.6 5.5 %copy-start.1 = (bf16[4,2,4,64,128]{4,3,2,1,0:T(8,128)(2,1)S(1)}, bf16[4,2,4,64,128]{4,3,2,1,0:T(8,128)(2,1)}, u32[]{:S(2)}) copy-start(bf16[4,2,4,64,128]{4,3,2,1,0:T(8,128)(2,1)} %frs.1) | copy-start | bytes 1572868
  18.6 5.5 %copy-start.2 = (bf16[4,2,2,64,128]{4,3,2,1,0:T(8,128)(2,1)S(1)}, bf16[4,2,2,64,128]{4,3,2,1,0:T(8,128)(2,1)}, u32[]{:S(2)}) copy-start(bf16[4,2,2,64,128]{4,3,2,1,0:T(8,128)(2,1)} %has.1) | copy-start | bytes 786436
  18.6 5.5 %copy-start.5 = (bf16[4,1,4,64,128]{4,3,2,1,0:T(8,128)(2,1)S(1)}, bf16[4,1,4,64,128]{4,3,2,1,0:T(8,128)(2,1)}, u32[]{:S(2)}) copy-start(bf16[4,1,4,64,128]{4,3,2,1,0:T(8,128)(2,1)} %cos.1) | copy-start | bytes 786436
  18.6 5.5 %copy-start.6 = (bf16[2,128,128]{2,1,0:T(8,128)(2,1)S(1)}, bf16[2,128,128]{2,1,0:T(8,128)(2,1)}, u32[]{:S(2)}) copy-start(bf16[2,128,128]{2,1,0:T(8,128)(2,1)} %sw.1) | copy-start | bytes 196612
  18.6 5.5 %copy-start.7 = (f32[128]{0:T(128)S(1)}, f32[128]{0:T(128)}, u32[]{:S(2)}) copy-start(f32[128]{0:T(128)} %param.14) | copy-start | bytes 1540
  18.6 5.5 %copy-start.8 = (f32[128]{0:T(128)S(1)}, f32[128]{0:T(128)}, u32[]{:S(2)}) copy-start(f32[128]{0:T(128)} %param.16) | copy-start | bytes 1540
  22.7 1.4 %collective-permute-start.4 = (bf16[6,64,128]{2,1,0:T(8,128)(2,1)S(1)}, bf16[6,64,128]{2,1,0:T(8,128)(2,1)S(1)}, u32[]{:S(2)}, u32[]{:S(2)}) collective-permute-start(bf16[6,64,128]{2,1,0:T(8,128)(2,1)S(1)} %fusion.2), channel_id=1, source_target_pairs={{0,1},{1,0},{2,3},{3,2},{4,5},{5,4},{6,7},{7,6},{8,9},{9,8},{10,11... | collective-permute-start | bytes 294920 | tf_op jit(solution)/shard_map/ppermute | solution.py:390
  27.0 1.9 %collective-permute-start.5 = (bf16[1920,128]{1,0:T(8,128)(2,1)S(1)}, bf16[1920,128]{1,0:T(8,128)(2,1)S(1)}, u32[]{:S(2)}, u32[]{:S(2)}) collective-permute-start(bf16[1920,128]{1,0:T(8,128)(2,1)S(1)} %get-tuple-element.59), channel_id=1, source_target_pairs={{0,1},{1,0},{2,3},{3,2},{4,5},{5,4},{6,7},{7,6},{8,9},{9,8},{10,11... | collective-permute-start | bytes 1474568 | tf_op jit(solution)/shard_map/ppermute | solution.py:390
  28.3 2.4 %collective-permute-start.6 = (bf16[512,128]{1,0:T(8,128)(2,1)S(1)}, bf16[512,128]{1,0:T(8,128)(2,1)S(1)}, u32[]{:S(2)}, u32[]{:S(2)}) collective-permute-start(bf16[512,128]{1,0:T(8,128)(2,1)S(1)} %shard_map.141.mine), channel_id=1, source_target_pairs={{0,1},{1,0},{2,3},{3,2},{4,5},{5,4},{6,7},{7,6},{8,9},{9,8},{10,11... | collective-permute-start | bytes 393224 | tf_op jit(solution)/shard_map/ppermute | solution.py:390
  30.2 6.5 %collective-permute-start.8 = (bf16[480,128]{1,0:T(8,128)(2,1)}, bf16[480,128]{1,0:T(8,128)(2,1)}, u32[]{:S(2)}, u32[]{:S(2)}) collective-permute-start(bf16[480,128]{1,0:T(8,128)(2,1)} %get-tuple-element.64), channel_id=1, source_target_pairs={{0,2},{1,3},{2,0},{3,1},{4,6},{5,7},{6,4},{7,5},{8,10},{9,11},{10,... | collective-permute-start | bytes 368648 | tf_op jit(solution)/shard_map/ppermute | solution.py:390
  31.3 9.7 %collective-permute-start.7 = (bf16[736,128]{1,0:T(8,128)(2,1)S(1)}, bf16[736,128]{1,0:T(8,128)(2,1)S(1)}, u32[]{:S(2)}, u32[]{:S(2)}) collective-permute-start(bf16[736,128]{1,0:T(8,128)(2,1)S(1)} %get-tuple-element.63), channel_id=1, source_target_pairs={{0,2},{1,3},{2,0},{3,1},{4,6},{5,7},{6,4},{7,5},{8,10},{9,11},{10,... | collective-permute-start | bytes 565256 | tf_op jit(solution)/shard_map/ppermute | solution.py:390
  37.5 9.9 %collective-permute-start.9 = (bf16[240,128]{1,0:T(8,128)(2,1)S(1)}, bf16[240,128]{1,0:T(8,128)(2,1)S(1)}, u32[]{:S(2)}, u32[]{:S(2)}) collective-permute-start(bf16[240,128]{1,0:T(8,128)(2,1)S(1)} %get-tuple-element.86), channel_id=1, source_target_pairs={{0,12},{1,13},{2,14},{3,15},{4,8},{5,9},{6,10},{7,11},{8,4},{9,5},... | collective-permute-start | bytes 184328 | tf_op jit(solution)/shard_map/ppermute | solution.py:390
  41.1 6.4 %collective-permute-start.10 = (bf16[240,128]{1,0:T(8,128)(2,1)S(1)}, bf16[240,128]{1,0:T(8,128)(2,1)S(1)}, u32[]{:S(2)}, u32[]{:S(2)}) collective-permute-start(bf16[240,128]{1,0:T(8,128)(2,1)S(1)} %get-tuple-element.87), channel_id=1, source_target_pairs={{0,8},{1,9},{2,10},{3,11},{4,12},{5,13},{6,14},{7,15},{8,0},{9,1},... | collective-permute-start | bytes 184328 | tf_op jit(solution)/shard_map/ppermute | solution.py:390
  41.1 10.0 %collective-permute-start.18 = (bf16[128,128]{1,0:T(8,128)(2,1)S(1)}, bf16[128,128]{1,0:T(8,128)(2,1)S(1)}, u32[]{:S(2)}, u32[]{:S(2)}) collective-permute-start(bf16[128,128]{1,0:T(8,128)(2,1)S(1)} %fusion.15), channel_id=1, source_target_pairs={{0,4},{1,5},{2,6},{3,7},{4,0},{5,1},{6,2},{7,3},{8,12},{9,13},{10,... | collective-permute-start | bytes 98312 | tf_op jit(solution)/shard_map/ppermute | solution.py:390
  42.1 20.6 %copy-start.4 = (bf16[3,4,64,128]{3,2,1,0:T(8,128)(2,1)S(1)}, bf16[3,4,64,128]{3,2,1,0:T(8,128)(2,1)}, u32[]{:S(2)}) copy-start(bf16[3,4,64,128]{3,2,1,0:T(8,128)(2,1)} %copy-done.3) | copy-start | bytes 589828
  42.1 5.4 %collective-permute-start.11 = (bf16[240,128]{1,0:T(8,128)(2,1)S(1)}, bf16[240,128]{1,0:T(8,128)(2,1)S(1)}, u32[]{:S(2)}, u32[]{:S(2)}) collective-permute-start(bf16[240,128]{1,0:T(8,128)(2,1)S(1)} %add_convert_fusion.1), channel_id=1, source_target_pairs={{0,4},{1,5},{2,6},{3,7},{4,0},{5,1},{6,2},{7,3},{8,12},{9,13},{10,... | collective-permute-start | bytes 184328 | tf_op jit(solution)/shard_map/ppermute | solution.py:390
  47.6 5.1 %collective-permute-start.15 = (bf16[240,128]{1,0:T(8,128)(2,1)S(1)}, bf16[240,128]{1,0:T(8,128)(2,1)S(1)}, u32[]{:S(2)}, u32[]{:S(2)}) collective-permute-start(bf16[240,128]{1,0:T(8,128)(2,1)S(1)} %get-tuple-element.85), channel_id=1, source_target_pairs={{0,2},{1,3},{2,0},{3,1},{4,6},{5,7},{6,4},{7,5},{8,10},{9,11},{10,... | collective-permute-start | bytes 184328 | tf_op jit(solution)/shard_map/ppermute | solution.py:390
  48.1 6.7 %collective-permute-start.14 = (bf16[240,128]{1,0:T(8,128)(2,1)S(1)}, bf16[240,128]{1,0:T(8,128)(2,1)S(1)}, u32[]{:S(2)}, u32[]{:S(2)}) collective-permute-start(bf16[240,128]{1,0:T(8,128)(2,1)S(1)} %get-tuple-element.85), channel_id=1, source_target_pairs={{0,12},{1,13},{2,14},{3,15},{4,8},{5,9},{6,10},{7,11},{8,4},{9,5},... | collective-permute-start | bytes 184328 | tf_op jit(solution)/shard_map/ppermute | solution.py:390
  50.5 5.8 %collective-permute-start.13 = (bf16[240,128]{1,0:T(8,128)(2,1)S(1)}, bf16[240,128]{1,0:T(8,128)(2,1)S(1)}, u32[]{:S(2)}, u32[]{:S(2)}) collective-permute-start(bf16[240,128]{1,0:T(8,128)(2,1)S(1)} %get-tuple-element.85), channel_id=1, source_target_pairs={{0,8},{1,9},{2,10},{3,11},{4,12},{5,13},{6,14},{7,15},{8,0},{9,1},... | collective-permute-start | bytes 184328 | tf_op jit(solution)/shard_map/ppermute | solution.py:390
  51.1 6.8 %collective-permute-start.12 = (bf16[240,128]{1,0:T(8,128)(2,1)S(1)}, bf16[240,128]{1,0:T(8,128)(2,1)S(1)}, u32[]{:S(2)}, u32[]{:S(2)}) collective-permute-start(bf16[240,128]{1,0:T(8,128)(2,1)S(1)} %get-tuple-element.85), channel_id=1, source_target_pairs={{0,4},{1,5},{2,6},{3,7},{4,0},{5,1},{6,2},{7,3},{8,12},{9,13},{10,... | collective-permute-start | bytes 184328 | tf_op jit(solution)/shard_map/ppermute | solution.py:390
  52.6 5.9 %collective-permute-start.19 = (bf16[128,128]{1,0:T(8,128)(2,1)S(1)}, bf16[128,128]{1,0:T(8,128)(2,1)S(1)}, u32[]{:S(2)}, u32[]{:S(2)}) collective-permute-start(bf16[128,128]{1,0:T(8,128)(2,1)S(1)} %fusion.16), channel_id=1, source_target_pairs={{0,8},{1,9},{2,10},{3,11},{4,12},{5,13},{6,14},{7,15},{8,0},{9,1},... | collective-permute-start | bytes 98312 | tf_op jit(solution)/shard_map/ppermute | solution.py:390
  56.3 6.2 %collective-permute-start.17 = (bf16[480,128]{1,0:T(8,128)(2,1)S(1)}, bf16[480,128]{1,0:T(8,128)(2,1)S(1)}, u32[]{:S(2)}, u32[]{:S(2)}) collective-permute-start(bf16[480,128]{1,0:T(8,128)(2,1)S(1)} %pad_maximum_fusion), channel_id=1, source_target_pairs={{0,2},{1,3},{2,0},{3,1},{4,6},{5,7},{6,4},{7,5},{8,10},{9,11},{10,... | collective-permute-start | bytes 368648 | tf_op jit(solution)/shard_map/ppermute | solution.py:390
  57.9 4.2 %collective-permute-start.16 = (bf16[240,128]{1,0:T(8,128)(2,1)S(1)}, bf16[240,128]{1,0:T(8,128)(2,1)S(1)}, u32[]{:S(2)}, u32[]{:S(2)}) collective-permute-start(bf16[240,128]{1,0:T(8,128)(2,1)S(1)} %collective-permute-done.12), channel_id=1, source_target_pairs={{0,2},{1,3},{2,0},{3,1},{4,6},{5,7},{6,4},{7,5},{8,10},{9,11},{10,... | collective-permute-start | bytes 184328 | tf_op jit(solution)/shard_map/ppermute | solution.py:390
  58.5 4.0 %collective-permute-start.20 = (bf16[128,128]{1,0:T(8,128)(2,1)S(1)}, bf16[128,128]{1,0:T(8,128)(2,1)S(1)}, u32[]{:S(2)}, u32[]{:S(2)}) collective-permute-start(bf16[128,128]{1,0:T(8,128)(2,1)S(1)} %fusion.14), channel_id=1, source_target_pairs={{0,2},{1,3},{2,0},{3,1},{4,6},{5,7},{6,4},{7,5},{8,10},{9,11},{10,... | collective-permute-start | bytes 98312 | tf_op jit(solution)/shard_map/ppermute | solution.py:390
  62.6 2.0 %collective-permute-start.21 = (bf16[2176,128]{1,0:T(8,128)(2,1)S(1)}, bf16[2176,128]{1,0:T(8,128)(2,1)S(1)}, u32[]{:S(2)}, u32[]{:S(2)}) collective-permute-start(bf16[2176,128]{1,0:T(8,128)(2,1)S(1)} %fusion.8.mine), channel_id=1, source_target_pairs={{0,1},{1,0},{2,3},{3,2},{4,5},{5,4},{6,7},{7,6},{8,9},{9,8},{10,11... | collective-permute-start | bytes 1671176 | tf_op jit(solution)/shard_map/ppermute | solution.py:390

commit v11 on v10

--- a/solution.py
+++ b/solution.py
@@ -298,34 +298,21 @@
     return lax.shift_right_logical(chip, 1), lax.bitwise_and(chip, 1), core
 
 
-def _piece(sc, keep, got, j, side):
+def _across_x_kernel(sc, keep, got, send_far, send_near, kept):
+    z, x, _ = _place(sc)
+    half = keep.shape[0]
     blocks = 4
-    rows = keep.shape[0] // (2 * blocks)
-    p = 2 * lax.bitwise_xor(_place(sc)[0], j) + side
-    at = pl.ds(pl.multiple_of(p * rows, 16), rows)
-    return keep[at] + got[at].astype(F32)
-
-
-def _far_kernel(sc, keep, got, send, kept):
-    x = _place(sc)[1]
-    rows = kept.shape[0] // 2
-    for i, j in enumerate((2, 3)):
-        kept[i * rows : (i + 1) * rows] = _piece(sc, keep, got, j, x)
-        send[i * rows : (i + 1) * rows] = _piece(sc, keep, got, j, 1 - x).astype(BF)
-
-
-def _near_kernel(sc, keep, got, mine, theirs, send, kept, chip_first):
-    _, x, core = _place(sc)
-    rows = kept.shape[0] // 2
-    for j in (0, 1):
-        kept[j * rows : (j + 1) * rows] = _piece(sc, keep, got, j, x)
-        send[j * rows : (j + 1) * rows] = _piece(sc, keep, got, j, 1 - x).astype(BF)
-    part = mine.shape[0] // 2
-    at = pl.ds(pl.multiple_of(core * part, 16), part)
-    a, b = mine[at], theirs[at]
-    first = jnp.where(core == 0, _first_live(a, b), _first_live(b, a))
-    chip_first[...] = first
-    send[2 * rows :] = first
+    rows = half // (2 * blocks)
+
+    def piece(j, side):
+        p = 2 * lax.bitwise_xor(z, j) + side
+        at = pl.ds(pl.multiple_of(p * rows, 16), rows)
+        return keep[at] + got[at].astype(F32)
+
+    for j in range(blocks):
+        kept[j * rows : (j + 1) * rows] = piece(j, x)
+        send, i = (send_near, j) if j < 2 else (send_far, j - 2)
+        send[i * rows : (i + 1) * rows] = piece(j, 1 - x).astype(BF)
 
 
 def _tail_kernel(sc, fr, ha, out):
@@ -575,26 +562,18 @@
         moved=1 << 20,
         room=8,
     )(sc, g0, wt)
-    got_first = _xor(first_grad, 1, n, axis)
-    pieces = (
-        jax.ShapeDtypeStruct((2 * piece, c), BF),
-        jax.ShapeDtypeStruct((2 * piece, c), F32),
-    )
-    send_far, kept_far = _call(_far_kernel, pieces, [_SMEM] + [_VMEM] * 2, room=4)(
-        sc, _after(keep, first_grad), got
-    )
+    send_far, send_near, kept = _call(
+        _across_x_kernel,
+        [
+            jax.ShapeDtypeStruct((2 * piece, c), BF),
+            jax.ShapeDtypeStruct((2 * piece, c), BF),
+            jax.ShapeDtypeStruct((blocks * piece, c), F32),
+        ],
+        [_SMEM] + [_VMEM] * 2,
+        room=8,
+    )(sc, _after(keep, first_grad), got)
     got_far = _xor(send_far, 2, n, axis)
-    send_near, kept_near, chip_first = _call(
-        _near_kernel,
-        (
-            jax.ShapeDtypeStruct((2 * piece + carried // 2, c), BF),
-            pieces[1],
-            jax.ShapeDtypeStruct((carried // 2, c), BF),
-        ),
-        [_SMEM] + [_VMEM] * 4,
-        room=4,
-    )(sc, _after(keep, kept_far), got, first_grad, got_first)
-    got_near = _xor(send_near, 2, n, axis)
+    got_first = _xor(_after(first_grad, kept), 1, n, axis)
     core, pair = index & 1, (index >> 1) & 1
 
     def by(bit, a, b):
@@ -607,10 +586,29 @@
     def ordered(bit, ours, theirs):
         return by(bit, _first_live(ours, theirs), _first_live(theirs, ours))
 
+    chip_first = ordered(core, by_half(core, first_grad), by_half(core, got_first))
+    send_near = jnp.concatenate([send_near, chip_first], axis=0)
+    got_near = _xor(send_near, 2, n, axis)
+    slabs, last = _call(
+        _back_kernel,
+        [
+            jax.ShapeDtypeStruct((slots, 2, h, w, c), BF),
+            jax.ShapeDtypeStruct((2, h, w, c), F32),
+        ],
+        [_SMEM] + [_VMEM] * 3,
+        [
+            pltpu.VMEM((3, slots, 4, h + 2, w, c), BF),
+            pltpu.VMEM((slots, 2, h, w, c), F32),
+        ],
+        flops=1,
+        moved=1,
+        room=24,
+    )(_after(sc, send_near), g0, g1, wt)
+    got_far = _after(got_far, last)
+
     def summed(j, came):
-        kept = kept_near if j < 2 else kept_far
-        rows = slice((j % 2) * piece, (j % 2 + 1) * piece)
-        return kept[rows] + came[rows].astype(F32)
+        i = j % 2
+        return kept[j * piece : (j + 1) * piece] + came[i * piece : (i + 1) * piece].astype(F32)
 
     outs = {j: summed(j, got_far).astype(BF) for j in (3, 2)}
     got_near = _after(got_near, outs[3], outs[2])
@@ -619,22 +617,7 @@
     beside_first = got_near[2 * piece :]
     lead = ordered(pair, by_half(pair, chip_first), by_half(pair, beside_first))
     near_lead = _xor(lead, 4, n, axis)
-    slabs, last = _call(
-        _back_kernel,
-        [
-            jax.ShapeDtypeStruct((slots, 2, h, w, c), BF),
-            jax.ShapeDtypeStruct((2, h, w, c), F32),
-        ],
-        [_SMEM] + [_VMEM] * 3,
-        [
-            pltpu.VMEM((3, slots, 4, h + 2, w, c), BF),
-            pltpu.VMEM((slots, 2, h, w, c), F32),
-        ],
-        flops=1,
-        moved=1,
-        room=24,
-    )(_after(sc, outs[1], lead), g0, g1, wt)
-    mine = summed(0, _after(got_near, last))
+    mine = summed(0, _after(got_near, outs[1]))
     for j in (3, 2):
         mine = mine + gots[j].astype(F32)
     gots[1] = _after(gots[1], mine)

time: 67.5 us -> 66.5 us (0.985)
  waiting for transfers between devices: 12.2 us -> 16.4 us
  starting transfers between devices: 27.1 us -> 24.7 us
  Pallas kernels: 22.6 us -> 21.4 us
  other arithmetic: 2.74 us -> 1.96 us
  local copies, waits for them, and re-layouts: 0.8 us -> 0.12 us
    ppermute x22, waiting for transfers between devices: 12.2 us -> 16.4 us  [_xor(): return lax.ppermute(x, axis, [(i, i ^ k) for i in range(n)])]
    ppermute x22, starting transfers between devices: 27.1 us -> 24.7 us  [_xor(): return lax.ppermute(x, axis, [(i, i ^ k) for i in range(n)])]
    pallas_call x2 -> x1, Pallas kernels: 1.87 us -> 0.64 us  [body(): _call(_across_x_kernel, [jax.ShapeDtypeStruct((2 * piece, c), BF), jax.Sh...]
    convert_element_type x1, other arithmetic: 0.89 us -> 0.03 us  [body(): outs = {j: summed(j, got_far).astype(BF) for j in (3, 2)}]
    unnamed x24 -> x20, local copies, waits for them, and re-layouts: 0.8 us -> 0.12 us
  transfers between devices with their start and end apart: 22 -> 22, of which waited for: 10 -> 13; matrix products, arithmetic and copies ran while one was open for 4% -> 3% of each run, Pallas kernels for 24% -> 22%
where the time goes in v11:
time: 66.5 us; the launch traced here: 66.3 us
  starting transfers between devices  24.7 us (37%)
  Pallas kernels  21.4 us (32%)
  waiting for transfers between devices  16.4 us (25%)
  other arithmetic  1.96 us (3%)
  between operations  1.74 us (3%)
    ppermute x22, starting transfers between devices, _xor(): return lax.ppermute(x, axis, [(i, i ^ k) for i in range(n)])  24.7 us
    ppermute x22, waiting for transfers between devices, _xor(): return lax.ppermute(x, axis, [(i, i ^ k) for i in range(n)])  16.4 us
    pallas_call x1, Pallas kernels, early_conv(): _call(_early_conv_kernel, [jax.ShapeDtypeStruct(wide, F32), jax.ShapeDtyp...  4.41 us
    pallas_call x1, Pallas kernels, body(): _call(_back_kernel, [jax.ShapeDtypeStruct((slots, 2, h, w, c), BF), jax.S...  4.19 us
    pallas_call x1, Pallas kernels, early_sums(): _call(_early_sums_kernel, jax.ShapeDtypeStruct((rows, c), F32), [_SMEM, _...  3.95 us
    pallas_call x1, Pallas kernels, body(): _call(_late_kernel, [jax.ShapeDtypeStruct((h, w, c), BF), jax.ShapeDtypeS...  2.81 us
    pallas_call x1, Pallas kernels, body(): _call(_final_kernel, [jax.ShapeDtypeStruct((27 * c, c), F32), jax.ShapeDt...  2.44 us
  transfers between devices with their start and end apart: 22, of which 13 were waited for; matrix products, arithmetic and copies ran while one was open for 3% of the time, Pallas kernels for 22%

profile of v11, /device:TPU:0, one launch (start us, length us, event | category | flops | bytes accessed | tf_op | source)
XLA Modules:
  0.0 66.3 jit_solution(2479832869456947412)
XLA Ops:
  1.3 1.0 %shard_map.136 = bf16[12,64,128]{2,1,0:T(8,128)(2,1)S(1)} custom-call(s32[1]{0:T(128)S(6)} %copy.25.sc, bf16[4,2,4,64,128]{4,3,2,1,0:T(8,128)(2,1)} %frs.1, bf16[4,2,2,64,128]{4,3,2,1,0:T(8,128)(2,1)} %has.1), custom_call_target="tpu_custom_call" | custom-call | tf_op jit(solution)/shard_map/pallas_call | solution.py:458
  2.2 0.5 collective-permute-start
  2.8 0.7 %pad_add_fusion.sc = s32[7]{0:T(128)S(1)} fusion(s32[1]{0:T(128)} %bitcast.1, s32[1]{0:T(128)} %bitcast, s32[4]{0:T(128)} %param.11, s32[1]{0:T(128)S(6)} %copy.25.sc), kind=kLoop, calls=%fused_computation.62 | loop fusion | flops 21 | bytes 56 | tf_op jit(solution)/shard_map/concatenate | solution.py:440
  3.5 0.3 collective-permute-done
  3.9 2.9 %collective-permute-start.1 = (bf16[6,64,128]{2,1,0:T(8,128)(2,1)S(1)}, bf16[6,64,128]{2,1,0:T(8,128)(2,1)S(1)}, u32[]{:S(2)}, u32[]{:S(2)}) collective-permute-start(bf16[6,64,128]{2,1,0:T(8,128)(2,1)S(1)} %fusion.7), channel_id=1, source_target_pairs={{0,2},{1,3},{2,0},{3,1},{4,6},{5,7},{6,4},{7,5},{8,10},{9,11},{10,... | collective-permute-start | bytes 294920 | tf_op jit(solution)/shard_map/ppermute | solution.py:377
  6.8 4.4 %shard_map.137 = (f32[768,256]{1,0:T(8,128)S(1)}, bf16[768,128]{1,0:T(8,128)(2,1)S(1)}, bf16[2,128,128]{2,1,0:T(8,128)(2,1)S(1)}, f32[1,128]{1,0:T(1,128)S(1)}) custom-call(s32[7]{0:T(128)S(1)} %pad_add_fusion.sc, bf16[4,2,4,64,128]{4,3,2,1,0:T(8,128)(2,1)} %frs.1, bf16[4,2,2,64,128]{4,3,2,1,0:T(8,128)(2,1)} %has.1, bf16[4,1,4,64,128]{4,3,2,1,0:T(8,128)(2,1)} %cos.1, ...), custom_call_target="tpu_custom_call" | custom-call | flops 1811939328 | bytes 4194304 | tf_op jit(solution)/shard_map/pallas_call | solution.py:485
  11.2 0.0 collective-permute-done.1
  11.2 1.6 %collective-permute-start.2 = (bf16[6,64,128]{2,1,0:T(8,128)(2,1)S(1)}, bf16[6,64,128]{2,1,0:T(8,128)(2,1)S(1)}, u32[]{:S(2)}, u32[]{:S(2)}) collective-permute-start(bf16[6,64,128]{2,1,0:T(8,128)(2,1)S(1)} %fusion.8), channel_id=1, source_target_pairs={{0,4},{1,5},{2,6},{3,7},{4,0},{5,1},{6,2},{7,3},{8,12},{9,13},{10,... | collective-permute-start | bytes 294920 | tf_op jit(solution)/shard_map/ppermute | solution.py:377
  12.9 1.0 %shard_map.138 = (bf16[3,4,64,128]{3,2,1,0:T(8,128)(2,1)S(1)}, bf16[768,256]{1,0:T(8,128)(2,1)S(1)}, bf16[768,256]{1,0:T(8,128)(2,1)S(1)}) custom-call(s32[7]{0:T(128)S(1)} %pad_add_fusion.sc, f32[768,256]{1,0:T(8,128)S(1)} %get-tuple-element.42.pre_ref, bf16[768,128]{1,0:T(8,128)(2,1)S(1)} %get-tuple-element.45.gout_ref, ...), custom_call_target="tpu_custom_call" | custom-call | bytes 2097152 | tf_op jit(solution)/shard_map/pallas_call | solution.py:503
  13.8 2.1 %collective-permute-done.2 = bf16[6,64,128]{2,1,0:T(8,128)(2,1)S(1)} collective-permute-done((bf16[6,64,128]{2,1,0:T(8,128)(2,1)S(1)}, bf16[6,64,128]{2,1,0:T(8,128)(2,1)S(1)}, u32[]{:S(2)}, u32[]{:S(2)}) %collective-permute-start.2) | collective-permute-done | bytes 98336 | tf_op jit(solution)/shard_map/ppermute | solution.py:377
  15.9 2.7 %collective-permute-start.3 = (bf16[6,64,128]{2,1,0:T(8,128)(2,1)S(1)}, bf16[6,64,128]{2,1,0:T(8,128)(2,1)S(1)}, u32[]{:S(2)}, u32[]{:S(2)}) collective-permute-start(bf16[6,64,128]{2,1,0:T(8,128)(2,1)S(1)} %fusion.9), channel_id=1, source_target_pairs={{0,8},{1,9},{2,10},{3,11},{4,12},{5,13},{6,14},{7,15},{8,0},{9,1},... | collective-permute-start | bytes 294920 | tf_op jit(solution)/shard_map/ppermute | solution.py:377
  18.6 0.0 copy-start.4
  18.6 0.0 copy-start.5
  18.6 0.0 copy-start.6
  18.6 3.9 %shard_map.139.early = f32[3840,128]{1,0:T(8,128)S(1)} custom-call(s32[7]{0:T(128)S(1)} %pad_add_fusion.sc, bf16[4,2,4,64,128]{4,3,2,1,0:T(8,128)(2,1)} %frs.1, bf16[4,2,2,64,128]{4,3,2,1,0:T(8,128)(2,1)} %has.1, bf16[768,256]{1,0:T(8,128)(2,1)S(1)} %get-tuple-element.48.g_ref.g1, bf16[768,256]{1,0:T(8,128)(2,1)S(1)} %get-tuple-element.51.hid_ref, ...), custom_call_target="tpu_custom_call" | custom-call | flops 1811939328 | bytes 4194304 | tf_op jit(solution)/shard_map/pallas_call | solution.py:519
  22.6 0.0 collective-permute-done.3
  22.7 0.1 collective-permute-start.4
  22.7 1.3 %collective-permute-done.4 = bf16[6,64,128]{2,1,0:T(8,128)(2,1)S(1)} collective-permute-done((bf16[6,64,128]{2,1,0:T(8,128)(2,1)S(1)}, bf16[6,64,128]{2,1,0:T(8,128)(2,1)S(1)}, u32[]{:S(2)}, u32[]{:S(2)}) %collective-permute-start.4) | collective-permute-done | bytes 98336 | tf_op jit(solution)/shard_map/ppermute | solution.py:377
  24.1 0.0 copy-done
  24.1 0.0 copy-done.1
  24.1 0.0 copy-done.2
  24.1 0.0 copy-done.3
  24.2 0.0 copy-done.4
  24.2 2.8 %shard_map.140 = (bf16[4,64,128]{2,1,0:T(8,128)(2,1)S(1)}, bf16[256,256]{1,0:T(8,128)(2,1)S(1)}, bf16[1920,128]{1,0:T(8,128)(2,1)S(1)}, f32[1920,128]{1,0:T(8,128)S(1)}) custom-call(s32[7]{0:T(128)S(1)} %pad_add_fusion.sc, bf16[4,2,4,64,128]{4,3,2,1,0:T(8,128)(2,1)S(1)} %copy-done.1, bf16[4,2,2,64,128]{4,3,2,1,0:T(8,128)(2,1)S(1)} %copy-done.2, ...), custom_call_target="tpu_custom_call" | custom-call | flops 1207959552 | bytes 6291456 | tf_op jit(solution)/shard_map/pallas_call | solution.py:538
  27.0 0.2 collective-permute-start.5
  27.2 1.1 %shard_map.141 = bf16[512,128]{1,0:T(8,128)(2,1)S(1)} custom-call(s32[7]{0:T(128)S(1)} %pad_add_fusion.sc, bf16[256,256]{1,0:T(8,128)(2,1)S(1)} %get-tuple-element.56.g_ref.g0, bf16[27,128,128]{2,1,0:T(8,128)(2,1)S(1)} %bitcast.16), custom_call_target="tpu_custom_call" | custom-call | flops 301989888 | bytes 1048576 | tf_op jit(solution)/shard_map/pallas_call | solution.py:556
  28.3 0.7 collective-permute-done.5.got
  28.9 0.6 shard_map.142
  29.6 0.2 collective-permute-start.6
  29.8 0.6 collective-permute-start.8
  30.3 0.6 collective-permute-done.6.beside
  31.0 0.1 fusion.11
  31.1 0.9 %collective-permute-start.7 = (bf16[736,128]{1,0:T(8,128)(2,1)S(1)}, bf16[736,128]{1,0:T(8,128)(2,1)S(1)}, u32[]{:S(2)}, u32[]{:S(2)}) collective-permute-start(bf16[736,128]{1,0:T(8,128)(2,1)S(1)} %pad_maximum_fusion), channel_id=1, source_target_pairs={{0,2},{1,3},{2,0},{3,1},{4,6},{5,7},{6,4},{7,5},{8,10},{9,11},{10,... | collective-permute-start | bytes 565256 | tf_op jit(solution)/shard_map/ppermute | solution.py:377
  32.0 4.2 %shard_map.143 = (bf16[4,2,4,64,128]{4,3,2,1,0:T(8,128)(2,1)}, f32[2,4,64,128]{3,2,1,0:T(8,128)S(1)}) custom-call(s32[7]{0:T(128)S(1)} %pad_add_fusion.sc, bf16[256,256]{1,0:T(8,128)(2,1)S(1)} %get-tuple-element.56.g_ref.g0, bf16[768,256]{1,0:T(8,128)(2,1)S(1)} %get-tuple-element.48.g_ref.g1, bf16[27,128,128]{2,1,0:T(8,128)(2,1)S(1)} %bitcast.17), custom_call_target="tpu_custom_call" | custom-call | flops 1 | bytes 1 | tf_op jit(solution)/shard_map/pallas_call | solution.py:592
  36.2 0.0 collective-permute-done.8
  36.2 3.5 %collective-permute-start.9 = (bf16[240,128]{1,0:T(8,128)(2,1)S(1)}, bf16[240,128]{1,0:T(8,128)(2,1)S(1)}, u32[]{:S(2)}, u32[]{:S(2)}) collective-permute-start(bf16[240,128]{1,0:T(8,128)(2,1)S(1)} %get-tuple-element.84), channel_id=1, source_target_pairs={{0,12},{1,13},{2,14},{3,15},{4,8},{5,9},{6,10},{7,11},{8,4},{9,5},... | collective-permute-start | bytes 184328 | tf_op jit(solution)/shard_map/ppermute | solution.py:377
  39.7 0.0 collective-permute-start.10
  39.7 0.0 collective-permute-done.7
  39.8 1.3 %collective-permute-start.11 = (bf16[240,128]{1,0:T(8,128)(2,1)S(1)}, bf16[240,128]{1,0:T(8,128)(2,1)S(1)}, u32[]{:S(2)}, u32[]{:S(2)}) collective-permute-start(bf16[240,128]{1,0:T(8,128)(2,1)S(1)} %add_convert_fusion.1), channel_id=1, source_target_pairs={{0,4},{1,5},{2,6},{3,7},{4,0},{5,1},{6,2},{7,3},{8,12},{9,13},{10,... | collective-permute-start | bytes 184328 | tf_op jit(solution)/shard_map/ppermute | solution.py:377
  41.1 0.8 %collective-permute-start.18 = (bf16[128,128]{1,0:T(8,128)(2,1)S(1)}, bf16[128,128]{1,0:T(8,128)(2,1)S(1)}, u32[]{:S(2)}, u32[]{:S(2)}) collective-permute-start(bf16[128,128]{1,0:T(8,128)(2,1)S(1)} %fusion.18), channel_id=1, source_target_pairs={{0,4},{1,5},{2,6},{3,7},{4,0},{5,1},{6,2},{7,3},{8,12},{9,13},{10,... | collective-permute-start | bytes 98312 | tf_op jit(solution)/shard_map/ppermute | solution.py:377
  41.9 0.8 %collective-permute-done.9 = bf16[240,128]{1,0:T(8,128)(2,1)S(1)} collective-permute-done((bf16[240,128]{1,0:T(8,128)(2,1)S(1)}, bf16[240,128]{1,0:T(8,128)(2,1)S(1)}, u32[]{:S(2)}, u32[]{:S(2)}) %collective-permute-start.9) | collective-permute-done | bytes 61472 | tf_op jit(solution)/shard_map/ppermute | solution.py:377
  42.6 2.5 %collective-permute-done.10 = bf16[240,128]{1,0:T(8,128)(2,1)S(1)} collective-permute-done((bf16[240,128]{1,0:T(8,128)(2,1)S(1)}, bf16[240,128]{1,0:T(8,128)(2,1)S(1)}, u32[]{:S(2)}, u32[]{:S(2)}) %collective-permute-start.10) | collective-permute-done | bytes 61472 | tf_op jit(solution)/shard_map/ppermute | solution.py:377
  45.2 0.3 collective-permute-done.11
  45.5 1.3 %collective-permute-start.15 = (bf16[240,128]{1,0:T(8,128)(2,1)S(1)}, bf16[240,128]{1,0:T(8,128)(2,1)S(1)}, u32[]{:S(2)}, u32[]{:S(2)}) collective-permute-start(bf16[240,128]{1,0:T(8,128)(2,1)S(1)} %get-tuple-element.83), channel_id=1, source_target_pairs={{0,2},{1,3},{2,0},{3,1},{4,6},{5,7},{6,4},{7,5},{8,10},{9,11},{10,... | collective-permute-start | bytes 184328 | tf_op jit(solution)/shard_map/ppermute | solution.py:377
  46.8 2.1 %collective-permute-start.14 = (bf16[240,128]{1,0:T(8,128)(2,1)S(1)}, bf16[240,128]{1,0:T(8,128)(2,1)S(1)}, u32[]{:S(2)}, u32[]{:S(2)}) collective-permute-start(bf16[240,128]{1,0:T(8,128)(2,1)S(1)} %get-tuple-element.83), channel_id=1, source_target_pairs={{0,12},{1,13},{2,14},{3,15},{4,8},{5,9},{6,10},{7,11},{8,4},{9,5},... | collective-permute-start | bytes 184328 | tf_op jit(solution)/shard_map/ppermute | solution.py:377
  48.9 0.3 collective-permute-start.13
  49.2 0.0 collective-permute-done.18
  49.2 2.0 %collective-permute-start.12 = (bf16[240,128]{1,0:T(8,128)(2,1)S(1)}, bf16[240,128]{1,0:T(8,128)(2,1)S(1)}, u32[]{:S(2)}, u32[]{:S(2)}) collective-permute-start(bf16[240,128]{1,0:T(8,128)(2,1)S(1)} %get-tuple-element.83), channel_id=1, source_target_pairs={{0,4},{1,5},{2,6},{3,7},{4,0},{5,1},{6,2},{7,3},{8,12},{9,13},{10,... | collective-permute-start | bytes 184328 | tf_op jit(solution)/shard_map/ppermute | solution.py:377
  51.3 0.0 collective-permute-done.15
  51.3 0.7 %collective-permute-start.19 = (bf16[128,128]{1,0:T(8,128)(2,1)S(1)}, bf16[128,128]{1,0:T(8,128)(2,1)S(1)}, u32[]{:S(2)}, u32[]{:S(2)}) collective-permute-start(bf16[128,128]{1,0:T(8,128)(2,1)S(1)} %fusion.19), channel_id=1, source_target_pairs={{0,8},{1,9},{2,10},{3,11},{4,12},{5,13},{6,14},{7,15},{8,0},{9,1},... | collective-permute-start | bytes 98312 | tf_op jit(solution)/shard_map/ppermute | solution.py:377
  52.0 1.4 %collective-permute-done.14 = bf16[240,128]{1,0:T(8,128)(2,1)S(1)} collective-permute-done((bf16[240,128]{1,0:T(8,128)(2,1)S(1)}, bf16[240,128]{1,0:T(8,128)(2,1)S(1)}, u32[]{:S(2)}, u32[]{:S(2)}) %collective-permute-start.14) | collective-permute-done | bytes 61472 | tf_op jit(solution)/shard_map/ppermute | solution.py:377
  53.4 2.1 %collective-permute-done.13 = bf16[240,128]{1,0:T(8,128)(2,1)S(1)} collective-permute-done((bf16[240,128]{1,0:T(8,128)(2,1)S(1)}, bf16[240,128]{1,0:T(8,128)(2,1)S(1)}, u32[]{:S(2)}, u32[]{:S(2)}) %collective-permute-start.13) | collective-permute-done | bytes 61472 | tf_op jit(solution)/shard_map/ppermute | solution.py:377
  55.4 0.8 %collective-permute-start.17 = (bf16[480,128]{1,0:T(8,128)(2,1)S(1)}, bf16[480,128]{1,0:T(8,128)(2,1)S(1)}, u32[]{:S(2)}, u32[]{:S(2)}) collective-permute-start(bf16[480,128]{1,0:T(8,128)(2,1)S(1)} %pad_maximum_fusion.1), channel_id=1, source_target_pairs={{0,2},{1,3},{2,0},{3,1},{4,6},{5,7},{6,4},{7,5},{8,10},{9,11},{10,... | collective-permute-start | bytes 368648 | tf_op jit(solution)/shard_map/ppermute | solution.py:377
  56.3 0.0 collective-permute-done.12
  56.3 1.3 %collective-permute-start.16 = (bf16[240,128]{1,0:T(8,128)(2,1)S(1)}, bf16[240,128]{1,0:T(8,128)(2,1)S(1)}, u32[]{:S(2)}, u32[]{:S(2)}) collective-permute-start(bf16[240,128]{1,0:T(8,128)(2,1)S(1)} %collective-permute-done.12), channel_id=1, source_target_pairs={{0,2},{1,3},{2,0},{3,1},{4,6},{5,7},{6,4},{7,5},{8,10},{9,11},{10,... | collective-permute-start | bytes 184328 | tf_op jit(solution)/shard_map/ppermute | solution.py:377
  57.6 0.0 collective-permute-done.19
  57.7 0.8 %collective-permute-start.20 = (bf16[128,128]{1,0:T(8,128)(2,1)S(1)}, bf16[128,128]{1,0:T(8,128)(2,1)S(1)}, u32[]{:S(2)}, u32[]{:S(2)}) collective-permute-start(bf16[128,128]{1,0:T(8,128)(2,1)S(1)} %fusion.17), channel_id=1, source_target_pairs={{0,2},{1,3},{2,0},{3,1},{4,6},{5,7},{6,4},{7,5},{8,10},{9,11},{10,... | collective-permute-start | bytes 98312 | tf_op jit(solution)/shard_map/ppermute | solution.py:377
  58.5 2.6 %collective-permute-done.16 = bf16[240,128]{1,0:T(8,128)(2,1)S(1)} collective-permute-done((bf16[240,128]{1,0:T(8,128)(2,1)S(1)}, bf16[240,128]{1,0:T(8,128)(2,1)S(1)}, u32[]{:S(2)}, u32[]{:S(2)}) %collective-permute-start.16) | collective-permute-done | bytes 61472 | tf_op jit(solution)/shard_map/ppermute | solution.py:377
  61.1 0.6 collective-permute-done.20
  61.6 0.0 collective-permute-done.17
  61.7 0.1 collective-permute-start.21
  61.8 0.7 %maximum_bitcast_fusion = bf16[4,1,4,64,128]{4,3,2,1,0:T(8,128)(2,1)} fusion(bf16[3,4,64,128]{3,2,1,0:T(8,128)(2,1)S(1)} %get-tuple-element.54, bf16[1,4,64,128]{3,2,1,0:T(8,128)(2,1)S(1)} %bitcast.18), kind=kLoop, calls=%fused_computation.11 | loop fusion | flops 131072 | bytes 524288
  62.5 1.2 %collective-permute-done.21.other = bf16[2176,128]{1,0:T(8,128)(2,1)S(1)} collective-permute-done((bf16[2176,128]{1,0:T(8,128)(2,1)S(1)}, bf16[2176,128]{1,0:T(8,128)(2,1)S(1)}, u32[]{:S(2)}, u32[]{:S(2)}) %collective-permute-start.21) | collective-permute-done | bytes 557088 | tf_op jit(solution)/shard_map/ppermute | solution.py:377
  63.8 2.4 %shard_map.144 = (f32[3456,128]{1,0:T(8,128)}, f32[256,128]{1,0:T(8,128)}, f32[1,128]{1,0:T(1,128)}, f32[1,128]{1,0:T(1,128)}, bf16[4,2,4,64,128]{4,3,2,1,0:T(8,128)(2,1)}) custom-call(s32[7]{0:T(128)S(1)} %pad_add_fusion.sc, bf16[2176,128]{1,0:T(8,128)(2,1)S(1)} %fusion.10.mine, ...), custom_call_target="tpu_custom_call", output_to_operand_aliasing={{4}: (5, {})} | custom-call | tf_op jit(solution)/shard_map/pallas_call | solution.py:648
  (30 shorter events, 0.5 us)
Async XLA Ops:
  2.2 1.6 %collective-permute-start = (bf16[12,64,128]{2,1,0:T(8,128)(2,1)S(1)}, bf16[12,64,128]{2,1,0:T(8,128)(2,1)S(1)}, u32[]{:S(2)}, u32[]{:S(2)}) collective-permute-start(bf16[12,64,128]{2,1,0:T(8,128)(2,1)S(1)} %shard_map.136), channel_id=1, source_target_pairs={{0,1},{1,0},{2,3},{3,2},{4,5},{5,4},{6,7},{7,6},{8,9},{9,8},{10,11... | collective-permute-start | bytes 589832 | tf_op jit(solution)/shard_map/ppermute | solution.py:377
  3.9 7.3 %collective-permute-start.1 = (bf16[6,64,128]{2,1,0:T(8,128)(2,1)S(1)}, bf16[6,64,128]{2,1,0:T(8,128)(2,1)S(1)}, u32[]{:S(2)}, u32[]{:S(2)}) collective-permute-start(bf16[6,64,128]{2,1,0:T(8,128)(2,1)S(1)} %fusion.7), channel_id=1, source_target_pairs={{0,2},{1,3},{2,0},{3,1},{4,6},{5,7},{6,4},{7,5},{8,10},{9,11},{10,... | collective-permute-start | bytes 294920 | tf_op jit(solution)/shard_map/ppermute | solution.py:377
  11.2 4.7 %collective-permute-start.2 = (bf16[6,64,128]{2,1,0:T(8,128)(2,1)S(1)}, bf16[6,64,128]{2,1,0:T(8,128)(2,1)S(1)}, u32[]{:S(2)}, u32[]{:S(2)}) collective-permute-start(bf16[6,64,128]{2,1,0:T(8,128)(2,1)S(1)} %fusion.8), channel_id=1, source_target_pairs={{0,4},{1,5},{2,6},{3,7},{4,0},{5,1},{6,2},{7,3},{8,12},{9,13},{10,... | collective-permute-start | bytes 294920 | tf_op jit(solution)/shard_map/ppermute | solution.py:377
  15.9 6.7 %collective-permute-start.3 = (bf16[6,64,128]{2,1,0:T(8,128)(2,1)S(1)}, bf16[6,64,128]{2,1,0:T(8,128)(2,1)S(1)}, u32[]{:S(2)}, u32[]{:S(2)}) collective-permute-start(bf16[6,64,128]{2,1,0:T(8,128)(2,1)S(1)} %fusion.9), channel_id=1, source_target_pairs={{0,8},{1,9},{2,10},{3,11},{4,12},{5,13},{6,14},{7,15},{8,0},{9,1},... | collective-permute-start | bytes 294920 | tf_op jit(solution)/shard_map/ppermute | solution.py:377
  18.6 5.5 %copy-start = (bf16[3,3,3,128,128]{4,3,2,1,0:T(8,128)(2,1)S(1)}, bf16[3,3,3,128,128]{4,3,2,1,0:T(8,128)(2,1)}, u32[]{:S(2)}) copy-start(bf16[3,3,3,128,128]{4,3,2,1,0:T(8,128)(2,1)} %param.13) | copy-start | bytes 2654212
  18.6 5.5 %copy-start.1 = (bf16[4,2,4,64,128]{4,3,2,1,0:T(8,128)(2,1)S(1)}, bf16[4,2,4,64,128]{4,3,2,1,0:T(8,128)(2,1)}, u32[]{:S(2)}) copy-start(bf16[4,2,4,64,128]{4,3,2,1,0:T(8,128)(2,1)} %frs.1) | copy-start | bytes 1572868
  18.6 5.5 %copy-start.2 = (bf16[4,2,2,64,128]{4,3,2,1,0:T(8,128)(2,1)S(1)}, bf16[4,2,2,64,128]{4,3,2,1,0:T(8,128)(2,1)}, u32[]{:S(2)}) copy-start(bf16[4,2,2,64,128]{4,3,2,1,0:T(8,128)(2,1)} %has.1) | copy-start | bytes 786436
  18.6 5.5 %copy-start.3 = (bf16[4,1,4,64,128]{4,3,2,1,0:T(8,128)(2,1)S(1)}, bf16[4,1,4,64,128]{4,3,2,1,0:T(8,128)(2,1)}, u32[]{:S(2)}) copy-start(bf16[4,1,4,64,128]{4,3,2,1,0:T(8,128)(2,1)} %cos.1) | copy-start | bytes 786436
  18.6 5.5 %copy-start.4 = (bf16[2,128,128]{2,1,0:T(8,128)(2,1)S(1)}, bf16[2,128,128]{2,1,0:T(8,128)(2,1)}, u32[]{:S(2)}) copy-start(bf16[2,128,128]{2,1,0:T(8,128)(2,1)} %sw.1) | copy-start | bytes 196612
  18.6 5.5 %copy-start.5 = (f32[128]{0:T(128)S(1)}, f32[128]{0:T(128)}, u32[]{:S(2)}) copy-start(f32[128]{0:T(128)} %param.14) | copy-start | bytes 1540
  18.6 5.5 %copy-start.6 = (f32[128]{0:T(128)S(1)}, f32[128]{0:T(128)}, u32[]{:S(2)}) copy-start(f32[128]{0:T(128)} %param.16) | copy-start | bytes 1540
  22.7 1.4 %collective-permute-start.4 = (bf16[6,64,128]{2,1,0:T(8,128)(2,1)S(1)}, bf16[6,64,128]{2,1,0:T(8,128)(2,1)S(1)}, u32[]{:S(2)}, u32[]{:S(2)}) collective-permute-start(bf16[6,64,128]{2,1,0:T(8,128)(2,1)S(1)} %fusion.2), channel_id=1, source_target_pairs={{0,1},{1,0},{2,3},{3,2},{4,5},{5,4},{6,7},{7,6},{8,9},{9,8},{10,11... | collective-permute-start | bytes 294920 | tf_op jit(solution)/shard_map/ppermute | solution.py:377
  27.0 1.9 %collective-permute-start.5 = (bf16[1920,128]{1,0:T(8,128)(2,1)S(1)}, bf16[1920,128]{1,0:T(8,128)(2,1)S(1)}, u32[]{:S(2)}, u32[]{:S(2)}) collective-permute-start(bf16[1920,128]{1,0:T(8,128)(2,1)S(1)} %get-tuple-element.58), channel_id=1, source_target_pairs={{0,1},{1,0},{2,3},{3,2},{4,5},{5,4},{6,7},{7,6},{8,9},{9,8},{10,11... | collective-permute-start | bytes 1474568 | tf_op jit(solution)/shard_map/ppermute | solution.py:377
  29.6 1.4 %collective-permute-start.6 = (bf16[512,128]{1,0:T(8,128)(2,1)S(1)}, bf16[512,128]{1,0:T(8,128)(2,1)S(1)}, u32[]{:S(2)}, u32[]{:S(2)}) collective-permute-start(bf16[512,128]{1,0:T(8,128)(2,1)S(1)} %shard_map.141), channel_id=1, source_target_pairs={{0,1},{1,0},{2,3},{3,2},{4,5},{5,4},{6,7},{7,6},{8,9},{9,8},{10,11... | collective-permute-start | bytes 393224 | tf_op jit(solution)/shard_map/ppermute | solution.py:377
  29.8 6.4 %collective-permute-start.8 = (bf16[480,128]{1,0:T(8,128)(2,1)S(1)}, bf16[480,128]{1,0:T(8,128)(2,1)S(1)}, u32[]{:S(2)}, u32[]{:S(2)}) collective-permute-start(bf16[480,128]{1,0:T(8,128)(2,1)S(1)} %get-tuple-element.62), channel_id=1, source_target_pairs={{0,2},{1,3},{2,0},{3,1},{4,6},{5,7},{6,4},{7,5},{8,10},{9,11},{10,... | collective-permute-start | bytes 368648 | tf_op jit(solution)/shard_map/ppermute | solution.py:377
  31.1 8.7 %collective-permute-start.7 = (bf16[736,128]{1,0:T(8,128)(2,1)S(1)}, bf16[736,128]{1,0:T(8,128)(2,1)S(1)}, u32[]{:S(2)}, u32[]{:S(2)}) collective-permute-start(bf16[736,128]{1,0:T(8,128)(2,1)S(1)} %pad_maximum_fusion), channel_id=1, source_target_pairs={{0,2},{1,3},{2,0},{3,1},{4,6},{5,7},{6,4},{7,5},{8,10},{9,11},{10,... | collective-permute-start | bytes 565256 | tf_op jit(solution)/shard_map/ppermute | solution.py:377
  36.2 6.4 %collective-permute-start.9 = (bf16[240,128]{1,0:T(8,128)(2,1)S(1)}, bf16[240,128]{1,0:T(8,128)(2,1)S(1)}, u32[]{:S(2)}, u32[]{:S(2)}) collective-permute-start(bf16[240,128]{1,0:T(8,128)(2,1)S(1)} %get-tuple-element.84), channel_id=1, source_target_pairs={{0,12},{1,13},{2,14},{3,15},{4,8},{5,9},{6,10},{7,11},{8,4},{9,5},... | collective-permute-start | bytes 184328 | tf_op jit(solution)/shard_map/ppermute | solution.py:377
  39.7 5.5 %collective-permute-start.10 = (bf16[240,128]{1,0:T(8,128)(2,1)S(1)}, bf16[240,128]{1,0:T(8,128)(2,1)S(1)}, u32[]{:S(2)}, u32[]{:S(2)}) collective-permute-start(bf16[240,128]{1,0:T(8,128)(2,1)S(1)} %get-tuple-element.85), channel_id=1, source_target_pairs={{0,8},{1,9},{2,10},{3,11},{4,12},{5,13},{6,14},{7,15},{8,0},{9,1},... | collective-permute-start | bytes 184328 | tf_op jit(solution)/shard_map/ppermute | solution.py:377
  39.8 5.7 %collective-permute-start.11 = (bf16[240,128]{1,0:T(8,128)(2,1)S(1)}, bf16[240,128]{1,0:T(8,128)(2,1)S(1)}, u32[]{:S(2)}, u32[]{:S(2)}) collective-permute-start(bf16[240,128]{1,0:T(8,128)(2,1)S(1)} %add_convert_fusion.1), channel_id=1, source_target_pairs={{0,4},{1,5},{2,6},{3,7},{4,0},{5,1},{6,2},{7,3},{8,12},{9,13},{10,... | collective-permute-start | bytes 184328 | tf_op jit(solution)/shard_map/ppermute | solution.py:377
  41.1 8.1 %collective-permute-start.18 = (bf16[128,128]{1,0:T(8,128)(2,1)S(1)}, bf16[128,128]{1,0:T(8,128)(2,1)S(1)}, u32[]{:S(2)}, u32[]{:S(2)}) collective-permute-start(bf16[128,128]{1,0:T(8,128)(2,1)S(1)} %fusion.18), channel_id=1, source_target_pairs={{0,4},{1,5},{2,6},{3,7},{4,0},{5,1},{6,2},{7,3},{8,12},{9,13},{10,... | collective-permute-start | bytes 98312 | tf_op jit(solution)/shard_map/ppermute | solution.py:377
  45.5 5.8 %collective-permute-start.15 = (bf16[240,128]{1,0:T(8,128)(2,1)S(1)}, bf16[240,128]{1,0:T(8,128)(2,1)S(1)}, u32[]{:S(2)}, u32[]{:S(2)}) collective-permute-start(bf16[240,128]{1,0:T(8,128)(2,1)S(1)} %get-tuple-element.83), channel_id=1, source_target_pairs={{0,2},{1,3},{2,0},{3,1},{4,6},{5,7},{6,4},{7,5},{8,10},{9,11},{10,... | collective-permute-start | bytes 184328 | tf_op jit(solution)/shard_map/ppermute | solution.py:377
  46.8 6.6 %collective-permute-start.14 = (bf16[240,128]{1,0:T(8,128)(2,1)S(1)}, bf16[240,128]{1,0:T(8,128)(2,1)S(1)}, u32[]{:S(2)}, u32[]{:S(2)}) collective-permute-start(bf16[240,128]{1,0:T(8,128)(2,1)S(1)} %get-tuple-element.83), channel_id=1, source_target_pairs={{0,12},{1,13},{2,14},{3,15},{4,8},{5,9},{6,10},{7,11},{8,4},{9,5},... | collective-permute-start | bytes 184328 | tf_op jit(solution)/shard_map/ppermute | solution.py:377
  48.9 6.5 %collective-permute-start.13 = (bf16[240,128]{1,0:T(8,128)(2,1)S(1)}, bf16[240,128]{1,0:T(8,128)(2,1)S(1)}, u32[]{:S(2)}, u32[]{:S(2)}) collective-permute-start(bf16[240,128]{1,0:T(8,128)(2,1)S(1)} %get-tuple-element.83), channel_id=1, source_target_pairs={{0,8},{1,9},{2,10},{3,11},{4,12},{5,13},{6,14},{7,15},{8,0},{9,1},... | collective-permute-start | bytes 184328 | tf_op jit(solution)/shard_map/ppermute | solution.py:377
  49.2 7.0 %collective-permute-start.12 = (bf16[240,128]{1,0:T(8,128)(2,1)S(1)}, bf16[240,128]{1,0:T(8,128)(2,1)S(1)}, u32[]{:S(2)}, u32[]{:S(2)}) collective-permute-start(bf16[240,128]{1,0:T(8,128)(2,1)S(1)} %get-tuple-element.83), channel_id=1, source_target_pairs={{0,4},{1,5},{2,6},{3,7},{4,0},{5,1},{6,2},{7,3},{8,12},{9,13},{10,... | collective-permute-start | bytes 184328 | tf_op jit(solution)/shard_map/ppermute | solution.py:377
  51.3 6.3 %collective-permute-start.19 = (bf16[128,128]{1,0:T(8,128)(2,1)S(1)}, bf16[128,128]{1,0:T(8,128)(2,1)S(1)}, u32[]{:S(2)}, u32[]{:S(2)}) collective-permute-start(bf16[128,128]{1,0:T(8,128)(2,1)S(1)} %fusion.19), channel_id=1, source_target_pairs={{0,8},{1,9},{2,10},{3,11},{4,12},{5,13},{6,14},{7,15},{8,0},{9,1},... | collective-permute-start | bytes 98312 | tf_op jit(solution)/shard_map/ppermute | solution.py:377
  55.4 6.2 %collective-permute-start.17 = (bf16[480,128]{1,0:T(8,128)(2,1)S(1)}, bf16[480,128]{1,0:T(8,128)(2,1)S(1)}, u32[]{:S(2)}, u32[]{:S(2)}) collective-permute-start(bf16[480,128]{1,0:T(8,128)(2,1)S(1)} %pad_maximum_fusion.1), channel_id=1, source_target_pairs={{0,2},{1,3},{2,0},{3,1},{4,6},{5,7},{6,4},{7,5},{8,10},{9,11},{10,... | collective-permute-start | bytes 368648 | tf_op jit(solution)/shard_map/ppermute | solution.py:377
  56.3 4.8 %collective-permute-start.16 = (bf16[240,128]{1,0:T(8,128)(2,1)S(1)}, bf16[240,128]{1,0:T(8,128)(2,1)S(1)}, u32[]{:S(2)}, u32[]{:S(2)}) collective-permute-start(bf16[240,128]{1,0:T(8,128)(2,1)S(1)} %collective-permute-done.12), channel_id=1, source_target_pairs={{0,2},{1,3},{2,0},{3,1},{4,6},{5,7},{6,4},{7,5},{8,10},{9,11},{10,... | collective-permute-start | bytes 184328 | tf_op jit(solution)/shard_map/ppermute | solution.py:377
  57.7 4.0 %collective-permute-start.20 = (bf16[128,128]{1,0:T(8,128)(2,1)S(1)}, bf16[128,128]{1,0:T(8,128)(2,1)S(1)}, u32[]{:S(2)}, u32[]{:S(2)}) collective-permute-start(bf16[128,128]{1,0:T(8,128)(2,1)S(1)} %fusion.17), channel_id=1, source_target_pairs={{0,2},{1,3},{2,0},{3,1},{4,6},{5,7},{6,4},{7,5},{8,10},{9,11},{10,... | collective-permute-start | bytes 98312 | tf_op jit(solution)/shard_map/ppermute | solution.py:377
  61.7 2.0 %collective-permute-start.21 = (bf16[2176,128]{1,0:T(8,128)(2,1)S(1)}, bf16[2176,128]{1,0:T(8,128)(2,1)S(1)}, u32[]{:S(2)}, u32[]{:S(2)}) collective-permute-start(bf16[2176,128]{1,0:T(8,128)(2,1)S(1)} %fusion.10.mine), channel_id=1, source_target_pairs={{0,1},{1,0},{2,3},{3,2},{4,5},{5,4},{6,7},{7,6},{8,9},{9,8},{10,11... | collective-permute-start | bytes 1671176 | tf_op jit(solution)/shard_map/ppermute | solution.py:377

commit v12 on v9

--- a/solution.py
+++ b/solution.py
@@ -539,7 +539,6 @@
         moved=1 << 20,
         room=8,
     )(sc, g0, wt)
-    keep = _after(keep, first_grad)
     send_far, send_near, kept = _call(
         _across_x_kernel,
         [
@@ -549,9 +548,8 @@
         ],
         [_SMEM] + [_VMEM] * 2,
         room=8,
-    )(sc, keep, got)
+    )(sc, _after(keep, first_grad), got)
     got_far = _xor(send_far, 2, n, axis)
-    got_near = _xor(send_near, 2, n, axis)
     got_first = _xor(_after(first_grad, kept), 1, n, axis)
     core, pair = index & 1, (index >> 1) & 1
 
@@ -566,19 +564,8 @@
         return by(bit, _first_live(ours, theirs), _first_live(theirs, ours))
 
     chip_first = ordered(core, by_half(core, first_grad), by_half(core, got_first))
-    beside_first = _xor(chip_first, 2, n, axis)
-    got_far = _after(got_far, chip_first)
-
-    def summed(j, came):
-        i = j % 2
-        return kept[j * piece : (j + 1) * piece] + came[i * piece : (i + 1) * piece].astype(F32)
-
-    outs = {j: summed(j, got_far).astype(BF) for j in (3, 2)}
-    got_near = _after(got_near, outs[3], outs[2])
-    outs[1] = summed(1, got_near).astype(BF)
-    gots = {j: _xor(outs[j], 4 * j, n, axis) for j in (3, 2, 1)}
-    lead = ordered(pair, by_half(pair, chip_first), by_half(pair, beside_first))
-    near_lead = _xor(lead, 4, n, axis)
+    send_near = jnp.concatenate([send_near, chip_first], axis=0)
+    got_near = _xor(send_near, 2, n, axis)
     grad = _call(
         _back_kernel,
         jax.ShapeDtypeStruct((slots, 2, h, w, c), F32),
@@ -587,8 +574,21 @@
         flops=1,
         moved=1,
         room=24,
-    )(_after(sc, outs[1]), g0, g1, wt)
-    mine = summed(0, _after(got_near, grad))
+    )(_after(sc, send_near), g0, g1, wt)
+    got_far = _after(got_far, grad)
+
+    def summed(j, came):
+        i = j % 2
+        return kept[j * piece : (j + 1) * piece] + came[i * piece : (i + 1) * piece].astype(F32)
+
+    outs = {j: summed(j, got_far).astype(BF) for j in (3, 2)}
+    got_near = _after(got_near, outs[3], outs[2])
+    outs[1] = summed(1, got_near).astype(BF)
+    gots = {j: _xor(outs[j], 4 * j, n, axis) for j in (3, 2, 1)}
+    beside_first = got_near[2 * piece :]
+    lead = ordered(pair, by_half(pair, chip_first), by_half(pair, beside_first))
+    near_lead = _xor(lead, 4, n, axis)
+    mine = summed(0, _after(got_near, outs[1]))
     for j in (3, 2):
         mine = mine + gots[j].astype(F32)
     gots[1] = _after(gots[1], mine)
@@ -602,7 +602,7 @@
     x_near = _xor(others[1], 2, n, axis)
     x_far = _xor(jnp.concatenate([others[2], others[3]], axis=0), 2, n, axis)
     beyond = by(index & 4, near_lead, jnp.full_like(lead, EMPTY_GRAD))
-    lead, k = _after(ordered(index & 4, lead, near_lead), mine), 8
+    lead, k = _after(ordered(index & 4, lead, near_lead), x_own), 8
     while k < n:
         came = _xor(lead, k, n, axis)
         beyond = by(index & k, _first_live(beyond, came), beyond)

time: 68.5 us -> 65.7 us (0.959)
  starting transfers between devices: 26.9 us -> 24.9 us
  waiting for transfers between devices: 17.4 us -> 16.7 us
    ppermute x23 -> x22, starting transfers between devices: 26.9 us -> 24.9 us  [_xor(): return lax.ppermute(x, axis, [(i, i ^ k) for i in range(n)])]
    ppermute x23 -> x22, waiting for transfers between devices: 17.4 us -> 16.7 us  [_xor(): return lax.ppermute(x, axis, [(i, i ^ k) for i in range(n)])]
  transfers between devices with their start and end apart: 23 -> 22, of which waited for: 11 -> 14; matrix products, arithmetic and copies ran while one was open for 3% -> 3% of each run, Pallas kernels for 20% -> 21%
where the time goes in v12:
time: 65.7 us; the launch traced here: 65.5 us
  starting transfers between devices  24.9 us (38%)
  Pallas kernels  20.3 us (31%)
  waiting for transfers between devices  16.7 us (25%)
  other arithmetic  1.96 us (3%)
  between operations  1.59 us (2%)
    ppermute x22, starting transfers between devices, _xor(): return lax.ppermute(x, axis, [(i, i ^ k) for i in range(n)])  24.9 us
    ppermute x22, waiting for transfers between devices, _xor(): return lax.ppermute(x, axis, [(i, i ^ k) for i in range(n)])  16.7 us
    pallas_call x1, Pallas kernels, early_conv(): _call(_early_conv_kernel, [jax.ShapeDtypeStruct(wide, F32), jax.ShapeDtyp...  4.4 us
    pallas_call x1, Pallas kernels, early_sums(): _call(_early_sums_kernel, jax.ShapeDtypeStruct((rows, c), F32), [_SMEM, _...  3.94 us
    pallas_call x1, Pallas kernels, body(): _call(_back_kernel, jax.ShapeDtypeStruct((slots, 2, h, w, c), F32), [_SME...  3.39 us
    pallas_call x1, Pallas kernels, body(): _call(_late_kernel, [jax.ShapeDtypeStruct((h, w, c), BF), jax.ShapeDtypeS...  2.78 us
    pallas_call x1, Pallas kernels, body(): _call(_final_kernel, [jax.ShapeDtypeStruct((27 * c, c), F32), jax.ShapeDt...  2.18 us
  transfers between devices with their start and end apart: 22, of which 14 were waited for; matrix products, arithmetic and copies ran while one was open for 3% of the time, Pallas kernels for 21%

profile of v12, /device:TPU:0, one launch (start us, length us, event | category | flops | bytes accessed | tf_op | source)
XLA Modules:
  0.0 65.5 jit_solution(3116982999475925901)
XLA Ops:
  1.3 1.0 %shard_map.136 = bf16[12,64,128]{2,1,0:T(8,128)(2,1)S(1)} custom-call(s32[1]{0:T(128)S(6)} %copy.23.sc, bf16[4,2,4,64,128]{4,3,2,1,0:T(8,128)(2,1)} %frs.1, bf16[4,2,2,64,128]{4,3,2,1,0:T(8,128)(2,1)} %has.1), custom_call_target="tpu_custom_call" | custom-call | tf_op jit(solution)/shard_map/pallas_call | solution.py:435
  2.2 0.5 collective-permute-start
  2.8 0.7 %pad_add_fusion.sc = s32[7]{0:T(128)S(1)} fusion(s32[1]{0:T(128)} %bitcast.1, s32[1]{0:T(128)} %bitcast, s32[4]{0:T(128)} %param.11, s32[1]{0:T(128)S(6)} %copy.23.sc), kind=kLoop, calls=%fused_computation.62 | loop fusion | flops 21 | bytes 56 | tf_op jit(solution)/shard_map/concatenate | solution.py:417
  3.5 0.3 collective-permute-done
  3.9 2.9 %collective-permute-start.1 = (bf16[6,64,128]{2,1,0:T(8,128)(2,1)S(1)}, bf16[6,64,128]{2,1,0:T(8,128)(2,1)S(1)}, u32[]{:S(2)}, u32[]{:S(2)}) collective-permute-start(bf16[6,64,128]{2,1,0:T(8,128)(2,1)S(1)} %fusion.7), channel_id=1, source_target_pairs={{0,2},{1,3},{2,0},{3,1},{4,6},{5,7},{6,4},{7,5},{8,10},{9,11},{10,... | collective-permute-start | bytes 294920 | tf_op jit(solution)/shard_map/ppermute | solution.py:354
  6.8 4.4 %shard_map.137 = (f32[768,256]{1,0:T(8,128)S(1)}, bf16[768,128]{1,0:T(8,128)(2,1)S(1)}, bf16[2,128,128]{2,1,0:T(8,128)(2,1)S(1)}, f32[1,128]{1,0:T(1,128)S(1)}) custom-call(s32[7]{0:T(128)S(1)} %pad_add_fusion.sc, bf16[4,2,4,64,128]{4,3,2,1,0:T(8,128)(2,1)} %frs.1, bf16[4,2,2,64,128]{4,3,2,1,0:T(8,128)(2,1)} %has.1, bf16[4,1,4,64,128]{4,3,2,1,0:T(8,128)(2,1)} %cos.1, ...), custom_call_target="tpu_custom_call" | custom-call | flops 1811939328 | bytes 4194304 | tf_op jit(solution)/shard_map/pallas_call | solution.py:462
  11.2 0.0 collective-permute-done.1
  11.2 1.6 %collective-permute-start.2 = (bf16[6,64,128]{2,1,0:T(8,128)(2,1)S(1)}, bf16[6,64,128]{2,1,0:T(8,128)(2,1)S(1)}, u32[]{:S(2)}, u32[]{:S(2)}) collective-permute-start(bf16[6,64,128]{2,1,0:T(8,128)(2,1)S(1)} %fusion.8), channel_id=1, source_target_pairs={{0,4},{1,5},{2,6},{3,7},{4,0},{5,1},{6,2},{7,3},{8,12},{9,13},{10,... | collective-permute-start | bytes 294920 | tf_op jit(solution)/shard_map/ppermute | solution.py:354
  12.9 1.0 %shard_map.138 = (bf16[3,4,64,128]{3,2,1,0:T(8,128)(2,1)S(1)}, bf16[768,256]{1,0:T(8,128)(2,1)S(1)}, bf16[768,256]{1,0:T(8,128)(2,1)S(1)}) custom-call(s32[7]{0:T(128)S(1)} %pad_add_fusion.sc, f32[768,256]{1,0:T(8,128)S(1)} %get-tuple-element.40.pre_ref, bf16[768,128]{1,0:T(8,128)(2,1)S(1)} %get-tuple-element.43.gout_ref, ...), custom_call_target="tpu_custom_call" | custom-call | bytes 2097152 | tf_op jit(solution)/shard_map/pallas_call | solution.py:480
  13.9 2.1 %collective-permute-done.2 = bf16[6,64,128]{2,1,0:T(8,128)(2,1)S(1)} collective-permute-done((bf16[6,64,128]{2,1,0:T(8,128)(2,1)S(1)}, bf16[6,64,128]{2,1,0:T(8,128)(2,1)S(1)}, u32[]{:S(2)}, u32[]{:S(2)}) %collective-permute-start.2) | collective-permute-done | bytes 98336 | tf_op jit(solution)/shard_map/ppermute | solution.py:354
  16.0 2.7 %collective-permute-start.3 = (bf16[6,64,128]{2,1,0:T(8,128)(2,1)S(1)}, bf16[6,64,128]{2,1,0:T(8,128)(2,1)S(1)}, u32[]{:S(2)}, u32[]{:S(2)}) collective-permute-start(bf16[6,64,128]{2,1,0:T(8,128)(2,1)S(1)} %fusion.9), channel_id=1, source_target_pairs={{0,8},{1,9},{2,10},{3,11},{4,12},{5,13},{6,14},{7,15},{8,0},{9,1},... | collective-permute-start | bytes 294920 | tf_op jit(solution)/shard_map/ppermute | solution.py:354
  18.6 0.0 copy-start.4
  18.6 0.0 copy-start.5
  18.6 0.0 copy-start.6
  18.7 3.9 %shard_map.139.early = f32[3840,128]{1,0:T(8,128)S(1)} custom-call(s32[7]{0:T(128)S(1)} %pad_add_fusion.sc, bf16[4,2,4,64,128]{4,3,2,1,0:T(8,128)(2,1)} %frs.1, bf16[4,2,2,64,128]{4,3,2,1,0:T(8,128)(2,1)} %has.1, bf16[768,256]{1,0:T(8,128)(2,1)S(1)} %get-tuple-element.46.g_ref.g1, bf16[768,256]{1,0:T(8,128)(2,1)S(1)} %get-tuple-element.49.hid_ref, ...), custom_call_target="tpu_custom_call" | custom-call | flops 1811939328 | bytes 4194304 | tf_op jit(solution)/shard_map/pallas_call | solution.py:496
  22.6 0.0 collective-permute-done.3
  22.7 0.1 collective-permute-start.4
  22.7 1.3 %collective-permute-done.4 = bf16[6,64,128]{2,1,0:T(8,128)(2,1)S(1)} collective-permute-done((bf16[6,64,128]{2,1,0:T(8,128)(2,1)S(1)}, bf16[6,64,128]{2,1,0:T(8,128)(2,1)S(1)}, u32[]{:S(2)}, u32[]{:S(2)}) %collective-permute-start.4) | collective-permute-done | bytes 98336 | tf_op jit(solution)/shard_map/ppermute | solution.py:354
  24.1 0.1 compare_select_fusion.tail
  24.1 0.0 copy-done
  24.1 0.0 copy-done.1
  24.1 0.0 copy-done.2
  24.1 0.0 copy-done.3
  24.2 2.8 %shard_map.140 = (bf16[4,64,128]{2,1,0:T(8,128)(2,1)S(1)}, bf16[256,256]{1,0:T(8,128)(2,1)S(1)}, bf16[1920,128]{1,0:T(8,128)(2,1)S(1)}, f32[1920,128]{1,0:T(8,128)S(1)}) custom-call(s32[7]{0:T(128)S(1)} %pad_add_fusion.sc, bf16[4,2,4,64,128]{4,3,2,1,0:T(8,128)(2,1)S(1)} %copy-done.1, bf16[4,2,2,64,128]{4,3,2,1,0:T(8,128)(2,1)S(1)} %copy-done.2, ...), custom_call_target="tpu_custom_call" | custom-call | flops 1207959552 | bytes 6291456 | tf_op jit(solution)/shard_map/pallas_call | solution.py:515
  27.0 0.2 collective-permute-start.5
  27.2 1.1 %shard_map.141 = bf16[512,128]{1,0:T(8,128)(2,1)S(1)} custom-call(s32[7]{0:T(128)S(1)} %pad_add_fusion.sc, bf16[256,256]{1,0:T(8,128)(2,1)S(1)} %get-tuple-element.54.g_ref.g0, bf16[27,128,128]{2,1,0:T(8,128)(2,1)S(1)} %bitcast.16), custom_call_target="tpu_custom_call" | custom-call | flops 301989888 | bytes 1048576 | tf_op jit(solution)/shard_map/pallas_call | solution.py:533
  28.2 0.6 collective-permute-done.5.got
  28.9 0.6 shard_map.142
  29.5 0.2 collective-permute-start.6
  29.8 0.6 collective-permute-start.8
  30.3 0.6 collective-permute-done.6.got
  31.0 0.1 fusion.11
  31.0 0.9 %collective-permute-start.7 = (bf16[736,128]{1,0:T(8,128)(2,1)S(1)}, bf16[736,128]{1,0:T(8,128)(2,1)S(1)}, u32[]{:S(2)}, u32[]{:S(2)}) collective-permute-start(bf16[736,128]{1,0:T(8,128)(2,1)S(1)} %pad_maximum_fusion), channel_id=1, source_target_pairs={{0,2},{1,3},{2,0},{3,1},{4,6},{5,7},{6,4},{7,5},{8,10},{9,11},{10,... | collective-permute-start | bytes 565256 | tf_op jit(solution)/shard_map/ppermute | solution.py:354
  31.9 3.4 %shard_map.143.grad = f32[4,2,4,64,128]{4,3,2,1,0:T(8,128)S(1)} custom-call(s32[7]{0:T(128)S(1)} %pad_add_fusion.sc, bf16[256,256]{1,0:T(8,128)(2,1)S(1)} %get-tuple-element.54.g_ref.g0, bf16[768,256]{1,0:T(8,128)(2,1)S(1)} %get-tuple-element.46.g_ref.g1, bf16[27,128,128]{2,1,0:T(8,128)(2,1)S(1)} %bitcast.17), custom_call_target="tpu_custom_call" | custom-call | flops 1 | bytes 1 | tf_op jit(solution)/shard_map/pallas_call | solution.py:569
  35.3 0.6 collective-permute-done.8
  35.9 3.5 %collective-permute-start.9 = (bf16[240,128]{1,0:T(8,128)(2,1)S(1)}, bf16[240,128]{1,0:T(8,128)(2,1)S(1)}, u32[]{:S(2)}, u32[]{:S(2)}) collective-permute-start(bf16[240,128]{1,0:T(8,128)(2,1)S(1)} %get-tuple-element.80), channel_id=1, source_target_pairs={{0,12},{1,13},{2,14},{3,15},{4,8},{5,9},{6,10},{7,11},{8,4},{9,5},... | collective-permute-start | bytes 184328 | tf_op jit(solution)/shard_map/ppermute | solution.py:354
  39.5 0.0 collective-permute-start.10
  39.5 0.0 collective-permute-done.7
  39.5 1.6 %collective-permute-start.11 = (bf16[240,128]{1,0:T(8,128)(2,1)S(1)}, bf16[240,128]{1,0:T(8,128)(2,1)S(1)}, u32[]{:S(2)}, u32[]{:S(2)}) collective-permute-start(bf16[240,128]{1,0:T(8,128)(2,1)S(1)} %add_convert_fusion.1), channel_id=1, source_target_pairs={{0,4},{1,5},{2,6},{3,7},{4,0},{5,1},{6,2},{7,3},{8,12},{9,13},{10,... | collective-permute-start | bytes 184328 | tf_op jit(solution)/shard_map/ppermute | solution.py:354
  41.1 0.5 collective-permute-start.18
  41.6 0.5 collective-permute-done.9
  42.1 2.5 %collective-permute-done.10 = bf16[240,128]{1,0:T(8,128)(2,1)S(1)} collective-permute-done((bf16[240,128]{1,0:T(8,128)(2,1)S(1)}, bf16[240,128]{1,0:T(8,128)(2,1)S(1)}, u32[]{:S(2)}, u32[]{:S(2)}) %collective-permute-start.10) | collective-permute-done | bytes 61472 | tf_op jit(solution)/shard_map/ppermute | solution.py:354
  44.7 0.5 collective-permute-done.11
  45.2 0.8 %collective-permute-start.15 = (bf16[240,128]{1,0:T(8,128)(2,1)S(1)}, bf16[240,128]{1,0:T(8,128)(2,1)S(1)}, u32[]{:S(2)}, u32[]{:S(2)}) collective-permute-start(bf16[240,128]{1,0:T(8,128)(2,1)S(1)} %get-tuple-element.79), channel_id=1, source_target_pairs={{0,2},{1,3},{2,0},{3,1},{4,6},{5,7},{6,4},{7,5},{8,10},{9,11},{10,... | collective-permute-start | bytes 184328 | tf_op jit(solution)/shard_map/ppermute | solution.py:354
  46.0 2.5 %collective-permute-start.14 = (bf16[240,128]{1,0:T(8,128)(2,1)S(1)}, bf16[240,128]{1,0:T(8,128)(2,1)S(1)}, u32[]{:S(2)}, u32[]{:S(2)}) collective-permute-start(bf16[240,128]{1,0:T(8,128)(2,1)S(1)} %get-tuple-element.79), channel_id=1, source_target_pairs={{0,12},{1,13},{2,14},{3,15},{4,8},{5,9},{6,10},{7,11},{8,4},{9,5},... | collective-permute-start | bytes 184328 | tf_op jit(solution)/shard_map/ppermute | solution.py:354
  48.5 0.0 collective-permute-start.13
  48.5 0.0 collective-permute-done.18
  48.6 1.9 %collective-permute-start.12 = (bf16[240,128]{1,0:T(8,128)(2,1)S(1)}, bf16[240,128]{1,0:T(8,128)(2,1)S(1)}, u32[]{:S(2)}, u32[]{:S(2)}) collective-permute-start(bf16[240,128]{1,0:T(8,128)(2,1)S(1)} %get-tuple-element.79), channel_id=1, source_target_pairs={{0,4},{1,5},{2,6},{3,7},{4,0},{5,1},{6,2},{7,3},{8,12},{9,13},{10,... | collective-permute-start | bytes 184328 | tf_op jit(solution)/shard_map/ppermute | solution.py:354
  50.5 0.0 collective-permute-done.15
  50.5 1.2 %collective-permute-start.19 = (bf16[128,128]{1,0:T(8,128)(2,1)S(1)}, bf16[128,128]{1,0:T(8,128)(2,1)S(1)}, u32[]{:S(2)}, u32[]{:S(2)}) collective-permute-start(bf16[128,128]{1,0:T(8,128)(2,1)S(1)} %fusion.19), channel_id=1, source_target_pairs={{0,8},{1,9},{2,10},{3,11},{4,12},{5,13},{6,14},{7,15},{8,0},{9,1},... | collective-permute-start | bytes 98312 | tf_op jit(solution)/shard_map/ppermute | solution.py:354
  51.6 0.5 collective-permute-done.14
  52.1 2.5 %collective-permute-done.13 = bf16[240,128]{1,0:T(8,128)(2,1)S(1)} collective-permute-done((bf16[240,128]{1,0:T(8,128)(2,1)S(1)}, bf16[240,128]{1,0:T(8,128)(2,1)S(1)}, u32[]{:S(2)}, u32[]{:S(2)}) %collective-permute-start.13) | collective-permute-done | bytes 61472 | tf_op jit(solution)/shard_map/ppermute | solution.py:354
  54.6 1.0 %collective-permute-start.17 = (bf16[480,128]{1,0:T(8,128)(2,1)S(1)}, bf16[480,128]{1,0:T(8,128)(2,1)S(1)}, u32[]{:S(2)}, u32[]{:S(2)}) collective-permute-start(bf16[480,128]{1,0:T(8,128)(2,1)S(1)} %pad_maximum_fusion.1), channel_id=1, source_target_pairs={{0,2},{1,3},{2,0},{3,1},{4,6},{5,7},{6,4},{7,5},{8,10},{9,11},{10,... | collective-permute-start | bytes 368648 | tf_op jit(solution)/shard_map/ppermute | solution.py:354
  55.6 0.0 collective-permute-done.12
  55.6 1.1 %collective-permute-start.16 = (bf16[240,128]{1,0:T(8,128)(2,1)S(1)}, bf16[240,128]{1,0:T(8,128)(2,1)S(1)}, u32[]{:S(2)}, u32[]{:S(2)}) collective-permute-start(bf16[240,128]{1,0:T(8,128)(2,1)S(1)} %collective-permute-done.12), channel_id=1, source_target_pairs={{0,2},{1,3},{2,0},{3,1},{4,6},{5,7},{6,4},{7,5},{8,10},{9,11},{10,... | collective-permute-start | bytes 184328 | tf_op jit(solution)/shard_map/ppermute | solution.py:354
  56.8 0.0 collective-permute-done.19
  56.8 1.0 %collective-permute-start.20 = (bf16[128,128]{1,0:T(8,128)(2,1)S(1)}, bf16[128,128]{1,0:T(8,128)(2,1)S(1)}, u32[]{:S(2)}, u32[]{:S(2)}) collective-permute-start(bf16[128,128]{1,0:T(8,128)(2,1)S(1)} %fusion.17), channel_id=1, source_target_pairs={{0,2},{1,3},{2,0},{3,1},{4,6},{5,7},{6,4},{7,5},{8,10},{9,11},{10,... | collective-permute-start | bytes 98312 | tf_op jit(solution)/shard_map/ppermute | solution.py:354
  57.8 3.0 %collective-permute-done.16 = bf16[240,128]{1,0:T(8,128)(2,1)S(1)} collective-permute-done((bf16[240,128]{1,0:T(8,128)(2,1)S(1)}, bf16[240,128]{1,0:T(8,128)(2,1)S(1)}, u32[]{:S(2)}, u32[]{:S(2)}) %collective-permute-start.16) | collective-permute-done | bytes 61472 | tf_op jit(solution)/shard_map/ppermute | solution.py:354
  60.9 0.3 collective-permute-done.20
  61.2 0.0 collective-permute-done.17
  61.3 0.1 collective-permute-start.21
  61.4 0.7 %maximum_bitcast_fusion = bf16[4,1,4,64,128]{4,3,2,1,0:T(8,128)(2,1)} fusion(bf16[3,4,64,128]{3,2,1,0:T(8,128)(2,1)S(1)} %get-tuple-element.52, bf16[1,4,64,128]{3,2,1,0:T(8,128)(2,1)S(1)} %bitcast.18), kind=kLoop, calls=%fused_computation.11 | loop fusion | flops 131072 | bytes 524288
  62.1 1.2 %collective-permute-done.21.other = bf16[2176,128]{1,0:T(8,128)(2,1)S(1)} collective-permute-done((bf16[2176,128]{1,0:T(8,128)(2,1)S(1)}, bf16[2176,128]{1,0:T(8,128)(2,1)S(1)}, u32[]{:S(2)}, u32[]{:S(2)}) %collective-permute-start.21) | collective-permute-done | bytes 557088 | tf_op jit(solution)/shard_map/ppermute | solution.py:354
  63.3 2.2 %shard_map.144 = (f32[3456,128]{1,0:T(8,128)}, f32[256,128]{1,0:T(8,128)}, f32[1,128]{1,0:T(1,128)}, f32[1,128]{1,0:T(1,128)}, bf16[4,2,4,64,128]{4,3,2,1,0:T(8,128)(2,1)}) custom-call(s32[7]{0:T(128)S(1)} %pad_add_fusion.sc, bf16[2176,128]{1,0:T(8,128)(2,1)S(1)} %fusion.10.mine, bf16[2176,128]{1,0:T(8,128)(2,1)S(1)} %collective-permute-done.21.other, ...), custom_call_target="tpu_custom_call" | custom-call | tf_op jit(solution)/shard_map/pallas_call | solution.py:619
  (30 shorter events, 0.5 us)
Async XLA Ops:
  2.2 1.6 %collective-permute-start = (bf16[12,64,128]{2,1,0:T(8,128)(2,1)S(1)}, bf16[12,64,128]{2,1,0:T(8,128)(2,1)S(1)}, u32[]{:S(2)}, u32[]{:S(2)}) collective-permute-start(bf16[12,64,128]{2,1,0:T(8,128)(2,1)S(1)} %shard_map.136), channel_id=1, source_target_pairs={{0,1},{1,0},{2,3},{3,2},{4,5},{5,4},{6,7},{7,6},{8,9},{9,8},{10,11... | collective-permute-start | bytes 589832 | tf_op jit(solution)/shard_map/ppermute | solution.py:354
  3.9 7.3 %collective-permute-start.1 = (bf16[6,64,128]{2,1,0:T(8,128)(2,1)S(1)}, bf16[6,64,128]{2,1,0:T(8,128)(2,1)S(1)}, u32[]{:S(2)}, u32[]{:S(2)}) collective-permute-start(bf16[6,64,128]{2,1,0:T(8,128)(2,1)S(1)} %fusion.7), channel_id=1, source_target_pairs={{0,2},{1,3},{2,0},{3,1},{4,6},{5,7},{6,4},{7,5},{8,10},{9,11},{10,... | collective-permute-start | bytes 294920 | tf_op jit(solution)/shard_map/ppermute | solution.py:354
  11.2 4.7 %collective-permute-start.2 = (bf16[6,64,128]{2,1,0:T(8,128)(2,1)S(1)}, bf16[6,64,128]{2,1,0:T(8,128)(2,1)S(1)}, u32[]{:S(2)}, u32[]{:S(2)}) collective-permute-start(bf16[6,64,128]{2,1,0:T(8,128)(2,1)S(1)} %fusion.8), channel_id=1, source_target_pairs={{0,4},{1,5},{2,6},{3,7},{4,0},{5,1},{6,2},{7,3},{8,12},{9,13},{10,... | collective-permute-start | bytes 294920 | tf_op jit(solution)/shard_map/ppermute | solution.py:354
  16.0 6.7 %collective-permute-start.3 = (bf16[6,64,128]{2,1,0:T(8,128)(2,1)S(1)}, bf16[6,64,128]{2,1,0:T(8,128)(2,1)S(1)}, u32[]{:S(2)}, u32[]{:S(2)}) collective-permute-start(bf16[6,64,128]{2,1,0:T(8,128)(2,1)S(1)} %fusion.9), channel_id=1, source_target_pairs={{0,8},{1,9},{2,10},{3,11},{4,12},{5,13},{6,14},{7,15},{8,0},{9,1},... | collective-permute-start | bytes 294920 | tf_op jit(solution)/shard_map/ppermute | solution.py:354
  18.6 5.5 %copy-start = (bf16[3,3,3,128,128]{4,3,2,1,0:T(8,128)(2,1)S(1)}, bf16[3,3,3,128,128]{4,3,2,1,0:T(8,128)(2,1)}, u32[]{:S(2)}) copy-start(bf16[3,3,3,128,128]{4,3,2,1,0:T(8,128)(2,1)} %param.13) | copy-start | bytes 2654212
  18.6 5.5 %copy-start.1 = (bf16[4,2,4,64,128]{4,3,2,1,0:T(8,128)(2,1)S(1)}, bf16[4,2,4,64,128]{4,3,2,1,0:T(8,128)(2,1)}, u32[]{:S(2)}) copy-start(bf16[4,2,4,64,128]{4,3,2,1,0:T(8,128)(2,1)} %frs.1) | copy-start | bytes 1572868
  18.6 5.5 %copy-start.2 = (bf16[4,2,2,64,128]{4,3,2,1,0:T(8,128)(2,1)S(1)}, bf16[4,2,2,64,128]{4,3,2,1,0:T(8,128)(2,1)}, u32[]{:S(2)}) copy-start(bf16[4,2,2,64,128]{4,3,2,1,0:T(8,128)(2,1)} %has.1) | copy-start | bytes 786436
  18.6 5.5 %copy-start.3 = (bf16[4,1,4,64,128]{4,3,2,1,0:T(8,128)(2,1)S(1)}, bf16[4,1,4,64,128]{4,3,2,1,0:T(8,128)(2,1)}, u32[]{:S(2)}) copy-start(bf16[4,1,4,64,128]{4,3,2,1,0:T(8,128)(2,1)} %cos.1) | copy-start | bytes 786436
  18.6 5.5 %copy-start.4 = (bf16[2,128,128]{2,1,0:T(8,128)(2,1)S(1)}, bf16[2,128,128]{2,1,0:T(8,128)(2,1)}, u32[]{:S(2)}) copy-start(bf16[2,128,128]{2,1,0:T(8,128)(2,1)} %sw.1) | copy-start | bytes 196612
  18.6 5.5 %copy-start.5 = (f32[128]{0:T(128)S(1)}, f32[128]{0:T(128)}, u32[]{:S(2)}) copy-start(f32[128]{0:T(128)} %param.14) | copy-start | bytes 1540
  18.6 5.5 %copy-start.6 = (f32[128]{0:T(128)S(1)}, f32[128]{0:T(128)}, u32[]{:S(2)}) copy-start(f32[128]{0:T(128)} %param.16) | copy-start | bytes 1540
  22.7 1.4 %collective-permute-start.4 = (bf16[6,64,128]{2,1,0:T(8,128)(2,1)S(1)}, bf16[6,64,128]{2,1,0:T(8,128)(2,1)S(1)}, u32[]{:S(2)}, u32[]{:S(2)}) collective-permute-start(bf16[6,64,128]{2,1,0:T(8,128)(2,1)S(1)} %fusion.2), channel_id=1, source_target_pairs={{0,1},{1,0},{2,3},{3,2},{4,5},{5,4},{6,7},{7,6},{8,9},{9,8},{10,11... | collective-permute-start | bytes 294920 | tf_op jit(solution)/shard_map/ppermute | solution.py:354
  27.0 1.9 %collective-permute-start.5 = (bf16[1920,128]{1,0:T(8,128)(2,1)S(1)}, bf16[1920,128]{1,0:T(8,128)(2,1)S(1)}, u32[]{:S(2)}, u32[]{:S(2)}) collective-permute-start(bf16[1920,128]{1,0:T(8,128)(2,1)S(1)} %get-tuple-element.56), channel_id=1, source_target_pairs={{0,1},{1,0},{2,3},{3,2},{4,5},{5,4},{6,7},{7,6},{8,9},{9,8},{10,11... | collective-permute-start | bytes 1474568 | tf_op jit(solution)/shard_map/ppermute | solution.py:354
  29.5 1.4 %collective-permute-start.6 = (bf16[512,128]{1,0:T(8,128)(2,1)S(1)}, bf16[512,128]{1,0:T(8,128)(2,1)S(1)}, u32[]{:S(2)}, u32[]{:S(2)}) collective-permute-start(bf16[512,128]{1,0:T(8,128)(2,1)S(1)} %shard_map.141), channel_id=1, source_target_pairs={{0,1},{1,0},{2,3},{3,2},{4,5},{5,4},{6,7},{7,6},{8,9},{9,8},{10,11... | collective-permute-start | bytes 393224 | tf_op jit(solution)/shard_map/ppermute | solution.py:354
  29.8 6.1 %collective-permute-start.8 = (bf16[480,128]{1,0:T(8,128)(2,1)S(1)}, bf16[480,128]{1,0:T(8,128)(2,1)S(1)}, u32[]{:S(2)}, u32[]{:S(2)}) collective-permute-start(bf16[480,128]{1,0:T(8,128)(2,1)S(1)} %get-tuple-element.60), channel_id=1, source_target_pairs={{0,2},{1,3},{2,0},{3,1},{4,6},{5,7},{6,4},{7,5},{8,10},{9,11},{10,... | collective-permute-start | bytes 368648 | tf_op jit(solution)/shard_map/ppermute | solution.py:354
  31.0 8.4 %collective-permute-start.7 = (bf16[736,128]{1,0:T(8,128)(2,1)S(1)}, bf16[736,128]{1,0:T(8,128)(2,1)S(1)}, u32[]{:S(2)}, u32[]{:S(2)}) collective-permute-start(bf16[736,128]{1,0:T(8,128)(2,1)S(1)} %pad_maximum_fusion), channel_id=1, source_target_pairs={{0,2},{1,3},{2,0},{3,1},{4,6},{5,7},{6,4},{7,5},{8,10},{9,11},{10,... | collective-permute-start | bytes 565256 | tf_op jit(solution)/shard_map/ppermute | solution.py:354
  35.9 6.2 %collective-permute-start.9 = (bf16[240,128]{1,0:T(8,128)(2,1)S(1)}, bf16[240,128]{1,0:T(8,128)(2,1)S(1)}, u32[]{:S(2)}, u32[]{:S(2)}) collective-permute-start(bf16[240,128]{1,0:T(8,128)(2,1)S(1)} %get-tuple-element.80), channel_id=1, source_target_pairs={{0,12},{1,13},{2,14},{3,15},{4,8},{5,9},{6,10},{7,11},{8,4},{9,5},... | collective-permute-start | bytes 184328 | tf_op jit(solution)/shard_map/ppermute | solution.py:354
  39.5 5.2 %collective-permute-start.10 = (bf16[240,128]{1,0:T(8,128)(2,1)S(1)}, bf16[240,128]{1,0:T(8,128)(2,1)S(1)}, u32[]{:S(2)}, u32[]{:S(2)}) collective-permute-start(bf16[240,128]{1,0:T(8,128)(2,1)S(1)} %get-tuple-element.81), channel_id=1, source_target_pairs={{0,8},{1,9},{2,10},{3,11},{4,12},{5,13},{6,14},{7,15},{8,0},{9,1},... | collective-permute-start | bytes 184328 | tf_op jit(solution)/shard_map/ppermute | solution.py:354
  39.5 5.7 %collective-permute-start.11 = (bf16[240,128]{1,0:T(8,128)(2,1)S(1)}, bf16[240,128]{1,0:T(8,128)(2,1)S(1)}, u32[]{:S(2)}, u32[]{:S(2)}) collective-permute-start(bf16[240,128]{1,0:T(8,128)(2,1)S(1)} %add_convert_fusion.1), channel_id=1, source_target_pairs={{0,4},{1,5},{2,6},{3,7},{4,0},{5,1},{6,2},{7,3},{8,12},{9,13},{10,... | collective-permute-start | bytes 184328 | tf_op jit(solution)/shard_map/ppermute | solution.py:354
  41.1 7.4 %collective-permute-start.18 = (bf16[128,128]{1,0:T(8,128)(2,1)S(1)}, bf16[128,128]{1,0:T(8,128)(2,1)S(1)}, u32[]{:S(2)}, u32[]{:S(2)}) collective-permute-start(bf16[128,128]{1,0:T(8,128)(2,1)S(1)} %fusion.18), channel_id=1, source_target_pairs={{0,4},{1,5},{2,6},{3,7},{4,0},{5,1},{6,2},{7,3},{8,12},{9,13},{10,... | collective-permute-start | bytes 98312 | tf_op jit(solution)/shard_map/ppermute | solution.py:354
  45.2 5.3 %collective-permute-start.15 = (bf16[240,128]{1,0:T(8,128)(2,1)S(1)}, bf16[240,128]{1,0:T(8,128)(2,1)S(1)}, u32[]{:S(2)}, u32[]{:S(2)}) collective-permute-start(bf16[240,128]{1,0:T(8,128)(2,1)S(1)} %get-tuple-element.79), channel_id=1, source_target_pairs={{0,2},{1,3},{2,0},{3,1},{4,6},{5,7},{6,4},{7,5},{8,10},{9,11},{10,... | collective-permute-start | bytes 184328 | tf_op jit(solution)/shard_map/ppermute | solution.py:354
  46.0 6.1 %collective-permute-start.14 = (bf16[240,128]{1,0:T(8,128)(2,1)S(1)}, bf16[240,128]{1,0:T(8,128)(2,1)S(1)}, u32[]{:S(2)}, u32[]{:S(2)}) collective-permute-start(bf16[240,128]{1,0:T(8,128)(2,1)S(1)} %get-tuple-element.79), channel_id=1, source_target_pairs={{0,12},{1,13},{2,14},{3,15},{4,8},{5,9},{6,10},{7,11},{8,4},{9,5},... | collective-permute-start | bytes 184328 | tf_op jit(solution)/shard_map/ppermute | solution.py:354
  48.5 6.1 %collective-permute-start.13 = (bf16[240,128]{1,0:T(8,128)(2,1)S(1)}, bf16[240,128]{1,0:T(8,128)(2,1)S(1)}, u32[]{:S(2)}, u32[]{:S(2)}) collective-permute-start(bf16[240,128]{1,0:T(8,128)(2,1)S(1)} %get-tuple-element.79), channel_id=1, source_target_pairs={{0,8},{1,9},{2,10},{3,11},{4,12},{5,13},{6,14},{7,15},{8,0},{9,1},... | collective-permute-start | bytes 184328 | tf_op jit(solution)/shard_map/ppermute | solution.py:354
  48.6 7.1 %collective-permute-start.12 = (bf16[240,128]{1,0:T(8,128)(2,1)S(1)}, bf16[240,128]{1,0:T(8,128)(2,1)S(1)}, u32[]{:S(2)}, u32[]{:S(2)}) collective-permute-start(bf16[240,128]{1,0:T(8,128)(2,1)S(1)} %get-tuple-element.79), channel_id=1, source_target_pairs={{0,4},{1,5},{2,6},{3,7},{4,0},{5,1},{6,2},{7,3},{8,12},{9,13},{10,... | collective-permute-start | bytes 184328 | tf_op jit(solution)/shard_map/ppermute | solution.py:354
  50.5 6.3 %collective-permute-start.19 = (bf16[128,128]{1,0:T(8,128)(2,1)S(1)}, bf16[128,128]{1,0:T(8,128)(2,1)S(1)}, u32[]{:S(2)}, u32[]{:S(2)}) collective-permute-start(bf16[128,128]{1,0:T(8,128)(2,1)S(1)} %fusion.19), channel_id=1, source_target_pairs={{0,8},{1,9},{2,10},{3,11},{4,12},{5,13},{6,14},{7,15},{8,0},{9,1},... | collective-permute-start | bytes 98312 | tf_op jit(solution)/shard_map/ppermute | solution.py:354
  54.6 6.6 %collective-permute-start.17 = (bf16[480,128]{1,0:T(8,128)(2,1)S(1)}, bf16[480,128]{1,0:T(8,128)(2,1)S(1)}, u32[]{:S(2)}, u32[]{:S(2)}) collective-permute-start(bf16[480,128]{1,0:T(8,128)(2,1)S(1)} %pad_maximum_fusion.1), channel_id=1, source_target_pairs={{0,2},{1,3},{2,0},{3,1},{4,6},{5,7},{6,4},{7,5},{8,10},{9,11},{10,... | collective-permute-start | bytes 368648 | tf_op jit(solution)/shard_map/ppermute | solution.py:354
  55.6 5.2 %collective-permute-start.16 = (bf16[240,128]{1,0:T(8,128)(2,1)S(1)}, bf16[240,128]{1,0:T(8,128)(2,1)S(1)}, u32[]{:S(2)}, u32[]{:S(2)}) collective-permute-start(bf16[240,128]{1,0:T(8,128)(2,1)S(1)} %collective-permute-done.12), channel_id=1, source_target_pairs={{0,2},{1,3},{2,0},{3,1},{4,6},{5,7},{6,4},{7,5},{8,10},{9,11},{10,... | collective-permute-start | bytes 184328 | tf_op jit(solution)/shard_map/ppermute | solution.py:354
  56.8 4.4 %collective-permute-start.20 = (bf16[128,128]{1,0:T(8,128)(2,1)S(1)}, bf16[128,128]{1,0:T(8,128)(2,1)S(1)}, u32[]{:S(2)}, u32[]{:S(2)}) collective-permute-start(bf16[128,128]{1,0:T(8,128)(2,1)S(1)} %fusion.17), channel_id=1, source_target_pairs={{0,2},{1,3},{2,0},{3,1},{4,6},{5,7},{6,4},{7,5},{8,10},{9,11},{10,... | collective-permute-start | bytes 98312 | tf_op jit(solution)/shard_map/ppermute | solution.py:354
  61.3 2.0 %collective-permute-start.21 = (bf16[2176,128]{1,0:T(8,128)(2,1)S(1)}, bf16[2176,128]{1,0:T(8,128)(2,1)S(1)}, u32[]{:S(2)}, u32[]{:S(2)}) collective-permute-start(bf16[2176,128]{1,0:T(8,128)(2,1)S(1)} %fusion.10.mine), channel_id=1, source_target_pairs={{0,1},{1,0},{2,3},{3,2},{4,5},{5,4},{6,7},{7,6},{8,9},{9,8},{10,11... | collective-permute-start | bytes 1671176 | tf_op jit(solution)/shard_map/ppermute | solution.py:354

commit v13 on v12

--- a/solution.py
+++ b/solution.py
@@ -597,12 +597,11 @@
     while k < n:
         mine = (mine.astype(F32) + _xor(mine, k, n, axis).astype(F32)).astype(BF)
         k *= 2
-    others = {j: _xor(mine, 4 * j, n, axis) for j in (3, 2, 1)}
-    x_own = _xor(mine, 2, n, axis)
-    x_near = _xor(others[1], 2, n, axis)
+    others = {j: _xor(mine, 4 * j, n, axis) for j in (1, 3, 2)}
+    x_near = _xor(jnp.concatenate([mine, others[1]], axis=0), 2, n, axis)
     x_far = _xor(jnp.concatenate([others[2], others[3]], axis=0), 2, n, axis)
     beyond = by(index & 4, near_lead, jnp.full_like(lead, EMPTY_GRAD))
-    lead, k = _after(ordered(index & 4, lead, near_lead), x_own), 8
+    lead, k = _after(ordered(index & 4, lead, near_lead), others[1]), 8
     while k < n:
         came = _xor(lead, k, n, axis)
         beyond = by(index & k, _first_live(beyond, came), beyond)
@@ -613,7 +612,7 @@
     beyond = jnp.concatenate([by(pair, beyond, theirs), by(pair, theirs, beyond)], axis=0)
     beyond = by(pair, _first_live(beside_first, beyond), beyond)
     ours = jnp.concatenate(
-        [mine, others[1], others[2], others[3], x_own, x_near, x_far, beyond], axis=0
+        [mine, others[1], others[2], others[3], x_near, x_far, beyond], axis=0
     )
     other = _xor(ours, 1, n, axis)
     cwg, swg, cbg, sbg, frames_grad = _call(

time: 65.7 us -> 65.2 us (level)
  starting transfers between devices: 24.9 us -> 22.9 us
  waiting for transfers between devices: 16.7 us -> 18.1 us
    ppermute x22 -> x21, starting transfers between devices: 24.9 us -> 22.9 us  [_xor(): return lax.ppermute(x, axis, [(i, i ^ k) for i in range(n)])]
    ppermute x22 -> x21, waiting for transfers between devices: 16.7 us -> 18.1 us  [_xor(): return lax.ppermute(x, axis, [(i, i ^ k) for i in range(n)])]
  transfers between devices with their start and end apart: 22 -> 21, of which waited for: 14 -> 15; matrix products, arithmetic and copies ran while one was open for 3% -> 3% of each run, Pallas kernels for 21% -> 21%
where the time goes in v13:
time: 65.2 us; the launch traced here: 65 us
  starting transfers between devices  22.9 us (35%)
  Pallas kernels  20.3 us (31%)
  waiting for transfers between devices  18.1 us (28%)
  other arithmetic  1.96 us (3%)
  between operations  1.58 us (2%)
    ppermute x21, starting transfers between devices, _xor(): return lax.ppermute(x, axis, [(i, i ^ k) for i in range(n)])  22.9 us
    ppermute x21, waiting for transfers between devices, _xor(): return lax.ppermute(x, axis, [(i, i ^ k) for i in range(n)])  18.1 us
    pallas_call x1, Pallas kernels, early_conv(): _call(_early_conv_kernel, [jax.ShapeDtypeStruct(wide, F32), jax.ShapeDtyp...  4.4 us
    pallas_call x1, Pallas kernels, early_sums(): _call(_early_sums_kernel, jax.ShapeDtypeStruct((rows, c), F32), [_SMEM, _...  3.94 us
    pallas_call x1, Pallas kernels, body(): _call(_back_kernel, jax.ShapeDtypeStruct((slots, 2, h, w, c), F32), [_SME...  3.39 us
    pallas_call x1, Pallas kernels, body(): _call(_late_kernel, [jax.ShapeDtypeStruct((h, w, c), BF), jax.ShapeDtypeS...  2.78 us
    pallas_call x1, Pallas kernels, body(): _call(_final_kernel, [jax.ShapeDtypeStruct((27 * c, c), F32), jax.ShapeDt...  2.18 us
  transfers between devices with their start and end apart: 21, of which 15 were waited for; matrix products, arithmetic and copies ran while one was open for 3% of the time, Pallas kernels for 21%

profile of v13, /device:TPU:0, one launch (start us, length us, event | category | flops | bytes accessed | tf_op | source)
XLA Modules:
  0.0 65.0 jit_solution(10052411946642538226)
XLA Ops:
  1.3 1.0 %shard_map.136 = bf16[12,64,128]{2,1,0:T(8,128)(2,1)S(1)} custom-call(s32[1]{0:T(128)S(6)} %copy.22.sc, bf16[4,2,4,64,128]{4,3,2,1,0:T(8,128)(2,1)} %frs.1, bf16[4,2,2,64,128]{4,3,2,1,0:T(8,128)(2,1)} %has.1), custom_call_target="tpu_custom_call" | custom-call | tf_op jit(solution)/shard_map/pallas_call | solution.py:435
  2.2 0.5 collective-permute-start
  2.8 0.7 %pad_add_fusion.sc = s32[7]{0:T(128)S(1)} fusion(s32[1]{0:T(128)} %bitcast.1, s32[1]{0:T(128)} %bitcast, s32[4]{0:T(128)} %param.11, s32[1]{0:T(128)S(6)} %copy.22.sc), kind=kLoop, calls=%fused_computation.62 | loop fusion | flops 21 | bytes 56 | tf_op jit(solution)/shard_map/concatenate | solution.py:417
  3.5 0.3 collective-permute-done
  3.9 2.9 %collective-permute-start.1 = (bf16[6,64,128]{2,1,0:T(8,128)(2,1)S(1)}, bf16[6,64,128]{2,1,0:T(8,128)(2,1)S(1)}, u32[]{:S(2)}, u32[]{:S(2)}) collective-permute-start(bf16[6,64,128]{2,1,0:T(8,128)(2,1)S(1)} %fusion.7), channel_id=1, source_target_pairs={{0,2},{1,3},{2,0},{3,1},{4,6},{5,7},{6,4},{7,5},{8,10},{9,11},{10,... | collective-permute-start | bytes 294920 | tf_op jit(solution)/shard_map/ppermute | solution.py:354
  6.8 4.4 %shard_map.137 = (f32[768,256]{1,0:T(8,128)S(1)}, bf16[768,128]{1,0:T(8,128)(2,1)S(1)}, bf16[2,128,128]{2,1,0:T(8,128)(2,1)S(1)}, f32[1,128]{1,0:T(1,128)S(1)}) custom-call(s32[7]{0:T(128)S(1)} %pad_add_fusion.sc, bf16[4,2,4,64,128]{4,3,2,1,0:T(8,128)(2,1)} %frs.1, bf16[4,2,2,64,128]{4,3,2,1,0:T(8,128)(2,1)} %has.1, bf16[4,1,4,64,128]{4,3,2,1,0:T(8,128)(2,1)} %cos.1, ...), custom_call_target="tpu_custom_call" | custom-call | flops 1811939328 | bytes 4194304 | tf_op jit(solution)/shard_map/pallas_call | solution.py:462
  11.2 0.0 collective-permute-done.1
  11.2 1.6 %collective-permute-start.2 = (bf16[6,64,128]{2,1,0:T(8,128)(2,1)S(1)}, bf16[6,64,128]{2,1,0:T(8,128)(2,1)S(1)}, u32[]{:S(2)}, u32[]{:S(2)}) collective-permute-start(bf16[6,64,128]{2,1,0:T(8,128)(2,1)S(1)} %fusion.8), channel_id=1, source_target_pairs={{0,4},{1,5},{2,6},{3,7},{4,0},{5,1},{6,2},{7,3},{8,12},{9,13},{10,... | collective-permute-start | bytes 294920 | tf_op jit(solution)/shard_map/ppermute | solution.py:354
  12.9 1.0 %shard_map.138 = (bf16[3,4,64,128]{3,2,1,0:T(8,128)(2,1)S(1)}, bf16[768,256]{1,0:T(8,128)(2,1)S(1)}, bf16[768,256]{1,0:T(8,128)(2,1)S(1)}) custom-call(s32[7]{0:T(128)S(1)} %pad_add_fusion.sc, f32[768,256]{1,0:T(8,128)S(1)} %get-tuple-element.40.pre_ref, bf16[768,128]{1,0:T(8,128)(2,1)S(1)} %get-tuple-element.43.gout_ref, ...), custom_call_target="tpu_custom_call" | custom-call | bytes 2097152 | tf_op jit(solution)/shard_map/pallas_call | solution.py:480
  13.9 2.1 %collective-permute-done.2 = bf16[6,64,128]{2,1,0:T(8,128)(2,1)S(1)} collective-permute-done((bf16[6,64,128]{2,1,0:T(8,128)(2,1)S(1)}, bf16[6,64,128]{2,1,0:T(8,128)(2,1)S(1)}, u32[]{:S(2)}, u32[]{:S(2)}) %collective-permute-start.2) | collective-permute-done | bytes 98336 | tf_op jit(solution)/shard_map/ppermute | solution.py:354
  16.0 2.7 %collective-permute-start.3 = (bf16[6,64,128]{2,1,0:T(8,128)(2,1)S(1)}, bf16[6,64,128]{2,1,0:T(8,128)(2,1)S(1)}, u32[]{:S(2)}, u32[]{:S(2)}) collective-permute-start(bf16[6,64,128]{2,1,0:T(8,128)(2,1)S(1)} %fusion.9), channel_id=1, source_target_pairs={{0,8},{1,9},{2,10},{3,11},{4,12},{5,13},{6,14},{7,15},{8,0},{9,1},... | collective-permute-start | bytes 294920 | tf_op jit(solution)/shard_map/ppermute | solution.py:354
  18.6 0.0 copy-start.4
  18.6 0.0 copy-start.5
  18.6 0.0 copy-start.6
  18.7 3.9 %shard_map.139.early = f32[3840,128]{1,0:T(8,128)S(1)} custom-call(s32[7]{0:T(128)S(1)} %pad_add_fusion.sc, bf16[4,2,4,64,128]{4,3,2,1,0:T(8,128)(2,1)} %frs.1, bf16[4,2,2,64,128]{4,3,2,1,0:T(8,128)(2,1)} %has.1, bf16[768,256]{1,0:T(8,128)(2,1)S(1)} %get-tuple-element.46.g_ref.g1, bf16[768,256]{1,0:T(8,128)(2,1)S(1)} %get-tuple-element.49.hid_ref, ...), custom_call_target="tpu_custom_call" | custom-call | flops 1811939328 | bytes 4194304 | tf_op jit(solution)/shard_map/pallas_call | solution.py:496
  22.6 0.0 collective-permute-done.3
  22.7 0.1 collective-permute-start.4
  22.7 1.3 %collective-permute-done.4 = bf16[6,64,128]{2,1,0:T(8,128)(2,1)S(1)} collective-permute-done((bf16[6,64,128]{2,1,0:T(8,128)(2,1)S(1)}, bf16[6,64,128]{2,1,0:T(8,128)(2,1)S(1)}, u32[]{:S(2)}, u32[]{:S(2)}) %collective-permute-start.4) | collective-permute-done | bytes 98336 | tf_op jit(solution)/shard_map/ppermute | solution.py:354
  24.1 0.1 compare_select_fusion.tail
  24.1 0.0 copy-done
  24.1 0.0 copy-done.1
  24.1 0.0 copy-done.2
  24.1 0.0 copy-done.3
  24.2 0.0 copy-done.4
  24.2 0.0 copy-done.5
  24.2 2.8 %shard_map.140 = (bf16[4,64,128]{2,1,0:T(8,128)(2,1)S(1)}, bf16[256,256]{1,0:T(8,128)(2,1)S(1)}, bf16[1920,128]{1,0:T(8,128)(2,1)S(1)}, f32[1920,128]{1,0:T(8,128)S(1)}) custom-call(s32[7]{0:T(128)S(1)} %pad_add_fusion.sc, bf16[4,2,4,64,128]{4,3,2,1,0:T(8,128)(2,1)S(1)} %copy-done.1, bf16[4,2,2,64,128]{4,3,2,1,0:T(8,128)(2,1)S(1)} %copy-done.2, ...), custom_call_target="tpu_custom_call" | custom-call | flops 1207959552 | bytes 6291456 | tf_op jit(solution)/shard_map/pallas_call | solution.py:515
  27.0 0.2 collective-permute-start.5
  27.2 1.1 %shard_map.141 = bf16[512,128]{1,0:T(8,128)(2,1)S(1)} custom-call(s32[7]{0:T(128)S(1)} %pad_add_fusion.sc, bf16[256,256]{1,0:T(8,128)(2,1)S(1)} %get-tuple-element.54.g_ref.g0, bf16[27,128,128]{2,1,0:T(8,128)(2,1)S(1)} %bitcast.16), custom_call_target="tpu_custom_call" | custom-call | flops 301989888 | bytes 1048576 | tf_op jit(solution)/shard_map/pallas_call | solution.py:533
  28.2 0.6 collective-permute-done.5.got
  28.9 0.6 shard_map.142
  29.5 0.2 collective-permute-start.6
  29.8 0.6 collective-permute-start.8
  30.3 0.6 collective-permute-done.6.got
  31.0 0.1 fusion.11
  31.0 0.9 %collective-permute-start.7 = (bf16[736,128]{1,0:T(8,128)(2,1)S(1)}, bf16[736,128]{1,0:T(8,128)(2,1)S(1)}, u32[]{:S(2)}, u32[]{:S(2)}) collective-permute-start(bf16[736,128]{1,0:T(8,128)(2,1)S(1)} %pad_maximum_fusion), channel_id=1, source_target_pairs={{0,2},{1,3},{2,0},{3,1},{4,6},{5,7},{6,4},{7,5},{8,10},{9,11},{10,... | collective-permute-start | bytes 565256 | tf_op jit(solution)/shard_map/ppermute | solution.py:354
  31.9 3.4 %shard_map.143.grad = f32[4,2,4,64,128]{4,3,2,1,0:T(8,128)S(1)} custom-call(s32[7]{0:T(128)S(1)} %pad_add_fusion.sc, bf16[256,256]{1,0:T(8,128)(2,1)S(1)} %get-tuple-element.54.g_ref.g0, bf16[768,256]{1,0:T(8,128)(2,1)S(1)} %get-tuple-element.46.g_ref.g1, bf16[27,128,128]{2,1,0:T(8,128)(2,1)S(1)} %bitcast.17), custom_call_target="tpu_custom_call" | custom-call | flops 1 | bytes 1 | tf_op jit(solution)/shard_map/pallas_call | solution.py:569
  35.3 0.6 collective-permute-done.8
  35.9 3.5 %collective-permute-start.9 = (bf16[240,128]{1,0:T(8,128)(2,1)S(1)}, bf16[240,128]{1,0:T(8,128)(2,1)S(1)}, u32[]{:S(2)}, u32[]{:S(2)}) collective-permute-start(bf16[240,128]{1,0:T(8,128)(2,1)S(1)} %get-tuple-element.80), channel_id=1, source_target_pairs={{0,12},{1,13},{2,14},{3,15},{4,8},{5,9},{6,10},{7,11},{8,4},{9,5},... | collective-permute-start | bytes 184328 | tf_op jit(solution)/shard_map/ppermute | solution.py:354
  39.5 0.0 collective-permute-start.10
  39.5 0.0 collective-permute-done.7
  39.5 1.6 %collective-permute-start.11 = (bf16[240,128]{1,0:T(8,128)(2,1)S(1)}, bf16[240,128]{1,0:T(8,128)(2,1)S(1)}, u32[]{:S(2)}, u32[]{:S(2)}) collective-permute-start(bf16[240,128]{1,0:T(8,128)(2,1)S(1)} %add_convert_fusion.1), channel_id=1, source_target_pairs={{0,4},{1,5},{2,6},{3,7},{4,0},{5,1},{6,2},{7,3},{8,12},{9,13},{10,... | collective-permute-start | bytes 184328 | tf_op jit(solution)/shard_map/ppermute | solution.py:354
  41.1 0.5 collective-permute-start.17
  41.6 0.5 collective-permute-done.9
  42.1 2.5 %collective-permute-done.10 = bf16[240,128]{1,0:T(8,128)(2,1)S(1)} collective-permute-done((bf16[240,128]{1,0:T(8,128)(2,1)S(1)}, bf16[240,128]{1,0:T(8,128)(2,1)S(1)}, u32[]{:S(2)}, u32[]{:S(2)}) %collective-permute-start.10) | collective-permute-done | bytes 61472 | tf_op jit(solution)/shard_map/ppermute | solution.py:354
  44.7 0.5 collective-permute-done.11
  45.2 0.9 %collective-permute-start.12 = (bf16[240,128]{1,0:T(8,128)(2,1)S(1)}, bf16[240,128]{1,0:T(8,128)(2,1)S(1)}, u32[]{:S(2)}, u32[]{:S(2)}) collective-permute-start(bf16[240,128]{1,0:T(8,128)(2,1)S(1)} %get-tuple-element.79), channel_id=1, source_target_pairs={{0,4},{1,5},{2,6},{3,7},{4,0},{5,1},{6,2},{7,3},{8,12},{9,13},{10,... | collective-permute-start | bytes 184328 | tf_op jit(solution)/shard_map/ppermute | solution.py:354
  46.1 0.0 collective-permute-done.17
  46.1 2.3 %collective-permute-start.14 = (bf16[240,128]{1,0:T(8,128)(2,1)S(1)}, bf16[240,128]{1,0:T(8,128)(2,1)S(1)}, u32[]{:S(2)}, u32[]{:S(2)}) collective-permute-start(bf16[240,128]{1,0:T(8,128)(2,1)S(1)} %get-tuple-element.79), channel_id=1, source_target_pairs={{0,12},{1,13},{2,14},{3,15},{4,8},{5,9},{6,10},{7,11},{8,4},{9,5},... | collective-permute-start | bytes 184328 | tf_op jit(solution)/shard_map/ppermute | solution.py:354
  48.4 0.5 collective-permute-start.13
  48.9 1.2 %collective-permute-done.12 = bf16[240,128]{1,0:T(8,128)(2,1)S(1)} collective-permute-done((bf16[240,128]{1,0:T(8,128)(2,1)S(1)}, bf16[240,128]{1,0:T(8,128)(2,1)S(1)}, u32[]{:S(2)}, u32[]{:S(2)}) %collective-permute-start.12) | collective-permute-done | bytes 61472 | tf_op jit(solution)/shard_map/ppermute | solution.py:354
  50.1 1.3 %collective-permute-start.18 = (bf16[128,128]{1,0:T(8,128)(2,1)S(1)}, bf16[128,128]{1,0:T(8,128)(2,1)S(1)}, u32[]{:S(2)}, u32[]{:S(2)}) collective-permute-start(bf16[128,128]{1,0:T(8,128)(2,1)S(1)} %fusion.19), channel_id=1, source_target_pairs={{0,8},{1,9},{2,10},{3,11},{4,12},{5,13},{6,14},{7,15},{8,0},{9,1},... | collective-permute-start | bytes 98312 | tf_op jit(solution)/shard_map/ppermute | solution.py:354
  51.3 0.7 %collective-permute-start.15 = (bf16[480,128]{1,0:T(8,128)(2,1)S(1)}, bf16[480,128]{1,0:T(8,128)(2,1)S(1)}, u32[]{:S(2)}, u32[]{:S(2)}) collective-permute-start(bf16[480,128]{1,0:T(8,128)(2,1)S(1)} %pad_maximum_fusion.1), channel_id=1, source_target_pairs={{0,2},{1,3},{2,0},{3,1},{4,6},{5,7},{6,4},{7,5},{8,10},{9,11},{10,... | collective-permute-start | bytes 368648 | tf_op jit(solution)/shard_map/ppermute | solution.py:354
  52.0 0.5 collective-permute-done.14
  52.6 2.8 %collective-permute-done.13 = bf16[240,128]{1,0:T(8,128)(2,1)S(1)} collective-permute-done((bf16[240,128]{1,0:T(8,128)(2,1)S(1)}, bf16[240,128]{1,0:T(8,128)(2,1)S(1)}, u32[]{:S(2)}, u32[]{:S(2)}) %collective-permute-start.13) | collective-permute-done | bytes 61472 | tf_op jit(solution)/shard_map/ppermute | solution.py:354
  55.4 0.1 collective-permute-start.16
  55.6 0.2 collective-permute-done.18
  55.8 1.9 %collective-permute-start.19 = (bf16[128,128]{1,0:T(8,128)(2,1)S(1)}, bf16[128,128]{1,0:T(8,128)(2,1)S(1)}, u32[]{:S(2)}, u32[]{:S(2)}) collective-permute-start(bf16[128,128]{1,0:T(8,128)(2,1)S(1)} %fusion.17), channel_id=1, source_target_pairs={{0,2},{1,3},{2,0},{3,1},{4,6},{5,7},{6,4},{7,5},{8,10},{9,11},{10,... | collective-permute-start | bytes 98312 | tf_op jit(solution)/shard_map/ppermute | solution.py:354
  57.7 3.1 %collective-permute-done.19 = bf16[128,128]{1,0:T(8,128)(2,1)S(1)} collective-permute-done((bf16[128,128]{1,0:T(8,128)(2,1)S(1)}, bf16[128,128]{1,0:T(8,128)(2,1)S(1)}, u32[]{:S(2)}, u32[]{:S(2)}) %collective-permute-start.19) | collective-permute-done | bytes 32800 | tf_op jit(solution)/shard_map/ppermute | solution.py:354
  60.7 0.0 collective-permute-done.15
  60.8 0.0 collective-permute-done.16
  60.8 0.1 collective-permute-start.20
  60.9 0.7 %maximum_bitcast_fusion = bf16[4,1,4,64,128]{4,3,2,1,0:T(8,128)(2,1)} fusion(bf16[3,4,64,128]{3,2,1,0:T(8,128)(2,1)S(1)} %get-tuple-element.52, bf16[1,4,64,128]{3,2,1,0:T(8,128)(2,1)S(1)} %bitcast.18), kind=kLoop, calls=%fused_computation.11 | loop fusion | flops 131072 | bytes 524288
  61.6 1.2 %collective-permute-done.20.other = bf16[2176,128]{1,0:T(8,128)(2,1)S(1)} collective-permute-done((bf16[2176,128]{1,0:T(8,128)(2,1)S(1)}, bf16[2176,128]{1,0:T(8,128)(2,1)S(1)}, u32[]{:S(2)}, u32[]{:S(2)}) %collective-permute-start.20) | collective-permute-done | bytes 557088 | tf_op jit(solution)/shard_map/ppermute | solution.py:354
  62.9 2.2 %shard_map.144 = (f32[3456,128]{1,0:T(8,128)}, f32[256,128]{1,0:T(8,128)}, f32[1,128]{1,0:T(1,128)}, f32[1,128]{1,0:T(1,128)}, bf16[4,2,4,64,128]{4,3,2,1,0:T(8,128)(2,1)}) custom-call(s32[7]{0:T(128)S(1)} %pad_add_fusion.sc, bf16[2176,128]{1,0:T(8,128)(2,1)S(1)} %fusion.10.mine, bf16[2176,128]{1,0:T(8,128)(2,1)S(1)} %collective-permute-done.20.other, ...), custom_call_target="tpu_custom_call" | custom-call | tf_op jit(solution)/shard_map/pallas_call | solution.py:618
  (28 shorter events, 0.5 us)
Async XLA Ops:
  2.2 1.6 %collective-permute-start = (bf16[12,64,128]{2,1,0:T(8,128)(2,1)S(1)}, bf16[12,64,128]{2,1,0:T(8,128)(2,1)S(1)}, u32[]{:S(2)}, u32[]{:S(2)}) collective-permute-start(bf16[12,64,128]{2,1,0:T(8,128)(2,1)S(1)} %shard_map.136), channel_id=1, source_target_pairs={{0,1},{1,0},{2,3},{3,2},{4,5},{5,4},{6,7},{7,6},{8,9},{9,8},{10,11... | collective-permute-start | bytes 589832 | tf_op jit(solution)/shard_map/ppermute | solution.py:354
  3.9 7.3 %collective-permute-start.1 = (bf16[6,64,128]{2,1,0:T(8,128)(2,1)S(1)}, bf16[6,64,128]{2,1,0:T(8,128)(2,1)S(1)}, u32[]{:S(2)}, u32[]{:S(2)}) collective-permute-start(bf16[6,64,128]{2,1,0:T(8,128)(2,1)S(1)} %fusion.7), channel_id=1, source_target_pairs={{0,2},{1,3},{2,0},{3,1},{4,6},{5,7},{6,4},{7,5},{8,10},{9,11},{10,... | collective-permute-start | bytes 294920 | tf_op jit(solution)/shard_map/ppermute | solution.py:354
  11.2 4.7 %collective-permute-start.2 = (bf16[6,64,128]{2,1,0:T(8,128)(2,1)S(1)}, bf16[6,64,128]{2,1,0:T(8,128)(2,1)S(1)}, u32[]{:S(2)}, u32[]{:S(2)}) collective-permute-start(bf16[6,64,128]{2,1,0:T(8,128)(2,1)S(1)} %fusion.8), channel_id=1, source_target_pairs={{0,4},{1,5},{2,6},{3,7},{4,0},{5,1},{6,2},{7,3},{8,12},{9,13},{10,... | collective-permute-start | bytes 294920 | tf_op jit(solution)/shard_map/ppermute | solution.py:354
  16.0 6.7 %collective-permute-start.3 = (bf16[6,64,128]{2,1,0:T(8,128)(2,1)S(1)}, bf16[6,64,128]{2,1,0:T(8,128)(2,1)S(1)}, u32[]{:S(2)}, u32[]{:S(2)}) collective-permute-start(bf16[6,64,128]{2,1,0:T(8,128)(2,1)S(1)} %fusion.9), channel_id=1, source_target_pairs={{0,8},{1,9},{2,10},{3,11},{4,12},{5,13},{6,14},{7,15},{8,0},{9,1},... | collective-permute-start | bytes 294920 | tf_op jit(solution)/shard_map/ppermute | solution.py:354
  18.6 5.5 %copy-start = (bf16[3,3,3,128,128]{4,3,2,1,0:T(8,128)(2,1)S(1)}, bf16[3,3,3,128,128]{4,3,2,1,0:T(8,128)(2,1)}, u32[]{:S(2)}) copy-start(bf16[3,3,3,128,128]{4,3,2,1,0:T(8,128)(2,1)} %param.13) | copy-start | bytes 2654212
  18.6 5.5 %copy-start.1 = (bf16[4,2,4,64,128]{4,3,2,1,0:T(8,128)(2,1)S(1)}, bf16[4,2,4,64,128]{4,3,2,1,0:T(8,128)(2,1)}, u32[]{:S(2)}) copy-start(bf16[4,2,4,64,128]{4,3,2,1,0:T(8,128)(2,1)} %frs.1) | copy-start | bytes 1572868
  18.6 5.5 %copy-start.2 = (bf16[4,2,2,64,128]{4,3,2,1,0:T(8,128)(2,1)S(1)}, bf16[4,2,2,64,128]{4,3,2,1,0:T(8,128)(2,1)}, u32[]{:S(2)}) copy-start(bf16[4,2,2,64,128]{4,3,2,1,0:T(8,128)(2,1)} %has.1) | copy-start | bytes 786436
  18.6 5.5 %copy-start.3 = (bf16[4,1,4,64,128]{4,3,2,1,0:T(8,128)(2,1)S(1)}, bf16[4,1,4,64,128]{4,3,2,1,0:T(8,128)(2,1)}, u32[]{:S(2)}) copy-start(bf16[4,1,4,64,128]{4,3,2,1,0:T(8,128)(2,1)} %cos.1) | copy-start | bytes 786436
  18.6 5.5 %copy-start.4 = (bf16[2,128,128]{2,1,0:T(8,128)(2,1)S(1)}, bf16[2,128,128]{2,1,0:T(8,128)(2,1)}, u32[]{:S(2)}) copy-start(bf16[2,128,128]{2,1,0:T(8,128)(2,1)} %sw.1) | copy-start | bytes 196612
  18.6 5.5 %copy-start.5 = (f32[128]{0:T(128)S(1)}, f32[128]{0:T(128)}, u32[]{:S(2)}) copy-start(f32[128]{0:T(128)} %param.14) | copy-start | bytes 1540
  18.6 5.5 %copy-start.6 = (f32[128]{0:T(128)S(1)}, f32[128]{0:T(128)}, u32[]{:S(2)}) copy-start(f32[128]{0:T(128)} %param.16) | copy-start | bytes 1540
  22.7 1.4 %collective-permute-start.4 = (bf16[6,64,128]{2,1,0:T(8,128)(2,1)S(1)}, bf16[6,64,128]{2,1,0:T(8,128)(2,1)S(1)}, u32[]{:S(2)}, u32[]{:S(2)}) collective-permute-start(bf16[6,64,128]{2,1,0:T(8,128)(2,1)S(1)} %fusion.2), channel_id=1, source_target_pairs={{0,1},{1,0},{2,3},{3,2},{4,5},{5,4},{6,7},{7,6},{8,9},{9,8},{10,11... | collective-permute-start | bytes 294920 | tf_op jit(solution)/shard_map/ppermute | solution.py:354
  27.0 1.9 %collective-permute-start.5 = (bf16[1920,128]{1,0:T(8,128)(2,1)S(1)}, bf16[1920,128]{1,0:T(8,128)(2,1)S(1)}, u32[]{:S(2)}, u32[]{:S(2)}) collective-permute-start(bf16[1920,128]{1,0:T(8,128)(2,1)S(1)} %get-tuple-element.56), channel_id=1, source_target_pairs={{0,1},{1,0},{2,3},{3,2},{4,5},{5,4},{6,7},{7,6},{8,9},{9,8},{10,11... | collective-permute-start | bytes 1474568 | tf_op jit(solution)/shard_map/ppermute | solution.py:354
  29.5 1.4 %collective-permute-start.6 = (bf16[512,128]{1,0:T(8,128)(2,1)S(1)}, bf16[512,128]{1,0:T(8,128)(2,1)S(1)}, u32[]{:S(2)}, u32[]{:S(2)}) collective-permute-start(bf16[512,128]{1,0:T(8,128)(2,1)S(1)} %shard_map.141), channel_id=1, source_target_pairs={{0,1},{1,0},{2,3},{3,2},{4,5},{5,4},{6,7},{7,6},{8,9},{9,8},{10,11... | collective-permute-start | bytes 393224 | tf_op jit(solution)/shard_map/ppermute | solution.py:354
  29.8 6.1 %collective-permute-start.8 = (bf16[480,128]{1,0:T(8,128)(2,1)S(1)}, bf16[480,128]{1,0:T(8,128)(2,1)S(1)}, u32[]{:S(2)}, u32[]{:S(2)}) collective-permute-start(bf16[480,128]{1,0:T(8,128)(2,1)S(1)} %get-tuple-element.60), channel_id=1, source_target_pairs={{0,2},{1,3},{2,0},{3,1},{4,6},{5,7},{6,4},{7,5},{8,10},{9,11},{10,... | collective-permute-start | bytes 368648 | tf_op jit(solution)/shard_map/ppermute | solution.py:354
  31.0 8.4 %collective-permute-start.7 = (bf16[736,128]{1,0:T(8,128)(2,1)S(1)}, bf16[736,128]{1,0:T(8,128)(2,1)S(1)}, u32[]{:S(2)}, u32[]{:S(2)}) collective-permute-start(bf16[736,128]{1,0:T(8,128)(2,1)S(1)} %pad_maximum_fusion), channel_id=1, source_target_pairs={{0,2},{1,3},{2,0},{3,1},{4,6},{5,7},{6,4},{7,5},{8,10},{9,11},{10,... | collective-permute-start | bytes 565256 | tf_op jit(solution)/shard_map/ppermute | solution.py:354
  35.9 6.2 %collective-permute-start.9 = (bf16[240,128]{1,0:T(8,128)(2,1)S(1)}, bf16[240,128]{1,0:T(8,128)(2,1)S(1)}, u32[]{:S(2)}, u32[]{:S(2)}) collective-permute-start(bf16[240,128]{1,0:T(8,128)(2,1)S(1)} %get-tuple-element.80), channel_id=1, source_target_pairs={{0,12},{1,13},{2,14},{3,15},{4,8},{5,9},{6,10},{7,11},{8,4},{9,5},... | collective-permute-start | bytes 184328 | tf_op jit(solution)/shard_map/ppermute | solution.py:354
  39.5 5.2 %collective-permute-start.10 = (bf16[240,128]{1,0:T(8,128)(2,1)S(1)}, bf16[240,128]{1,0:T(8,128)(2,1)S(1)}, u32[]{:S(2)}, u32[]{:S(2)}) collective-permute-start(bf16[240,128]{1,0:T(8,128)(2,1)S(1)} %get-tuple-element.81), channel_id=1, source_target_pairs={{0,8},{1,9},{2,10},{3,11},{4,12},{5,13},{6,14},{7,15},{8,0},{9,1},... | collective-permute-start | bytes 184328 | tf_op jit(solution)/shard_map/ppermute | solution.py:354
  39.5 5.7 %collective-permute-start.11 = (bf16[240,128]{1,0:T(8,128)(2,1)S(1)}, bf16[240,128]{1,0:T(8,128)(2,1)S(1)}, u32[]{:S(2)}, u32[]{:S(2)}) collective-permute-start(bf16[240,128]{1,0:T(8,128)(2,1)S(1)} %add_convert_fusion.1), channel_id=1, source_target_pairs={{0,4},{1,5},{2,6},{3,7},{4,0},{5,1},{6,2},{7,3},{8,12},{9,13},{10,... | collective-permute-start | bytes 184328 | tf_op jit(solution)/shard_map/ppermute | solution.py:354
  41.1 5.0 %collective-permute-start.17 = (bf16[128,128]{1,0:T(8,128)(2,1)S(1)}, bf16[128,128]{1,0:T(8,128)(2,1)S(1)}, u32[]{:S(2)}, u32[]{:S(2)}) collective-permute-start(bf16[128,128]{1,0:T(8,128)(2,1)S(1)} %fusion.18), channel_id=1, source_target_pairs={{0,4},{1,5},{2,6},{3,7},{4,0},{5,1},{6,2},{7,3},{8,12},{9,13},{10,... | collective-permute-start | bytes 98312 | tf_op jit(solution)/shard_map/ppermute | solution.py:354
  45.2 4.9 %collective-permute-start.12 = (bf16[240,128]{1,0:T(8,128)(2,1)S(1)}, bf16[240,128]{1,0:T(8,128)(2,1)S(1)}, u32[]{:S(2)}, u32[]{:S(2)}) collective-permute-start(bf16[240,128]{1,0:T(8,128)(2,1)S(1)} %get-tuple-element.79), channel_id=1, source_target_pairs={{0,4},{1,5},{2,6},{3,7},{4,0},{5,1},{6,2},{7,3},{8,12},{9,13},{10,... | collective-permute-start | bytes 184328 | tf_op jit(solution)/shard_map/ppermute | solution.py:354
  46.1 6.4 %collective-permute-start.14 = (bf16[240,128]{1,0:T(8,128)(2,1)S(1)}, bf16[240,128]{1,0:T(8,128)(2,1)S(1)}, u32[]{:S(2)}, u32[]{:S(2)}) collective-permute-start(bf16[240,128]{1,0:T(8,128)(2,1)S(1)} %get-tuple-element.79), channel_id=1, source_target_pairs={{0,12},{1,13},{2,14},{3,15},{4,8},{5,9},{6,10},{7,11},{8,4},{9,5},... | collective-permute-start | bytes 184328 | tf_op jit(solution)/shard_map/ppermute | solution.py:354
  48.4 7.0 %collective-permute-start.13 = (bf16[240,128]{1,0:T(8,128)(2,1)S(1)}, bf16[240,128]{1,0:T(8,128)(2,1)S(1)}, u32[]{:S(2)}, u32[]{:S(2)}) collective-permute-start(bf16[240,128]{1,0:T(8,128)(2,1)S(1)} %get-tuple-element.79), channel_id=1, source_target_pairs={{0,8},{1,9},{2,10},{3,11},{4,12},{5,13},{6,14},{7,15},{8,0},{9,1},... | collective-permute-start | bytes 184328 | tf_op jit(solution)/shard_map/ppermute | solution.py:354
  50.1 5.7 %collective-permute-start.18 = (bf16[128,128]{1,0:T(8,128)(2,1)S(1)}, bf16[128,128]{1,0:T(8,128)(2,1)S(1)}, u32[]{:S(2)}, u32[]{:S(2)}) collective-permute-start(bf16[128,128]{1,0:T(8,128)(2,1)S(1)} %fusion.19), channel_id=1, source_target_pairs={{0,8},{1,9},{2,10},{3,11},{4,12},{5,13},{6,14},{7,15},{8,0},{9,1},... | collective-permute-start | bytes 98312 | tf_op jit(solution)/shard_map/ppermute | solution.py:354
  51.3 9.4 %collective-permute-start.15 = (bf16[480,128]{1,0:T(8,128)(2,1)S(1)}, bf16[480,128]{1,0:T(8,128)(2,1)S(1)}, u32[]{:S(2)}, u32[]{:S(2)}) collective-permute-start(bf16[480,128]{1,0:T(8,128)(2,1)S(1)} %pad_maximum_fusion.1), channel_id=1, source_target_pairs={{0,2},{1,3},{2,0},{3,1},{4,6},{5,7},{6,4},{7,5},{8,10},{9,11},{10,... | collective-permute-start | bytes 368648 | tf_op jit(solution)/shard_map/ppermute | solution.py:354
  55.4 5.3 %collective-permute-start.16 = (bf16[480,128]{1,0:T(8,128)(2,1)S(1)}, bf16[480,128]{1,0:T(8,128)(2,1)S(1)}, u32[]{:S(2)}, u32[]{:S(2)}) collective-permute-start(bf16[480,128]{1,0:T(8,128)(2,1)S(1)} %pad_maximum_fusion.2), channel_id=1, source_target_pairs={{0,2},{1,3},{2,0},{3,1},{4,6},{5,7},{6,4},{7,5},{8,10},{9,11},{10,... | collective-permute-start | bytes 368648 | tf_op jit(solution)/shard_map/ppermute | solution.py:354
  55.8 4.9 %collective-permute-start.19 = (bf16[128,128]{1,0:T(8,128)(2,1)S(1)}, bf16[128,128]{1,0:T(8,128)(2,1)S(1)}, u32[]{:S(2)}, u32[]{:S(2)}) collective-permute-start(bf16[128,128]{1,0:T(8,128)(2,1)S(1)} %fusion.17), channel_id=1, source_target_pairs={{0,2},{1,3},{2,0},{3,1},{4,6},{5,7},{6,4},{7,5},{8,10},{9,11},{10,... | collective-permute-start | bytes 98312 | tf_op jit(solution)/shard_map/ppermute | solution.py:354
  60.8 2.0 %collective-permute-start.20 = (bf16[2176,128]{1,0:T(8,128)(2,1)S(1)}, bf16[2176,128]{1,0:T(8,128)(2,1)S(1)}, u32[]{:S(2)}, u32[]{:S(2)}) collective-permute-start(bf16[2176,128]{1,0:T(8,128)(2,1)S(1)} %fusion.10.mine), channel_id=1, source_target_pairs={{0,1},{1,0},{2,3},{3,2},{4,5},{5,4},{6,7},{7,6},{8,9},{9,8},{10,11... | collective-permute-start | bytes 1671176 | tf_op jit(solution)/shard_map/ppermute | solution.py:354

commit v14 on v13

--- a/solution.py
+++ b/solution.py
@@ -599,7 +599,6 @@
         k *= 2
     others = {j: _xor(mine, 4 * j, n, axis) for j in (1, 3, 2)}
     x_near = _xor(jnp.concatenate([mine, others[1]], axis=0), 2, n, axis)
-    x_far = _xor(jnp.concatenate([others[2], others[3]], axis=0), 2, n, axis)
     beyond = by(index & 4, near_lead, jnp.full_like(lead, EMPTY_GRAD))
     lead, k = _after(ordered(index & 4, lead, near_lead), others[1]), 8
     while k < n:
@@ -608,11 +607,12 @@
         if 2 * k < n:
             lead = ordered(index & k, lead, came)
         k *= 2
-    theirs = _xor(beyond, 2, n, axis)
+    x_far = _xor(jnp.concatenate([others[2], others[3], beyond], axis=0), 2, n, axis)
+    theirs = x_far[2 * piece :]
     beyond = jnp.concatenate([by(pair, beyond, theirs), by(pair, theirs, beyond)], axis=0)
     beyond = by(pair, _first_live(beside_first, beyond), beyond)
     ours = jnp.concatenate(
-        [mine, others[1], others[2], others[3], x_near, x_far, beyond], axis=0
+        [mine, others[1], others[2], others[3], x_near, x_far[: 2 * piece], beyond], axis=0
     )
     other = _xor(ours, 1, n, axis)
     cwg, swg, cbg, sbg, frames_grad = _call(

time: 65.2 us -> 66 us (1.012)
  waiting for transfers between devices: 18.1 us -> 20.1 us
  starting transfers between devices: 22.9 us -> 21.7 us
    ppermute x21 -> x20, waiting for transfers between devices: 18.1 us -> 20.1 us  [_xor(): return lax.ppermute(x, axis, [(i, i ^ k) for i in range(n)])]
    ppermute x21 -> x20, starting transfers between devices: 22.9 us -> 21.7 us  [_xor(): return lax.ppermute(x, axis, [(i, i ^ k) for i in range(n)])]
  transfers between devices with their start and end apart: 21 -> 20, of which waited for: 15 -> 14; matrix products, arithmetic and copies ran while one was open for 3% -> 3% of each run, Pallas kernels for 21% -> 21%
where the time goes in v14:
time: 66 us; the launch traced here: 65.8 us
  starting transfers between devices  21.7 us (33%)
  Pallas kernels  20.3 us (31%)
  waiting for transfers between devices  20.1 us (30%)
  other arithmetic  1.97 us (3%)
  between operations  1.58 us (2%)
    ppermute x20, starting transfers between devices, _xor(): return lax.ppermute(x, axis, [(i, i ^ k) for i in range(n)])  21.7 us
    ppermute x20, waiting for transfers between devices, _xor(): return lax.ppermute(x, axis, [(i, i ^ k) for i in range(n)])  20.1 us
    pallas_call x1, Pallas kernels, early_conv(): _call(_early_conv_kernel, [jax.ShapeDtypeStruct(wide, F32), jax.ShapeDtyp...  4.4 us
    pallas_call x1, Pallas kernels, early_sums(): _call(_early_sums_kernel, jax.ShapeDtypeStruct((rows, c), F32), [_SMEM, _...  3.94 us
    pallas_call x1, Pallas kernels, body(): _call(_back_kernel, jax.ShapeDtypeStruct((slots, 2, h, w, c), F32), [_SME...  3.39 us
    pallas_call x1, Pallas kernels, body(): _call(_late_kernel, [jax.ShapeDtypeStruct((h, w, c), BF), jax.ShapeDtypeS...  2.78 us
    pallas_call x1, Pallas kernels, body(): _call(_final_kernel, [jax.ShapeDtypeStruct((27 * c, c), F32), jax.ShapeDt...  2.18 us
  transfers between devices with their start and end apart: 20, of which 14 were waited for; matrix products, arithmetic and copies ran while one was open for 3% of the time, Pallas kernels for 21%

profile of v14, /device:TPU:0, one launch (start us, length us, event | category | flops | bytes accessed | tf_op | source)
XLA Modules:
  0.0 65.8 jit_solution(1387671620668311463)
XLA Ops:
  1.3 1.0 %shard_map.136 = bf16[12,64,128]{2,1,0:T(8,128)(2,1)S(1)} custom-call(s32[1]{0:T(128)S(6)} %copy.22.sc, bf16[4,2,4,64,128]{4,3,2,1,0:T(8,128)(2,1)} %frs.1, bf16[4,2,2,64,128]{4,3,2,1,0:T(8,128)(2,1)} %has.1), custom_call_target="tpu_custom_call" | custom-call | tf_op jit(solution)/shard_map/pallas_call | solution.py:435
  2.2 0.5 collective-permute-start
  2.8 0.7 %pad_add_fusion.sc = s32[7]{0:T(128)S(1)} fusion(s32[1]{0:T(128)} %bitcast.1, s32[1]{0:T(128)} %bitcast, s32[4]{0:T(128)} %param.11, s32[1]{0:T(128)S(6)} %copy.22.sc), kind=kLoop, calls=%fused_computation.62 | loop fusion | flops 21 | bytes 56 | tf_op jit(solution)/shard_map/concatenate | solution.py:417
  3.5 0.3 collective-permute-done
  3.9 2.9 %collective-permute-start.1 = (bf16[6,64,128]{2,1,0:T(8,128)(2,1)S(1)}, bf16[6,64,128]{2,1,0:T(8,128)(2,1)S(1)}, u32[]{:S(2)}, u32[]{:S(2)}) collective-permute-start(bf16[6,64,128]{2,1,0:T(8,128)(2,1)S(1)} %fusion.7), channel_id=1, source_target_pairs={{0,2},{1,3},{2,0},{3,1},{4,6},{5,7},{6,4},{7,5},{8,10},{9,11},{10,... | collective-permute-start | bytes 294920 | tf_op jit(solution)/shard_map/ppermute | solution.py:354
  6.8 4.4 %shard_map.137 = (f32[768,256]{1,0:T(8,128)S(1)}, bf16[768,128]{1,0:T(8,128)(2,1)S(1)}, bf16[2,128,128]{2,1,0:T(8,128)(2,1)S(1)}, f32[1,128]{1,0:T(1,128)S(1)}) custom-call(s32[7]{0:T(128)S(1)} %pad_add_fusion.sc, bf16[4,2,4,64,128]{4,3,2,1,0:T(8,128)(2,1)} %frs.1, bf16[4,2,2,64,128]{4,3,2,1,0:T(8,128)(2,1)} %has.1, bf16[4,1,4,64,128]{4,3,2,1,0:T(8,128)(2,1)} %cos.1, ...), custom_call_target="tpu_custom_call" | custom-call | flops 1811939328 | bytes 4194304 | tf_op jit(solution)/shard_map/pallas_call | solution.py:462
  11.2 0.0 collective-permute-done.1
  11.2 1.6 %collective-permute-start.2 = (bf16[6,64,128]{2,1,0:T(8,128)(2,1)S(1)}, bf16[6,64,128]{2,1,0:T(8,128)(2,1)S(1)}, u32[]{:S(2)}, u32[]{:S(2)}) collective-permute-start(bf16[6,64,128]{2,1,0:T(8,128)(2,1)S(1)} %fusion.8), channel_id=1, source_target_pairs={{0,4},{1,5},{2,6},{3,7},{4,0},{5,1},{6,2},{7,3},{8,12},{9,13},{10,... | collective-permute-start | bytes 294920 | tf_op jit(solution)/shard_map/ppermute | solution.py:354
  12.9 1.0 %shard_map.138 = (bf16[3,4,64,128]{3,2,1,0:T(8,128)(2,1)S(1)}, bf16[768,256]{1,0:T(8,128)(2,1)S(1)}, bf16[768,256]{1,0:T(8,128)(2,1)S(1)}) custom-call(s32[7]{0:T(128)S(1)} %pad_add_fusion.sc, f32[768,256]{1,0:T(8,128)S(1)} %get-tuple-element.40.pre_ref, bf16[768,128]{1,0:T(8,128)(2,1)S(1)} %get-tuple-element.43.gout_ref, ...), custom_call_target="tpu_custom_call" | custom-call | bytes 2097152 | tf_op jit(solution)/shard_map/pallas_call | solution.py:480
  13.9 2.1 %collective-permute-done.2 = bf16[6,64,128]{2,1,0:T(8,128)(2,1)S(1)} collective-permute-done((bf16[6,64,128]{2,1,0:T(8,128)(2,1)S(1)}, bf16[6,64,128]{2,1,0:T(8,128)(2,1)S(1)}, u32[]{:S(2)}, u32[]{:S(2)}) %collective-permute-start.2) | collective-permute-done | bytes 98336 | tf_op jit(solution)/shard_map/ppermute | solution.py:354
  16.0 2.7 %collective-permute-start.3 = (bf16[6,64,128]{2,1,0:T(8,128)(2,1)S(1)}, bf16[6,64,128]{2,1,0:T(8,128)(2,1)S(1)}, u32[]{:S(2)}, u32[]{:S(2)}) collective-permute-start(bf16[6,64,128]{2,1,0:T(8,128)(2,1)S(1)} %fusion.9), channel_id=1, source_target_pairs={{0,8},{1,9},{2,10},{3,11},{4,12},{5,13},{6,14},{7,15},{8,0},{9,1},... | collective-permute-start | bytes 294920 | tf_op jit(solution)/shard_map/ppermute | solution.py:354
  18.6 0.0 copy-start
  18.6 0.0 copy-start.4
  18.6 0.0 copy-start.5
  18.6 0.0 copy-start.6
  18.7 3.9 %shard_map.139.early = f32[3840,128]{1,0:T(8,128)S(1)} custom-call(s32[7]{0:T(128)S(1)} %pad_add_fusion.sc, bf16[4,2,4,64,128]{4,3,2,1,0:T(8,128)(2,1)} %frs.1, bf16[4,2,2,64,128]{4,3,2,1,0:T(8,128)(2,1)} %has.1, bf16[768,256]{1,0:T(8,128)(2,1)S(1)} %get-tuple-element.46.g_ref.g1, bf16[768,256]{1,0:T(8,128)(2,1)S(1)} %get-tuple-element.49.hid_ref, ...), custom_call_target="tpu_custom_call" | custom-call | flops 1811939328 | bytes 4194304 | tf_op jit(solution)/shard_map/pallas_call | solution.py:496
  22.6 0.0 collective-permute-done.3
  22.7 0.1 collective-permute-start.4
  22.7 1.3 %collective-permute-done.4 = bf16[6,64,128]{2,1,0:T(8,128)(2,1)S(1)} collective-permute-done((bf16[6,64,128]{2,1,0:T(8,128)(2,1)S(1)}, bf16[6,64,128]{2,1,0:T(8,128)(2,1)S(1)}, u32[]{:S(2)}, u32[]{:S(2)}) %collective-permute-start.4) | collective-permute-done | bytes 98336 | tf_op jit(solution)/shard_map/ppermute | solution.py:354
  24.1 0.1 compare_select_fusion.tail
  24.1 0.0 copy-done
  24.1 0.0 copy-done.1
  24.1 0.0 copy-done.2
  24.1 0.0 copy-done.3
  24.2 0.0 copy-done.4
  24.2 0.0 copy-done.5
  24.2 0.0 copy-done.6
  24.2 2.8 %shard_map.140 = (bf16[4,64,128]{2,1,0:T(8,128)(2,1)S(1)}, bf16[256,256]{1,0:T(8,128)(2,1)S(1)}, bf16[1920,128]{1,0:T(8,128)(2,1)S(1)}, f32[1920,128]{1,0:T(8,128)S(1)}) custom-call(s32[7]{0:T(128)S(1)} %pad_add_fusion.sc, bf16[4,2,4,64,128]{4,3,2,1,0:T(8,128)(2,1)S(1)} %copy-done.1, bf16[4,2,2,64,128]{4,3,2,1,0:T(8,128)(2,1)S(1)} %copy-done.2, ...), custom_call_target="tpu_custom_call" | custom-call | flops 1207959552 | bytes 6291456 | tf_op jit(solution)/shard_map/pallas_call | solution.py:515
  27.0 0.2 collective-permute-start.5
  27.2 1.1 %shard_map.141 = bf16[512,128]{1,0:T(8,128)(2,1)S(1)} custom-call(s32[7]{0:T(128)S(1)} %pad_add_fusion.sc, bf16[256,256]{1,0:T(8,128)(2,1)S(1)} %get-tuple-element.54.g_ref.g0, bf16[27,128,128]{2,1,0:T(8,128)(2,1)S(1)} %bitcast.16), custom_call_target="tpu_custom_call" | custom-call | flops 301989888 | bytes 1048576 | tf_op jit(solution)/shard_map/pallas_call | solution.py:533
  28.2 0.6 collective-permute-done.5.got
  28.9 0.6 shard_map.142
  29.5 0.2 collective-permute-start.6
  29.8 0.6 collective-permute-start.8
  30.3 0.6 collective-permute-done.6.got
  31.0 0.1 fusion.11
  31.0 0.9 %collective-permute-start.7 = (bf16[736,128]{1,0:T(8,128)(2,1)S(1)}, bf16[736,128]{1,0:T(8,128)(2,1)S(1)}, u32[]{:S(2)}, u32[]{:S(2)}) collective-permute-start(bf16[736,128]{1,0:T(8,128)(2,1)S(1)} %pad_maximum_fusion), channel_id=1, source_target_pairs={{0,2},{1,3},{2,0},{3,1},{4,6},{5,7},{6,4},{7,5},{8,10},{9,11},{10,... | collective-permute-start | bytes 565256 | tf_op jit(solution)/shard_map/ppermute | solution.py:354
  31.9 3.4 %shard_map.143.grad = f32[4,2,4,64,128]{4,3,2,1,0:T(8,128)S(1)} custom-call(s32[7]{0:T(128)S(1)} %pad_add_fusion.sc, bf16[256,256]{1,0:T(8,128)(2,1)S(1)} %get-tuple-element.54.g_ref.g0, bf16[768,256]{1,0:T(8,128)(2,1)S(1)} %get-tuple-element.46.g_ref.g1, bf16[27,128,128]{2,1,0:T(8,128)(2,1)S(1)} %bitcast.17), custom_call_target="tpu_custom_call" | custom-call | flops 1 | bytes 1 | tf_op jit(solution)/shard_map/pallas_call | solution.py:569
  35.3 0.6 collective-permute-done.8
  35.9 3.5 %collective-permute-start.9 = (bf16[240,128]{1,0:T(8,128)(2,1)S(1)}, bf16[240,128]{1,0:T(8,128)(2,1)S(1)}, u32[]{:S(2)}, u32[]{:S(2)}) collective-permute-start(bf16[240,128]{1,0:T(8,128)(2,1)S(1)} %get-tuple-element.80), channel_id=1, source_target_pairs={{0,12},{1,13},{2,14},{3,15},{4,8},{5,9},{6,10},{7,11},{8,4},{9,5},... | collective-permute-start | bytes 184328 | tf_op jit(solution)/shard_map/ppermute | solution.py:354
  39.5 0.0 collective-permute-start.10
  39.5 0.0 collective-permute-done.7
  39.5 1.6 %collective-permute-start.11 = (bf16[240,128]{1,0:T(8,128)(2,1)S(1)}, bf16[240,128]{1,0:T(8,128)(2,1)S(1)}, u32[]{:S(2)}, u32[]{:S(2)}) collective-permute-start(bf16[240,128]{1,0:T(8,128)(2,1)S(1)} %add_convert_fusion.1), channel_id=1, source_target_pairs={{0,4},{1,5},{2,6},{3,7},{4,0},{5,1},{6,2},{7,3},{8,12},{9,13},{10,... | collective-permute-start | bytes 184328 | tf_op jit(solution)/shard_map/ppermute | solution.py:354
  41.1 0.5 collective-permute-start.16
  41.6 0.5 collective-permute-done.9
  42.1 2.5 %collective-permute-done.10 = bf16[240,128]{1,0:T(8,128)(2,1)S(1)} collective-permute-done((bf16[240,128]{1,0:T(8,128)(2,1)S(1)}, bf16[240,128]{1,0:T(8,128)(2,1)S(1)}, u32[]{:S(2)}, u32[]{:S(2)}) %collective-permute-start.10) | collective-permute-done | bytes 61472 | tf_op jit(solution)/shard_map/ppermute | solution.py:354
  44.7 0.5 collective-permute-done.11
  45.2 0.9 %collective-permute-start.12 = (bf16[240,128]{1,0:T(8,128)(2,1)S(1)}, bf16[240,128]{1,0:T(8,128)(2,1)S(1)}, u32[]{:S(2)}, u32[]{:S(2)}) collective-permute-start(bf16[240,128]{1,0:T(8,128)(2,1)S(1)} %get-tuple-element.79), channel_id=1, source_target_pairs={{0,4},{1,5},{2,6},{3,7},{4,0},{5,1},{6,2},{7,3},{8,12},{9,13},{10,... | collective-permute-start | bytes 184328 | tf_op jit(solution)/shard_map/ppermute | solution.py:354
  46.1 0.0 collective-permute-done.16
  46.1 2.3 %collective-permute-start.14 = (bf16[240,128]{1,0:T(8,128)(2,1)S(1)}, bf16[240,128]{1,0:T(8,128)(2,1)S(1)}, u32[]{:S(2)}, u32[]{:S(2)}) collective-permute-start(bf16[240,128]{1,0:T(8,128)(2,1)S(1)} %get-tuple-element.79), channel_id=1, source_target_pairs={{0,12},{1,13},{2,14},{3,15},{4,8},{5,9},{6,10},{7,11},{8,4},{9,5},... | collective-permute-start | bytes 184328 | tf_op jit(solution)/shard_map/ppermute | solution.py:354
  48.4 0.5 collective-permute-start.13
  48.9 1.2 %collective-permute-done.12 = bf16[240,128]{1,0:T(8,128)(2,1)S(1)} collective-permute-done((bf16[240,128]{1,0:T(8,128)(2,1)S(1)}, bf16[240,128]{1,0:T(8,128)(2,1)S(1)}, u32[]{:S(2)}, u32[]{:S(2)}) %collective-permute-start.12) | collective-permute-done | bytes 61472 | tf_op jit(solution)/shard_map/ppermute | solution.py:354
  50.1 1.3 %collective-permute-start.17 = (bf16[128,128]{1,0:T(8,128)(2,1)S(1)}, bf16[128,128]{1,0:T(8,128)(2,1)S(1)}, u32[]{:S(2)}, u32[]{:S(2)}) collective-permute-start(bf16[128,128]{1,0:T(8,128)(2,1)S(1)} %fusion.19), channel_id=1, source_target_pairs={{0,8},{1,9},{2,10},{3,11},{4,12},{5,13},{6,14},{7,15},{8,0},{9,1},... | collective-permute-start | bytes 98312 | tf_op jit(solution)/shard_map/ppermute | solution.py:354
  51.3 0.7 %collective-permute-start.15 = (bf16[480,128]{1,0:T(8,128)(2,1)S(1)}, bf16[480,128]{1,0:T(8,128)(2,1)S(1)}, u32[]{:S(2)}, u32[]{:S(2)}) collective-permute-start(bf16[480,128]{1,0:T(8,128)(2,1)S(1)} %pad_maximum_fusion.2), channel_id=1, source_target_pairs={{0,2},{1,3},{2,0},{3,1},{4,6},{5,7},{6,4},{7,5},{8,10},{9,11},{10,... | collective-permute-start | bytes 368648 | tf_op jit(solution)/shard_map/ppermute | solution.py:354
  52.0 3.4 %collective-permute-done.13 = bf16[240,128]{1,0:T(8,128)(2,1)S(1)} collective-permute-done((bf16[240,128]{1,0:T(8,128)(2,1)S(1)}, bf16[240,128]{1,0:T(8,128)(2,1)S(1)}, u32[]{:S(2)}, u32[]{:S(2)}) %collective-permute-start.13) | collective-permute-done | bytes 61472 | tf_op jit(solution)/shard_map/ppermute | solution.py:354
  55.4 0.3 collective-permute-done.17
  55.8 0.0 collective-permute-done.14
  55.8 0.8 %collective-permute-start.18 = (bf16[608,128]{1,0:T(8,128)(2,1)S(1)}, bf16[608,128]{1,0:T(8,128)(2,1)S(1)}, u32[]{:S(2)}, u32[]{:S(2)}) collective-permute-start(bf16[608,128]{1,0:T(8,128)(2,1)S(1)} %pad_maximum_fusion.1), channel_id=1, source_target_pairs={{0,2},{1,3},{2,0},{3,1},{4,6},{5,7},{6,4},{7,5},{8,10},{9,11},{10,... | collective-permute-start | bytes 466952 | tf_op jit(solution)/shard_map/ppermute | solution.py:354
  56.6 0.0 collective-permute-done.15
  56.6 4.9 %collective-permute-done.18 = bf16[608,128]{1,0:T(8,128)(2,1)S(1)} collective-permute-done((bf16[608,128]{1,0:T(8,128)(2,1)S(1)}, bf16[608,128]{1,0:T(8,128)(2,1)S(1)}, u32[]{:S(2)}, u32[]{:S(2)}) %collective-permute-start.18) | collective-permute-done | bytes 155680 | tf_op jit(solution)/shard_map/ppermute | solution.py:354
  61.6 0.1 collective-permute-start.19
  61.7 0.7 %maximum_bitcast_fusion = bf16[4,1,4,64,128]{4,3,2,1,0:T(8,128)(2,1)} fusion(bf16[3,4,64,128]{3,2,1,0:T(8,128)(2,1)S(1)} %get-tuple-element.52, bf16[1,4,64,128]{3,2,1,0:T(8,128)(2,1)S(1)} %bitcast.18), kind=kLoop, calls=%fused_computation.11 | loop fusion | flops 131072 | bytes 524288
  62.4 1.2 %collective-permute-done.19.other = bf16[2176,128]{1,0:T(8,128)(2,1)S(1)} collective-permute-done((bf16[2176,128]{1,0:T(8,128)(2,1)S(1)}, bf16[2176,128]{1,0:T(8,128)(2,1)S(1)}, u32[]{:S(2)}, u32[]{:S(2)}) %collective-permute-start.19) | collective-permute-done | bytes 557088 | tf_op jit(solution)/shard_map/ppermute | solution.py:354
  63.6 2.2 %shard_map.144 = (f32[3456,128]{1,0:T(8,128)}, f32[256,128]{1,0:T(8,128)}, f32[1,128]{1,0:T(1,128)}, f32[1,128]{1,0:T(1,128)}, bf16[4,2,4,64,128]{4,3,2,1,0:T(8,128)(2,1)}) custom-call(s32[7]{0:T(128)S(1)} %pad_add_fusion.sc, bf16[2176,128]{1,0:T(8,128)(2,1)S(1)} %fusion.10.mine, bf16[2176,128]{1,0:T(8,128)(2,1)S(1)} %collective-permute-done.19.other, ...), custom_call_target="tpu_custom_call" | custom-call | tf_op jit(solution)/shard_map/pallas_call | solution.py:618
  (26 shorter events, 0.5 us)
Async XLA Ops:
  2.2 1.6 %collective-permute-start = (bf16[12,64,128]{2,1,0:T(8,128)(2,1)S(1)}, bf16[12,64,128]{2,1,0:T(8,128)(2,1)S(1)}, u32[]{:S(2)}, u32[]{:S(2)}) collective-permute-start(bf16[12,64,128]{2,1,0:T(8,128)(2,1)S(1)} %shard_map.136), channel_id=1, source_target_pairs={{0,1},{1,0},{2,3},{3,2},{4,5},{5,4},{6,7},{7,6},{8,9},{9,8},{10,11... | collective-permute-start | bytes 589832 | tf_op jit(solution)/shard_map/ppermute | solution.py:354
  3.9 7.3 %collective-permute-start.1 = (bf16[6,64,128]{2,1,0:T(8,128)(2,1)S(1)}, bf16[6,64,128]{2,1,0:T(8,128)(2,1)S(1)}, u32[]{:S(2)}, u32[]{:S(2)}) collective-permute-start(bf16[6,64,128]{2,1,0:T(8,128)(2,1)S(1)} %fusion.7), channel_id=1, source_target_pairs={{0,2},{1,3},{2,0},{3,1},{4,6},{5,7},{6,4},{7,5},{8,10},{9,11},{10,... | collective-permute-start | bytes 294920 | tf_op jit(solution)/shard_map/ppermute | solution.py:354
  11.2 4.7 %collective-permute-start.2 = (bf16[6,64,128]{2,1,0:T(8,128)(2,1)S(1)}, bf16[6,64,128]{2,1,0:T(8,128)(2,1)S(1)}, u32[]{:S(2)}, u32[]{:S(2)}) collective-permute-start(bf16[6,64,128]{2,1,0:T(8,128)(2,1)S(1)} %fusion.8), channel_id=1, source_target_pairs={{0,4},{1,5},{2,6},{3,7},{4,0},{5,1},{6,2},{7,3},{8,12},{9,13},{10,... | collective-permute-start | bytes 294920 | tf_op jit(solution)/shard_map/ppermute | solution.py:354
  16.0 6.7 %collective-permute-start.3 = (bf16[6,64,128]{2,1,0:T(8,128)(2,1)S(1)}, bf16[6,64,128]{2,1,0:T(8,128)(2,1)S(1)}, u32[]{:S(2)}, u32[]{:S(2)}) collective-permute-start(bf16[6,64,128]{2,1,0:T(8,128)(2,1)S(1)} %fusion.9), channel_id=1, source_target_pairs={{0,8},{1,9},{2,10},{3,11},{4,12},{5,13},{6,14},{7,15},{8,0},{9,1},... | collective-permute-start | bytes 294920 | tf_op jit(solution)/shard_map/ppermute | solution.py:354
  18.6 5.5 %copy-start = (bf16[3,3,3,128,128]{4,3,2,1,0:T(8,128)(2,1)S(1)}, bf16[3,3,3,128,128]{4,3,2,1,0:T(8,128)(2,1)}, u32[]{:S(2)}) copy-start(bf16[3,3,3,128,128]{4,3,2,1,0:T(8,128)(2,1)} %param.13) | copy-start | bytes 2654212
  18.6 5.5 %copy-start.1 = (bf16[4,2,4,64,128]{4,3,2,1,0:T(8,128)(2,1)S(1)}, bf16[4,2,4,64,128]{4,3,2,1,0:T(8,128)(2,1)}, u32[]{:S(2)}) copy-start(bf16[4,2,4,64,128]{4,3,2,1,0:T(8,128)(2,1)} %frs.1) | copy-start | bytes 1572868
  18.6 5.5 %copy-start.2 = (bf16[4,2,2,64,128]{4,3,2,1,0:T(8,128)(2,1)S(1)}, bf16[4,2,2,64,128]{4,3,2,1,0:T(8,128)(2,1)}, u32[]{:S(2)}) copy-start(bf16[4,2,2,64,128]{4,3,2,1,0:T(8,128)(2,1)} %has.1) | copy-start | bytes 786436
  18.6 5.5 %copy-start.3 = (bf16[4,1,4,64,128]{4,3,2,1,0:T(8,128)(2,1)S(1)}, bf16[4,1,4,64,128]{4,3,2,1,0:T(8,128)(2,1)}, u32[]{:S(2)}) copy-start(bf16[4,1,4,64,128]{4,3,2,1,0:T(8,128)(2,1)} %cos.1) | copy-start | bytes 786436
  18.6 5.5 %copy-start.4 = (bf16[2,128,128]{2,1,0:T(8,128)(2,1)S(1)}, bf16[2,128,128]{2,1,0:T(8,128)(2,1)}, u32[]{:S(2)}) copy-start(bf16[2,128,128]{2,1,0:T(8,128)(2,1)} %sw.1) | copy-start | bytes 196612
  18.6 5.5 %copy-start.5 = (f32[128]{0:T(128)S(1)}, f32[128]{0:T(128)}, u32[]{:S(2)}) copy-start(f32[128]{0:T(128)} %param.14) | copy-start | bytes 1540
  18.6 5.5 %copy-start.6 = (f32[128]{0:T(128)S(1)}, f32[128]{0:T(128)}, u32[]{:S(2)}) copy-start(f32[128]{0:T(128)} %param.16) | copy-start | bytes 1540
  22.7 1.4 %collective-permute-start.4 = (bf16[6,64,128]{2,1,0:T(8,128)(2,1)S(1)}, bf16[6,64,128]{2,1,0:T(8,128)(2,1)S(1)}, u32[]{:S(2)}, u32[]{:S(2)}) collective-permute-start(bf16[6,64,128]{2,1,0:T(8,128)(2,1)S(1)} %fusion.2), channel_id=1, source_target_pairs={{0,1},{1,0},{2,3},{3,2},{4,5},{5,4},{6,7},{7,6},{8,9},{9,8},{10,11... | collective-permute-start | bytes 294920 | tf_op jit(solution)/shard_map/ppermute | solution.py:354
  27.0 1.9 %collective-permute-start.5 = (bf16[1920,128]{1,0:T(8,128)(2,1)S(1)}, bf16[1920,128]{1,0:T(8,128)(2,1)S(1)}, u32[]{:S(2)}, u32[]{:S(2)}) collective-permute-start(bf16[1920,128]{1,0:T(8,128)(2,1)S(1)} %get-tuple-element.56), channel_id=1, source_target_pairs={{0,1},{1,0},{2,3},{3,2},{4,5},{5,4},{6,7},{7,6},{8,9},{9,8},{10,11... | collective-permute-start | bytes 1474568 | tf_op jit(solution)/shard_map/ppermute | solution.py:354
  29.5 1.4 %collective-permute-start.6 = (bf16[512,128]{1,0:T(8,128)(2,1)S(1)}, bf16[512,128]{1,0:T(8,128)(2,1)S(1)}, u32[]{:S(2)}, u32[]{:S(2)}) collective-permute-start(bf16[512,128]{1,0:T(8,128)(2,1)S(1)} %shard_map.141), channel_id=1, source_target_pairs={{0,1},{1,0},{2,3},{3,2},{4,5},{5,4},{6,7},{7,6},{8,9},{9,8},{10,11... | collective-permute-start | bytes 393224 | tf_op jit(solution)/shard_map/ppermute | solution.py:354
  29.8 6.1 %collective-permute-start.8 = (bf16[480,128]{1,0:T(8,128)(2,1)S(1)}, bf16[480,128]{1,0:T(8,128)(2,1)S(1)}, u32[]{:S(2)}, u32[]{:S(2)}) collective-permute-start(bf16[480,128]{1,0:T(8,128)(2,1)S(1)} %get-tuple-element.60), channel_id=1, source_target_pairs={{0,2},{1,3},{2,0},{3,1},{4,6},{5,7},{6,4},{7,5},{8,10},{9,11},{10,... | collective-permute-start | bytes 368648 | tf_op jit(solution)/shard_map/ppermute | solution.py:354
  31.0 8.4 %collective-permute-start.7 = (bf16[736,128]{1,0:T(8,128)(2,1)S(1)}, bf16[736,128]{1,0:T(8,128)(2,1)S(1)}, u32[]{:S(2)}, u32[]{:S(2)}) collective-permute-start(bf16[736,128]{1,0:T(8,128)(2,1)S(1)} %pad_maximum_fusion), channel_id=1, source_target_pairs={{0,2},{1,3},{2,0},{3,1},{4,6},{5,7},{6,4},{7,5},{8,10},{9,11},{10,... | collective-permute-start | bytes 565256 | tf_op jit(solution)/shard_map/ppermute | solution.py:354
  35.9 6.2 %collective-permute-start.9 = (bf16[240,128]{1,0:T(8,128)(2,1)S(1)}, bf16[240,128]{1,0:T(8,128)(2,1)S(1)}, u32[]{:S(2)}, u32[]{:S(2)}) collective-permute-start(bf16[240,128]{1,0:T(8,128)(2,1)S(1)} %get-tuple-element.80), channel_id=1, source_target_pairs={{0,12},{1,13},{2,14},{3,15},{4,8},{5,9},{6,10},{7,11},{8,4},{9,5},... | collective-permute-start | bytes 184328 | tf_op jit(solution)/shard_map/ppermute | solution.py:354
  39.5 5.2 %collective-permute-start.10 = (bf16[240,128]{1,0:T(8,128)(2,1)S(1)}, bf16[240,128]{1,0:T(8,128)(2,1)S(1)}, u32[]{:S(2)}, u32[]{:S(2)}) collective-permute-start(bf16[240,128]{1,0:T(8,128)(2,1)S(1)} %get-tuple-element.81), channel_id=1, source_target_pairs={{0,8},{1,9},{2,10},{3,11},{4,12},{5,13},{6,14},{7,15},{8,0},{9,1},... | collective-permute-start | bytes 184328 | tf_op jit(solution)/shard_map/ppermute | solution.py:354
  39.5 5.7 %collective-permute-start.11 = (bf16[240,128]{1,0:T(8,128)(2,1)S(1)}, bf16[240,128]{1,0:T(8,128)(2,1)S(1)}, u32[]{:S(2)}, u32[]{:S(2)}) collective-permute-start(bf16[240,128]{1,0:T(8,128)(2,1)S(1)} %add_convert_fusion.1), channel_id=1, source_target_pairs={{0,4},{1,5},{2,6},{3,7},{4,0},{5,1},{6,2},{7,3},{8,12},{9,13},{10,... | collective-permute-start | bytes 184328 | tf_op jit(solution)/shard_map/ppermute | solution.py:354
  41.1 5.0 %collective-permute-start.16 = (bf16[128,128]{1,0:T(8,128)(2,1)S(1)}, bf16[128,128]{1,0:T(8,128)(2,1)S(1)}, u32[]{:S(2)}, u32[]{:S(2)}) collective-permute-start(bf16[128,128]{1,0:T(8,128)(2,1)S(1)} %fusion.18), channel_id=1, source_target_pairs={{0,4},{1,5},{2,6},{3,7},{4,0},{5,1},{6,2},{7,3},{8,12},{9,13},{10,... | collective-permute-start | bytes 98312 | tf_op jit(solution)/shard_map/ppermute | solution.py:354
  45.2 4.9 %collective-permute-start.12 = (bf16[240,128]{1,0:T(8,128)(2,1)S(1)}, bf16[240,128]{1,0:T(8,128)(2,1)S(1)}, u32[]{:S(2)}, u32[]{:S(2)}) collective-permute-start(bf16[240,128]{1,0:T(8,128)(2,1)S(1)} %get-tuple-element.79), channel_id=1, source_target_pairs={{0,4},{1,5},{2,6},{3,7},{4,0},{5,1},{6,2},{7,3},{8,12},{9,13},{10,... | collective-permute-start | bytes 184328 | tf_op jit(solution)/shard_map/ppermute | solution.py:354
  46.1 9.6 %collective-permute-start.14 = (bf16[240,128]{1,0:T(8,128)(2,1)S(1)}, bf16[240,128]{1,0:T(8,128)(2,1)S(1)}, u32[]{:S(2)}, u32[]{:S(2)}) collective-permute-start(bf16[240,128]{1,0:T(8,128)(2,1)S(1)} %get-tuple-element.79), channel_id=1, source_target_pairs={{0,12},{1,13},{2,14},{3,15},{4,8},{5,9},{6,10},{7,11},{8,4},{9,5},... | collective-permute-start | bytes 184328 | tf_op jit(solution)/shard_map/ppermute | solution.py:354
  48.4 7.0 %collective-permute-start.13 = (bf16[240,128]{1,0:T(8,128)(2,1)S(1)}, bf16[240,128]{1,0:T(8,128)(2,1)S(1)}, u32[]{:S(2)}, u32[]{:S(2)}) collective-permute-start(bf16[240,128]{1,0:T(8,128)(2,1)S(1)} %get-tuple-element.79), channel_id=1, source_target_pairs={{0,8},{1,9},{2,10},{3,11},{4,12},{5,13},{6,14},{7,15},{8,0},{9,1},... | collective-permute-start | bytes 184328 | tf_op jit(solution)/shard_map/ppermute | solution.py:354
  50.1 5.7 %collective-permute-start.17 = (bf16[128,128]{1,0:T(8,128)(2,1)S(1)}, bf16[128,128]{1,0:T(8,128)(2,1)S(1)}, u32[]{:S(2)}, u32[]{:S(2)}) collective-permute-start(bf16[128,128]{1,0:T(8,128)(2,1)S(1)} %fusion.19), channel_id=1, source_target_pairs={{0,8},{1,9},{2,10},{3,11},{4,12},{5,13},{6,14},{7,15},{8,0},{9,1},... | collective-permute-start | bytes 98312 | tf_op jit(solution)/shard_map/ppermute | solution.py:354
  51.3 5.3 %collective-permute-start.15 = (bf16[480,128]{1,0:T(8,128)(2,1)S(1)}, bf16[480,128]{1,0:T(8,128)(2,1)S(1)}, u32[]{:S(2)}, u32[]{:S(2)}) collective-permute-start(bf16[480,128]{1,0:T(8,128)(2,1)S(1)} %pad_maximum_fusion.2), channel_id=1, source_target_pairs={{0,2},{1,3},{2,0},{3,1},{4,6},{5,7},{6,4},{7,5},{8,10},{9,11},{10,... | collective-permute-start | bytes 368648 | tf_op jit(solution)/shard_map/ppermute | solution.py:354
  55.8 5.7 %collective-permute-start.18 = (bf16[608,128]{1,0:T(8,128)(2,1)S(1)}, bf16[608,128]{1,0:T(8,128)(2,1)S(1)}, u32[]{:S(2)}, u32[]{:S(2)}) collective-permute-start(bf16[608,128]{1,0:T(8,128)(2,1)S(1)} %pad_maximum_fusion.1), channel_id=1, source_target_pairs={{0,2},{1,3},{2,0},{3,1},{4,6},{5,7},{6,4},{7,5},{8,10},{9,11},{10,... | collective-permute-start | bytes 466952 | tf_op jit(solution)/shard_map/ppermute | solution.py:354
  61.6 2.0 %collective-permute-start.19 = (bf16[2176,128]{1,0:T(8,128)(2,1)S(1)}, bf16[2176,128]{1,0:T(8,128)(2,1)S(1)}, u32[]{:S(2)}, u32[]{:S(2)}) collective-permute-start(bf16[2176,128]{1,0:T(8,128)(2,1)S(1)} %fusion.10.mine), channel_id=1, source_target_pairs={{0,1},{1,0},{2,3},{3,2},{4,5},{5,4},{6,7},{7,6},{8,9},{9,8},{10,11... | collective-permute-start | bytes 1671176 | tf_op jit(solution)/shard_map/ppermute | solution.py:354

commit v15 on v13

--- a/solution.py
+++ b/solution.py
@@ -586,7 +586,7 @@
     outs[1] = summed(1, got_near).astype(BF)
     gots = {j: _xor(outs[j], 4 * j, n, axis) for j in (3, 2, 1)}
     beside_first = got_near[2 * piece :]
-    lead = ordered(pair, by_half(pair, chip_first), by_half(pair, beside_first))
+    lead = ordered(pair, chip_first, beside_first)
     near_lead = _xor(lead, 4, n, axis)
     mine = summed(0, _after(got_near, outs[1]))
     for j in (3, 2):
@@ -608,8 +608,6 @@
         if 2 * k < n:
             lead = ordered(index & k, lead, came)
         k *= 2
-    theirs = _xor(beyond, 2, n, axis)
-    beyond = jnp.concatenate([by(pair, beyond, theirs), by(pair, theirs, beyond)], axis=0)
     beyond = by(pair, _first_live(beside_first, beyond), beyond)
     ours = jnp.concatenate(
         [mine, others[1], others[2], others[3], x_near, x_far, beyond], axis=0

time: 65.2 us -> 66.2 us (1.015)
  starting transfers between devices: 22.9 us -> 25 us
  waiting for transfers between devices: 18.1 us -> 17.1 us
    ppermute x21 -> x20, starting transfers between devices: 22.9 us -> 25 us  [_xor(): return lax.ppermute(x, axis, [(i, i ^ k) for i in range(n)])]
    ppermute x21 -> x20, waiting for transfers between devices: 18.1 us -> 17.1 us  [_xor(): return lax.ppermute(x, axis, [(i, i ^ k) for i in range(n)])]
  transfers between devices with their start and end apart: 21 -> 20, of which waited for: 15 -> 13; matrix products, arithmetic and copies ran while one was open for 3% -> 3% of each run, Pallas kernels for 21% -> 21%
where the time goes in v15:
time: 66.2 us; the launch traced here: 66 us
  starting transfers between devices  25 us (38%)
  Pallas kernels  20.3 us (31%)
  waiting for transfers between devices  17.1 us (26%)
  other arithmetic  1.99 us (3%)
  between operations  1.57 us (2%)
    ppermute x20, starting transfers between devices, _xor(): return lax.ppermute(x, axis, [(i, i ^ k) for i in range(n)])  25 us
    ppermute x20, waiting for transfers between devices, _xor(): return lax.ppermute(x, axis, [(i, i ^ k) for i in range(n)])  17.1 us
    pallas_call x1, Pallas kernels, early_conv(): _call(_early_conv_kernel, [jax.ShapeDtypeStruct(wide, F32), jax.ShapeDtyp...  4.4 us
    pallas_call x1, Pallas kernels, early_sums(): _call(_early_sums_kernel, jax.ShapeDtypeStruct((rows, c), F32), [_SMEM, _...  3.94 us
    pallas_call x1, Pallas kernels, body(): _call(_back_kernel, jax.ShapeDtypeStruct((slots, 2, h, w, c), F32), [_SME...  3.39 us
    pallas_call x1, Pallas kernels, body(): _call(_late_kernel, [jax.ShapeDtypeStruct((h, w, c), BF), jax.ShapeDtypeS...  2.78 us
    pallas_call x1, Pallas kernels, body(): _call(_final_kernel, [jax.ShapeDtypeStruct((27 * c, c), F32), jax.ShapeDt...  2.18 us
  transfers between devices with their start and end apart: 20, of which 13 were waited for; matrix products, arithmetic and copies ran while one was open for 3% of the time, Pallas kernels for 21%

profile of v15, /device:TPU:0, one launch (start us, length us, event | category | flops | bytes accessed | tf_op | source)
XLA Modules:
  0.0 66.0 jit_solution(9619895893804547667)
XLA Ops:
  1.3 1.0 %shard_map.136 = bf16[12,64,128]{2,1,0:T(8,128)(2,1)S(1)} custom-call(s32[1]{0:T(128)S(6)} %copy.22.sc, bf16[4,2,4,64,128]{4,3,2,1,0:T(8,128)(2,1)} %frs.1, bf16[4,2,2,64,128]{4,3,2,1,0:T(8,128)(2,1)} %has.1), custom_call_target="tpu_custom_call" | custom-call | tf_op jit(solution)/shard_map/pallas_call | solution.py:435
  2.2 0.5 collective-permute-start
  2.8 0.7 %pad_add_fusion.sc = s32[7]{0:T(128)S(1)} fusion(s32[1]{0:T(128)} %bitcast.1, s32[1]{0:T(128)} %bitcast, s32[4]{0:T(128)} %param.11, s32[1]{0:T(128)S(6)} %copy.22.sc), kind=kLoop, calls=%fused_computation.58 | loop fusion | flops 21 | bytes 56 | tf_op jit(solution)/shard_map/concatenate | solution.py:417
  3.5 0.3 collective-permute-done
  3.9 2.9 %collective-permute-start.1 = (bf16[6,64,128]{2,1,0:T(8,128)(2,1)S(1)}, bf16[6,64,128]{2,1,0:T(8,128)(2,1)S(1)}, u32[]{:S(2)}, u32[]{:S(2)}) collective-permute-start(bf16[6,64,128]{2,1,0:T(8,128)(2,1)S(1)} %fusion.13), channel_id=1, source_target_pairs={{0,2},{1,3},{2,0},{3,1},{4,6},{5,7},{6,4},{7,5},{8,10},{9,11},{10,... | collective-permute-start | bytes 294920 | tf_op jit(solution)/shard_map/ppermute | solution.py:354
  6.8 4.4 %shard_map.137 = (f32[768,256]{1,0:T(8,128)S(1)}, bf16[768,128]{1,0:T(8,128)(2,1)S(1)}, bf16[2,128,128]{2,1,0:T(8,128)(2,1)S(1)}, f32[1,128]{1,0:T(1,128)S(1)}) custom-call(s32[7]{0:T(128)S(1)} %pad_add_fusion.sc, bf16[4,2,4,64,128]{4,3,2,1,0:T(8,128)(2,1)} %frs.1, bf16[4,2,2,64,128]{4,3,2,1,0:T(8,128)(2,1)} %has.1, bf16[4,1,4,64,128]{4,3,2,1,0:T(8,128)(2,1)} %cos.1, ...), custom_call_target="tpu_custom_call" | custom-call | flops 1811939328 | bytes 4194304 | tf_op jit(solution)/shard_map/pallas_call | solution.py:462
  11.2 0.0 collective-permute-done.1
  11.2 1.6 %collective-permute-start.2 = (bf16[6,64,128]{2,1,0:T(8,128)(2,1)S(1)}, bf16[6,64,128]{2,1,0:T(8,128)(2,1)S(1)}, u32[]{:S(2)}, u32[]{:S(2)}) collective-permute-start(bf16[6,64,128]{2,1,0:T(8,128)(2,1)S(1)} %fusion.14), channel_id=1, source_target_pairs={{0,4},{1,5},{2,6},{3,7},{4,0},{5,1},{6,2},{7,3},{8,12},{9,13},{10,... | collective-permute-start | bytes 294920 | tf_op jit(solution)/shard_map/ppermute | solution.py:354
  12.9 1.0 %shard_map.138 = (bf16[3,4,64,128]{3,2,1,0:T(8,128)(2,1)S(1)}, bf16[768,256]{1,0:T(8,128)(2,1)S(1)}, bf16[768,256]{1,0:T(8,128)(2,1)S(1)}) custom-call(s32[7]{0:T(128)S(1)} %pad_add_fusion.sc, f32[768,256]{1,0:T(8,128)S(1)} %get-tuple-element.40.pre_ref, bf16[768,128]{1,0:T(8,128)(2,1)S(1)} %get-tuple-element.43.gout_ref, ...), custom_call_target="tpu_custom_call" | custom-call | bytes 2097152 | tf_op jit(solution)/shard_map/pallas_call | solution.py:480
  13.9 2.1 %collective-permute-done.2 = bf16[6,64,128]{2,1,0:T(8,128)(2,1)S(1)} collective-permute-done((bf16[6,64,128]{2,1,0:T(8,128)(2,1)S(1)}, bf16[6,64,128]{2,1,0:T(8,128)(2,1)S(1)}, u32[]{:S(2)}, u32[]{:S(2)}) %collective-permute-start.2) | collective-permute-done | bytes 98336 | tf_op jit(solution)/shard_map/ppermute | solution.py:354
  16.0 2.7 %collective-permute-start.3 = (bf16[6,64,128]{2,1,0:T(8,128)(2,1)S(1)}, bf16[6,64,128]{2,1,0:T(8,128)(2,1)S(1)}, u32[]{:S(2)}, u32[]{:S(2)}) collective-permute-start(bf16[6,64,128]{2,1,0:T(8,128)(2,1)S(1)} %fusion.15), channel_id=1, source_target_pairs={{0,8},{1,9},{2,10},{3,11},{4,12},{5,13},{6,14},{7,15},{8,0},{9,1},... | collective-permute-start | bytes 294920 | tf_op jit(solution)/shard_map/ppermute | solution.py:354
  18.6 0.0 copy-start.4
  18.6 0.0 copy-start.5
  18.6 0.0 copy-start.6
  18.7 3.9 %shard_map.139.early = f32[3840,128]{1,0:T(8,128)S(1)} custom-call(s32[7]{0:T(128)S(1)} %pad_add_fusion.sc, bf16[4,2,4,64,128]{4,3,2,1,0:T(8,128)(2,1)} %frs.1, bf16[4,2,2,64,128]{4,3,2,1,0:T(8,128)(2,1)} %has.1, bf16[768,256]{1,0:T(8,128)(2,1)S(1)} %get-tuple-element.46.g_ref.g1, bf16[768,256]{1,0:T(8,128)(2,1)S(1)} %get-tuple-element.49.hid_ref, ...), custom_call_target="tpu_custom_call" | custom-call | flops 1811939328 | bytes 4194304 | tf_op jit(solution)/shard_map/pallas_call | solution.py:496
  22.6 0.0 collective-permute-done.3
  22.7 0.1 collective-permute-start.4
  22.7 1.3 %collective-permute-done.4 = bf16[6,64,128]{2,1,0:T(8,128)(2,1)S(1)} collective-permute-done((bf16[6,64,128]{2,1,0:T(8,128)(2,1)S(1)}, bf16[6,64,128]{2,1,0:T(8,128)(2,1)S(1)}, u32[]{:S(2)}, u32[]{:S(2)}) %collective-permute-start.4) | collective-permute-done | bytes 98336 | tf_op jit(solution)/shard_map/ppermute | solution.py:354
  24.1 0.1 compare_select_fusion.tail
  24.1 0.0 copy-done
  24.1 0.0 copy-done.1
  24.1 0.0 copy-done.2
  24.1 0.0 copy-done.3
  24.2 0.0 copy-done.4
  24.2 0.0 copy-done.5
  24.2 0.0 copy-done.6
  24.2 2.8 %shard_map.140 = (bf16[4,64,128]{2,1,0:T(8,128)(2,1)S(1)}, bf16[256,256]{1,0:T(8,128)(2,1)S(1)}, bf16[1920,128]{1,0:T(8,128)(2,1)S(1)}, f32[1920,128]{1,0:T(8,128)S(1)}) custom-call(s32[7]{0:T(128)S(1)} %pad_add_fusion.sc, bf16[4,2,4,64,128]{4,3,2,1,0:T(8,128)(2,1)S(1)} %copy-done.1, bf16[4,2,2,64,128]{4,3,2,1,0:T(8,128)(2,1)S(1)} %copy-done.2, ...), custom_call_target="tpu_custom_call" | custom-call | flops 1207959552 | bytes 6291456 | tf_op jit(solution)/shard_map/pallas_call | solution.py:515
  27.0 0.2 collective-permute-start.5
  27.2 1.1 %shard_map.141 = bf16[512,128]{1,0:T(8,128)(2,1)S(1)} custom-call(s32[7]{0:T(128)S(1)} %pad_add_fusion.sc, bf16[256,256]{1,0:T(8,128)(2,1)S(1)} %get-tuple-element.54.g_ref.g0, bf16[27,128,128]{2,1,0:T(8,128)(2,1)S(1)} %bitcast.16), custom_call_target="tpu_custom_call" | custom-call | flops 301989888 | bytes 1048576 | tf_op jit(solution)/shard_map/pallas_call | solution.py:533
  28.2 0.6 collective-permute-done.5.got
  28.9 0.6 shard_map.142
  29.5 0.2 collective-permute-start.6
  29.8 0.6 collective-permute-start.8
  30.3 0.6 collective-permute-done.6.got
  31.0 0.1 fusion.17
  31.0 0.9 %collective-permute-start.7 = (bf16[736,128]{1,0:T(8,128)(2,1)S(1)}, bf16[736,128]{1,0:T(8,128)(2,1)S(1)}, u32[]{:S(2)}, u32[]{:S(2)}) collective-permute-start(bf16[736,128]{1,0:T(8,128)(2,1)S(1)} %pad_maximum_fusion), channel_id=1, source_target_pairs={{0,2},{1,3},{2,0},{3,1},{4,6},{5,7},{6,4},{7,5},{8,10},{9,11},{10,... | collective-permute-start | bytes 565256 | tf_op jit(solution)/shard_map/ppermute | solution.py:354
  31.9 3.4 %shard_map.143.grad = f32[4,2,4,64,128]{4,3,2,1,0:T(8,128)S(1)} custom-call(s32[7]{0:T(128)S(1)} %pad_add_fusion.sc, bf16[256,256]{1,0:T(8,128)(2,1)S(1)} %get-tuple-element.54.g_ref.g0, bf16[768,256]{1,0:T(8,128)(2,1)S(1)} %get-tuple-element.46.g_ref.g1, bf16[27,128,128]{2,1,0:T(8,128)(2,1)S(1)} %bitcast.17), custom_call_target="tpu_custom_call" | custom-call | flops 1 | bytes 1 | tf_op jit(solution)/shard_map/pallas_call | solution.py:569
  35.3 0.6 collective-permute-done.8
  35.9 3.5 %collective-permute-start.9 = (bf16[240,128]{1,0:T(8,128)(2,1)S(1)}, bf16[240,128]{1,0:T(8,128)(2,1)S(1)}, u32[]{:S(2)}, u32[]{:S(2)}) collective-permute-start(bf16[240,128]{1,0:T(8,128)(2,1)S(1)} %get-tuple-element.80), channel_id=1, source_target_pairs={{0,12},{1,13},{2,14},{3,15},{4,8},{5,9},{6,10},{7,11},{8,4},{9,5},... | collective-permute-start | bytes 184328 | tf_op jit(solution)/shard_map/ppermute | solution.py:354
  39.5 0.0 collective-permute-start.10
  39.5 0.0 collective-permute-done.7
  39.5 1.6 %collective-permute-start.11 = (bf16[240,128]{1,0:T(8,128)(2,1)S(1)}, bf16[240,128]{1,0:T(8,128)(2,1)S(1)}, u32[]{:S(2)}, u32[]{:S(2)}) collective-permute-start(bf16[240,128]{1,0:T(8,128)(2,1)S(1)} %add_convert_fusion.1), channel_id=1, source_target_pairs={{0,4},{1,5},{2,6},{3,7},{4,0},{5,1},{6,2},{7,3},{8,12},{9,13},{10,... | collective-permute-start | bytes 184328 | tf_op jit(solution)/shard_map/ppermute | solution.py:354
  41.1 0.5 collective-permute-start.17
  41.6 0.5 collective-permute-done.9
  42.1 2.5 %collective-permute-done.10 = bf16[240,128]{1,0:T(8,128)(2,1)S(1)} collective-permute-done((bf16[240,128]{1,0:T(8,128)(2,1)S(1)}, bf16[240,128]{1,0:T(8,128)(2,1)S(1)}, u32[]{:S(2)}, u32[]{:S(2)}) %collective-permute-start.10) | collective-permute-done | bytes 61472 | tf_op jit(solution)/shard_map/ppermute | solution.py:354
  44.7 0.9 %collective-permute-done.11 = bf16[240,128]{1,0:T(8,128)(2,1)S(1)} collective-permute-done((bf16[240,128]{1,0:T(8,128)(2,1)S(1)}, bf16[240,128]{1,0:T(8,128)(2,1)S(1)}, u32[]{:S(2)}, u32[]{:S(2)}) %collective-permute-start.11) | collective-permute-done | bytes 61472 | tf_op jit(solution)/shard_map/ppermute | solution.py:354
  45.6 2.4 %collective-permute-start.14 = (bf16[240,128]{1,0:T(8,128)(2,1)S(1)}, bf16[240,128]{1,0:T(8,128)(2,1)S(1)}, u32[]{:S(2)}, u32[]{:S(2)}) collective-permute-start(bf16[240,128]{1,0:T(8,128)(2,1)S(1)} %get-tuple-element.79), channel_id=1, source_target_pairs={{0,12},{1,13},{2,14},{3,15},{4,8},{5,9},{6,10},{7,11},{8,4},{9,5},... | collective-permute-start | bytes 184328 | tf_op jit(solution)/shard_map/ppermute | solution.py:354
  48.0 0.0 collective-permute-start.13
  48.0 2.0 %collective-permute-start.12 = (bf16[240,128]{1,0:T(8,128)(2,1)S(1)}, bf16[240,128]{1,0:T(8,128)(2,1)S(1)}, u32[]{:S(2)}, u32[]{:S(2)}) collective-permute-start(bf16[240,128]{1,0:T(8,128)(2,1)S(1)} %get-tuple-element.79), channel_id=1, source_target_pairs={{0,4},{1,5},{2,6},{3,7},{4,0},{5,1},{6,2},{7,3},{8,12},{9,13},{10,... | collective-permute-start | bytes 184328 | tf_op jit(solution)/shard_map/ppermute | solution.py:354
  50.0 0.0 collective-permute-done.17
  50.1 2.4 %collective-permute-done.12 = bf16[240,128]{1,0:T(8,128)(2,1)S(1)} collective-permute-done((bf16[240,128]{1,0:T(8,128)(2,1)S(1)}, bf16[240,128]{1,0:T(8,128)(2,1)S(1)}, u32[]{:S(2)}, u32[]{:S(2)}) %collective-permute-start.12) | collective-permute-done | bytes 61472 | tf_op jit(solution)/shard_map/ppermute | solution.py:354
  52.4 3.0 %collective-permute-start.18 = (bf16[256,128]{1,0:T(8,128)(2,1)S(1)}, bf16[256,128]{1,0:T(8,128)(2,1)S(1)}, u32[]{:S(2)}, u32[]{:S(2)}) collective-permute-start(bf16[256,128]{1,0:T(8,128)(2,1)S(1)} %fusion.19), channel_id=1, source_target_pairs={{0,8},{1,9},{2,10},{3,11},{4,12},{5,13},{6,14},{7,15},{8,0},{9,1},... | collective-permute-start | bytes 196616 | tf_op jit(solution)/shard_map/ppermute | solution.py:354
  55.5 0.3 collective-permute-start.15
  55.8 0.0 collective-permute-done.14
  55.8 0.0 collective-permute-done.13
  55.8 1.9 %collective-permute-start.16 = (bf16[480,128]{1,0:T(8,128)(2,1)S(1)}, bf16[480,128]{1,0:T(8,128)(2,1)S(1)}, u32[]{:S(2)}, u32[]{:S(2)}) collective-permute-start(bf16[480,128]{1,0:T(8,128)(2,1)S(1)} %pad_maximum_fusion.2), channel_id=1, source_target_pairs={{0,2},{1,3},{2,0},{3,1},{4,6},{5,7},{6,4},{7,5},{8,10},{9,11},{10,... | collective-permute-start | bytes 368648 | tf_op jit(solution)/shard_map/ppermute | solution.py:354
  57.7 2.7 %collective-permute-done.15 = bf16[480,128]{1,0:T(8,128)(2,1)S(1)} collective-permute-done((bf16[480,128]{1,0:T(8,128)(2,1)S(1)}, bf16[480,128]{1,0:T(8,128)(2,1)S(1)}, u32[]{:S(2)}, u32[]{:S(2)}) %collective-permute-start.15) | collective-permute-done | bytes 122912 | tf_op jit(solution)/shard_map/ppermute | solution.py:354
  60.4 1.3 %collective-permute-done.16 = bf16[480,128]{1,0:T(8,128)(2,1)S(1)} collective-permute-done((bf16[480,128]{1,0:T(8,128)(2,1)S(1)}, bf16[480,128]{1,0:T(8,128)(2,1)S(1)}, u32[]{:S(2)}, u32[]{:S(2)}) %collective-permute-start.16) | collective-permute-done | bytes 122912 | tf_op jit(solution)/shard_map/ppermute | solution.py:354
  61.8 0.0 collective-permute-done.18
  61.8 0.1 fusion.16.mine
  61.8 0.1 collective-permute-start.19
  61.9 0.7 %maximum_bitcast_fusion = bf16[4,1,4,64,128]{4,3,2,1,0:T(8,128)(2,1)} fusion(bf16[3,4,64,128]{3,2,1,0:T(8,128)(2,1)S(1)} %get-tuple-element.52, bf16[1,4,64,128]{3,2,1,0:T(8,128)(2,1)S(1)} %bitcast.18), kind=kLoop, calls=%fused_computation.11 | loop fusion | flops 131072 | bytes 524288
  62.7 1.2 %collective-permute-done.19.other = bf16[2176,128]{1,0:T(8,128)(2,1)S(1)} collective-permute-done((bf16[2176,128]{1,0:T(8,128)(2,1)S(1)}, bf16[2176,128]{1,0:T(8,128)(2,1)S(1)}, u32[]{:S(2)}, u32[]{:S(2)}) %collective-permute-start.19) | collective-permute-done | bytes 557088 | tf_op jit(solution)/shard_map/ppermute | solution.py:354
  63.9 2.2 %shard_map.144 = (f32[3456,128]{1,0:T(8,128)}, f32[256,128]{1,0:T(8,128)}, f32[1,128]{1,0:T(1,128)}, f32[1,128]{1,0:T(1,128)}, bf16[4,2,4,64,128]{4,3,2,1,0:T(8,128)(2,1)}) custom-call(s32[7]{0:T(128)S(1)} %pad_add_fusion.sc, bf16[2176,128]{1,0:T(8,128)(2,1)S(1)} %fusion.16.mine, bf16[2176,128]{1,0:T(8,128)(2,1)S(1)} %collective-permute-done.19.other, ...), custom_call_target="tpu_custom_call" | custom-call | tf_op jit(solution)/shard_map/pallas_call | solution.py:616
  (24 shorter events, 0.4 us)
Async XLA Ops:
  2.2 1.6 %collective-permute-start = (bf16[12,64,128]{2,1,0:T(8,128)(2,1)S(1)}, bf16[12,64,128]{2,1,0:T(8,128)(2,1)S(1)}, u32[]{:S(2)}, u32[]{:S(2)}) collective-permute-start(bf16[12,64,128]{2,1,0:T(8,128)(2,1)S(1)} %shard_map.136), channel_id=1, source_target_pairs={{0,1},{1,0},{2,3},{3,2},{4,5},{5,4},{6,7},{7,6},{8,9},{9,8},{10,11... | collective-permute-start | bytes 589832 | tf_op jit(solution)/shard_map/ppermute | solution.py:354
  3.9 7.3 %collective-permute-start.1 = (bf16[6,64,128]{2,1,0:T(8,128)(2,1)S(1)}, bf16[6,64,128]{2,1,0:T(8,128)(2,1)S(1)}, u32[]{:S(2)}, u32[]{:S(2)}) collective-permute-start(bf16[6,64,128]{2,1,0:T(8,128)(2,1)S(1)} %fusion.13), channel_id=1, source_target_pairs={{0,2},{1,3},{2,0},{3,1},{4,6},{5,7},{6,4},{7,5},{8,10},{9,11},{10,... | collective-permute-start | bytes 294920 | tf_op jit(solution)/shard_map/ppermute | solution.py:354
  11.2 4.7 %collective-permute-start.2 = (bf16[6,64,128]{2,1,0:T(8,128)(2,1)S(1)}, bf16[6,64,128]{2,1,0:T(8,128)(2,1)S(1)}, u32[]{:S(2)}, u32[]{:S(2)}) collective-permute-start(bf16[6,64,128]{2,1,0:T(8,128)(2,1)S(1)} %fusion.14), channel_id=1, source_target_pairs={{0,4},{1,5},{2,6},{3,7},{4,0},{5,1},{6,2},{7,3},{8,12},{9,13},{10,... | collective-permute-start | bytes 294920 | tf_op jit(solution)/shard_map/ppermute | solution.py:354
  16.0 6.7 %collective-permute-start.3 = (bf16[6,64,128]{2,1,0:T(8,128)(2,1)S(1)}, bf16[6,64,128]{2,1,0:T(8,128)(2,1)S(1)}, u32[]{:S(2)}, u32[]{:S(2)}) collective-permute-start(bf16[6,64,128]{2,1,0:T(8,128)(2,1)S(1)} %fusion.15), channel_id=1, source_target_pairs={{0,8},{1,9},{2,10},{3,11},{4,12},{5,13},{6,14},{7,15},{8,0},{9,1},... | collective-permute-start | bytes 294920 | tf_op jit(solution)/shard_map/ppermute | solution.py:354
  18.6 5.5 %copy-start = (bf16[3,3,3,128,128]{4,3,2,1,0:T(8,128)(2,1)S(1)}, bf16[3,3,3,128,128]{4,3,2,1,0:T(8,128)(2,1)}, u32[]{:S(2)}) copy-start(bf16[3,3,3,128,128]{4,3,2,1,0:T(8,128)(2,1)} %param.13) | copy-start | bytes 2654212
  18.6 5.5 %copy-start.1 = (bf16[4,2,4,64,128]{4,3,2,1,0:T(8,128)(2,1)S(1)}, bf16[4,2,4,64,128]{4,3,2,1,0:T(8,128)(2,1)}, u32[]{:S(2)}) copy-start(bf16[4,2,4,64,128]{4,3,2,1,0:T(8,128)(2,1)} %frs.1) | copy-start | bytes 1572868
  18.6 5.5 %copy-start.2 = (bf16[4,2,2,64,128]{4,3,2,1,0:T(8,128)(2,1)S(1)}, bf16[4,2,2,64,128]{4,3,2,1,0:T(8,128)(2,1)}, u32[]{:S(2)}) copy-start(bf16[4,2,2,64,128]{4,3,2,1,0:T(8,128)(2,1)} %has.1) | copy-start | bytes 786436
  18.6 5.5 %copy-start.3 = (bf16[4,1,4,64,128]{4,3,2,1,0:T(8,128)(2,1)S(1)}, bf16[4,1,4,64,128]{4,3,2,1,0:T(8,128)(2,1)}, u32[]{:S(2)}) copy-start(bf16[4,1,4,64,128]{4,3,2,1,0:T(8,128)(2,1)} %cos.1) | copy-start | bytes 786436
  18.6 5.5 %copy-start.4 = (bf16[2,128,128]{2,1,0:T(8,128)(2,1)S(1)}, bf16[2,128,128]{2,1,0:T(8,128)(2,1)}, u32[]{:S(2)}) copy-start(bf16[2,128,128]{2,1,0:T(8,128)(2,1)} %sw.1) | copy-start | bytes 196612
  18.6 5.5 %copy-start.5 = (f32[128]{0:T(128)S(1)}, f32[128]{0:T(128)}, u32[]{:S(2)}) copy-start(f32[128]{0:T(128)} %param.14) | copy-start | bytes 1540
  18.6 5.5 %copy-start.6 = (f32[128]{0:T(128)S(1)}, f32[128]{0:T(128)}, u32[]{:S(2)}) copy-start(f32[128]{0:T(128)} %param.16) | copy-start | bytes 1540
  22.7 1.4 %collective-permute-start.4 = (bf16[6,64,128]{2,1,0:T(8,128)(2,1)S(1)}, bf16[6,64,128]{2,1,0:T(8,128)(2,1)S(1)}, u32[]{:S(2)}, u32[]{:S(2)}) collective-permute-start(bf16[6,64,128]{2,1,0:T(8,128)(2,1)S(1)} %fusion.2), channel_id=1, source_target_pairs={{0,1},{1,0},{2,3},{3,2},{4,5},{5,4},{6,7},{7,6},{8,9},{9,8},{10,11... | collective-permute-start | bytes 294920 | tf_op jit(solution)/shard_map/ppermute | solution.py:354
  27.0 1.9 %collective-permute-start.5 = (bf16[1920,128]{1,0:T(8,128)(2,1)S(1)}, bf16[1920,128]{1,0:T(8,128)(2,1)S(1)}, u32[]{:S(2)}, u32[]{:S(2)}) collective-permute-start(bf16[1920,128]{1,0:T(8,128)(2,1)S(1)} %get-tuple-element.56), channel_id=1, source_target_pairs={{0,1},{1,0},{2,3},{3,2},{4,5},{5,4},{6,7},{7,6},{8,9},{9,8},{10,11... | collective-permute-start | bytes 1474568 | tf_op jit(solution)/shard_map/ppermute | solution.py:354
  29.5 1.4 %collective-permute-start.6 = (bf16[512,128]{1,0:T(8,128)(2,1)S(1)}, bf16[512,128]{1,0:T(8,128)(2,1)S(1)}, u32[]{:S(2)}, u32[]{:S(2)}) collective-permute-start(bf16[512,128]{1,0:T(8,128)(2,1)S(1)} %shard_map.141), channel_id=1, source_target_pairs={{0,1},{1,0},{2,3},{3,2},{4,5},{5,4},{6,7},{7,6},{8,9},{9,8},{10,11... | collective-permute-start | bytes 393224 | tf_op jit(solution)/shard_map/ppermute | solution.py:354
  29.8 6.1 %collective-permute-start.8 = (bf16[480,128]{1,0:T(8,128)(2,1)S(1)}, bf16[480,128]{1,0:T(8,128)(2,1)S(1)}, u32[]{:S(2)}, u32[]{:S(2)}) collective-permute-start(bf16[480,128]{1,0:T(8,128)(2,1)S(1)} %get-tuple-element.60), channel_id=1, source_target_pairs={{0,2},{1,3},{2,0},{3,1},{4,6},{5,7},{6,4},{7,5},{8,10},{9,11},{10,... | collective-permute-start | bytes 368648 | tf_op jit(solution)/shard_map/ppermute | solution.py:354
  31.0 8.4 %collective-permute-start.7 = (bf16[736,128]{1,0:T(8,128)(2,1)S(1)}, bf16[736,128]{1,0:T(8,128)(2,1)S(1)}, u32[]{:S(2)}, u32[]{:S(2)}) collective-permute-start(bf16[736,128]{1,0:T(8,128)(2,1)S(1)} %pad_maximum_fusion), channel_id=1, source_target_pairs={{0,2},{1,3},{2,0},{3,1},{4,6},{5,7},{6,4},{7,5},{8,10},{9,11},{10,... | collective-permute-start | bytes 565256 | tf_op jit(solution)/shard_map/ppermute | solution.py:354
  35.9 6.2 %collective-permute-start.9 = (bf16[240,128]{1,0:T(8,128)(2,1)S(1)}, bf16[240,128]{1,0:T(8,128)(2,1)S(1)}, u32[]{:S(2)}, u32[]{:S(2)}) collective-permute-start(bf16[240,128]{1,0:T(8,128)(2,1)S(1)} %get-tuple-element.80), channel_id=1, source_target_pairs={{0,12},{1,13},{2,14},{3,15},{4,8},{5,9},{6,10},{7,11},{8,4},{9,5},... | collective-permute-start | bytes 184328 | tf_op jit(solution)/shard_map/ppermute | solution.py:354
  39.5 5.2 %collective-permute-start.10 = (bf16[240,128]{1,0:T(8,128)(2,1)S(1)}, bf16[240,128]{1,0:T(8,128)(2,1)S(1)}, u32[]{:S(2)}, u32[]{:S(2)}) collective-permute-start(bf16[240,128]{1,0:T(8,128)(2,1)S(1)} %get-tuple-element.81), channel_id=1, source_target_pairs={{0,8},{1,9},{2,10},{3,11},{4,12},{5,13},{6,14},{7,15},{8,0},{9,1},... | collective-permute-start | bytes 184328 | tf_op jit(solution)/shard_map/ppermute | solution.py:354
  39.5 6.0 %collective-permute-start.11 = (bf16[240,128]{1,0:T(8,128)(2,1)S(1)}, bf16[240,128]{1,0:T(8,128)(2,1)S(1)}, u32[]{:S(2)}, u32[]{:S(2)}) collective-permute-start(bf16[240,128]{1,0:T(8,128)(2,1)S(1)} %add_convert_fusion.1), channel_id=1, source_target_pairs={{0,4},{1,5},{2,6},{3,7},{4,0},{5,1},{6,2},{7,3},{8,12},{9,13},{10,... | collective-permute-start | bytes 184328 | tf_op jit(solution)/shard_map/ppermute | solution.py:354
  41.1 8.9 %collective-permute-start.17 = (bf16[256,128]{1,0:T(8,128)(2,1)S(1)}, bf16[256,128]{1,0:T(8,128)(2,1)S(1)}, u32[]{:S(2)}, u32[]{:S(2)}) collective-permute-start(bf16[256,128]{1,0:T(8,128)(2,1)S(1)} %fusion.18), channel_id=1, source_target_pairs={{0,4},{1,5},{2,6},{3,7},{4,0},{5,1},{6,2},{7,3},{8,12},{9,13},{10,... | collective-permute-start | bytes 196616 | tf_op jit(solution)/shard_map/ppermute | solution.py:354
  45.6 10.2 %collective-permute-start.14 = (bf16[240,128]{1,0:T(8,128)(2,1)S(1)}, bf16[240,128]{1,0:T(8,128)(2,1)S(1)}, u32[]{:S(2)}, u32[]{:S(2)}) collective-permute-start(bf16[240,128]{1,0:T(8,128)(2,1)S(1)} %get-tuple-element.79), channel_id=1, source_target_pairs={{0,12},{1,13},{2,14},{3,15},{4,8},{5,9},{6,10},{7,11},{8,4},{9,5},... | collective-permute-start | bytes 184328 | tf_op jit(solution)/shard_map/ppermute | solution.py:354
  48.0 7.8 %collective-permute-start.13 = (bf16[240,128]{1,0:T(8,128)(2,1)S(1)}, bf16[240,128]{1,0:T(8,128)(2,1)S(1)}, u32[]{:S(2)}, u32[]{:S(2)}) collective-permute-start(bf16[240,128]{1,0:T(8,128)(2,1)S(1)} %get-tuple-element.79), channel_id=1, source_target_pairs={{0,8},{1,9},{2,10},{3,11},{4,12},{5,13},{6,14},{7,15},{8,0},{9,1},... | collective-permute-start | bytes 184328 | tf_op jit(solution)/shard_map/ppermute | solution.py:354
  48.0 4.5 %collective-permute-start.12 = (bf16[240,128]{1,0:T(8,128)(2,1)S(1)}, bf16[240,128]{1,0:T(8,128)(2,1)S(1)}, u32[]{:S(2)}, u32[]{:S(2)}) collective-permute-start(bf16[240,128]{1,0:T(8,128)(2,1)S(1)} %get-tuple-element.79), channel_id=1, source_target_pairs={{0,4},{1,5},{2,6},{3,7},{4,0},{5,1},{6,2},{7,3},{8,12},{9,13},{10,... | collective-permute-start | bytes 184328 | tf_op jit(solution)/shard_map/ppermute | solution.py:354
  52.4 9.3 %collective-permute-start.18 = (bf16[256,128]{1,0:T(8,128)(2,1)S(1)}, bf16[256,128]{1,0:T(8,128)(2,1)S(1)}, u32[]{:S(2)}, u32[]{:S(2)}) collective-permute-start(bf16[256,128]{1,0:T(8,128)(2,1)S(1)} %fusion.19), channel_id=1, source_target_pairs={{0,8},{1,9},{2,10},{3,11},{4,12},{5,13},{6,14},{7,15},{8,0},{9,1},... | collective-permute-start | bytes 196616 | tf_op jit(solution)/shard_map/ppermute | solution.py:354
  55.5 4.9 %collective-permute-start.15 = (bf16[480,128]{1,0:T(8,128)(2,1)S(1)}, bf16[480,128]{1,0:T(8,128)(2,1)S(1)}, u32[]{:S(2)}, u32[]{:S(2)}) collective-permute-start(bf16[480,128]{1,0:T(8,128)(2,1)S(1)} %pad_maximum_fusion.1), channel_id=1, source_target_pairs={{0,2},{1,3},{2,0},{3,1},{4,6},{5,7},{6,4},{7,5},{8,10},{9,11},{10,... | collective-permute-start | bytes 368648 | tf_op jit(solution)/shard_map/ppermute | solution.py:354
  55.8 6.0 %collective-permute-start.16 = (bf16[480,128]{1,0:T(8,128)(2,1)S(1)}, bf16[480,128]{1,0:T(8,128)(2,1)S(1)}, u32[]{:S(2)}, u32[]{:S(2)}) collective-permute-start(bf16[480,128]{1,0:T(8,128)(2,1)S(1)} %pad_maximum_fusion.2), channel_id=1, source_target_pairs={{0,2},{1,3},{2,0},{3,1},{4,6},{5,7},{6,4},{7,5},{8,10},{9,11},{10,... | collective-permute-start | bytes 368648 | tf_op jit(solution)/shard_map/ppermute | solution.py:354
  61.8 2.0 %collective-permute-start.19 = (bf16[2176,128]{1,0:T(8,128)(2,1)S(1)}, bf16[2176,128]{1,0:T(8,128)(2,1)S(1)}, u32[]{:S(2)}, u32[]{:S(2)}) collective-permute-start(bf16[2176,128]{1,0:T(8,128)(2,1)S(1)} %fusion.16.mine), channel_id=1, source_target_pairs={{0,1},{1,0},{2,3},{3,2},{4,5},{5,4},{6,7},{7,6},{8,9},{9,8},{10,11... | collective-permute-start | bytes 1671176 | tf_op jit(solution)/shard_map/ppermute | solution.py:354
